TPU v7x, 256 devices: a whole 4x4x8 slice. The times are simulated.
256 devices in a mesh: ctx: 64 (over x, z, core), head: 4 (over y).
Axes of the slice: x: 4, y: 4, z: 8, core: 2. Of those that a mesh axis runs over, the one named last changes fastest.
Arguments:
- tokens_in: bfloat16 [16384, 2048], P('ctx'), may hold values from -6 to 6
- w_qkv: bfloat16 [3, 2048, 2048], P(None, None, 'head'), may hold values from -0.125 to 0.125
- conv_weight: float32 [3, 4, 2048], P(None, None, 'head'), may hold values from -2.5 to 2.5
- beta_weight: bfloat16 [16, 2048], P('head'), may hold values from -0.125 to 0.125
- beta_bias: float32 [16], P('head'), may hold values from -4 to 1
- norm_gain: float32 [2048], P('head'), may hold values from 0.1 to 1.9
- w_out: bfloat16 [2048, 2048], P('head'), may hold values from -0.125 to 0.125
Outputs:
- layer_out: bfloat16 [16384, 2048], P(('ctx', 'head'))
All inputs are finite; a program needn't handle non-finite values.
Results may differ from a plain program's by a relative error of at most 0.019.
Values may be sent and summed in bfloat16 or wider, within the bound.
No kernel may reach another device: no remote copies, remote signals or barrier semaphores. Data moves between devices by JAX's collectives and lax.ppermute only.
A program may use at most 128 MiB of HBM per device.

v0:
```python
import jax
import jax.numpy as jnp
from jax import lax
from jax.sharding import PartitionSpec as P

DK = 128
BLOCK = 128


precise = lax.Precision.HIGHEST


def carried_in(x, axis, combine, identity):
    peers, mine = (lax.axis_size(axis), lax.axis_index(axis))
    everything = jax.tree.map(
        lambda part, kind: lax.all_gather(part.astype(kind), axis), x, (jnp.bfloat16, jnp.bfloat16)
    )
    start = jax.tree.map(
        lambda part, zero: jnp.broadcast_to(jnp.asarray(zero, part.dtype), part.shape), x, identity
    )

    def hop(k, before):
        reached = k < mine
        new = combine(
            before, jax.tree.map(lambda part, own: part[k].astype(own.dtype), everything, x)
        )
        return jax.tree.map(lambda a, b: jnp.where(reached, a, b), new, before)

    return lax.fori_loop(0, peers, hop, start)


def passed_along(x, axis, by):
    peers = lax.axis_size(axis)
    pairs = [(i, i + by) for i in range(peers) if 0 <= i + by < peers]
    return lax.ppermute(x, axis, pairs)


def unit_rows(vector):
    return vector / jnp.sqrt(jnp.sum(vector * vector, axis=-1, keepdims=True) + 1e-06)


def block_terms(queries, keys, values, betas):
    size = keys.shape[-2]
    width = keys.shape[-1]
    strict = jnp.tril(jnp.ones((size, size), jnp.float32), -1)
    inclusive = jnp.tril(jnp.ones((size, size), jnp.float32))
    gram = jnp.einsum("...ik,...jk->...ij", keys, keys, precision=precise)
    system = jnp.eye(size, dtype=jnp.float32) + betas[..., :, None] * gram * strict
    weighted = betas[..., :, None] * jnp.concatenate([values, keys], axis=-1)
    solved = jax.scipy.linalg.solve_triangular(system, weighted, lower=True, unit_diagonal=True)
    scores = jnp.einsum("...ik,...jk->...ij", queries, keys, precision=precise) * inclusive
    return (solved[..., :width], solved[..., width:], scores)


def run_blocks(start, u_terms, w_terms, keys, queries, scores, want_out):

    def advance(state, items):
        u_block, w_block, key_block, query_block, score_block = items
        delta = u_block - jnp.einsum("hck,hrk->hcr", w_block, state, precision=precise)
        new_state = state + jnp.einsum("hcr,hck->hrk", delta, key_block, precision=precise)
        if want_out:
            result = jnp.einsum("hck,hrk->hcr", query_block, state, precision=precise)
            result = result + jnp.einsum("hcj,hjr->hcr", score_block, delta, precision=precise)
            return (new_state, result)
        return (new_state, None)

    return lax.scan(advance, start, (u_terms, w_terms, keys, queries, scores))


def combine(earlier, later):
    product = jnp.einsum("hij,hjk->hik", earlier[0], later[0], precision=precise)
    carried = jnp.einsum("hij,hjk->hik", earlier[1], later[0], precision=precise) + later[1]
    return (product, carried)


def combine_shards(local_map, local_state, identity, zero_state):
    prefix = carried_in((local_map, local_state), "ctx", combine, (identity, zero_state))
    return prefix[1]


def per_device(tokens_in, w_qkv, conv_weight, beta_weight, beta_bias, norm_gain, w_out):
    length = tokens_in.shape[0]
    heads_here = beta_weight.shape[0]
    taps = conv_weight.shape[1]
    count = length // BLOCK
    projected = jnp.einsum(
        "td,sdc->stc", tokens_in, w_qkv, preferred_element_type=jnp.float32
    ).astype(jnp.bfloat16)
    border = passed_along(projected[:, length - (taps - 1) :, :], "ctx", 1)
    padded = jnp.concatenate([border, projected], axis=1).astype(jnp.float32)
    total = jnp.zeros(projected.shape, jnp.float32)
    for offset in range(taps):
        total = total + conv_weight[:, offset, None, :] * padded[:, offset : offset + length]
    mixed = jax.nn.silu(total)

    def to_blocks(array):
        return array.reshape(count, BLOCK, heads_here, DK).transpose(0, 2, 1, 3)

    queries = to_blocks(unit_rows(mixed[0].reshape(length, heads_here, DK)))
    keys = to_blocks(unit_rows(mixed[1].reshape(length, heads_here, DK)))
    values = to_blocks(mixed[2].reshape(length, heads_here, DK))
    logits = (
        jnp.dot(tokens_in, beta_weight.T, preferred_element_type=jnp.float32) + beta_bias[None, :]
    )
    betas = jax.nn.sigmoid(logits).reshape(count, BLOCK, heads_here).transpose(0, 2, 1)
    u_terms, w_terms, scores = block_terms(queries, keys, values, betas)
    identity = jnp.broadcast_to(jnp.eye(DK, dtype=jnp.float32), (heads_here, DK, DK))
    zero_state = jnp.zeros((heads_here, DK, DK), jnp.float32)
    stacked_start = jnp.concatenate([zero_state, identity], axis=1)
    stacked_terms = jnp.concatenate([u_terms, jnp.zeros_like(u_terms)], axis=-1)
    ends, _ = run_blocks(stacked_start, stacked_terms, w_terms, keys, queries, scores, False)
    start_state = combine_shards(ends[:, DK:], ends[:, :DK], identity, zero_state)
    _, outputs = run_blocks(start_state, u_terms, w_terms, keys, queries, scores, True)
    gain = norm_gain.reshape(heads_here, DK)[None, :, None, :]
    normed = outputs * lax.rsqrt(jnp.mean(outputs * outputs, axis=-1, keepdims=True) + 1e-06) * gain
    normed = normed.transpose(0, 2, 1, 3).reshape(length, heads_here * DK).astype(jnp.bfloat16)
    return lax.psum_scatter(
        jnp.dot(normed, w_out, preferred_element_type=jnp.float32).astype(jnp.bfloat16),
        "head",
        scatter_dimension=0,
        tiled=True,
    )


def solution(mesh):
    return jax.shard_map(
        per_device,
        mesh=mesh,
        in_specs=(
            P("ctx", None),
            P(None, None, "head"),
            P(None, None, "head"),
            P("head", None),
            P("head"),
            P("head"),
            P("head", None),
        ),
        out_specs=P(("ctx", "head"), None),
        check_vma=False,
    )
```

profile of v0, /device:TPU:1, one launch (start us, length us, event | category | flops | bytes accessed | tf_op | source)
XLA Modules:
  0.0 589.4 jit_solution(17493922851801470339)
XLA Ops:
  6.6 5.0 fusion.33
  11.7 4.9 collective-permute-start
  23.0 2.0 reshape_squeeze.6
  26.3 2.0 fusion.38
  28.3 80.0 %custom-call.4 = f32[2,4,1,128,128]{3,4,2,1,0:T(8,128)} custom-call(f32[2,4,1,128,128]{4,3,2,1,0:T(8,128)} %fusion.38), custom_call_target="InvertDiagBlocksLowerTriangular" | custom-call | tf_op jit(solution)/shard_map/jit(_solve_triangular)/vmap(vmap())/triangular_solve | solution.py:50
  108.4 2.0 reshape_reshape_squeeze.3
  111.5 3.3 broadcast_select_fusion
  115.8 5.6 while.39
  127.2 2.0 convolution_multiply_fusion
  129.2 79.9 %all-gather.5.cloned.1.call-done = bf16[256,128,128]{2,1,0:T(8,128)(2,1)} async-done(((bf16[4,128,128]{2,1,0:T(8,128)(2,1)}), bf16[256,128,128]{2,1,0:T(8,128)(2,1)}) %all-gather.5.cloned.1.call-update) | async-done | bytes 8388624 | tf_op jit(solution)/shard_map/all_gather | solution.py:16
  209.1 83.1 %all-gather.7.cloned.1.call-done = bf16[256,128,128]{2,1,0:T(8,128)(2,1)} async-done(((bf16[4,128,128]{2,1,0:T(8,128)(2,1)}), bf16[256,128,128]{2,1,0:T(8,128)(2,1)}) %all-gather.7.cloned.1.call-update) | async-done | bytes 8388624 | tf_op jit(solution)/shard_map/all_gather | solution.py:16
  292.2 253.0 %while.41 = (s32[]{:T(128)}, f32[4,128,128]{1,2,0:T(8,128)}, s32[]{:T(128)}, bf16[64,4,128,128]{3,2,1,0:T(8,128)(2,1)}, bf16[64,4,128,128]{3,2,1,0:T(8,128)(2,1)}) while((s32[]{:T(128)}, f32[4,128,128]{1,2,0:T(8,128)}, s32[]{:T(128)}, bf16[64,4,128,128]{3,2,1,0:T(8,128)(2,1)}, ...), condition=%wide.region_4.5_spmd.clone.clone, body=%wide.region_3.4_spmd.clone.sunk.clone | while | flops 100990976 | bytes 2099283 | solution.py:29
  294.2 1.9 fusion.126
  302.1 1.9 fusion.126
  306.1 1.9 fusion.126
  310.0 1.9 fusion.126
  314.0 1.9 fusion.126
  318.0 1.9 fusion.126
  321.9 1.9 fusion.126
  329.8 1.9 fusion.126
  333.8 1.9 fusion.126
  337.7 1.9 fusion.126
  341.7 1.9 fusion.126
  345.6 1.9 fusion.126
  349.6 1.9 fusion.126
  357.5 1.9 fusion.126
  361.4 1.9 fusion.126
  365.4 1.9 fusion.126
  369.3 1.9 fusion.126
  373.3 1.9 fusion.126
  377.2 1.9 fusion.126
  385.1 1.9 fusion.126
  389.1 1.9 fusion.126
  393.0 1.9 fusion.126
  397.0 1.9 fusion.126
  400.9 1.9 fusion.126
  404.9 1.9 fusion.126
  412.8 1.9 fusion.126
  416.7 1.9 fusion.126
  420.7 1.9 fusion.126
  424.7 1.9 fusion.126
  428.6 1.9 fusion.126
  432.6 1.9 fusion.126
  440.5 1.9 fusion.126
  444.4 1.9 fusion.126
  448.4 1.9 fusion.126
  452.3 1.9 fusion.126
  456.3 1.9 fusion.126
  460.2 1.9 fusion.126
  468.1 1.9 fusion.126
  472.1 1.9 fusion.126
  476.0 1.9 fusion.126
  480.0 1.9 fusion.126
  483.9 1.9 fusion.126
  487.9 1.9 fusion.126
  503.7 1.9 fusion.126
  511.6 1.9 fusion.126
  515.5 1.9 fusion.126
  531.4 1.9 fusion.126
  535.3 1.9 fusion.126
  539.3 1.9 fusion.126
  543.2 1.9 fusion.126
  546.3 10.4 %while.40 = (s32[]{:T(128)}, f32[4,128,128]{2,1,0:T(8,128)S(1)}, f32[2,4,128,128]{3,2,1,0:T(8,128)}, f32[2,4,128,128]{3,2,1,0:T(8,128)}, f32[2,4,128,128]{3,2,1,...) while((s32[]{:T(128)}, f32[4,128,128]{2,1,0:T(8,128)S(1)}, ...), condition=%wide.region_7.8_spmd.clone, body=%wide.region_6.7_spmd.sunk.clone | while | flops 402849792 | bytes 10226349 | solution.py:67
  561.2 21.7 %reduce-scatter.2.cloned.1.call-done = bf16[64,2048]{1,0:T(8,128)(2,1)} async-done(((bf16[256,2048]{1,0:T(8,128)(2,1)}), bf16[64,2048]{1,0:T(8,128)(2,1)}) %reduce-scatter.2.cloned.1.call-update) | async-done | bytes 262160 | tf_op jit(solution)/shard_map/reduce_scatter | solution.py:117
  (297 shorter events, 191.8 us)
Async XLA Ops:
  6.5 552.9 %copy-start = (bf16[512,2048]{1,0:T(8,128)(2,1)S(1)}, bf16[512,2048]{1,0:T(8,128)(2,1)}, u32[]{:S(2)}) copy-start(bf16[512,2048]{1,0:T(8,128)(2,1)} %param.19) | copy-start | bytes 6291460
  6.5 10.3 %copy-start.9 = (f32[3,4,512]{2,1,0:T(4,128)S(1)}, f32[3,4,512]{2,1,0:T(4,128)}, u32[]{:S(2)}) copy-start(f32[3,4,512]{2,1,0:T(4,128)} %param.15) | copy-start | bytes 73732
  6.5 10.3 %copy-start.10 = (bf16[4,2048]{1,0:T(4,128)(2,1)S(1)}, bf16[4,2048]{1,0:T(4,128)(2,1)}, u32[]{:S(2)}) copy-start(bf16[4,2048]{1,0:T(4,128)(2,1)} %param.16) | copy-start | bytes 49156
  6.5 10.3 %copy-start.12 = (f32[4]{0:T(128)S(1)}, f32[4]{0:T(128)}, u32[]{:S(2)}) copy-start(f32[4]{0:T(128)} %param.17) | copy-start | bytes 52
  6.5 202.5 %all-gather.5.cloned.1.call-start = ((), (), s32[]{:S(2)}) async-start(), calls=%async_computation.2 | async-start | bytes 8519680 | tf_op jit(solution)/shard_map/all_gather | solution.py:16
  6.6 10.3 %copy-start.6 = (bf16[256,2048]{1,0:T(8,128)(2,1)S(1)}, bf16[256,2048]{1,0:T(8,128)(2,1)}, u32[]{:S(2)}) copy-start(bf16[256,2048]{1,0:T(8,128)(2,1)} %param.13) | copy-start | bytes 3145732
  11.6 5.7 copy-start.7
  11.7 5.8 collective-permute-start
  17.3 1.1 copy-start.8
  26.3 85.2 %copy-start.13 = (pred[256]{0:T(512)(128)(4,1)S(1)}, pred[256]{0:T(512)(128)(4,1)}, u32[]{:S(2)}) copy-start(pred[256]{0:T(512)(128)(4,1)} %constant.77.clone.1) | copy-start | bytes 772
  122.3 169.9 %all-gather.7.cloned.1.call-start = ((), (), s32[]{:S(2)}) async-start(), calls=%async_computation.3 | async-start | bytes 8519680 | tf_op jit(solution)/shard_map/all_gather | solution.py:16
  123.0 459.9 %reduce-scatter.2.cloned.1.call-start = ((), (), s32[]{:S(2)}) async-start(), calls=%async_computation.1 | async-start | bytes 1310720 | tf_op jit(solution)/shard_map/reduce_scatter | solution.py:117
  126.4 0.8 copy-start.2
  292.2 254.1 %copy-start.1 = (f32[2,4,128,128]{3,2,1,0:T(8,128)S(1)}, f32[2,4,128,128]{3,2,1,0:T(8,128)}, u32[]{:S(2)}) copy-start(f32[2,4,128,128]{3,2,1,0:T(8,128)} %get-tuple-element.510) | copy-start | bytes 1572868
  546.2 11.7 %copy-start.11 = (f32[512]{0:T(512)S(1)}, f32[512]{0:T(512)}, u32[]{:S(2)}) copy-start(f32[512]{0:T(512)} %param.18) | copy-start | bytes 6148
  546.3 3.4 copy-start.3
  546.3 3.3 copy-start.4
  550.0 0.8 copy-start.5
  551.5 3.4 copy-start.3
  551.5 3.4 copy-start.4
  555.2 0.8 copy-start.5
Sparse Core Ops, SparseCore 0:
  122.4 86.6 all-gather.4
  211.9 80.2 all-gather.6
  561.3 21.5 reduce-scatter.1
where the time goes:
time: 595 us; the launch traced here: 589 us
  waiting for transfers between devices  185 us (31%)
  matrix products  153 us (26%)
  local copies, waits for them, and re-layouts  143 us (24%)
  other arithmetic  87.8 us (15%)
  between operations  13.5 us (2%)
    all_gather x2, waiting for transfers between devices, carried_in(): lax.all_gather(part.astype(kind), axis)  163 us
    dot_general x64, matrix products, combine(): jnp.einsum('hij,hjk->hik', earlier[1], later[0], precision=precise)  124 us
    another operation x5, other arithmetic, block_terms(): jax.scipy.linalg.solve_triangular(system, weighted, lower=True, unit_diag...  80.1 us
    dynamic_slice x128, local copies, waits for them, and re-layouts, hop(): part[k].astype(own.dtype)  66.9 us
    while x76, local copies, waits for them, and re-layouts  62.6 us
    reduce_scatter x1, waiting for transfers between devices, per_device(): lax.psum_scatter(jnp.dot(normed, w_out, preferred_element_type=jnp.float3...  21.7 us
  transfers between devices with their start and end apart: 4, of which 3 were waited for; matrix products, arithmetic and copies ran while one was open for 1% of the time, Pallas kernels for 0%

commit v1 on v0

v1 whole, which is shorter than its diff:
```python
import functools

import jax
import jax.numpy as jnp
from jax import lax
from jax.experimental import pallas as pl
from jax.experimental.pallas import tpu as pltpu
from jax.sharding import PartitionSpec as P

DK = 128
BLOCK = 128
WIDTH = 2 * BLOCK
EDGE = 16
EPS = 1e-06
FAN = 4

f32 = jnp.float32
bf16 = jnp.bfloat16


def dot(a, b):
    return lax.dot_general(a, b, (((1,), (0,)), ((), ())), preferred_element_type=f32)


def dot_t(a, b):
    return lax.dot_general(a, b, (((1,), (1,)), ((), ())), preferred_element_type=f32)


def params(megabytes=48):
    return pltpu.CompilerParams(vmem_limit_bytes=megabytes << 20)


def whole(count):
    return [pl.BlockSpec(memory_space=pltpu.VMEM)] * count


def shape(dims, kind):
    return jax.ShapeDtypeStruct(dims, kind)


def project_kernel(tokens_ref, w_ref, beta_w_ref, beta_b_ref, out_ref, edge_ref, betas_ref):
    length = tokens_ref.shape[0]
    result = dot(tokens_ref[...], w_ref[0]).astype(bf16)
    out_ref[0] = result
    edge_ref[0] = result[length - EDGE :]

    @pl.when((pl.program_id(0) == 0) & (pl.program_id(1) == 0))
    def _():
        logits = dot_t(tokens_ref[...], beta_w_ref[...]) + beta_b_ref[...]
        betas_ref[...] = 1.0 / (1.0 + jnp.exp(-logits))


def project(tokens, w_qkv, beta_weight, beta_bias):
    length, depth = tokens.shape
    columns = w_qkv.shape[2]
    heads = beta_weight.shape[0]
    part = columns // 2
    return pl.pallas_call(
        project_kernel,
        grid=(3, 2),
        in_specs=[
            pl.BlockSpec((length, depth), lambda s, n: (0, 0)),
            pl.BlockSpec((1, depth, part), lambda s, n: (s, 0, n)),
            pl.BlockSpec((heads, depth), lambda s, n: (0, 0)),
            pl.BlockSpec((1, heads), lambda s, n: (0, 0)),
        ],
        out_specs=[
            pl.BlockSpec((1, length, part), lambda s, n: (s, 0, n)),
            pl.BlockSpec((1, EDGE, part), lambda s, n: (s, 0, n)),
            pl.BlockSpec((length, heads), lambda s, n: (0, 0)),
        ],
        out_shape=[
            shape((3, length, columns), bf16),
            shape((3, EDGE, columns), bf16),
            shape((length, heads), f32),
        ],
        compiler_params=params(),
        name="project",
    )(tokens, w_qkv, beta_weight, beta_bias[None, :])


def grid_index(rows, columns):
    row = lax.broadcasted_iota(jnp.int32, (rows, columns), 0)
    column = lax.broadcasted_iota(jnp.int32, (rows, columns), 1)
    return row, column


def on_diagonal(pair, left):
    zero = jnp.zeros_like(pair)
    return jnp.concatenate([jnp.where(left, pair, zero), jnp.where(left, zero, pair)], axis=0)


def inverse_pairs(systems):
    row, wide = grid_index(BLOCK, 2 * BLOCK)
    column = wide % BLOCK
    left = wide < BLOCK
    eye = jnp.where(row == column, 1.0, 0.0).astype(f32)

    def below(size):
        same = (row // (2 * size)) == (column // (2 * size))
        return same & ((row % (2 * size)) >= size) & ((column % (2 * size)) < size)

    found = [eye - jnp.where(below(1), system, 0.0) for system in systems]
    size = 2
    while size < BLOCK:
        mask = below(size)
        steps = [jnp.where(mask, system, 0.0).astype(bf16) for system in systems]
        small = [x.astype(bf16) for x in found]
        half = [dot(x, on_diagonal(n, left)).astype(bf16) for x, n in zip(small, steps)]
        found = [
            x - dot(y, on_diagonal(b, left)) for x, y, b in zip(found, half, small)
        ]
        size *= 2
    small = [x.astype(bf16) for x in found]
    high = [system.astype(bf16) for system in systems]
    low = [(system - h.astype(f32)).astype(bf16) for system, h in zip(systems, high)]
    rest = [
        (eye - x.astype(f32)) - dot(x, on_diagonal(h, left)) - dot(x, on_diagonal(l, left))
        for x, h, l in zip(small, high, low)
    ]
    fixed = [
        x.astype(f32) + dot(r.astype(bf16), on_diagonal(x, left)) for x, r in zip(small, rest)
    ]
    return [x - eye for x in fixed]


def local_kernel(
    proj_ref, edge_ref, conv_ref, betas_ref,
    queries_ref, keys_t_ref, uw_ref, map0, map1, map2, map3, padded, maps
):
    length = proj_ref.shape[1]
    heads = betas_ref.shape[1]
    me = lax.axis_index("ctx") % FAN
    for s in range(3):
        padded[s, :EDGE] = edge_ref[s].astype(f32)
        padded[s, EDGE:] = proj_ref[s].astype(f32)
    row, column = grid_index(length, length)
    strict = row > column
    systems, corners, right, keys_t = [], [], [], []
    for h in range(heads):
        lanes = slice(h * DK, (h + 1) * DK)
        mixed = []
        for s in range(3):
            total = jnp.zeros((length, DK), f32)
            for j in range(4):
                start = EDGE - 3 + j
                total = total + conv_ref[s, j : j + 1, lanes] * padded[s, start : start + length, lanes]
            mixed.append(total / (1.0 + jnp.exp(-total)))
        query, key, value = mixed
        query = query * lax.rsqrt(jnp.sum(query * query, axis=-1, keepdims=True) + EPS)
        key = key * lax.rsqrt(jnp.sum(key * key, axis=-1, keepdims=True) + EPS)
        queries_ref[:, lanes] = query.astype(bf16)
        small = key.astype(bf16)
        small_t = key.T.astype(bf16)
        keys_t_ref[h] = small_t
        keys_t.append(small_t)
        beta = betas_ref[:, h : h + 1]
        system = jnp.where(strict, beta * dot(small, small_t), 0.0)
        systems.append(jnp.concatenate([system[:BLOCK, :BLOCK], system[BLOCK:, BLOCK:]], axis=1))
        corners.append(system[BLOCK:, :BLOCK].astype(bf16))
        right.append(beta * jnp.concatenate([value, small.astype(f32)], axis=1))
    lowers = [x.astype(bf16) for x in inverse_pairs(systems)]
    firsts = [
        r[:BLOCK] + dot(low[:, :BLOCK], r[:BLOCK].astype(bf16)) for low, r in zip(lowers, right)
    ]
    seconds = [
        r[BLOCK:] - dot(corner, first.astype(bf16))
        for corner, r, first in zip(corners, right, firsts)
    ]
    seconds = [r + dot(low[:, BLOCK:], r.astype(bf16)) for low, r in zip(lowers, seconds)]
    for h in range(heads):
        uw = jnp.concatenate([firsts[h], seconds[h]], axis=0).astype(bf16)
        uw_ref[h] = uw
        maps[h] = dot(keys_t[h], uw).astype(bf16)
    for s, out in enumerate((map0, map1, map2, map3)):
        out[...] = maps[me ^ s]


def local_maps(projected, edge, conv_weight, betas):
    length, columns = projected.shape[1:]
    heads = betas.shape[1]
    one = shape((DK, 2 * DK), bf16)
    return pl.pallas_call(
        local_kernel,
        in_specs=whole(4),
        out_specs=whole(7),
        out_shape=[
            shape((length, columns), bf16),
            shape((heads, DK, length), bf16),
            shape((heads, length, 2 * DK), bf16),
            one, one, one, one,
        ],
        scratch_shapes=[
            pltpu.VMEM((3, EDGE + length, columns), f32),
            pltpu.VMEM((heads, DK, 2 * DK), bf16),
        ],
        compiler_params=params(),
        name="local_maps",
    )(projected, edge, conv_weight, betas)


def inner_kernel(queries_ref, keys_t_ref, uw_ref, base_ref, gate_ref):
    length = queries_ref.shape[0]
    row, column = grid_index(length, length)
    for h in range(keys_t_ref.shape[0]):
        lanes = slice(h * DK, (h + 1) * DK)
        query = queries_ref[:, lanes]
        scores = jnp.where(row >= column, dot(query, keys_t_ref[h]), 0.0).astype(bf16)
        both = dot(scores, uw_ref[h])
        base_ref[:, lanes] = both[:, :DK]
        gate_ref[:, lanes] = (query.astype(f32) - both[:, DK:]).astype(bf16)


def inner_outputs(queries, keys_t, uw):
    length, columns = queries.shape
    heads = keys_t.shape[0]
    return pl.pallas_call(
        inner_kernel,
        in_specs=whole(3),
        out_specs=whole(2),
        out_shape=[shape((length, columns), f32), shape((length, columns), bf16)],
        compiler_params=params(),
        cost_estimate=pl.CostEstimate(
            flops=2 * heads * length * length * 3 * DK, bytes_accessed=2 << 20, transcendentals=0
        ),
        name="inner_outputs",
    )(queries, keys_t, uw)


def then(earlier, later):
    return earlier + later - dot(later[:, DK:].astype(bf16), earlier.astype(bf16))


def advance(state, later):
    return state + later[:, :DK] - dot(later[:, DK:].astype(bf16), state.astype(bf16))


def group_kernel(m0, m1, m2, m3, out_ref, kept):
    me = lax.axis_index("ctx") % FAN
    for s, ref in enumerate((m0, m1, m2, m3)):
        kept[me ^ s] = ref[...].astype(f32)
    out_ref[...] = then(then(kept[0], kept[1]), then(kept[2], kept[3])).astype(bf16)


def group_map(parts):
    return pl.pallas_call(
        group_kernel,
        in_specs=whole(4),
        out_specs=pl.BlockSpec(memory_space=pltpu.VMEM),
        out_shape=shape((DK, 2 * DK), bf16),
        scratch_shapes=[pltpu.VMEM((FAN, DK, 2 * DK), f32)],
        compiler_params=params(),
        name="group_map",
    )(*parts)


def row_kernel(m0, m1, m2, m3, total_ref, before_ref, kept):
    me = (lax.axis_index("ctx") // FAN) % FAN
    for s, ref in enumerate((m0, m1, m2, m3)):
        kept[(me + FAN - s) % FAN] = ref[...].astype(f32)
    two = then(kept[0], kept[1])
    three = then(two, kept[2])
    total_ref[...] = then(three, kept[3]).astype(bf16)
    zero = jnp.zeros((DK, 2 * DK), f32)
    one = kept[0]
    before = jnp.where(me == 0, zero, jnp.where(me == 1, one, jnp.where(me == 2, two, three)))
    before_ref[...] = before.astype(bf16)


def row_map(parts):
    return pl.pallas_call(
        row_kernel,
        in_specs=whole(4),
        out_specs=whole(2),
        out_shape=[shape((DK, 2 * DK), bf16)] * 2,
        scratch_shapes=[pltpu.VMEM((FAN, DK, 2 * DK), f32)],
        compiler_params=params(),
        name="row_map",
    )(*parts)


def start_kernel(r1, r2, r3, before_ref, m0, m1, m2, m3, s0, s1, s2, s3, kept, states):
    me = lax.axis_index("ctx") % FAN
    state = r3[:, :DK].astype(f32)
    state = advance(state, r2[...].astype(f32))
    state = advance(state, r1[...].astype(f32))
    state = advance(state, before_ref[...].astype(f32))
    for s, ref in enumerate((m0, m1, m2, m3)):
        kept[me ^ s] = ref[...]
    for j in range(FAN):
        states[j] = state.astype(bf16)
        if j < FAN - 1:
            state = advance(state, kept[j].astype(f32))
    for s, out in enumerate((s0, s1, s2, s3)):
        out[...] = states[me ^ s]


def start_states(rows, before, parts):
    return pl.pallas_call(
        start_kernel,
        in_specs=whole(8),
        out_specs=whole(4),
        out_shape=[shape((DK, DK), bf16)] * 4,
        scratch_shapes=[
            pltpu.VMEM((FAN, DK, 2 * DK), bf16),
            pltpu.VMEM((FAN, DK, DK), bf16),
        ],
        compiler_params=params(),
        name="start_states",
    )(*rows, before, *parts)


def finish_kernel(base_ref, gate_ref, s0, s1, s2, s3, gain_ref, w_ref, out_ref, states):
    me = lax.axis_index("ctx") % FAN
    for s, ref in enumerate((s0, s1, s2, s3)):
        states[me ^ s] = ref[...]
    pieces = []
    for h in range(FAN):
        lanes = slice(h * DK, (h + 1) * DK)
        heads_out = base_ref[:, lanes] + dot(gate_ref[:, lanes], states[h])
        scale = lax.rsqrt(jnp.mean(heads_out * heads_out, axis=-1, keepdims=True) + EPS)
        pieces.append((heads_out * scale * gain_ref[:, lanes]).astype(bf16))
    normed = jnp.concatenate(pieces, axis=1)
    out_ref[...] = dot(normed, w_ref[...]).astype(bf16)


def finish(base, gate, states, norm_gain, w_out):
    length, columns = base.shape
    return pl.pallas_call(
        finish_kernel,
        in_specs=whole(8),
        out_specs=pl.BlockSpec(memory_space=pltpu.VMEM),
        out_shape=shape((length, w_out.shape[1]), bf16),
        scratch_shapes=[pltpu.VMEM((FAN, DK, DK), bf16)],
        compiler_params=params(),
        name="finish",
    )(base, gate, *states, norm_gain[None, :], w_out)


def swaps(count, by):
    return [(i, i ^ by) for i in range(count)]


def row_shift(count, by):
    return [
        (i, i - (i // FAN % FAN) * FAN + (i // FAN + by) % FAN * FAN) for i in range(count)
    ]


def plane_shift(count, by):
    step = by * FAN * FAN
    return [(i, i + step) for i in range(count - step)]


def per_device(tokens_in, w_qkv, conv_weight, beta_weight, beta_bias, norm_gain, w_out):
    peers = lax.axis_size("ctx")
    projected, edge, betas = project(tokens_in, w_qkv, beta_weight, beta_bias)
    edge = lax.ppermute(edge, "ctx", [(i, i + 1) for i in range(peers - 1)])
    queries, keys_t, uw, *maps = local_maps(projected, edge, conv_weight, betas)
    parts = [maps[0]] + [lax.ppermute(maps[s], "ctx", swaps(peers, s)) for s in range(1, FAN)]
    base, gate = inner_outputs(queries, keys_t, uw)
    mine = group_map(parts)
    rows = [mine] + [lax.ppermute(mine, "ctx", row_shift(peers, s)) for s in range(1, FAN)]
    total, before = row_map(rows)
    planes = [lax.ppermute(total, "ctx", plane_shift(peers, s)) for s in range(1, FAN)]
    starts = start_states(planes, before, parts)
    states = [starts[0]] + [
        lax.ppermute(starts[s], "ctx", swaps(peers, s)) for s in range(1, FAN)
    ]
    partial = finish(base, gate, states, norm_gain, w_out)
    return lax.psum_scatter(partial, "head", scatter_dimension=0, tiled=True)


def solution(mesh):
    return jax.shard_map(
        per_device,
        mesh=mesh,
        in_specs=(
            P("ctx", None),
            P(None, None, "head"),
            P(None, None, "head"),
            P("head", None),
            P("head"),
            P("head"),
            P("head", None),
        ),
        out_specs=P(("ctx", "head"), None),
        check_vma=False,
    )
```

time: 595 us -> 99.3 us (0.17)
  matrix products: 153 us -> 0 us
  waiting for transfers between devices: 185 us -> 37.8 us
  local copies, waits for them, and re-layouts: 143 us -> 2.76 us
  other arithmetic: 87.8 us -> 0 us
  starting transfers between devices: 5.23 us -> 30.2 us
  Pallas kernels: 0 us -> 14.3 us
    all_gather x2 -> x0, waiting for transfers between devices: 163 us -> none  [carried_in(): lax.all_gather(part.astype(kind), axis)]
    dot_general x81 -> x0, matrix products: 149 us -> none  [the longest x64 124 us: combine(): jnp.einsum('hij,hjk->hik', earlier[1], later[0], precision=precise)]
    another operation x6 -> x0, other arithmetic: 80.2 us -> none  [the longest x5 80.1 us: block_terms(): jax.scipy.linalg.solve_triangular(system, weighted, lower=True, unit_diag...]
    dynamic_slice x128 -> x0, local copies, waits for them, and re-layouts: 66.9 us -> none  [hop(): part[k].astype(own.dtype)]
    while x77 -> x0, local copies, waits for them, and re-layouts: 63.7 us -> none
    ppermute x1 -> x13, starting transfers between devices: 4.94 us -> 30.2 us  [the longest x3 10.1 us: per_device(): lax.ppermute(mine, 'ctx', row_shift(peers, s))]
    pallas_call x0 -> x7, Pallas kernels: none -> 14.3 us  [the longest x1 6.16 us: project(): pl.pallas_call(project_kernel, grid=(3, 2), in_specs=[pl.BlockSpec((lengt...]
    ppermute x1 -> x13, waiting for transfers between devices: 0.01 us -> 13.8 us  [the longest x3 4.57 us: per_device(): lax.ppermute(mine, 'ctx', row_shift(peers, s))]
  transfers between devices with their start and end apart: 4 -> 14, of which waited for: 3 -> 9; matrix products, arithmetic and copies ran while one was open for 1% -> 0% of each run, Pallas kernels for 0% -> 1%
where the time goes in v1:
time: 99.3 us; the launch traced here: 98.5 us
  waiting for transfers between devices  37.8 us (38%)
  starting transfers between devices  30.2 us (30%)
  Pallas kernels  14.3 us (14%)
  between operations  13.5 us (14%)
  local copies, waits for them, and re-layouts  2.76 us (3%)
    reduce_scatter x1, waiting for transfers between devices, per_device(): return lax.psum_scatter(partial, 'head', scatter_dimension=0, tiled=True)  24 us
    ppermute x3, starting transfers between devices, per_device(): lax.ppermute(mine, 'ctx', row_shift(peers, s))  10.1 us
    ppermute x3, starting transfers between devices, per_device(): lax.ppermute(total, 'ctx', plane_shift(peers, s))  8.52 us
    pallas_call x1, Pallas kernels, project(): pl.pallas_call(project_kernel, grid=(3, 2), in_specs=[pl.BlockSpec((lengt...  6.16 us
    ppermute x1, starting transfers between devices, per_device(): edge = lax.ppermute(edge, 'ctx', [(i, i + 1) for i in range(peers - 1)])  4.93 us
    ppermute x3, waiting for transfers between devices, per_device(): lax.ppermute(mine, 'ctx', row_shift(peers, s))  4.57 us
    ppermute x3, starting transfers between devices, per_device(): lax.ppermute(starts[s], 'ctx', swaps(peers, s))  4.06 us
    ppermute x3, waiting for transfers between devices, per_device(): lax.ppermute(maps[s], 'ctx', swaps(peers, s))  4 us
  transfers between devices with their start and end apart: 14, of which 9 were waited for; matrix products, arithmetic and copies ran while one was open for 0% of the time, Pallas kernels for 1%

profile of v1, /device:TPU:1, one launch (start us, length us, event | category | flops | bytes accessed | tf_op | source)
XLA Modules:
  0.0 98.5 jit_solution(16475979861443400308)
XLA Ops:
  6.5 0.0 copy-start
  6.5 0.0 reduce-scatter.2.cloned.1.call-start
  6.5 0.0 copy-start.1
  6.5 1.4 %copy-done.1 = bf16[256,2048]{1,0:T(8,128)(2,1)S(1)} copy-done((bf16[256,2048]{1,0:T(8,128)(2,1)S(1)}, bf16[256,2048]{1,0:T(8,128)(2,1)}, u32[]{:S(2)}) %copy-start.1) | copy-done | bytes 1048600
  7.9 0.0 copy-start.3
  7.9 0.7 copy-done.3
  8.6 0.0 copy-start.5
  8.6 0.7 copy-done.5
  9.3 0.0 copy-start.2
  9.3 0.0 copy-start.4
  9.3 6.2 %project.1 = (bf16[3,256,512]{2,1,0:T(8,128)(2,1)S(1)}, bf16[3,16,512]{2,1,0:T(8,128)(2,1)S(1)}, f32[256,4]{1,0:T(8,128)S(1)}) custom-call(bf16[256,2048]{1,0:T(8,128)(2,1)S(1)} %copy-done.1, bf16[3,2048,512]{2,1,0:T(8,128)(2,1)} %w_ref.2, bf16[4,2048]{1,0:T(4,128)(2,1)S(1)} %copy-done.3, f32[1,4]{1,0:T(1,128)S(1)} %bitcast.3), custom_call_target="tpu_custom_call" | custom-call | tf_op jit(solution)/shard_map/project/pallas_call | solution.py:58
  15.5 4.9 %collective-permute-start = (bf16[3,16,512]{2,1,0:T(8,128)(2,1)S(1)}, bf16[3,16,512]{2,1,0:T(8,128)(2,1)S(1)}, u32[]{:S(2)}, u32[]{:S(2)}) collective-permute-start(bf16[3,16,512]{2,1,0:T(8,128)(2,1)S(1)} %get-tuple-element.24), channel_id=1, source_target_pairs={{0,4},{4,8},{8,12},{12,16},{16,20},{20,24},{24,28},{28,32},{32,36}... | collective-permute-start | bytes 147464 | tf_op jit(solution)/shard_map/ppermute | solution.py:358
  20.4 1.2 %collective-permute-done.edge_ref = bf16[3,16,512]{2,1,0:T(8,128)(2,1)S(1)} collective-permute-done((bf16[3,16,512]{2,1,0:T(8,128)(2,1)S(1)}, bf16[3,16,512]{2,1,0:T(8,128)(2,1)S(1)}, u32[]{:S(2)}, u32[]{:S(2)}) %collective-permute-start) | collective-permute-done | bytes 49184 | tf_op jit(solution)/shard_map/ppermute | solution.py:358
  21.5 0.0 copy-done.2
  21.6 3.9 %local_maps.1 = (bf16[256,512]{1,0:T(8,128)(2,1)S(1)}, bf16[4,128,256]{2,1,0:T(8,128)(2,1)S(1)}, bf16[4,256,256]{2,1,0:T(8,128)(2,1)S(1)}, bf16[128,256]{1,0:T(8...) custom-call(bf16[3,256,512]{2,1,0:T(8,128)(2,1)S(1)} %get-tuple-element.23., ...), custom_call_target="tpu_custom_call" | custom-call | tf_op jit(solution)/shard_map/local_maps/pallas_call | solution.py:183
  25.5 0.1 collective-permute-start.1
  25.6 2.5 %collective-permute-start.2 = (bf16[128,256]{1,0:T(8,128)(2,1)S(1)}, bf16[128,256]{1,0:T(8,128)(2,1)S(1)}, u32[]{:S(2)}, u32[]{:S(2)}) collective-permute-start(bf16[128,256]{1,0:T(8,128)(2,1)S(1)} %get-tuple-element.33), channel_id=1, source_target_pairs={{0,8},{4,12},{8,0},{12,4},{16,24},{20,28},{24,16},{28,20},{32,40},... | collective-permute-start | bytes 196616 | tf_op jit(solution)/shard_map/ppermute | solution.py:360
  28.1 0.1 collective-permute-start.3
  28.1 0.0 collective-permute-done.1.m1
  28.1 2.3 %collective-permute-done.2.m2 = bf16[128,256]{1,0:T(8,128)(2,1)S(1)} collective-permute-done((bf16[128,256]{1,0:T(8,128)(2,1)S(1)}, bf16[128,256]{1,0:T(8,128)(2,1)S(1)}, u32[]{:S(2)}, u32[]{:S(2)}) %collective-permute-start.2) | collective-permute-done | bytes 65568 | tf_op jit(solution)/shard_map/ppermute | solution.py:360
  30.4 1.7 %collective-permute-done.3.m3 = bf16[128,256]{1,0:T(8,128)(2,1)S(1)} collective-permute-done((bf16[128,256]{1,0:T(8,128)(2,1)S(1)}, bf16[128,256]{1,0:T(8,128)(2,1)S(1)}, u32[]{:S(2)}, u32[]{:S(2)}) %collective-permute-start.3) | collective-permute-done | bytes 65568 | tf_op jit(solution)/shard_map/ppermute | solution.py:360
  32.1 0.4 group_map.1.m0
  32.5 5.6 %collective-permute-start.6 = (bf16[128,256]{1,0:T(8,128)(2,1)S(1)}, bf16[128,256]{1,0:T(8,128)(2,1)S(1)}, u32[]{:S(2)}, u32[]{:S(2)}) collective-permute-start(bf16[128,256]{1,0:T(8,128)(2,1)S(1)} %group_map.1.m0), channel_id=1, source_target_pairs={{0,48},{4,52},{8,56},{12,60},{16,0},{20,4},{24,8},{28,12},{32,16},... | collective-permute-start | bytes 196616 | tf_op jit(solution)/shard_map/ppermute | solution.py:363
  38.1 2.2 %collective-permute-start.5 = (bf16[128,256]{1,0:T(8,128)(2,1)S(1)}, bf16[128,256]{1,0:T(8,128)(2,1)S(1)}, u32[]{:S(2)}, u32[]{:S(2)}) collective-permute-start(bf16[128,256]{1,0:T(8,128)(2,1)S(1)} %group_map.1.m0), channel_id=1, source_target_pairs={{0,32},{4,36},{8,40},{12,44},{16,48},{20,52},{24,56},{28,60},{32,0... | collective-permute-start | bytes 196616 | tf_op jit(solution)/shard_map/ppermute | solution.py:363
  40.3 2.3 %collective-permute-start.4 = (bf16[128,256]{1,0:T(8,128)(2,1)S(1)}, bf16[128,256]{1,0:T(8,128)(2,1)S(1)}, u32[]{:S(2)}, u32[]{:S(2)}) collective-permute-start(bf16[128,256]{1,0:T(8,128)(2,1)S(1)} %group_map.1.m0), channel_id=1, source_target_pairs={{0,16},{4,20},{8,24},{12,28},{16,32},{20,36},{24,40},{28,44},{32,4... | collective-permute-start | bytes 196616 | tf_op jit(solution)/shard_map/ppermute | solution.py:363
  42.6 0.0 collective-permute-done.6.m3
  42.6 2.7 %collective-permute-done.5.m2 = bf16[128,256]{1,0:T(8,128)(2,1)S(1)} collective-permute-done((bf16[128,256]{1,0:T(8,128)(2,1)S(1)}, bf16[128,256]{1,0:T(8,128)(2,1)S(1)}, u32[]{:S(2)}, u32[]{:S(2)}) %collective-permute-start.5) | collective-permute-done | bytes 65568 | tf_op jit(solution)/shard_map/ppermute | solution.py:363
  45.3 1.9 %collective-permute-done.4.m1 = bf16[128,256]{1,0:T(8,128)(2,1)S(1)} collective-permute-done((bf16[128,256]{1,0:T(8,128)(2,1)S(1)}, bf16[128,256]{1,0:T(8,128)(2,1)S(1)}, u32[]{:S(2)}, u32[]{:S(2)}) %collective-permute-start.4) | collective-permute-done | bytes 65568 | tf_op jit(solution)/shard_map/ppermute | solution.py:363
  47.2 0.5 row_map.1
  47.7 4.7 %collective-permute-start.9 = (bf16[128,256]{1,0:T(8,128)(2,1)S(1)}, bf16[128,256]{1,0:T(8,128)(2,1)S(1)}, u32[]{:S(2)}, u32[]{:S(2)}) collective-permute-start(bf16[128,256]{1,0:T(8,128)(2,1)S(1)} %get-tuple-element.35), channel_id=1, source_target_pairs={{0,192},{4,196},{8,200},{12,204},{16,208},{20,212},{24,216},{28,22... | collective-permute-start | bytes 196616 | tf_op jit(solution)/shard_map/ppermute | solution.py:365
  52.4 1.3 %collective-permute-start.8 = (bf16[128,256]{1,0:T(8,128)(2,1)S(1)}, bf16[128,256]{1,0:T(8,128)(2,1)S(1)}, u32[]{:S(2)}, u32[]{:S(2)}) collective-permute-start(bf16[128,256]{1,0:T(8,128)(2,1)S(1)} %get-tuple-element.35), channel_id=1, source_target_pairs={{0,128},{4,132},{8,136},{12,140},{16,144},{20,148},{24,152},{28,15... | collective-permute-start | bytes 196616 | tf_op jit(solution)/shard_map/ppermute | solution.py:365
  53.7 2.5 %collective-permute-start.7 = (bf16[128,256]{1,0:T(8,128)(2,1)S(1)}, bf16[128,256]{1,0:T(8,128)(2,1)S(1)}, u32[]{:S(2)}, u32[]{:S(2)}) collective-permute-start(bf16[128,256]{1,0:T(8,128)(2,1)S(1)} %get-tuple-element.35), channel_id=1, source_target_pairs={{0,64},{4,68},{8,72},{12,76},{16,80},{20,84},{24,88},{28,92},{32,9... | collective-permute-start | bytes 196616 | tf_op jit(solution)/shard_map/ppermute | solution.py:365
  56.2 0.0 collective-permute-done.9.r3
  56.2 0.0 collective-permute-done.8.r2
  56.2 1.3 %collective-permute-done.7.r1 = bf16[128,256]{1,0:T(8,128)(2,1)S(1)} collective-permute-done((bf16[128,256]{1,0:T(8,128)(2,1)S(1)}, bf16[128,256]{1,0:T(8,128)(2,1)S(1)}, u32[]{:S(2)}, u32[]{:S(2)}) %collective-permute-start.7) | collective-permute-done | bytes 65568 | tf_op jit(solution)/shard_map/ppermute | solution.py:365
  57.5 0.8 start_states.1
  58.4 1.9 %collective-permute-start.10 = (bf16[128,128]{1,0:T(8,128)(2,1)S(1)}, bf16[128,128]{1,0:T(8,128)(2,1)S(1)}, u32[]{:S(2)}, u32[]{:S(2)}) collective-permute-start(bf16[128,128]{1,0:T(8,128)(2,1)S(1)} %get-tuple-element.38), channel_id=1, source_target_pairs={{0,4},{4,0},{8,12},{12,8},{16,20},{20,16},{24,28},{28,24},{32,36},... | collective-permute-start | bytes 98312 | tf_op jit(solution)/shard_map/ppermute | solution.py:368
  60.3 2.1 %collective-permute-start.11 = (bf16[128,128]{1,0:T(8,128)(2,1)S(1)}, bf16[128,128]{1,0:T(8,128)(2,1)S(1)}, u32[]{:S(2)}, u32[]{:S(2)}) collective-permute-start(bf16[128,128]{1,0:T(8,128)(2,1)S(1)} %get-tuple-element.39), channel_id=1, source_target_pairs={{0,8},{4,12},{8,0},{12,4},{16,24},{20,28},{24,16},{28,20},{32,40},... | collective-permute-start | bytes 98312 | tf_op jit(solution)/shard_map/ppermute | solution.py:368
  62.3 0.1 collective-permute-start.12
  62.4 0.5 inner_outputs.1
  62.9 0.0 collective-permute-done.10.s1
  63.0 1.0 %collective-permute-done.11.s2 = bf16[128,128]{1,0:T(8,128)(2,1)S(1)} collective-permute-done((bf16[128,128]{1,0:T(8,128)(2,1)S(1)}, bf16[128,128]{1,0:T(8,128)(2,1)S(1)}, u32[]{:S(2)}, u32[]{:S(2)}) %collective-permute-start.11) | collective-permute-done | bytes 32800 | tf_op jit(solution)/shard_map/ppermute | solution.py:368
  64.0 1.7 %collective-permute-done.12.s3 = bf16[128,128]{1,0:T(8,128)(2,1)S(1)} collective-permute-done((bf16[128,128]{1,0:T(8,128)(2,1)S(1)}, bf16[128,128]{1,0:T(8,128)(2,1)S(1)}, u32[]{:S(2)}, u32[]{:S(2)}) %collective-permute-start.12) | collective-permute-done | bytes 32800 | tf_op jit(solution)/shard_map/ppermute | solution.py:368
  65.7 0.0 copy-done
  65.7 0.0 copy-done.4
  65.7 2.0 %finish.1 = bf16[256,2048]{1,0:T(8,128)(2,1)} custom-call(f32[256,512]{1,0:T(8,128)S(1)} %get-tuple-element.29.base_ref, bf16[256,512]{1,0:T(8,128)(2,1)S(1)} %get-tuple-element.30.gate_ref, bf16[128,128]{1,0:T(8,128)(2,1)S(1)} %get-tuple-element.37.s0, bf16[128,128]{1,0:T(8,128)(2,1)S(1)} %collective-permute-done.10.s1, ...), custom_call_target="tpu_custom_call" | custom-call | tf_op jit(solution)/shard_map/finish/pallas_call | solution.py:329
  67.7 0.0 reduce-scatter.2.cloned.1.call-update
  67.7 24.0 %reduce-scatter.2.cloned.1.call-done = bf16[64,2048]{1,0:T(8,128)(2,1)} async-done(((bf16[256,2048]{1,0:T(8,128)(2,1)}), bf16[64,2048]{1,0:T(8,128)(2,1)}) %reduce-scatter.2.cloned.1.call-update) | async-done | bytes 262160 | tf_op jit(solution)/shard_map/reduce_scatter | solution.py:371
Async XLA Ops:
  6.5 59.2 %copy-start = (bf16[512,2048]{1,0:T(8,128)(2,1)S(1)}, bf16[512,2048]{1,0:T(8,128)(2,1)}, u32[]{:S(2)}) copy-start(bf16[512,2048]{1,0:T(8,128)(2,1)} %w_ref.3) | copy-start | bytes 6291460
  6.5 85.2 %reduce-scatter.2.cloned.1.call-start = ((), (), s32[]{:S(2)}) async-start(), calls=%async_computation.1 | async-start | bytes 1310720 | tf_op jit(solution)/shard_map/reduce_scatter | solution.py:371
  6.5 1.4 %copy-start.1 = (bf16[256,2048]{1,0:T(8,128)(2,1)S(1)}, bf16[256,2048]{1,0:T(8,128)(2,1)}, u32[]{:S(2)}) copy-start(bf16[256,2048]{1,0:T(8,128)(2,1)} %tokens_ref.1) | copy-start | bytes 3145732
  7.9 0.7 copy-start.3
  8.6 0.7 copy-start.5
  9.3 12.3 %copy-start.2 = (f32[3,4,512]{2,1,0:T(4,128)S(1)}, f32[3,4,512]{2,1,0:T(4,128)}, u32[]{:S(2)}) copy-start(f32[3,4,512]{2,1,0:T(4,128)} %conv_ref.1) | copy-start | bytes 73732
  9.3 56.4 %copy-start.4 = (f32[512]{0:T(512)S(1)}, f32[512]{0:T(512)}, u32[]{:S(2)}) copy-start(f32[512]{0:T(512)} %param.12) | copy-start | bytes 6148
  15.5 6.1 %collective-permute-start = (bf16[3,16,512]{2,1,0:T(8,128)(2,1)S(1)}, bf16[3,16,512]{2,1,0:T(8,128)(2,1)S(1)}, u32[]{:S(2)}, u32[]{:S(2)}) collective-permute-start(bf16[3,16,512]{2,1,0:T(8,128)(2,1)S(1)} %get-tuple-element.24), channel_id=1, source_target_pairs={{0,4},{4,8},{8,12},{12,16},{16,20},{20,24},{24,28},{28,32},{32,36}... | collective-permute-start | bytes 147464 | tf_op jit(solution)/shard_map/ppermute | solution.py:358
  25.5 2.6 %collective-permute-start.1 = (bf16[128,256]{1,0:T(8,128)(2,1)S(1)}, bf16[128,256]{1,0:T(8,128)(2,1)S(1)}, u32[]{:S(2)}, u32[]{:S(2)}) collective-permute-start(bf16[128,256]{1,0:T(8,128)(2,1)S(1)} %get-tuple-element.32), channel_id=1, source_target_pairs={{0,4},{4,0},{8,12},{12,8},{16,20},{20,16},{24,28},{28,24},{32,36},... | collective-permute-start | bytes 196616 | tf_op jit(solution)/shard_map/ppermute | solution.py:360
  25.6 4.8 %collective-permute-start.2 = (bf16[128,256]{1,0:T(8,128)(2,1)S(1)}, bf16[128,256]{1,0:T(8,128)(2,1)S(1)}, u32[]{:S(2)}, u32[]{:S(2)}) collective-permute-start(bf16[128,256]{1,0:T(8,128)(2,1)S(1)} %get-tuple-element.33), channel_id=1, source_target_pairs={{0,8},{4,12},{8,0},{12,4},{16,24},{20,28},{24,16},{28,20},{32,40},... | collective-permute-start | bytes 196616 | tf_op jit(solution)/shard_map/ppermute | solution.py:360
  28.1 4.1 %collective-permute-start.3 = (bf16[128,256]{1,0:T(8,128)(2,1)S(1)}, bf16[128,256]{1,0:T(8,128)(2,1)S(1)}, u32[]{:S(2)}, u32[]{:S(2)}) collective-permute-start(bf16[128,256]{1,0:T(8,128)(2,1)S(1)} %get-tuple-element.34), channel_id=1, source_target_pairs={{0,12},{4,8},{8,4},{12,0},{16,28},{20,24},{24,20},{28,16},{32,44},... | collective-permute-start | bytes 196616 | tf_op jit(solution)/shard_map/ppermute | solution.py:360
  32.5 10.1 %collective-permute-start.6 = (bf16[128,256]{1,0:T(8,128)(2,1)S(1)}, bf16[128,256]{1,0:T(8,128)(2,1)S(1)}, u32[]{:S(2)}, u32[]{:S(2)}) collective-permute-start(bf16[128,256]{1,0:T(8,128)(2,1)S(1)} %group_map.1.m0), channel_id=1, source_target_pairs={{0,48},{4,52},{8,56},{12,60},{16,0},{20,4},{24,8},{28,12},{32,16},... | collective-permute-start | bytes 196616 | tf_op jit(solution)/shard_map/ppermute | solution.py:363
  38.1 7.2 %collective-permute-start.5 = (bf16[128,256]{1,0:T(8,128)(2,1)S(1)}, bf16[128,256]{1,0:T(8,128)(2,1)S(1)}, u32[]{:S(2)}, u32[]{:S(2)}) collective-permute-start(bf16[128,256]{1,0:T(8,128)(2,1)S(1)} %group_map.1.m0), channel_id=1, source_target_pairs={{0,32},{4,36},{8,40},{12,44},{16,48},{20,52},{24,56},{28,60},{32,0... | collective-permute-start | bytes 196616 | tf_op jit(solution)/shard_map/ppermute | solution.py:363
  40.3 6.8 %collective-permute-start.4 = (bf16[128,256]{1,0:T(8,128)(2,1)S(1)}, bf16[128,256]{1,0:T(8,128)(2,1)S(1)}, u32[]{:S(2)}, u32[]{:S(2)}) collective-permute-start(bf16[128,256]{1,0:T(8,128)(2,1)S(1)} %group_map.1.m0), channel_id=1, source_target_pairs={{0,16},{4,20},{8,24},{12,28},{16,32},{20,36},{24,40},{28,44},{32,4... | collective-permute-start | bytes 196616 | tf_op jit(solution)/shard_map/ppermute | solution.py:363
  47.7 8.5 %collective-permute-start.9 = (bf16[128,256]{1,0:T(8,128)(2,1)S(1)}, bf16[128,256]{1,0:T(8,128)(2,1)S(1)}, u32[]{:S(2)}, u32[]{:S(2)}) collective-permute-start(bf16[128,256]{1,0:T(8,128)(2,1)S(1)} %get-tuple-element.35), channel_id=1, source_target_pairs={{0,192},{4,196},{8,200},{12,204},{16,208},{20,212},{24,216},{28,22... | collective-permute-start | bytes 196616 | tf_op jit(solution)/shard_map/ppermute | solution.py:365
  52.4 3.8 %collective-permute-start.8 = (bf16[128,256]{1,0:T(8,128)(2,1)S(1)}, bf16[128,256]{1,0:T(8,128)(2,1)S(1)}, u32[]{:S(2)}, u32[]{:S(2)}) collective-permute-start(bf16[128,256]{1,0:T(8,128)(2,1)S(1)} %get-tuple-element.35), channel_id=1, source_target_pairs={{0,128},{4,132},{8,136},{12,140},{16,144},{20,148},{24,152},{28,15... | collective-permute-start | bytes 196616 | tf_op jit(solution)/shard_map/ppermute | solution.py:365
  53.7 3.8 %collective-permute-start.7 = (bf16[128,256]{1,0:T(8,128)(2,1)S(1)}, bf16[128,256]{1,0:T(8,128)(2,1)S(1)}, u32[]{:S(2)}, u32[]{:S(2)}) collective-permute-start(bf16[128,256]{1,0:T(8,128)(2,1)S(1)} %get-tuple-element.35), channel_id=1, source_target_pairs={{0,64},{4,68},{8,72},{12,76},{16,80},{20,84},{24,88},{28,92},{32,9... | collective-permute-start | bytes 196616 | tf_op jit(solution)/shard_map/ppermute | solution.py:365
  58.4 4.6 %collective-permute-start.10 = (bf16[128,128]{1,0:T(8,128)(2,1)S(1)}, bf16[128,128]{1,0:T(8,128)(2,1)S(1)}, u32[]{:S(2)}, u32[]{:S(2)}) collective-permute-start(bf16[128,128]{1,0:T(8,128)(2,1)S(1)} %get-tuple-element.38), channel_id=1, source_target_pairs={{0,4},{4,0},{8,12},{12,8},{16,20},{20,16},{24,28},{28,24},{32,36},... | collective-permute-start | bytes 98312 | tf_op jit(solution)/shard_map/ppermute | solution.py:368
  60.3 3.7 %collective-permute-start.11 = (bf16[128,128]{1,0:T(8,128)(2,1)S(1)}, bf16[128,128]{1,0:T(8,128)(2,1)S(1)}, u32[]{:S(2)}, u32[]{:S(2)}) collective-permute-start(bf16[128,128]{1,0:T(8,128)(2,1)S(1)} %get-tuple-element.39), channel_id=1, source_target_pairs={{0,8},{4,12},{8,0},{12,4},{16,24},{20,28},{24,16},{28,20},{32,40},... | collective-permute-start | bytes 98312 | tf_op jit(solution)/shard_map/ppermute | solution.py:368
  62.3 3.4 %collective-permute-start.12 = (bf16[128,128]{1,0:T(8,128)(2,1)S(1)}, bf16[128,128]{1,0:T(8,128)(2,1)S(1)}, u32[]{:S(2)}, u32[]{:S(2)}) collective-permute-start(bf16[128,128]{1,0:T(8,128)(2,1)S(1)} %get-tuple-element.40), channel_id=1, source_target_pairs={{0,12},{4,8},{8,4},{12,0},{16,28},{20,24},{24,20},{28,16},{32,44},... | collective-permute-start | bytes 98312 | tf_op jit(solution)/shard_map/ppermute | solution.py:368
Sparse Core Ops, SparseCore 0:
  67.8 23.8 reduce-scatter.1

commit v2 on v1

v2 whole, which is shorter than its diff:
```python
import jax
import jax.numpy as jnp
from jax import lax
from jax.experimental import pallas as pl
from jax.experimental.pallas import tpu as pltpu
from jax.sharding import PartitionSpec as P

DK = 128
BLOCK = 128
WIDTH = 2 * BLOCK
EDGE = 16
EPS = 1e-06
FAN = 4

f32 = jnp.float32
bf16 = jnp.bfloat16


def dot(a, b):
    return lax.dot_general(a, b, (((1,), (0,)), ((), ())), preferred_element_type=f32)


def dot_t(a, b):
    return lax.dot_general(a, b, (((1,), (1,)), ((), ())), preferred_element_type=f32)


def params(megabytes=48):
    return pltpu.CompilerParams(vmem_limit_bytes=megabytes << 20)


def whole(count):
    return [pl.BlockSpec(memory_space=pltpu.VMEM)] * count


def shape(dims, kind):
    return jax.ShapeDtypeStruct(dims, kind)


PIECES = 2


def project_kernel(
    tokens_hbm, w_hbm, beta_w_hbm, beta_b_ref, out_ref, edge_ref, betas_ref,
    tokens_ref, w_ref, beta_w_ref, small_sems, w_sems
):
    length, depth = tokens_ref.shape
    part = depth // PIECES
    first = pltpu.make_async_copy(tokens_hbm, tokens_ref, small_sems.at[0])
    first.start()
    copies = []
    for s in range(3):
        for k in range(PIECES):
            rows = pl.ds(k * part, part)
            copy = pltpu.make_async_copy(
                w_hbm.at[s, rows], w_ref.at[s, rows], w_sems.at[s * PIECES + k]
            )
            copy.start()
            copies.append(copy)
    last = pltpu.make_async_copy(beta_w_hbm, beta_w_ref, small_sems.at[1])
    last.start()
    first.wait()
    for s in range(3):
        total = None
        for k in range(PIECES):
            rows = slice(k * part, (k + 1) * part)
            copies[s * PIECES + k].wait()
            term = dot(tokens_ref[:, rows], w_ref[s, rows])
            total = term if total is None else total + term
        result = total.astype(bf16)
        out_ref[s] = result
        edge_ref[s] = result[length - EDGE :]
    last.wait()
    logits = dot_t(tokens_ref[...], beta_w_ref[...]) + beta_b_ref[...]
    betas_ref[...] = 1.0 / (1.0 + jnp.exp(-logits))


def project(tokens, w_qkv, beta_weight, beta_bias):
    length, depth = tokens.shape
    columns = w_qkv.shape[2]
    heads = beta_weight.shape[0]
    far = pl.BlockSpec(memory_space=pltpu.HBM)
    return pl.pallas_call(
        project_kernel,
        in_specs=[far, far, far, pl.BlockSpec(memory_space=pltpu.VMEM)],
        out_specs=whole(3),
        out_shape=[
            shape((3, length, columns), bf16),
            shape((3, EDGE, columns), bf16),
            shape((length, heads), f32),
        ],
        scratch_shapes=[
            pltpu.VMEM(tokens.shape, bf16),
            pltpu.VMEM(w_qkv.shape, bf16),
            pltpu.VMEM(beta_weight.shape, bf16),
            pltpu.SemaphoreType.DMA((2,)),
            pltpu.SemaphoreType.DMA((3 * PIECES,)),
        ],
        compiler_params=params(),
        name="project",
    )(tokens, w_qkv, beta_weight, beta_bias[None, :])


def grid_index(rows, columns):
    row = lax.broadcasted_iota(jnp.int32, (rows, columns), 0)
    column = lax.broadcasted_iota(jnp.int32, (rows, columns), 1)
    return row, column


def on_diagonal(pair, left):
    zero = jnp.zeros_like(pair)
    return jnp.concatenate([jnp.where(left, pair, zero), jnp.where(left, zero, pair)], axis=0)


def inverse_pairs(systems):
    row, wide = grid_index(BLOCK, 2 * BLOCK)
    column = wide % BLOCK
    left = wide < BLOCK
    eye = jnp.where(row == column, 1.0, 0.0).astype(f32)

    def below(size):
        same = (row // (2 * size)) == (column // (2 * size))
        return same & ((row % (2 * size)) >= size) & ((column % (2 * size)) < size)

    found = [eye - jnp.where(below(1), system, 0.0) for system in systems]
    size = 2
    while size < BLOCK:
        mask = below(size)
        steps = [jnp.where(mask, system, 0.0).astype(bf16) for system in systems]
        small = [x.astype(bf16) for x in found]
        half = [dot(x, on_diagonal(n, left)).astype(bf16) for x, n in zip(small, steps)]
        found = [
            x - dot(y, on_diagonal(b, left)) for x, y, b in zip(found, half, small)
        ]
        size *= 2
    small = [x.astype(bf16) for x in found]
    high = [system.astype(bf16) for system in systems]
    low = [(system - h.astype(f32)).astype(bf16) for system, h in zip(systems, high)]
    rest = [
        (eye - x.astype(f32)) - dot(x, on_diagonal(h, left)) - dot(x, on_diagonal(l, left))
        for x, h, l in zip(small, high, low)
    ]
    fixed = [
        x.astype(f32) + dot(r.astype(bf16), on_diagonal(x, left)) for x, r in zip(small, rest)
    ]
    return [x - eye for x in fixed]


def local_kernel(
    proj_ref, edge_ref, conv_ref, betas_ref,
    queries_ref, keys_t_ref, uw_ref, keep_ref, send_ref, padded, maps
):
    length = proj_ref.shape[1]
    heads = betas_ref.shape[1]
    core = lax.axis_index("ctx") % 2
    for s in range(3):
        padded[s, :EDGE] = edge_ref[s].astype(f32)
        padded[s, EDGE:] = proj_ref[s].astype(f32)
    row, column = grid_index(length, length)
    strict = row > column
    systems, corners, right, keys_t = [], [], [], []
    for h in range(heads):
        lanes = slice(h * DK, (h + 1) * DK)
        mixed = []
        for s in range(3):
            total = jnp.zeros((length, DK), f32)
            for j in range(4):
                start = EDGE - 3 + j
                total = total + conv_ref[s, j : j + 1, lanes] * padded[s, start : start + length, lanes]
            mixed.append(total / (1.0 + jnp.exp(-total)))
        query, key, value = mixed
        query = query * lax.rsqrt(jnp.sum(query * query, axis=-1, keepdims=True) + EPS)
        key = key * lax.rsqrt(jnp.sum(key * key, axis=-1, keepdims=True) + EPS)
        queries_ref[:, lanes] = query.astype(bf16)
        small = key.astype(bf16)
        small_t = key.T.astype(bf16)
        keys_t_ref[h] = small_t
        keys_t.append(small_t)
        beta = betas_ref[:, h : h + 1]
        system = jnp.where(strict, beta * dot(small, small_t), 0.0)
        systems.append(jnp.concatenate([system[:BLOCK, :BLOCK], system[BLOCK:, BLOCK:]], axis=1))
        corners.append(system[BLOCK:, :BLOCK].astype(bf16))
        right.append(beta * jnp.concatenate([value, small.astype(f32)], axis=1))
    lowers = [x.astype(bf16) for x in inverse_pairs(systems)]
    firsts = [
        r[:BLOCK] + dot(low[:, :BLOCK], r[:BLOCK].astype(bf16)) for low, r in zip(lowers, right)
    ]
    seconds = [
        r[BLOCK:] - dot(corner, first.astype(bf16))
        for corner, r, first in zip(corners, right, firsts)
    ]
    seconds = [r + dot(low[:, BLOCK:], r.astype(bf16)) for low, r in zip(lowers, seconds)]
    for h in range(heads):
        uw = jnp.concatenate([firsts[h], seconds[h]], axis=0).astype(bf16)
        uw_ref[h] = uw
        maps[h] = dot(keys_t[h], uw).astype(bf16)
    for j in range(heads // 2):
        keep_ref[j] = maps[2 * j + core]
        send_ref[j] = maps[2 * j + 1 - core]


def local_maps(projected, edge, conv_weight, betas):
    length, columns = projected.shape[1:]
    heads = betas.shape[1]
    two = shape((heads // 2, DK, 2 * DK), bf16)
    return pl.pallas_call(
        local_kernel,
        in_specs=whole(4),
        out_specs=whole(5),
        out_shape=[
            shape((length, columns), bf16),
            shape((heads, DK, length), bf16),
            shape((heads, length, 2 * DK), bf16),
            two, two,
        ],
        scratch_shapes=[
            pltpu.VMEM((3, EDGE + length, columns), f32),
            pltpu.VMEM((heads, DK, 2 * DK), bf16),
        ],
        compiler_params=params(),
        name="local_maps",
    )(projected, edge, conv_weight, betas)


def inner_kernel(queries_ref, keys_t_ref, uw_ref, base_ref, gate_ref):
    length = queries_ref.shape[0]
    row, column = grid_index(length, length)
    for h in range(keys_t_ref.shape[0]):
        lanes = slice(h * DK, (h + 1) * DK)
        query = queries_ref[:, lanes]
        scores = jnp.where(row >= column, dot(query, keys_t_ref[h]), 0.0).astype(bf16)
        both = dot(scores, uw_ref[h])
        base_ref[:, lanes] = both[:, :DK]
        gate_ref[:, lanes] = (query.astype(f32) - both[:, DK:]).astype(bf16)


def inner_outputs(queries, keys_t, uw):
    length, columns = queries.shape
    heads = keys_t.shape[0]
    return pl.pallas_call(
        inner_kernel,
        in_specs=whole(3),
        out_specs=whole(2),
        out_shape=[shape((length, columns), f32), shape((length, columns), bf16)],
        compiler_params=params(),
        cost_estimate=pl.CostEstimate(
            flops=2 * heads * length * length * 3 * DK, bytes_accessed=2 << 20, transcendentals=0
        ),
        name="inner_outputs",
    )(queries, keys_t, uw)


def then(earlier, later):
    return earlier + later - dot(later[:, DK:].astype(bf16), earlier.astype(bf16))


def advance(state, later):
    return state + later[:, :DK] - dot(later[:, DK:].astype(bf16), state.astype(bf16))


MAP = shape((DK, 2 * DK), bf16)
STATE = shape((DK, DK), bf16)


def small_call(kernel, outs, name, scratch=()):
    return pl.pallas_call(
        kernel,
        out_specs=whole(len(outs)),
        out_shape=list(outs),
        scratch_shapes=list(scratch),
        compiler_params=params(),
        name=name,
    )


def ordered(mine, other, late):
    return jnp.where(late, other, mine), jnp.where(late, mine, other)


def bit(position):
    return (lax.axis_index("ctx") // position) % 2


def chip_kernel(own_ref, other_ref, keep_ref, send_ref, kept):
    late = bit(1) == 1
    for j in range(2):
        first, second = ordered(own_ref[j].astype(f32), other_ref[j].astype(f32), late)
        kept[j] = then(first, second).astype(bf16)
    keep_ref[...] = kept[bit(2)]
    send_ref[...] = kept[1 - bit(2)]


def pair_kernel(own_ref, other_ref, total_ref):
    late = bit(2) == 1
    first, second = ordered(own_ref[...].astype(f32), other_ref[...].astype(f32), late)
    total_ref[...] = then(first, second).astype(bf16)


def near_kernel(own_ref, other_ref, total_ref, before_ref):
    late = bit(4) == 1
    own, other = own_ref[...].astype(f32), other_ref[...].astype(f32)
    first, second = ordered(own, other, late)
    total_ref[...] = then(first, second).astype(bf16)
    before_ref[...] = jnp.where(late, other, jnp.zeros_like(other)).astype(bf16)


def far_kernel(own_ref, other_ref, near_ref, total_ref, before_ref):
    late = bit(8) == 1
    own, other = own_ref[...].astype(f32), other_ref[...].astype(f32)
    near = near_ref[...].astype(f32)
    first, second = ordered(own, other, late)
    total_ref[...] = then(first, second).astype(bf16)
    before_ref[...] = jnp.where(late, then(other, near), near).astype(bf16)


def rows_kernel(own_ref, other_ref, total_ref):
    late = bit(16) == 1
    first, second = ordered(own_ref[...].astype(f32), other_ref[...].astype(f32), late)
    total_ref[...] = advance(first[:, :DK], second).astype(bf16)


def pair_start_kernel(rows_ref, row_ref, before_ref, own_ref, other_ref, keep_ref, send_ref):
    state = rows_ref[...].astype(f32)
    late_row = bit(16) == 1
    row = row_ref[...].astype(f32)
    state = jnp.where(late_row, advance(state, row), state)
    state = advance(state, before_ref[...].astype(f32))
    late = bit(2) == 1
    first = jnp.where(late, other_ref[...], own_ref[...]).astype(f32)
    after = advance(state, first)
    keep_ref[...] = jnp.where(late, after, state).astype(bf16)
    send_ref[...] = jnp.where(late, state, after).astype(bf16)


def chip_start_kernel(own_state, other_state, own_maps, other_maps, keep_ref, send_ref):
    late = bit(1) == 1
    upper = bit(2) == 1
    own, other = own_state[...].astype(f32), other_state[...].astype(f32)
    for j, state in enumerate(ordered(own, other, upper)):
        first = jnp.where(late, other_maps[j], own_maps[j]).astype(f32)
        after = advance(state, first)
        keep_ref[j] = jnp.where(late, after, state).astype(bf16)
        send_ref[j] = jnp.where(late, state, after).astype(bf16)


def finish_kernel(
    base_ref, gate_ref, own_ref, other_ref, gain_ref, w_ref, mine_ref, one, two, three, states, normed
):
    core = bit(1)
    here = lax.axis_index("head")
    for j in range(2):
        states[2 * j + core] = own_ref[j]
        states[2 * j + 1 - core] = other_ref[j]
    for h in range(4):
        lanes = slice(h * DK, (h + 1) * DK)
        heads_out = base_ref[:, lanes] + dot(gate_ref[:, lanes], states[h])
        scale = lax.rsqrt(jnp.mean(heads_out * heads_out, axis=-1, keepdims=True) + EPS)
        normed[:, lanes] = (heads_out * scale * gain_ref[:, lanes]).astype(bf16)
    rows = mine_ref.shape[0]
    for s, ref in enumerate((mine_ref, one, two, three)):
        start = pl.multiple_of((here + s) % 4 * rows, rows)
        ref[...] = dot(normed[pl.ds(start, rows), :], w_ref[...]).astype(ref.dtype)


def finish(base, gate, own, other, norm_gain, w_out):
    length, columns = base.shape
    rows, width = length // 4, w_out.shape[1]
    part = shape((rows, width), bf16)
    return small_call(
        finish_kernel,
        [shape((rows, width), f32), part, part, part],
        "finish",
        [pltpu.VMEM((4, DK, DK), bf16), pltpu.VMEM((length, columns), bf16)],
    )(base, gate, own, other, norm_gain[None, :], w_out)


def swapped(x, by):
    return lax.ppermute(x, "ctx", [(i, i ^ by) for i in range(lax.axis_size("ctx"))])


def per_device(tokens_in, w_qkv, conv_weight, beta_weight, beta_bias, norm_gain, w_out):
    peers = lax.axis_size("ctx")
    projected, edge, betas = project(tokens_in, w_qkv, beta_weight, beta_bias)
    edge = lax.ppermute(edge, "ctx", [(i, i + 1) for i in range(peers - 1)])
    queries, keys_t, uw, maps, send = local_maps(projected, edge, conv_weight, betas)
    sibling = swapped(send, 1)
    base, gate = inner_outputs(queries, keys_t, uw)
    chip, send = small_call(
        chip_kernel, [MAP, MAP], "chip_map", [pltpu.VMEM((2, DK, 2 * DK), bf16)]
    )(maps, sibling)
    neighbour = swapped(send, 2)
    (pair,) = small_call(pair_kernel, [MAP], "pair_map")(chip, neighbour)
    four, near = small_call(near_kernel, [MAP, MAP], "near_map")(pair, swapped(pair, 4))
    row, before = small_call(far_kernel, [MAP, MAP], "far_map")(four, swapped(four, 8), near)
    other_row = swapped(row, 16)
    (two_rows,) = small_call(rows_kernel, [STATE], "rows_state")(row, other_row)
    rows = lax.ppermute(two_rows, "ctx", [(i, i + 32) for i in range(peers - 32)])
    state, send = small_call(pair_start_kernel, [STATE, STATE], "pair_start")(
        rows, other_row, before, chip, neighbour
    )
    back = swapped(send, 2)
    both = shape((2, DK, DK), bf16)
    own, send = small_call(chip_start_kernel, [both, both], "chip_start")(
        state, back, maps, sibling
    )
    other = swapped(send, 1)
    mine, *parts = finish(base, gate, own, other, norm_gain, w_out)
    around = lax.axis_size("head")
    for s in (2, 1, 3):
        moved = lax.ppermute(parts[s - 1], "head", [(i, (i + s) % around) for i in range(around)])
        mine = mine + moved.astype(f32)
    return mine.astype(bf16)


def solution(mesh):
    return jax.shard_map(
        per_device,
        mesh=mesh,
        in_specs=(
            P("ctx", None),
            P(None, None, "head"),
            P(None, None, "head"),
            P("head", None),
            P("head"),
            P("head"),
            P("head", None),
        ),
        out_specs=P(("ctx", "head"), None),
        check_vma=False,
    )
```

time: 99.3 us -> 78.2 us (0.79)
  waiting for transfers between devices: 37.8 us -> 23.3 us
  between operations: 13.5 us -> 0.09 us
  starting transfers between devices: 30.2 us -> 37.7 us
  Pallas kernels: 14.3 us -> 12.9 us
    reduce_scatter x1 -> x0, waiting for transfers between devices: 24 us -> none  [per_device(): return lax.psum_scatter(partial, 'head', scatter_dimension=0, tiled=True)]
    ppermute x12 -> x11, waiting for transfers between devices: 12.6 us -> 22.2 us  [the longest x7 11.4 us: swapped(): lax.ppermute(x, 'ctx', [(i, i ^ by) for i in range(lax.axis_size('ctx'))])]
    ppermute x12 -> x11, starting transfers between devices: 25.3 us -> 32.7 us  [the longest x7 22.1 us: swapped(): lax.ppermute(x, 'ctx', [(i, i ^ by) for i in range(lax.axis_size('ctx'))])]
    pallas_call x6 -> x10, Pallas kernels: 13.7 us -> 12.4 us  [the longest x1 4.99 us: project(): pl.pallas_call(project_kernel, in_specs=[far, far, far, pl.BlockSpec(memo...]
  transfers between devices with their start and end apart: 14 -> 12, of which waited for: 9 -> 11; matrix products, arithmetic and copies ran while one was open for 0% -> 0% of each run, Pallas kernels for 1% -> 1%
where the time goes in v2:
time: 78.2 us; the launch traced here: 77.6 us
  starting transfers between devices  37.7 us (48%)
  waiting for transfers between devices  23.3 us (30%)
  Pallas kernels  12.9 us (16%)
  local copies, waits for them, and re-layouts  2.76 us (4%)
  other arithmetic  0.84 us (1%)
    ppermute x7, starting transfers between devices, swapped(): lax.ppermute(x, 'ctx', [(i, i ^ by) for i in range(lax.axis_size('ctx'))])  22.1 us
    ppermute x7, waiting for transfers between devices, swapped(): lax.ppermute(x, 'ctx', [(i, i ^ by) for i in range(lax.axis_size('ctx'))])  11.4 us
    ppermute x3, waiting for transfers between devices, per_device(): lax.ppermute(parts[s - 1], 'head', [(i, (i + s) % around) for i in range(...  9.76 us
    ppermute x3, starting transfers between devices, per_device(): lax.ppermute(parts[s - 1], 'head', [(i, (i + s) % around) for i in range(...  5.68 us
    pallas_call x1, Pallas kernels, project(): pl.pallas_call(project_kernel, in_specs=[far, far, far, pl.BlockSpec(memo...  4.99 us
    ppermute x1, starting transfers between devices, per_device(): edge = lax.ppermute(edge, 'ctx', [(i, i + 1) for i in range(peers - 1)])  4.94 us
    ppermute x1, starting transfers between devices, per_device(): lax.ppermute(two_rows, 'ctx', [(i, i + 32) for i in range(peers - 32)])  4.88 us
    pallas_call x1, Pallas kernels, local_maps(): pl.pallas_call(local_kernel, in_specs=whole(4), out_specs=whole(5), out_s...  3.96 us
  transfers between devices with their start and end apart: 12, of which 11 were waited for; matrix products, arithmetic and copies ran while one was open for 0% of the time, Pallas kernels for 1%

profile of v2, /device:TPU:1, one launch (start us, length us, event | category | flops | bytes accessed | tf_op | source)
XLA Modules:
  0.0 77.6 jit_solution(15066266570700065537)
XLA Ops:
  0.0 0.0 copy-start
  0.0 0.0 copy-start.1
  0.0 1.4 %copy-done.1 = bf16[256,2048]{1,0:T(8,128)(2,1)S(1)} copy-done((bf16[256,2048]{1,0:T(8,128)(2,1)S(1)}, bf16[256,2048]{1,0:T(8,128)(2,1)}, u32[]{:S(2)}) %copy-start.1) | copy-done | bytes 1048600
  1.4 0.0 copy-start.3
  1.4 0.7 copy-done.3
  2.1 0.0 copy-start.5
  2.1 0.7 copy-done.5
  2.8 0.0 copy-start.2
  2.8 0.0 copy-start.4
  2.8 5.0 %project.1 = (bf16[3,256,512]{2,1,0:T(8,128)(2,1)S(1)}, bf16[3,16,512]{2,1,0:T(8,128)(2,1)S(1)}, f32[256,4]{1,0:T(8,128)S(1)}) custom-call(bf16[256,2048]{1,0:T(8,128)(2,1)S(1)} %copy-done.1, bf16[3,2048,512]{2,1,0:T(8,128)(2,1)} %w_hbm.1, bf16[4,2048]{1,0:T(4,128)(2,1)S(1)} %copy-done.3, f32[1,4]{1,0:T(1,128)S(1)} %bitcast.3), custom_call_target="tpu_custom_call" | custom-call | tf_op jit(solution)/shard_map/project/pallas_call | solution.py:82
  7.8 4.9 %collective-permute-start = (bf16[3,16,512]{2,1,0:T(8,128)(2,1)S(1)}, bf16[3,16,512]{2,1,0:T(8,128)(2,1)S(1)}, u32[]{:S(2)}, u32[]{:S(2)}) collective-permute-start(bf16[3,16,512]{2,1,0:T(8,128)(2,1)S(1)} %get-tuple-element.30), channel_id=1, source_target_pairs={{0,4},{4,8},{8,12},{12,16},{16,20},{20,24},{24,28},{28,32},{32,36}... | collective-permute-start | bytes 147464 | tf_op jit(solution)/shard_map/ppermute | solution.py:383
  12.7 1.2 %collective-permute-done.edge_ref = bf16[3,16,512]{2,1,0:T(8,128)(2,1)S(1)} collective-permute-done((bf16[3,16,512]{2,1,0:T(8,128)(2,1)S(1)}, bf16[3,16,512]{2,1,0:T(8,128)(2,1)S(1)}, u32[]{:S(2)}, u32[]{:S(2)}) %collective-permute-start) | collective-permute-done | bytes 49184 | tf_op jit(solution)/shard_map/ppermute | solution.py:383
  13.9 0.0 copy-done.2
  13.9 4.0 %local_maps.1 = (bf16[256,512]{1,0:T(8,128)(2,1)S(1)}, bf16[4,128,256]{2,1,0:T(8,128)(2,1)S(1)}, bf16[4,256,256]{2,1,0:T(8,128)(2,1)S(1)}, bf16[2,128,256]{2,1,0:T(8,128)(2,1)S(1)}, bf16[2,128,256]{2,1,0:T(8,128)(2,1)S(1)}) custom-call(bf16[3,256,512]{2,1,0:T(8,128)(2,1)S(1)} %get-tuple-element.29.proj_ref, ...), custom_call_target="tpu_custom_call" | custom-call | tf_op jit(solution)/shard_map/local_maps/pallas_call | solution.py:205
  17.8 0.1 collective-permute-start.1
  17.9 1.3 %collective-permute-done.1.other_ref.other_maps = bf16[2,128,256]{2,1,0:T(8,128)(2,1)S(1)} collective-permute-done((bf16[2,128,256]{2,1,0:T(8,128)(2,1)S(1)}, bf16[2,128,256]{2,1,0:T(8,128)(2,1)S(1)}, u32[]{:S(2)}, u32[]{:S(2)}) %collective-permute-start.1) | collective-permute-done | bytes 131104 | tf_op jit(solution)/shard_map/ppermute | solution.py:377
  19.3 0.2 chip_map.1
  19.5 2.2 %collective-permute-start.2 = (bf16[128,256]{1,0:T(8,128)(2,1)S(1)}, bf16[128,256]{1,0:T(8,128)(2,1)S(1)}, u32[]{:S(2)}, u32[]{:S(2)}) collective-permute-start(bf16[128,256]{1,0:T(8,128)(2,1)S(1)} %get-tuple-element.40), channel_id=1, source_target_pairs={{0,8},{4,12},{8,0},{12,4},{16,24},{20,28},{24,16},{28,20},{32,40},... | collective-permute-start | bytes 196616 | tf_op jit(solution)/shard_map/ppermute | solution.py:377
  21.7 2.2 %collective-permute-done.2.other_ref = bf16[128,256]{1,0:T(8,128)(2,1)S(1)} collective-permute-done((bf16[128,256]{1,0:T(8,128)(2,1)S(1)}, bf16[128,256]{1,0:T(8,128)(2,1)S(1)}, u32[]{:S(2)}, u32[]{:S(2)}) %collective-permute-start.2) | collective-permute-done | bytes 65568 | tf_op jit(solution)/shard_map/ppermute | solution.py:377
  23.9 0.2 pair_map.1.own_ref
  24.0 4.0 %collective-permute-start.3 = (bf16[128,256]{1,0:T(8,128)(2,1)S(1)}, bf16[128,256]{1,0:T(8,128)(2,1)S(1)}, u32[]{:S(2)}, u32[]{:S(2)}) collective-permute-start(bf16[128,256]{1,0:T(8,128)(2,1)S(1)} %pair_map.1.own_ref), channel_id=1, source_target_pairs={{0,16},{4,20},{8,24},{12,28},{16,0},{20,4},{24,8},{28,12},{32,48},... | collective-permute-start | bytes 196616 | tf_op jit(solution)/shard_map/ppermute | solution.py:377
  28.0 1.7 %collective-permute-done.3.other_ref = bf16[128,256]{1,0:T(8,128)(2,1)S(1)} collective-permute-done((bf16[128,256]{1,0:T(8,128)(2,1)S(1)}, bf16[128,256]{1,0:T(8,128)(2,1)S(1)}, u32[]{:S(2)}, u32[]{:S(2)}) %collective-permute-start.3) | collective-permute-done | bytes 65568 | tf_op jit(solution)/shard_map/ppermute | solution.py:377
  29.7 0.2 near_map.1
  29.8 6.7 %collective-permute-start.4 = (bf16[128,256]{1,0:T(8,128)(2,1)S(1)}, bf16[128,256]{1,0:T(8,128)(2,1)S(1)}, u32[]{:S(2)}, u32[]{:S(2)}) collective-permute-start(bf16[128,256]{1,0:T(8,128)(2,1)S(1)} %get-tuple-element.41.own_ref), channel_id=1, source_target_pairs={{0,32},{4,36},{8,40},{12,44},{16,48},{20,52},{24,56},{28,60},{32,0... | collective-permute-start | bytes 196616 | tf_op jit(solution)/shard_map/ppermute | solution.py:377
  36.5 1.7 %collective-permute-done.4.other_ref = bf16[128,256]{1,0:T(8,128)(2,1)S(1)} collective-permute-done((bf16[128,256]{1,0:T(8,128)(2,1)S(1)}, bf16[128,256]{1,0:T(8,128)(2,1)S(1)}, u32[]{:S(2)}, u32[]{:S(2)}) %collective-permute-start.4) | collective-permute-done | bytes 65568 | tf_op jit(solution)/shard_map/ppermute | solution.py:377
  38.2 0.2 far_map.1
  38.4 2.1 %collective-permute-start.5 = (bf16[128,256]{1,0:T(8,128)(2,1)S(1)}, bf16[128,256]{1,0:T(8,128)(2,1)S(1)}, u32[]{:S(2)}, u32[]{:S(2)}) collective-permute-start(bf16[128,256]{1,0:T(8,128)(2,1)S(1)} %get-tuple-element.43.own_ref), channel_id=1, source_target_pairs={{0,64},{4,68},{8,72},{12,76},{16,80},{20,84},{24,88},{28,92},{32,9... | collective-permute-start | bytes 196616 | tf_op jit(solution)/shard_map/ppermute | solution.py:377
  40.5 1.7 %collective-permute-done.5.other_ref.row_ref = bf16[128,256]{1,0:T(8,128)(2,1)S(1)} collective-permute-done((bf16[128,256]{1,0:T(8,128)(2,1)S(1)}, bf16[128,256]{1,0:T(8,128)(2,1)S(1)}, u32[]{:S(2)}, u32[]{:S(2)}) %collective-permute-start.5) | collective-permute-done | bytes 65568 | tf_op jit(solution)/shard_map/ppermute | solution.py:377
  42.1 0.1 rows_state.1
  42.3 4.9 %collective-permute-start.6 = (bf16[128,128]{1,0:T(8,128)(2,1)S(1)}, bf16[128,128]{1,0:T(8,128)(2,1)S(1)}, u32[]{:S(2)}, u32[]{:S(2)}) collective-permute-start(bf16[128,128]{1,0:T(8,128)(2,1)S(1)} %rows_state.1), channel_id=1, source_target_pairs={{0,128},{4,132},{8,136},{12,140},{16,144},{20,148},{24,152},{28,15... | collective-permute-start | bytes 98312 | tf_op jit(solution)/shard_map/ppermute | solution.py:396
  47.2 1.0 %collective-permute-done.6.rows_ref = bf16[128,128]{1,0:T(8,128)(2,1)S(1)} collective-permute-done((bf16[128,128]{1,0:T(8,128)(2,1)S(1)}, bf16[128,128]{1,0:T(8,128)(2,1)S(1)}, u32[]{:S(2)}, u32[]{:S(2)}) %collective-permute-start.6) | collective-permute-done | bytes 32800 | tf_op jit(solution)/shard_map/ppermute | solution.py:396
  48.2 0.4 pair_start.1
  48.6 0.3 collective-permute-start.7
  48.9 2.5 %collective-permute-done.7.other_state = bf16[128,128]{1,0:T(8,128)(2,1)S(1)} collective-permute-done((bf16[128,128]{1,0:T(8,128)(2,1)S(1)}, bf16[128,128]{1,0:T(8,128)(2,1)S(1)}, u32[]{:S(2)}, u32[]{:S(2)}) %collective-permute-start.7) | collective-permute-done | bytes 32800 | tf_op jit(solution)/shard_map/ppermute | solution.py:377
  51.4 0.2 chip_start.1
  51.6 6.8 %collective-permute-start.8 = (bf16[2,128,128]{2,1,0:T(8,128)(2,1)S(1)}, bf16[2,128,128]{2,1,0:T(8,128)(2,1)S(1)}, u32[]{:S(2)}, u32[]{:S(2)}) collective-permute-start(bf16[2,128,128]{2,1,0:T(8,128)(2,1)S(1)} %get-tuple-element.48), channel_id=1, source_target_pairs={{0,4},{4,0},{8,12},{12,8},{16,20},{20,16},{24,28},{28,24},{32,36},... | collective-permute-start | bytes 196616 | tf_op jit(solution)/shard_map/ppermute | solution.py:377
  58.4 0.5 inner_outputs.1
  58.9 0.4 collective-permute-done.8.other_ref
  59.3 0.0 copy-done
  59.3 0.0 copy-done.4
  59.3 2.0 %finish.1 = (f32[64,2048]{1,0:T(8,128)S(1)}, bf16[64,2048]{1,0:T(8,128)(2,1)S(1)}, bf16[64,2048]{1,0:T(8,128)(2,1)S(1)}, bf16[64,2048]{1,0:T(8,128)(2,1)S(1)}) custom-call(f32[256,512]{1,0:T(8,128)S(1)} %get-tuple-element.35.base_ref, bf16[256,512]{1,0:T(8,128)(2,1)S(1)} %get-tuple-element.36.gate_ref, bf16[2,128,128]{2,1,0:T(8,128)(2,1)S(1)} %get-tuple-element.47.own_ref, ...), custom_call_target="tpu_custom_call" | custom-call | tf_op jit(solution)/shard_map/finish/pallas_call | solution.py:368
  61.3 3.0 %collective-permute-start.9 = (bf16[64,2048]{1,0:T(8,128)(2,1)S(1)}, bf16[64,2048]{1,0:T(8,128)(2,1)S(1)}, u32[]{:S(2)}, u32[]{:S(2)}) collective-permute-start(bf16[64,2048]{1,0:T(8,128)(2,1)S(1)} %get-tuple-element.50), channel_id=1, source_target_pairs={{0,2},{1,3},{2,0},{3,1},{4,6},{5,7},{6,4},{7,5},{8,10},{9,11},{10,... | collective-permute-start | bytes 786440 | tf_op jit(solution)/shard_map/ppermute | solution.py:409
  64.3 0.4 collective-permute-start.10
  64.7 2.3 %collective-permute-start.11 = (bf16[64,2048]{1,0:T(8,128)(2,1)S(1)}, bf16[64,2048]{1,0:T(8,128)(2,1)S(1)}, u32[]{:S(2)}, u32[]{:S(2)}) collective-permute-start(bf16[64,2048]{1,0:T(8,128)(2,1)S(1)} %get-tuple-element.52), channel_id=1, source_target_pairs={{0,3},{1,0},{2,1},{3,2},{4,7},{5,4},{6,5},{7,6},{8,11},{9,8},{10,9... | collective-permute-start | bytes 786440 | tf_op jit(solution)/shard_map/ppermute | solution.py:409
  67.0 3.5 %collective-permute-done.9 = bf16[64,2048]{1,0:T(8,128)(2,1)S(1)} collective-permute-done((bf16[64,2048]{1,0:T(8,128)(2,1)S(1)}, bf16[64,2048]{1,0:T(8,128)(2,1)S(1)}, u32[]{:S(2)}, u32[]{:S(2)}) %collective-permute-start.9) | collective-permute-done | bytes 262176 | tf_op jit(solution)/shard_map/ppermute | solution.py:409
  70.5 6.3 %collective-permute-done.10 = bf16[64,2048]{1,0:T(8,128)(2,1)S(1)} collective-permute-done((bf16[64,2048]{1,0:T(8,128)(2,1)S(1)}, bf16[64,2048]{1,0:T(8,128)(2,1)S(1)}, u32[]{:S(2)}, u32[]{:S(2)}) %collective-permute-start.10) | collective-permute-done | bytes 262176 | tf_op jit(solution)/shard_map/ppermute | solution.py:409
  76.7 0.0 collective-permute-done.11
  76.7 0.8 %add_convert_fusion = bf16[64,2048]{1,0:T(8,128)(2,1)} fusion(bf16[64,2048]{1,0:T(8,128)(2,1)S(1)} %collective-permute-done.11, bf16[64,2048]{1,0:T(8,128)(2,1)S(1)} %collective-permute-done.10, f32[64,2048]{1,0:T(8,128)S(1)} %get-tuple-element.49, bf16[64,2048]{1,0:T(8,128)(2,1)S(1)} %collective-permute-done.9), kind=kLoop, calls=%fused_computation | loop fusion | flops 917504 | bytes 1572864 | tf_op jit(solution)/shard_map/convert_element_type | solution.py:411
Async XLA Ops:
  0.0 59.3 %copy-start = (bf16[512,2048]{1,0:T(8,128)(2,1)S(1)}, bf16[512,2048]{1,0:T(8,128)(2,1)}, u32[]{:S(2)}) copy-start(bf16[512,2048]{1,0:T(8,128)(2,1)} %w_ref.1) | copy-start | bytes 6291460
  0.0 1.4 %copy-start.1 = (bf16[256,2048]{1,0:T(8,128)(2,1)S(1)}, bf16[256,2048]{1,0:T(8,128)(2,1)}, u32[]{:S(2)}) copy-start(bf16[256,2048]{1,0:T(8,128)(2,1)} %tokens_hbm.1) | copy-start | bytes 3145732
  1.4 0.7 copy-start.3
  2.1 0.7 copy-start.5
  2.8 11.1 %copy-start.2 = (f32[3,4,512]{2,1,0:T(4,128)S(1)}, f32[3,4,512]{2,1,0:T(4,128)}, u32[]{:S(2)}) copy-start(f32[3,4,512]{2,1,0:T(4,128)} %conv_ref.1) | copy-start | bytes 73732
  2.8 56.6 %copy-start.4 = (f32[512]{0:T(512)S(1)}, f32[512]{0:T(512)}, u32[]{:S(2)}) copy-start(f32[512]{0:T(512)} %param.12) | copy-start | bytes 6148
  7.8 6.1 %collective-permute-start = (bf16[3,16,512]{2,1,0:T(8,128)(2,1)S(1)}, bf16[3,16,512]{2,1,0:T(8,128)(2,1)S(1)}, u32[]{:S(2)}, u32[]{:S(2)}) collective-permute-start(bf16[3,16,512]{2,1,0:T(8,128)(2,1)S(1)} %get-tuple-element.30), channel_id=1, source_target_pairs={{0,4},{4,8},{8,12},{12,16},{16,20},{20,24},{24,28},{28,32},{32,36}... | collective-permute-start | bytes 147464 | tf_op jit(solution)/shard_map/ppermute | solution.py:383
  17.8 1.4 %collective-permute-start.1 = (bf16[2,128,256]{2,1,0:T(8,128)(2,1)S(1)}, bf16[2,128,256]{2,1,0:T(8,128)(2,1)S(1)}, u32[]{:S(2)}, u32[]{:S(2)}) collective-permute-start(bf16[2,128,256]{2,1,0:T(8,128)(2,1)S(1)} %get-tuple-element.38), channel_id=1, source_target_pairs={{0,4},{4,0},{8,12},{12,8},{16,20},{20,16},{24,28},{28,24},{32,36},... | collective-permute-start | bytes 393224 | tf_op jit(solution)/shard_map/ppermute | solution.py:377
  19.5 4.4 %collective-permute-start.2 = (bf16[128,256]{1,0:T(8,128)(2,1)S(1)}, bf16[128,256]{1,0:T(8,128)(2,1)S(1)}, u32[]{:S(2)}, u32[]{:S(2)}) collective-permute-start(bf16[128,256]{1,0:T(8,128)(2,1)S(1)} %get-tuple-element.40), channel_id=1, source_target_pairs={{0,8},{4,12},{8,0},{12,4},{16,24},{20,28},{24,16},{28,20},{32,40},... | collective-permute-start | bytes 196616 | tf_op jit(solution)/shard_map/ppermute | solution.py:377
  24.0 5.6 %collective-permute-start.3 = (bf16[128,256]{1,0:T(8,128)(2,1)S(1)}, bf16[128,256]{1,0:T(8,128)(2,1)S(1)}, u32[]{:S(2)}, u32[]{:S(2)}) collective-permute-start(bf16[128,256]{1,0:T(8,128)(2,1)S(1)} %pair_map.1.own_ref), channel_id=1, source_target_pairs={{0,16},{4,20},{8,24},{12,28},{16,0},{20,4},{24,8},{28,12},{32,48},... | collective-permute-start | bytes 196616 | tf_op jit(solution)/shard_map/ppermute | solution.py:377
  29.8 8.3 %collective-permute-start.4 = (bf16[128,256]{1,0:T(8,128)(2,1)S(1)}, bf16[128,256]{1,0:T(8,128)(2,1)S(1)}, u32[]{:S(2)}, u32[]{:S(2)}) collective-permute-start(bf16[128,256]{1,0:T(8,128)(2,1)S(1)} %get-tuple-element.41.own_ref), channel_id=1, source_target_pairs={{0,32},{4,36},{8,40},{12,44},{16,48},{20,52},{24,56},{28,60},{32,0... | collective-permute-start | bytes 196616 | tf_op jit(solution)/shard_map/ppermute | solution.py:377
  38.4 3.7 %collective-permute-start.5 = (bf16[128,256]{1,0:T(8,128)(2,1)S(1)}, bf16[128,256]{1,0:T(8,128)(2,1)S(1)}, u32[]{:S(2)}, u32[]{:S(2)}) collective-permute-start(bf16[128,256]{1,0:T(8,128)(2,1)S(1)} %get-tuple-element.43.own_ref), channel_id=1, source_target_pairs={{0,64},{4,68},{8,72},{12,76},{16,80},{20,84},{24,88},{28,92},{32,9... | collective-permute-start | bytes 196616 | tf_op jit(solution)/shard_map/ppermute | solution.py:377
  42.3 5.9 %collective-permute-start.6 = (bf16[128,128]{1,0:T(8,128)(2,1)S(1)}, bf16[128,128]{1,0:T(8,128)(2,1)S(1)}, u32[]{:S(2)}, u32[]{:S(2)}) collective-permute-start(bf16[128,128]{1,0:T(8,128)(2,1)S(1)} %rows_state.1), channel_id=1, source_target_pairs={{0,128},{4,132},{8,136},{12,140},{16,144},{20,148},{24,152},{28,15... | collective-permute-start | bytes 98312 | tf_op jit(solution)/shard_map/ppermute | solution.py:396
  48.6 2.9 %collective-permute-start.7 = (bf16[128,128]{1,0:T(8,128)(2,1)S(1)}, bf16[128,128]{1,0:T(8,128)(2,1)S(1)}, u32[]{:S(2)}, u32[]{:S(2)}) collective-permute-start(bf16[128,128]{1,0:T(8,128)(2,1)S(1)} %get-tuple-element.46), channel_id=1, source_target_pairs={{0,8},{4,12},{8,0},{12,4},{16,24},{20,28},{24,16},{28,20},{32,40},... | collective-permute-start | bytes 98312 | tf_op jit(solution)/shard_map/ppermute | solution.py:377
  51.6 7.7 %collective-permute-start.8 = (bf16[2,128,128]{2,1,0:T(8,128)(2,1)S(1)}, bf16[2,128,128]{2,1,0:T(8,128)(2,1)S(1)}, u32[]{:S(2)}, u32[]{:S(2)}) collective-permute-start(bf16[2,128,128]{2,1,0:T(8,128)(2,1)S(1)} %get-tuple-element.48), channel_id=1, source_target_pairs={{0,4},{4,0},{8,12},{12,8},{16,20},{20,16},{24,28},{28,24},{32,36},... | collective-permute-start | bytes 196616 | tf_op jit(solution)/shard_map/ppermute | solution.py:377
  61.3 9.2 %collective-permute-start.9 = (bf16[64,2048]{1,0:T(8,128)(2,1)S(1)}, bf16[64,2048]{1,0:T(8,128)(2,1)S(1)}, u32[]{:S(2)}, u32[]{:S(2)}) collective-permute-start(bf16[64,2048]{1,0:T(8,128)(2,1)S(1)} %get-tuple-element.50), channel_id=1, source_target_pairs={{0,2},{1,3},{2,0},{3,1},{4,6},{5,7},{6,4},{7,5},{8,10},{9,11},{10,... | collective-permute-start | bytes 786440 | tf_op jit(solution)/shard_map/ppermute | solution.py:409
  64.3 12.4 %collective-permute-start.10 = (bf16[64,2048]{1,0:T(8,128)(2,1)S(1)}, bf16[64,2048]{1,0:T(8,128)(2,1)S(1)}, u32[]{:S(2)}, u32[]{:S(2)}) collective-permute-start(bf16[64,2048]{1,0:T(8,128)(2,1)S(1)} %get-tuple-element.51), channel_id=1, source_target_pairs={{0,1},{1,2},{2,3},{3,0},{4,5},{5,6},{6,7},{7,4},{8,9},{9,10},{10,1... | collective-permute-start | bytes 786440 | tf_op jit(solution)/shard_map/ppermute | solution.py:409
  64.7 12.0 %collective-permute-start.11 = (bf16[64,2048]{1,0:T(8,128)(2,1)S(1)}, bf16[64,2048]{1,0:T(8,128)(2,1)S(1)}, u32[]{:S(2)}, u32[]{:S(2)}) collective-permute-start(bf16[64,2048]{1,0:T(8,128)(2,1)S(1)} %get-tuple-element.52), channel_id=1, source_target_pairs={{0,3},{1,0},{2,1},{3,2},{4,7},{5,4},{6,5},{7,6},{8,11},{9,8},{10,9... | collective-permute-start | bytes 786440 | tf_op jit(solution)/shard_map/ppermute | solution.py:409

commit v3 on v2

--- a/solution.py
+++ b/solution.py
@@ -36,52 +36,40 @@
     return jax.ShapeDtypeStruct(dims, kind)
 
 
-PIECES = 2
-
-
 def project_kernel(
-    tokens_hbm, w_hbm, beta_w_hbm, beta_b_ref, out_ref, edge_ref, betas_ref,
+    tokens_hbm, w_hbm, beta_w_hbm, out_ref, edge_ref, logits_ref,
     tokens_ref, w_ref, beta_w_ref, small_sems, w_sems
 ):
-    length, depth = tokens_ref.shape
-    part = depth // PIECES
+    length = tokens_ref.shape[0]
     first = pltpu.make_async_copy(tokens_hbm, tokens_ref, small_sems.at[0])
+    last = pltpu.make_async_copy(beta_w_hbm, beta_w_ref, small_sems.at[1])
+    copies = [pltpu.make_async_copy(w_hbm.at[s], w_ref.at[s], w_sems.at[s]) for s in range(3)]
     first.start()
-    copies = []
+    last.start()
+    copies[0].start()
+    copies[1].start()
+    last.wait()
+    first.wait()
+    logits_ref[...] = dot_t(tokens_ref[...], beta_w_ref[...])
     for s in range(3):
-        for k in range(PIECES):
-            rows = pl.ds(k * part, part)
-            copy = pltpu.make_async_copy(
-                w_hbm.at[s, rows], w_ref.at[s, rows], w_sems.at[s * PIECES + k]
-            )
-            copy.start()
-            copies.append(copy)
-    last = pltpu.make_async_copy(beta_w_hbm, beta_w_ref, small_sems.at[1])
-    last.start()
-    first.wait()
-    for s in range(3):
-        total = None
-        for k in range(PIECES):
-            rows = slice(k * part, (k + 1) * part)
-            copies[s * PIECES + k].wait()
-            term = dot(tokens_ref[:, rows], w_ref[s, rows])
-            total = term if total is None else total + term
-        result = total.astype(bf16)
+        copies[s].wait()
+        if s == 0:
+            copies[2].start()
+        result = dot(tokens_ref[...], w_ref[s]).astype(bf16)
         out_ref[s] = result
         edge_ref[s] = result[length - EDGE :]
-    last.wait()
-    logits = dot_t(tokens_ref[...], beta_w_ref[...]) + beta_b_ref[...]
-    betas_ref[...] = 1.0 / (1.0 + jnp.exp(-logits))
-
-
-def project(tokens, w_qkv, beta_weight, beta_bias):
+
+
+def project(tokens, w_qkv, beta_weight):
     length, depth = tokens.shape
     columns = w_qkv.shape[2]
     heads = beta_weight.shape[0]
-    far = pl.BlockSpec(memory_space=pltpu.HBM)
+    operands = [
+        pltpu.with_memory_space_constraint(x, pltpu.HBM) for x in (tokens, w_qkv, beta_weight)
+    ]
     return pl.pallas_call(
         project_kernel,
-        in_specs=[far, far, far, pl.BlockSpec(memory_space=pltpu.VMEM)],
+        in_specs=[pl.BlockSpec(memory_space=pltpu.HBM)] * 3,
         out_specs=whole(3),
         out_shape=[
             shape((3, length, columns), bf16),
@@ -93,11 +81,11 @@
             pltpu.VMEM(w_qkv.shape, bf16),
             pltpu.VMEM(beta_weight.shape, bf16),
             pltpu.SemaphoreType.DMA((2,)),
-            pltpu.SemaphoreType.DMA((3 * PIECES,)),
+            pltpu.SemaphoreType.DMA((3,)),
         ],
         compiler_params=params(),
         name="project",
-    )(tokens, w_qkv, beta_weight, beta_bias[None, :])
+    )(*operands)
 
 
 def grid_index(rows, columns):
@@ -146,11 +134,12 @@
 
 
 def local_kernel(
-    proj_ref, edge_ref, conv_ref, betas_ref,
+    proj_ref, edge_ref, conv_ref, logits_ref, bias_ref,
     queries_ref, keys_t_ref, uw_ref, keep_ref, send_ref, padded, maps
 ):
     length = proj_ref.shape[1]
-    heads = betas_ref.shape[1]
+    heads = logits_ref.shape[1]
+    betas = 1.0 / (1.0 + jnp.exp(-(logits_ref[...] + bias_ref[...])))
     core = lax.axis_index("ctx") % 2
     for s in range(3):
         padded[s, :EDGE] = edge_ref[s].astype(f32)
@@ -170,12 +159,12 @@
         query, key, value = mixed
         query = query * lax.rsqrt(jnp.sum(query * query, axis=-1, keepdims=True) + EPS)
         key = key * lax.rsqrt(jnp.sum(key * key, axis=-1, keepdims=True) + EPS)
-        queries_ref[:, lanes] = query.astype(bf16)
+        queries_ref[h] = query.astype(bf16)
         small = key.astype(bf16)
         small_t = key.T.astype(bf16)
         keys_t_ref[h] = small_t
         keys_t.append(small_t)
-        beta = betas_ref[:, h : h + 1]
+        beta = betas[:, h : h + 1]
         system = jnp.where(strict, beta * dot(small, small_t), 0.0)
         systems.append(jnp.concatenate([system[:BLOCK, :BLOCK], system[BLOCK:, BLOCK:]], axis=1))
         corners.append(system[BLOCK:, :BLOCK].astype(bf16))
@@ -198,16 +187,16 @@
         send_ref[j] = maps[2 * j + 1 - core]
 
 
-def local_maps(projected, edge, conv_weight, betas):
+def local_maps(projected, edge, conv_weight, logits, beta_bias):
     length, columns = projected.shape[1:]
-    heads = betas.shape[1]
+    heads = logits.shape[1]
     two = shape((heads // 2, DK, 2 * DK), bf16)
     return pl.pallas_call(
         local_kernel,
-        in_specs=whole(4),
+        in_specs=whole(5),
         out_specs=whole(5),
         out_shape=[
-            shape((length, columns), bf16),
+            shape((heads, length, DK), bf16),
             shape((heads, DK, length), bf16),
             shape((heads, length, 2 * DK), bf16),
             two, two,
@@ -218,29 +207,33 @@
         ],
         compiler_params=params(),
         name="local_maps",
-    )(projected, edge, conv_weight, betas)
-
-
-def inner_kernel(queries_ref, keys_t_ref, uw_ref, base_ref, gate_ref):
-    length = queries_ref.shape[0]
+    )(projected, edge, conv_weight, logits, beta_bias[None, :])
+
+
+def inner_kernel(queries_ref, keys_t_ref, uw_ref, base_ref, gate_ref, base_out, gate_out):
+    length = queries_ref.shape[1]
     row, column = grid_index(length, length)
-    for h in range(keys_t_ref.shape[0]):
-        lanes = slice(h * DK, (h + 1) * DK)
-        query = queries_ref[:, lanes]
-        scores = jnp.where(row >= column, dot(query, keys_t_ref[h]), 0.0).astype(bf16)
-        both = dot(scores, uw_ref[h])
-        base_ref[:, lanes] = both[:, :DK]
-        gate_ref[:, lanes] = (query.astype(f32) - both[:, DK:]).astype(bf16)
+    core = bit(1)
+    for j in range(2):
+        for h, base, gate in (
+            (2 * j + core, base_ref, gate_ref),
+            (2 * j + 1 - core, base_out, gate_out),
+        ):
+            query = queries_ref[h]
+            scores = jnp.where(row >= column, dot(query, keys_t_ref[h]), 0.0).astype(bf16)
+            both = dot(scores, uw_ref[h])
+            base[j] = both[:, :DK]
+            gate[j] = (query.astype(f32) - both[:, DK:]).astype(bf16)
 
 
 def inner_outputs(queries, keys_t, uw):
-    length, columns = queries.shape
-    heads = keys_t.shape[0]
+    heads, length, _ = queries.shape
+    outs = [shape((2, length, DK), f32), shape((2, length, DK), bf16)]
     return pl.pallas_call(
         inner_kernel,
         in_specs=whole(3),
-        out_specs=whole(2),
-        out_shape=[shape((length, columns), f32), shape((length, columns), bf16)],
+        out_specs=whole(4),
+        out_shape=outs + outs,
         compiler_params=params(),
         cost_estimate=pl.CostEstimate(
             flops=2 * heads * length * length * 3 * DK, bytes_accessed=2 << 20, transcendentals=0
@@ -331,84 +324,114 @@
     send_ref[...] = jnp.where(late, state, after).astype(bf16)
 
 
-def chip_start_kernel(own_state, other_state, own_maps, other_maps, keep_ref, send_ref):
-    late = bit(1) == 1
-    upper = bit(2) == 1
+def finish_kernel(
+    own_state, other_state, own_maps, other_maps, base_ref, gate_ref, base_in, gate_in, gain_ref,
+    mine_ref, one, two, three, normed
+):
+    late, upper = bit(1) == 1, bit(2) == 1
+    core = bit(1)
+    here = lax.axis_index("head")
     own, other = own_state[...].astype(f32), other_state[...].astype(f32)
     for j, state in enumerate(ordered(own, other, upper)):
         first = jnp.where(late, other_maps[j], own_maps[j]).astype(f32)
         after = advance(state, first)
-        keep_ref[j] = jnp.where(late, after, state).astype(bf16)
-        send_ref[j] = jnp.where(late, state, after).astype(bf16)
-
-
-def finish_kernel(
-    base_ref, gate_ref, own_ref, other_ref, gain_ref, w_ref, mine_ref, one, two, three, states, normed
-):
-    core = bit(1)
-    here = lax.axis_index("head")
-    for j in range(2):
-        states[2 * j + core] = own_ref[j]
-        states[2 * j + 1 - core] = other_ref[j]
-    for h in range(4):
-        lanes = slice(h * DK, (h + 1) * DK)
-        heads_out = base_ref[:, lanes] + dot(gate_ref[:, lanes], states[h])
-        scale = lax.rsqrt(jnp.mean(heads_out * heads_out, axis=-1, keepdims=True) + EPS)
-        normed[:, lanes] = (heads_out * scale * gain_ref[:, lanes]).astype(bf16)
-    rows = mine_ref.shape[0]
+        gain = gain_ref[2 * j + core]
+        for slot, start, base, gate in (
+            (0, jnp.where(late, after, state), base_ref, gate_ref),
+            (1, jnp.where(late, state, after), base_in, gate_in),
+        ):
+            heads_out = base[j] + dot(gate[j], start.astype(bf16))
+            scale = lax.rsqrt(jnp.mean(heads_out * heads_out, axis=-1, keepdims=True) + EPS)
+            normed[slot, :, j * DK : (j + 1) * DK] = (heads_out * scale * gain).astype(bf16)
+    rows = mine_ref.shape[1]
     for s, ref in enumerate((mine_ref, one, two, three)):
         start = pl.multiple_of((here + s) % 4 * rows, rows)
-        ref[...] = dot(normed[pl.ds(start, rows), :], w_ref[...]).astype(ref.dtype)
-
-
-def finish(base, gate, own, other, norm_gain, w_out):
-    length, columns = base.shape
-    rows, width = length // 4, w_out.shape[1]
-    part = shape((rows, width), bf16)
+        for slot in range(2):
+            ref[slot] = normed[slot, pl.ds(start, rows), :]
+
+
+def finish(states, maps, inner, inner_in, norm_gain):
+    length = inner[0].shape[1]
+    part = shape((2, length // 4, 2 * DK), bf16)
     return small_call(
-        finish_kernel,
-        [shape((rows, width), f32), part, part, part],
-        "finish",
-        [pltpu.VMEM((4, DK, DK), bf16), pltpu.VMEM((length, columns), bf16)],
-    )(base, gate, own, other, norm_gain[None, :], w_out)
+        finish_kernel, [part] * 4, "finish", [pltpu.VMEM((2, length, 2 * DK), bf16)]
+    )(*states, *maps, *inner, *inner_in, norm_gain.reshape(4, 1, DK))
+
+
+def merge_kernel(mine_ref, one, two, three, w_hbm, keep_ref, send_ref, w_ref, sems):
+    here = lax.axis_index("head")
+    copies = [
+        pltpu.make_async_copy(w_hbm.at[(here + 4 - s) % 4], w_ref.at[s], sems.at[s])
+        for s in range(4)
+    ]
+    for copy in copies:
+        copy.start()
+    _, rows, width = mine_ref.shape
+    total = None
+    for s, ref in enumerate((mine_ref, one, two, three)):
+        copies[s].wait()
+        term = dot(ref[...].reshape(2 * rows, width), w_ref[s])
+        total = term if total is None else total + term
+    keep_ref[...] = total[:rows]
+    send_ref[...] = total[rows:].astype(bf16)
+
+
+def merge(parts, weights):
+    rows = parts[0].shape[1]
+    width = weights.shape[-1]
+    far = pl.BlockSpec(memory_space=pltpu.HBM)
+    return pl.pallas_call(
+        merge_kernel,
+        in_specs=whole(4) + [far],
+        out_specs=whole(2),
+        out_shape=[shape((rows, width), f32), shape((rows, width), bf16)],
+        scratch_shapes=[pltpu.VMEM(weights.shape, bf16), pltpu.SemaphoreType.DMA((4,))],
+        compiler_params=params(),
+        name="merge",
+    )(*parts, pltpu.with_memory_space_constraint(weights, pltpu.HBM))
+
+
+def permuted(x, target):
+    pairs = [(i, target(i)) for i in range(lax.axis_size("ctx"))]
+    return lax.ppermute(x, "ctx", [p for p in pairs if p[1] is not None])
 
 
 def swapped(x, by):
-    return lax.ppermute(x, "ctx", [(i, i ^ by) for i in range(lax.axis_size("ctx"))])
+    return permuted(x, lambda i: i ^ by)
 
 
 def per_device(tokens_in, w_qkv, conv_weight, beta_weight, beta_bias, norm_gain, w_out):
-    peers = lax.axis_size("ctx")
-    projected, edge, betas = project(tokens_in, w_qkv, beta_weight, beta_bias)
-    edge = lax.ppermute(edge, "ctx", [(i, i + 1) for i in range(peers - 1)])
-    queries, keys_t, uw, maps, send = local_maps(projected, edge, conv_weight, betas)
+    peers, around = lax.axis_size("ctx"), lax.axis_size("head")
+    width = w_out.shape[1]
+    half = lax.dynamic_index_in_dim(w_out.reshape(2, 2, DK, width), bit(1), 1, keepdims=False)
+    weights = lax.all_gather(half.reshape(2 * DK, width), "head")
+    projected, edge, logits = project(tokens_in, w_qkv, beta_weight)
+    edge = permuted(edge, lambda i: i + 1 if i + 1 < peers else None)
+    queries, keys_t, uw, maps, send = local_maps(projected, edge, conv_weight, logits, beta_bias)
     sibling = swapped(send, 1)
-    base, gate = inner_outputs(queries, keys_t, uw)
+    base, gate, *sent = inner_outputs(queries, keys_t, uw)
+    inner_in = [swapped(x, 1) for x in sent]
     chip, send = small_call(
         chip_kernel, [MAP, MAP], "chip_map", [pltpu.VMEM((2, DK, 2 * DK), bf16)]
     )(maps, sibling)
     neighbour = swapped(send, 2)
     (pair,) = small_call(pair_kernel, [MAP], "pair_map")(chip, neighbour)
     four, near = small_call(near_kernel, [MAP, MAP], "near_map")(pair, swapped(pair, 4))
-    row, before = small_call(far_kernel, [MAP, MAP], "far_map")(four, swapped(four, 8), near)
+    row, before = small_call(far_kernel, [MAP, MAP], "far_map")(four, swapped(four, 12), near)
     other_row = swapped(row, 16)
     (two_rows,) = small_call(rows_kernel, [STATE], "rows_state")(row, other_row)
-    rows = lax.ppermute(two_rows, "ctx", [(i, i + 32) for i in range(peers - 32)])
+    rows = permuted(two_rows, lambda i: i ^ 48 if i < 32 else None)
     state, send = small_call(pair_start_kernel, [STATE, STATE], "pair_start")(
         rows, other_row, before, chip, neighbour
     )
     back = swapped(send, 2)
-    both = shape((2, DK, DK), bf16)
-    own, send = small_call(chip_start_kernel, [both, both], "chip_start")(
-        state, back, maps, sibling
-    )
-    other = swapped(send, 1)
-    mine, *parts = finish(base, gate, own, other, norm_gain, w_out)
-    around = lax.axis_size("head")
-    for s in (2, 1, 3):
-        moved = lax.ppermute(parts[s - 1], "head", [(i, (i + s) % around) for i in range(around)])
-        mine = mine + moved.astype(f32)
-    return mine.astype(bf16)
+    mine, *parts = finish((state, back), (maps, sibling), (base, gate), inner_in, norm_gain)
+    moved = [
+        lax.ppermute(part, "head", [(i, (i + s + 1) % around) for i in range(around)])
+        for s, part in enumerate(parts)
+    ]
+    keep, send = merge([mine, *moved], weights)
+    return (keep + swapped(send, 1).astype(f32)).astype(bf16)
 
 
 def solution(mesh):

time: 78.2 us -> 83.6 us (1.069)
  between operations: 0.09 us -> 13.5 us
  waiting for transfers between devices: 23.3 us -> 14.4 us
  starting transfers between devices: 37.7 us -> 38.6 us
    ppermute x12 -> x14, waiting for transfers between devices: 23.3 us -> 14.4 us  [the longest x11 12.2 us: permuted(): return lax.ppermute(x, 'ctx', [p for p in pairs if p[1] is not None])]
    unnamed x12 -> x8, local copies, waits for them, and re-layouts: 2.76 us -> 1.6 us
    dynamic_slice x0 -> x1, local copies, waits for them, and re-layouts: none -> 1.08 us  [per_device(): lax.dynamic_index_in_dim(w_out.reshape(2, 2, DK, width), bit(1), 1, keepd...]
    ppermute x12 -> x14, starting transfers between devices: 37.7 us -> 38.6 us  [the longest x11 33.5 us: permuted(): return lax.ppermute(x, 'ctx', [p for p in pairs if p[1] is not None])]
  transfers between devices with their start and end apart: 12 -> 15, of which waited for: 11 -> 11; matrix products, arithmetic and copies ran while one was open for 0% -> 0% of each run, Pallas kernels for 1% -> 13%
where the time goes in v3:
time: 83.6 us; the launch traced here: 83.5 us
  starting transfers between devices  38.6 us (46%)
  waiting for transfers between devices  14.4 us (17%)
  Pallas kernels  13.5 us (16%)
  between operations  13.5 us (16%)
  local copies, waits for them, and re-layouts  2.68 us (3%)
    ppermute x11, starting transfers between devices, permuted(): return lax.ppermute(x, 'ctx', [p for p in pairs if p[1] is not None])  33.5 us
    ppermute x11, waiting for transfers between devices, permuted(): return lax.ppermute(x, 'ctx', [p for p in pairs if p[1] is not None])  12.2 us
    ppermute x3, starting transfers between devices, per_device(): lax.ppermute(part, 'head', [(i, (i + s + 1) % around) for i in range(arou...  5.14 us
    pallas_call x1, Pallas kernels, project(): pl.pallas_call(project_kernel, in_specs=[pl.BlockSpec(memory_space=pltpu....  4.55 us
    pallas_call x1, Pallas kernels, local_maps(): pl.pallas_call(local_kernel, in_specs=whole(5), out_specs=whole(5), out_s...  3.96 us
    pallas_call x1, Pallas kernels, merge(): pl.pallas_call(merge_kernel, in_specs=whole(4) + [far], out_specs=whole(2...  2.52 us
    ppermute x3, waiting for transfers between devices, per_device(): lax.ppermute(part, 'head', [(i, (i + s + 1) % around) for i in range(arou...  2.15 us
  transfers between devices with their start and end apart: 15, of which 11 were waited for; matrix products, arithmetic and copies ran while one was open for 0% of the time, Pallas kernels for 13%

profile of v3, /device:TPU:1, one launch (start us, length us, event | category | flops | bytes accessed | tf_op | source)
XLA Modules:
  0.0 83.5 jit_solution(4705546237842124176)
XLA Ops:
  6.5 0.0 copy-start
  6.5 0.0 all-gather.2.cloned.1.call-start
  6.5 1.6 %copy-done = bf16[512,2048]{1,0:T(8,128)(2,1)S(1)} copy-done((bf16[512,2048]{1,0:T(8,128)(2,1)S(1)}, bf16[512,2048]{1,0:T(8,128)(2,1)}, u32[]{:S(2)}) %copy-start) | copy-done | bytes 2097176
  8.1 1.1 %constant_dynamic-slice_fusion = bf16[2,1,128,2048]{3,2,1,0:T(8,128)(2,1)} fusion(bf16[2,2,128,2048]{3,2,1,0:T(8,128)(2,1)S(1)} %bitcast.6, s32[]{:T(128)S(6)} %select_n.14), kind=kLoop, calls=%fused_computation.1 | loop fusion | bytes 2097156 | tf_op jit(solution)/shard_map/jit(dynamic_index_in_dim)/dynamic_slice | solution.py:406
  9.2 0.0 copy-start.1
  9.2 0.0 copy-start.3
  9.2 0.0 all-gather.2.cloned.1.call-update
  9.2 0.0 copy-start.2
  9.2 4.6 %project.1 = (bf16[3,256,512]{2,1,0:T(8,128)(2,1)S(1)}, bf16[3,16,512]{2,1,0:T(8,128)(2,1)S(1)}, f32[256,4]{1,0:T(8,128)S(1)}) custom-call(bf16[256,2048]{1,0:T(8,128)(2,1)} %tokens_hbm.1, bf16[3,2048,512]{2,1,0:T(8,128)(2,1)} %w_hbm.1, bf16[4,2048]{1,0:T(4,128)(2,1)} %beta_w_hbm.1), custom_call_target="tpu_custom_call" | custom-call | tf_op jit(solution)/shard_map/project/pallas_call | solution.py:70
  13.8 4.9 %collective-permute-start = (bf16[3,16,512]{2,1,0:T(8,128)(2,1)S(1)}, bf16[3,16,512]{2,1,0:T(8,128)(2,1)S(1)}, u32[]{:S(2)}, u32[]{:S(2)}) collective-permute-start(bf16[3,16,512]{2,1,0:T(8,128)(2,1)S(1)} %get-tuple-element.32), channel_id=1, source_target_pairs={{0,4},{4,8},{8,12},{12,16},{16,20},{20,24},{24,28},{28,32},{32,36}... | collective-permute-start | bytes 147464 | tf_op jit(solution)/shard_map/ppermute | solution.py:396
  18.7 1.2 %collective-permute-done.edge_ref = bf16[3,16,512]{2,1,0:T(8,128)(2,1)S(1)} collective-permute-done((bf16[3,16,512]{2,1,0:T(8,128)(2,1)S(1)}, bf16[3,16,512]{2,1,0:T(8,128)(2,1)S(1)}, u32[]{:S(2)}, u32[]{:S(2)}) %collective-permute-start) | collective-permute-done | bytes 49184 | tf_op jit(solution)/shard_map/ppermute | solution.py:396
  19.9 0.0 copy-done.1
  19.9 0.0 copy-done.3
  19.9 4.0 %local_maps.1 = (bf16[4,256,128]{2,1,0:T(8,128)(2,1)S(1)}, bf16[4,128,256]{2,1,0:T(8,128)(2,1)S(1)}, bf16[4,256,256]{2,1,0:T(8,128)(2,1)S(1)}, bf16[2,128,256]{2,1,0:T(8,128)(2,1)S(1)}, bf16[2,128,256]{2,1,0:T(8,128)(2,1)S(1)}) custom-call(bf16[3,256,512]{2,1,0:T(8,128)(2,1)S(1)} %get-tuple-element.31.proj_ref, ...), custom_call_target="tpu_custom_call" | custom-call | tf_op jit(solution)/shard_map/local_maps/pallas_call | solution.py:194
  23.9 0.1 collective-permute-start.1
  24.0 1.3 %collective-permute-done.1.other_ref.other_maps = bf16[2,128,256]{2,1,0:T(8,128)(2,1)S(1)} collective-permute-done((bf16[2,128,256]{2,1,0:T(8,128)(2,1)S(1)}, bf16[2,128,256]{2,1,0:T(8,128)(2,1)S(1)}, u32[]{:S(2)}, u32[]{:S(2)}) %collective-permute-start.1) | collective-permute-done | bytes 131104 | tf_op jit(solution)/shard_map/ppermute | solution.py:396
  25.3 0.2 chip_map.1
  25.6 2.2 %collective-permute-start.2 = (bf16[128,256]{1,0:T(8,128)(2,1)S(1)}, bf16[128,256]{1,0:T(8,128)(2,1)S(1)}, u32[]{:S(2)}, u32[]{:S(2)}) collective-permute-start(bf16[128,256]{1,0:T(8,128)(2,1)S(1)} %get-tuple-element.37), channel_id=1, source_target_pairs={{0,8},{4,12},{8,0},{12,4},{16,24},{20,28},{24,16},{28,20},{32,40},... | collective-permute-start | bytes 196616 | tf_op jit(solution)/shard_map/ppermute | solution.py:396
  27.7 2.2 %collective-permute-done.2.other_ref = bf16[128,256]{1,0:T(8,128)(2,1)S(1)} collective-permute-done((bf16[128,256]{1,0:T(8,128)(2,1)S(1)}, bf16[128,256]{1,0:T(8,128)(2,1)S(1)}, u32[]{:S(2)}, u32[]{:S(2)}) %collective-permute-start.2) | collective-permute-done | bytes 65568 | tf_op jit(solution)/shard_map/ppermute | solution.py:396
  29.9 0.2 pair_map.1.own_ref
  30.1 4.1 %collective-permute-start.3 = (bf16[128,256]{1,0:T(8,128)(2,1)S(1)}, bf16[128,256]{1,0:T(8,128)(2,1)S(1)}, u32[]{:S(2)}, u32[]{:S(2)}) collective-permute-start(bf16[128,256]{1,0:T(8,128)(2,1)S(1)} %pair_map.1.own_ref), channel_id=1, source_target_pairs={{0,16},{4,20},{8,24},{12,28},{16,0},{20,4},{24,8},{28,12},{32,48},... | collective-permute-start | bytes 196616 | tf_op jit(solution)/shard_map/ppermute | solution.py:396
  34.2 0.5 inner_outputs.1
  34.7 1.0 %collective-permute-start.8 = (f32[2,256,128]{2,1,0:T(8,128)S(1)}, f32[2,256,128]{2,1,0:T(8,128)S(1)}, u32[]{:S(2)}, u32[]{:S(2)}) collective-permute-start(f32[2,256,128]{2,1,0:T(8,128)S(1)} %get-tuple-element.49), channel_id=1, source_target_pairs={{0,4},{4,0},{8,12},{12,8},{16,20},{20,16},{24,28},{28,24},{32,36},... | collective-permute-start | bytes 786440 | tf_op jit(solution)/shard_map/ppermute | solution.py:396
  35.7 0.5 collective-permute-done.3.other_ref
  36.2 0.2 near_map.1
  36.4 4.2 %collective-permute-start.4 = (bf16[128,256]{1,0:T(8,128)(2,1)S(1)}, bf16[128,256]{1,0:T(8,128)(2,1)S(1)}, u32[]{:S(2)}, u32[]{:S(2)}) collective-permute-start(bf16[128,256]{1,0:T(8,128)(2,1)S(1)} %get-tuple-element.38.own_ref), channel_id=1, source_target_pairs={{0,48},{4,52},{8,56},{12,60},{16,32},{20,36},{24,40},{28,44},{32,1... | collective-permute-start | bytes 196616 | tf_op jit(solution)/shard_map/ppermute | solution.py:396
  40.6 1.7 %collective-permute-done.4.other_ref = bf16[128,256]{1,0:T(8,128)(2,1)S(1)} collective-permute-done((bf16[128,256]{1,0:T(8,128)(2,1)S(1)}, bf16[128,256]{1,0:T(8,128)(2,1)S(1)}, u32[]{:S(2)}, u32[]{:S(2)}) %collective-permute-start.4) | collective-permute-done | bytes 65568 | tf_op jit(solution)/shard_map/ppermute | solution.py:396
  42.3 0.2 far_map.1
  42.5 3.8 %collective-permute-start.5 = (bf16[128,256]{1,0:T(8,128)(2,1)S(1)}, bf16[128,256]{1,0:T(8,128)(2,1)S(1)}, u32[]{:S(2)}, u32[]{:S(2)}) collective-permute-start(bf16[128,256]{1,0:T(8,128)(2,1)S(1)} %get-tuple-element.40.own_ref), channel_id=1, source_target_pairs={{0,64},{4,68},{8,72},{12,76},{16,80},{20,84},{24,88},{28,92},{32,9... | collective-permute-start | bytes 196616 | tf_op jit(solution)/shard_map/ppermute | solution.py:396
  46.3 2.3 %collective-permute-start.9 = (bf16[2,256,128]{2,1,0:T(8,128)(2,1)S(1)}, bf16[2,256,128]{2,1,0:T(8,128)(2,1)S(1)}, u32[]{:S(2)}, u32[]{:S(2)}) collective-permute-start(bf16[2,256,128]{2,1,0:T(8,128)(2,1)S(1)} %get-tuple-element.50), channel_id=1, source_target_pairs={{0,4},{4,0},{8,12},{12,8},{16,20},{20,16},{24,28},{28,24},{32,36},... | collective-permute-start | bytes 393224 | tf_op jit(solution)/shard_map/ppermute | solution.py:396
  48.6 0.0 collective-permute-done.5.other_ref.row_ref
  48.6 0.2 rows_state.1
  48.7 4.6 %collective-permute-start.6 = (bf16[128,128]{1,0:T(8,128)(2,1)S(1)}, bf16[128,128]{1,0:T(8,128)(2,1)S(1)}, u32[]{:S(2)}, u32[]{:S(2)}) collective-permute-start(bf16[128,128]{1,0:T(8,128)(2,1)S(1)} %rows_state.1), channel_id=1, source_target_pairs={{0,192},{4,196},{8,200},{12,204},{16,208},{20,212},{24,216},{28,22... | collective-permute-start | bytes 98312 | tf_op jit(solution)/shard_map/ppermute | solution.py:396
  53.4 1.0 %collective-permute-done.6.rows_ref = bf16[128,128]{1,0:T(8,128)(2,1)S(1)} collective-permute-done((bf16[128,128]{1,0:T(8,128)(2,1)S(1)}, bf16[128,128]{1,0:T(8,128)(2,1)S(1)}, u32[]{:S(2)}, u32[]{:S(2)}) %collective-permute-start.6) | collective-permute-done | bytes 32800 | tf_op jit(solution)/shard_map/ppermute | solution.py:396
  54.4 0.4 pair_start.1
  54.8 0.1 collective-permute-start.7
  54.9 0.0 collective-permute-done.9.gate_in
  54.9 0.0 collective-permute-done.8.base_in
  54.9 3.1 %collective-permute-done.7.other_state = bf16[128,128]{1,0:T(8,128)(2,1)S(1)} collective-permute-done((bf16[128,128]{1,0:T(8,128)(2,1)S(1)}, bf16[128,128]{1,0:T(8,128)(2,1)S(1)}, u32[]{:S(2)}, u32[]{:S(2)}) %collective-permute-start.7) | collective-permute-done | bytes 32800 | tf_op jit(solution)/shard_map/ppermute | solution.py:396
  58.0 0.0 copy-done.2
  58.0 0.6 finish.1
  58.7 1.5 %collective-permute-start.10 = (bf16[2,64,256]{2,1,0:T(8,128)(2,1)S(1)}, bf16[2,64,256]{2,1,0:T(8,128)(2,1)S(1)}, u32[]{:S(2)}, u32[]{:S(2)}) collective-permute-start(bf16[2,64,256]{2,1,0:T(8,128)(2,1)S(1)} %get-tuple-element.52), channel_id=1, source_target_pairs={{0,1},{1,2},{2,3},{3,0},{4,5},{5,6},{6,7},{7,4},{8,9},{9,10},{10,1... | collective-permute-start | bytes 196616 | tf_op jit(solution)/shard_map/ppermute | solution.py:430
  60.2 2.7 %collective-permute-start.11 = (bf16[2,64,256]{2,1,0:T(8,128)(2,1)S(1)}, bf16[2,64,256]{2,1,0:T(8,128)(2,1)S(1)}, u32[]{:S(2)}, u32[]{:S(2)}) collective-permute-start(bf16[2,64,256]{2,1,0:T(8,128)(2,1)S(1)} %get-tuple-element.53), channel_id=1, source_target_pairs={{0,2},{1,3},{2,0},{3,1},{4,6},{5,7},{6,4},{7,5},{8,10},{9,11},{10,... | collective-permute-start | bytes 196616 | tf_op jit(solution)/shard_map/ppermute | solution.py:430
  62.9 1.0 %collective-permute-start.12 = (bf16[2,64,256]{2,1,0:T(8,128)(2,1)S(1)}, bf16[2,64,256]{2,1,0:T(8,128)(2,1)S(1)}, u32[]{:S(2)}, u32[]{:S(2)}) collective-permute-start(bf16[2,64,256]{2,1,0:T(8,128)(2,1)S(1)} %get-tuple-element.54), channel_id=1, source_target_pairs={{0,3},{1,0},{2,1},{3,2},{4,7},{5,4},{6,5},{7,6},{8,11},{9,8},{10,9... | collective-permute-start | bytes 196616 | tf_op jit(solution)/shard_map/ppermute | solution.py:430
  63.8 0.9 %collective-permute-done.10.one = bf16[2,64,256]{2,1,0:T(8,128)(2,1)S(1)} collective-permute-done((bf16[2,64,256]{2,1,0:T(8,128)(2,1)S(1)}, bf16[2,64,256]{2,1,0:T(8,128)(2,1)S(1)}, u32[]{:S(2)}, u32[]{:S(2)}) %collective-permute-start.10) | collective-permute-done | bytes 65568 | tf_op jit(solution)/shard_map/ppermute | solution.py:430
  64.7 0.6 collective-permute-done.11.two
  65.3 0.7 collective-permute-done.12.three
  66.0 0.0 all-gather.2.cloned.1.call-done.w_hbm
  66.0 2.5 %merge.1 = (f32[64,2048]{1,0:T(8,128)S(1)}, bf16[64,2048]{1,0:T(8,128)(2,1)S(1)}) custom-call(bf16[2,64,256]{2,1,0:T(8,128)(2,1)S(1)} %get-tuple-element.51.mine_ref, bf16[2,64,256]{2,1,0:T(8,128)(2,1)S(1)} %collective-permute-done.10.one, bf16[2,64,256]{2,1,0:T(8,128)(2,1)S(1)} %collective-permute-done.11.two, ...), custom_call_target="tpu_custom_call" | custom-call | tf_op jit(solution)/shard_map/merge/pallas_call | solution.py:383
  68.5 6.2 %collective-permute-start.13 = (bf16[64,2048]{1,0:T(8,128)(2,1)S(1)}, bf16[64,2048]{1,0:T(8,128)(2,1)S(1)}, u32[]{:S(2)}, u32[]{:S(2)}) collective-permute-start(bf16[64,2048]{1,0:T(8,128)(2,1)S(1)} %get-tuple-element.56), channel_id=1, source_target_pairs={{0,4},{4,0},{8,12},{12,8},{16,20},{20,16},{24,28},{28,24},{32,36},... | collective-permute-start | bytes 786440 | tf_op jit(solution)/shard_map/ppermute | solution.py:396
  74.7 1.2 %collective-permute-done.13 = bf16[64,2048]{1,0:T(8,128)(2,1)S(1)} collective-permute-done((bf16[64,2048]{1,0:T(8,128)(2,1)S(1)}, bf16[64,2048]{1,0:T(8,128)(2,1)S(1)}, u32[]{:S(2)}, u32[]{:S(2)}) %collective-permute-start.13) | collective-permute-done | bytes 262176 | tf_op jit(solution)/shard_map/ppermute | solution.py:396
  75.9 0.8 add_convert_fusion
Async XLA Ops:
  6.5 1.6 %copy-start = (bf16[512,2048]{1,0:T(8,128)(2,1)S(1)}, bf16[512,2048]{1,0:T(8,128)(2,1)}, u32[]{:S(2)}) copy-start(bf16[512,2048]{1,0:T(8,128)(2,1)} %param.13) | copy-start | bytes 6291460
  6.5 59.5 %all-gather.2.cloned.1.call-start = ((), (), s32[]{:S(2)}) async-start(), calls=%async_computation | async-start | bytes 5242880 | tf_op jit(solution)/shard_map/all_gather | solution.py:407
  9.2 10.7 %copy-start.1 = (f32[3,4,512]{2,1,0:T(4,128)S(1)}, f32[3,4,512]{2,1,0:T(4,128)}, u32[]{:S(2)}) copy-start(f32[3,4,512]{2,1,0:T(4,128)} %conv_ref.1) | copy-start | bytes 73732
  9.2 10.7 %copy-start.3 = (f32[4]{0:T(128)S(1)}, f32[4]{0:T(128)}, u32[]{:S(2)}) copy-start(f32[4]{0:T(128)} %param.11) | copy-start | bytes 52
  9.2 48.8 %copy-start.2 = (f32[512]{0:T(512)S(1)}, f32[512]{0:T(512)}, u32[]{:S(2)}) copy-start(f32[512]{0:T(512)} %param.12) | copy-start | bytes 6148
  13.8 6.1 %collective-permute-start = (bf16[3,16,512]{2,1,0:T(8,128)(2,1)S(1)}, bf16[3,16,512]{2,1,0:T(8,128)(2,1)S(1)}, u32[]{:S(2)}, u32[]{:S(2)}) collective-permute-start(bf16[3,16,512]{2,1,0:T(8,128)(2,1)S(1)} %get-tuple-element.32), channel_id=1, source_target_pairs={{0,4},{4,8},{8,12},{12,16},{16,20},{20,24},{24,28},{28,32},{32,36}... | collective-permute-start | bytes 147464 | tf_op jit(solution)/shard_map/ppermute | solution.py:396
  23.9 1.4 %collective-permute-start.1 = (bf16[2,128,256]{2,1,0:T(8,128)(2,1)S(1)}, bf16[2,128,256]{2,1,0:T(8,128)(2,1)S(1)}, u32[]{:S(2)}, u32[]{:S(2)}) collective-permute-start(bf16[2,128,256]{2,1,0:T(8,128)(2,1)S(1)} %get-tuple-element.35), channel_id=1, source_target_pairs={{0,4},{4,0},{8,12},{12,8},{16,20},{20,16},{24,28},{28,24},{32,36},... | collective-permute-start | bytes 393224 | tf_op jit(solution)/shard_map/ppermute | solution.py:396
  25.6 4.4 %collective-permute-start.2 = (bf16[128,256]{1,0:T(8,128)(2,1)S(1)}, bf16[128,256]{1,0:T(8,128)(2,1)S(1)}, u32[]{:S(2)}, u32[]{:S(2)}) collective-permute-start(bf16[128,256]{1,0:T(8,128)(2,1)S(1)} %get-tuple-element.37), channel_id=1, source_target_pairs={{0,8},{4,12},{8,0},{12,4},{16,24},{20,28},{24,16},{28,20},{32,40},... | collective-permute-start | bytes 196616 | tf_op jit(solution)/shard_map/ppermute | solution.py:396
  30.1 6.1 %collective-permute-start.3 = (bf16[128,256]{1,0:T(8,128)(2,1)S(1)}, bf16[128,256]{1,0:T(8,128)(2,1)S(1)}, u32[]{:S(2)}, u32[]{:S(2)}) collective-permute-start(bf16[128,256]{1,0:T(8,128)(2,1)S(1)} %pair_map.1.own_ref), channel_id=1, source_target_pairs={{0,16},{4,20},{8,24},{12,28},{16,0},{20,4},{24,8},{28,12},{32,48},... | collective-permute-start | bytes 196616 | tf_op jit(solution)/shard_map/ppermute | solution.py:396
  34.7 20.2 %collective-permute-start.8 = (f32[2,256,128]{2,1,0:T(8,128)S(1)}, f32[2,256,128]{2,1,0:T(8,128)S(1)}, u32[]{:S(2)}, u32[]{:S(2)}) collective-permute-start(f32[2,256,128]{2,1,0:T(8,128)S(1)} %get-tuple-element.49), channel_id=1, source_target_pairs={{0,4},{4,0},{8,12},{12,8},{16,20},{20,16},{24,28},{28,24},{32,36},... | collective-permute-start | bytes 786440 | tf_op jit(solution)/shard_map/ppermute | solution.py:396
  36.4 5.9 %collective-permute-start.4 = (bf16[128,256]{1,0:T(8,128)(2,1)S(1)}, bf16[128,256]{1,0:T(8,128)(2,1)S(1)}, u32[]{:S(2)}, u32[]{:S(2)}) collective-permute-start(bf16[128,256]{1,0:T(8,128)(2,1)S(1)} %get-tuple-element.38.own_ref), channel_id=1, source_target_pairs={{0,48},{4,52},{8,56},{12,60},{16,32},{20,36},{24,40},{28,44},{32,1... | collective-permute-start | bytes 196616 | tf_op jit(solution)/shard_map/ppermute | solution.py:396
  42.5 6.1 %collective-permute-start.5 = (bf16[128,256]{1,0:T(8,128)(2,1)S(1)}, bf16[128,256]{1,0:T(8,128)(2,1)S(1)}, u32[]{:S(2)}, u32[]{:S(2)}) collective-permute-start(bf16[128,256]{1,0:T(8,128)(2,1)S(1)} %get-tuple-element.40.own_ref), channel_id=1, source_target_pairs={{0,64},{4,68},{8,72},{12,76},{16,80},{20,84},{24,88},{28,92},{32,9... | collective-permute-start | bytes 196616 | tf_op jit(solution)/shard_map/ppermute | solution.py:396
  46.3 8.6 %collective-permute-start.9 = (bf16[2,256,128]{2,1,0:T(8,128)(2,1)S(1)}, bf16[2,256,128]{2,1,0:T(8,128)(2,1)S(1)}, u32[]{:S(2)}, u32[]{:S(2)}) collective-permute-start(bf16[2,256,128]{2,1,0:T(8,128)(2,1)S(1)} %get-tuple-element.50), channel_id=1, source_target_pairs={{0,4},{4,0},{8,12},{12,8},{16,20},{20,16},{24,28},{28,24},{32,36},... | collective-permute-start | bytes 393224 | tf_op jit(solution)/shard_map/ppermute | solution.py:396
  48.7 5.7 %collective-permute-start.6 = (bf16[128,128]{1,0:T(8,128)(2,1)S(1)}, bf16[128,128]{1,0:T(8,128)(2,1)S(1)}, u32[]{:S(2)}, u32[]{:S(2)}) collective-permute-start(bf16[128,128]{1,0:T(8,128)(2,1)S(1)} %rows_state.1), channel_id=1, source_target_pairs={{0,192},{4,196},{8,200},{12,204},{16,208},{20,212},{24,216},{28,22... | collective-permute-start | bytes 98312 | tf_op jit(solution)/shard_map/ppermute | solution.py:396
  54.8 3.3 %collective-permute-start.7 = (bf16[128,128]{1,0:T(8,128)(2,1)S(1)}, bf16[128,128]{1,0:T(8,128)(2,1)S(1)}, u32[]{:S(2)}, u32[]{:S(2)}) collective-permute-start(bf16[128,128]{1,0:T(8,128)(2,1)S(1)} %get-tuple-element.43), channel_id=1, source_target_pairs={{0,8},{4,12},{8,0},{12,4},{16,24},{20,28},{24,16},{28,20},{32,40},... | collective-permute-start | bytes 98312 | tf_op jit(solution)/shard_map/ppermute | solution.py:396
  58.7 6.0 %collective-permute-start.10 = (bf16[2,64,256]{2,1,0:T(8,128)(2,1)S(1)}, bf16[2,64,256]{2,1,0:T(8,128)(2,1)S(1)}, u32[]{:S(2)}, u32[]{:S(2)}) collective-permute-start(bf16[2,64,256]{2,1,0:T(8,128)(2,1)S(1)} %get-tuple-element.52), channel_id=1, source_target_pairs={{0,1},{1,2},{2,3},{3,0},{4,5},{5,6},{6,7},{7,4},{8,9},{9,10},{10,1... | collective-permute-start | bytes 196616 | tf_op jit(solution)/shard_map/ppermute | solution.py:430
  60.2 5.1 %collective-permute-start.11 = (bf16[2,64,256]{2,1,0:T(8,128)(2,1)S(1)}, bf16[2,64,256]{2,1,0:T(8,128)(2,1)S(1)}, u32[]{:S(2)}, u32[]{:S(2)}) collective-permute-start(bf16[2,64,256]{2,1,0:T(8,128)(2,1)S(1)} %get-tuple-element.53), channel_id=1, source_target_pairs={{0,2},{1,3},{2,0},{3,1},{4,6},{5,7},{6,4},{7,5},{8,10},{9,11},{10,... | collective-permute-start | bytes 196616 | tf_op jit(solution)/shard_map/ppermute | solution.py:430
  62.9 3.1 %collective-permute-start.12 = (bf16[2,64,256]{2,1,0:T(8,128)(2,1)S(1)}, bf16[2,64,256]{2,1,0:T(8,128)(2,1)S(1)}, u32[]{:S(2)}, u32[]{:S(2)}) collective-permute-start(bf16[2,64,256]{2,1,0:T(8,128)(2,1)S(1)} %get-tuple-element.54), channel_id=1, source_target_pairs={{0,3},{1,0},{2,1},{3,2},{4,7},{5,4},{6,5},{7,6},{8,11},{9,8},{10,9... | collective-permute-start | bytes 196616 | tf_op jit(solution)/shard_map/ppermute | solution.py:430
  68.5 7.3 %collective-permute-start.13 = (bf16[64,2048]{1,0:T(8,128)(2,1)S(1)}, bf16[64,2048]{1,0:T(8,128)(2,1)S(1)}, u32[]{:S(2)}, u32[]{:S(2)}) collective-permute-start(bf16[64,2048]{1,0:T(8,128)(2,1)S(1)} %get-tuple-element.56), channel_id=1, source_target_pairs={{0,4},{4,0},{8,12},{12,8},{16,20},{20,16},{24,28},{28,24},{32,36},... | collective-permute-start | bytes 786440 | tf_op jit(solution)/shard_map/ppermute | solution.py:396
Sparse Core Ops, SparseCore 0:
  9.4 55.0 all-gather.1

commit v4 on v3

--- a/solution.py
+++ b/solution.py
@@ -141,8 +141,10 @@
     heads = logits_ref.shape[1]
     betas = 1.0 / (1.0 + jnp.exp(-(logits_ref[...] + bias_ref[...])))
     core = lax.axis_index("ctx") % 2
+    first = lax.axis_index("ctx") == 0
     for s in range(3):
-        padded[s, :EDGE] = edge_ref[s].astype(f32)
+        edge = edge_ref[s].astype(f32)
+        padded[s, :EDGE] = jnp.where(first, jnp.zeros_like(edge), edge)
         padded[s, EDGE:] = proj_ref[s].astype(f32)
     row, column = grid_index(length, length)
     strict = row > column
@@ -282,17 +284,14 @@
     send_ref[...] = kept[1 - bit(2)]
 
 
-def pair_kernel(own_ref, other_ref, total_ref):
-    late = bit(2) == 1
-    first, second = ordered(own_ref[...].astype(f32), other_ref[...].astype(f32), late)
-    total_ref[...] = then(first, second).astype(bf16)
-
-
-def near_kernel(own_ref, other_ref, total_ref, before_ref):
-    late = bit(4) == 1
-    own, other = own_ref[...].astype(f32), other_ref[...].astype(f32)
-    first, second = ordered(own, other, late)
-    total_ref[...] = then(first, second).astype(bf16)
+def four_kernel(own_ref, pair_ref, across_ref, diagonal_ref, total_ref, before_ref):
+    upper, late = bit(2) == 1, bit(4) == 1
+    own, pair, across, diagonal = (
+        ref[...].astype(f32) for ref in (own_ref, pair_ref, across_ref, diagonal_ref)
+    )
+    mine = then(*ordered(own, pair, upper))
+    other = then(*ordered(across, diagonal, upper))
+    total_ref[...] = then(*ordered(mine, other, late)).astype(bf16)
     before_ref[...] = jnp.where(late, other, jnp.zeros_like(other)).astype(bf16)
 
 
@@ -313,6 +312,7 @@
 
 def pair_start_kernel(rows_ref, row_ref, before_ref, own_ref, other_ref, keep_ref, send_ref):
     state = rows_ref[...].astype(f32)
+    state = jnp.where(bit(32) == 1, state, jnp.zeros_like(state))
     late_row = bit(16) == 1
     row = row_ref[...].astype(f32)
     state = jnp.where(late_row, advance(state, row), state)
@@ -358,55 +358,63 @@
     )(*states, *maps, *inner, *inner_in, norm_gain.reshape(4, 1, DK))
 
 
-def merge_kernel(mine_ref, one, two, three, w_hbm, keep_ref, send_ref, w_ref, sems):
-    here = lax.axis_index("head")
+def rows_kernel_of(w_hbm, out_ref, sems):
     copies = [
-        pltpu.make_async_copy(w_hbm.at[(here + 4 - s) % 4], w_ref.at[s], sems.at[s])
-        for s in range(4)
+        pltpu.make_async_copy(
+            w_hbm.at[pl.ds(pl.multiple_of((2 * j + bit(1)) * DK, DK), DK)], out_ref.at[j], sems.at[j]
+        )
+        for j in range(2)
     ]
     for copy in copies:
         copy.start()
-    _, rows, width = mine_ref.shape
+    for copy in copies:
+        copy.wait()
+
+
+def own_rows(w_out):
+    return pl.pallas_call(
+        rows_kernel_of,
+        in_specs=[pl.BlockSpec(memory_space=pltpu.HBM)],
+        out_specs=pl.BlockSpec(memory_space=pltpu.VMEM),
+        out_shape=shape((2, DK, w_out.shape[1]), bf16),
+        scratch_shapes=[pltpu.SemaphoreType.DMA((2,))],
+        compiler_params=params(),
+        name="own_rows",
+    )(pltpu.with_memory_space_constraint(w_out, pltpu.HBM))
+
+
+def merge_kernel(*refs):
+    parts, weights, (keep_ref, send_ref) = refs[:4], refs[4:8], refs[8:]
+    _, rows, width = parts[0].shape
     total = None
-    for s, ref in enumerate((mine_ref, one, two, three)):
-        copies[s].wait()
-        term = dot(ref[...].reshape(2 * rows, width), w_ref[s])
+    for ref, weight in zip(parts, weights):
+        term = dot(ref[...].reshape(2 * rows, width), weight[...].reshape(width, -1))
         total = term if total is None else total + term
     keep_ref[...] = total[:rows]
     send_ref[...] = total[rows:].astype(bf16)
 
 
 def merge(parts, weights):
-    rows = parts[0].shape[1]
-    width = weights.shape[-1]
-    far = pl.BlockSpec(memory_space=pltpu.HBM)
-    return pl.pallas_call(
-        merge_kernel,
-        in_specs=whole(4) + [far],
-        out_specs=whole(2),
-        out_shape=[shape((rows, width), f32), shape((rows, width), bf16)],
-        scratch_shapes=[pltpu.VMEM(weights.shape, bf16), pltpu.SemaphoreType.DMA((4,))],
-        compiler_params=params(),
-        name="merge",
-    )(*parts, pltpu.with_memory_space_constraint(weights, pltpu.HBM))
-
-
-def permuted(x, target):
-    pairs = [(i, target(i)) for i in range(lax.axis_size("ctx"))]
-    return lax.ppermute(x, "ctx", [p for p in pairs if p[1] is not None])
+    rows, width = parts[0].shape[1], weights[0].shape[-1]
+    return small_call(
+        merge_kernel, [shape((rows, width), f32), shape((rows, width), bf16)], "merge"
+    )(*parts, *weights)
 
 
 def swapped(x, by):
-    return permuted(x, lambda i: i ^ by)
+    return lax.ppermute(x, "ctx", [(i, i ^ by) for i in range(lax.axis_size("ctx"))])
+
+
+def turned(x, axis, by):
+    count = lax.axis_size(axis)
+    return lax.ppermute(x, axis, [(i, (i + by) % count) for i in range(count)])
 
 
 def per_device(tokens_in, w_qkv, conv_weight, beta_weight, beta_bias, norm_gain, w_out):
-    peers, around = lax.axis_size("ctx"), lax.axis_size("head")
-    width = w_out.shape[1]
-    half = lax.dynamic_index_in_dim(w_out.reshape(2, 2, DK, width), bit(1), 1, keepdims=False)
-    weights = lax.all_gather(half.reshape(2 * DK, width), "head")
+    w_own = own_rows(w_out)
+    w_one, w_three, w_two = (turned(w_own, "head", s) for s in (1, 3, 2))
     projected, edge, logits = project(tokens_in, w_qkv, beta_weight)
-    edge = permuted(edge, lambda i: i + 1 if i + 1 < peers else None)
+    edge = turned(edge, "ctx", 1)
     queries, keys_t, uw, maps, send = local_maps(projected, edge, conv_weight, logits, beta_bias)
     sibling = swapped(send, 1)
     base, gate, *sent = inner_outputs(queries, keys_t, uw)
@@ -414,23 +422,21 @@
     chip, send = small_call(
         chip_kernel, [MAP, MAP], "chip_map", [pltpu.VMEM((2, DK, 2 * DK), bf16)]
     )(maps, sibling)
-    neighbour = swapped(send, 2)
-    (pair,) = small_call(pair_kernel, [MAP], "pair_map")(chip, neighbour)
-    four, near = small_call(near_kernel, [MAP, MAP], "near_map")(pair, swapped(pair, 4))
+    pair, across, diagonal = swapped(send, 2), swapped(chip, 4), swapped(send, 6)
+    four, near = small_call(four_kernel, [MAP, MAP], "four_map")(chip, pair, across, diagonal)
     row, before = small_call(far_kernel, [MAP, MAP], "far_map")(four, swapped(four, 12), near)
     other_row = swapped(row, 16)
     (two_rows,) = small_call(rows_kernel, [STATE], "rows_state")(row, other_row)
-    rows = permuted(two_rows, lambda i: i ^ 48 if i < 32 else None)
+    rows = swapped(two_rows, 48)
     state, send = small_call(pair_start_kernel, [STATE, STATE], "pair_start")(
-        rows, other_row, before, chip, neighbour
+        rows, other_row, before, chip, pair
     )
     back = swapped(send, 2)
-    mine, *parts = finish((state, back), (maps, sibling), (base, gate), inner_in, norm_gain)
-    moved = [
-        lax.ppermute(part, "head", [(i, (i + s + 1) % around) for i in range(around)])
-        for s, part in enumerate(parts)
-    ]
-    keep, send = merge([mine, *moved], weights)
+    mine, one, two, three = finish(
+        (state, back), (maps, sibling), (base, gate), inner_in, norm_gain
+    )
+    one, three, two = turned(one, "head", 1), turned(three, "head", 3), turned(two, "head", 2)
+    keep, send = merge([mine, one, two, three], [w_own, w_one, w_two, w_three])
     return (keep + swapped(send, 1).astype(f32)).astype(bf16)
 
 

time: 83.6 us -> 74.3 us (0.89)
  waiting for transfers between devices: 14.4 us -> 27.8 us
  between operations: 13.5 us -> 0.1 us
  starting transfers between devices: 38.6 us -> 32.3 us
  local copies, waits for them, and re-layouts: 2.68 us -> 0.01 us
    ppermute x14 -> x18, waiting for transfers between devices: 14.4 us -> 27.8 us  [the longest x11 22.4 us: swapped(): lax.ppermute(x, 'ctx', [(i, i ^ by) for i in range(lax.axis_size('ctx'))])]
    ppermute x14 -> x18, starting transfers between devices: 38.6 us -> 32.3 us  [the longest x11 20.5 us: swapped(): lax.ppermute(x, 'ctx', [(i, i ^ by) for i in range(lax.axis_size('ctx'))])]
    unnamed x8 -> x6, local copies, waits for them, and re-layouts: 1.6 us -> 0.01 us
    dynamic_slice x1 -> x0, local copies, waits for them, and re-layouts: 1.08 us -> none  [per_device(): lax.dynamic_index_in_dim(w_out.reshape(2, 2, DK, width), bit(1), 1, keepd...]
  transfers between devices with their start and end apart: 15 -> 18, of which waited for: 11 -> 12; matrix products, arithmetic and copies ran while one was open for 0% -> 0% of each run, Pallas kernels for 13% -> 15%
where the time goes in v4:
time: 74.3 us; the launch traced here: 74.1 us
  starting transfers between devices  32.3 us (43%)
  waiting for transfers between devices  27.8 us (37%)
  Pallas kernels  13.1 us (18%)
  other arithmetic  0.76 us (1%)
    ppermute x11, waiting for transfers between devices, swapped(): lax.ppermute(x, 'ctx', [(i, i ^ by) for i in range(lax.axis_size('ctx'))])  22.4 us
    ppermute x11, starting transfers between devices, swapped(): lax.ppermute(x, 'ctx', [(i, i ^ by) for i in range(lax.axis_size('ctx'))])  20.5 us
    ppermute x7, starting transfers between devices, turned(): return lax.ppermute(x, axis, [(i, (i + by) % count) for i in range(count)])  11.8 us
    ppermute x7, waiting for transfers between devices, turned(): return lax.ppermute(x, axis, [(i, (i + by) % count) for i in range(count)])  5.4 us
    pallas_call x1, Pallas kernels, project(): pl.pallas_call(project_kernel, in_specs=[pl.BlockSpec(memory_space=pltpu....  4.6 us
    pallas_call x1, Pallas kernels, local_maps(): pl.pallas_call(local_kernel, in_specs=whole(5), out_specs=whole(5), out_s...  3.96 us
  transfers between devices with their start and end apart: 18, of which 12 were waited for; matrix products, arithmetic and copies ran while one was open for 0% of the time, Pallas kernels for 15%

profile of v4, /device:TPU:1, one launch (start us, length us, event | category | flops | bytes accessed | tf_op | source)
XLA Modules:
  0.0 74.1 jit_solution(14626646109886259078)
XLA Ops:
  0.0 0.0 copy-start.2
  0.0 0.0 copy-start
  0.0 0.0 copy-start.1
  0.0 1.3 %own_rows.1.refs_4_ = bf16[2,128,2048]{2,1,0:T(8,128)(2,1)S(1)} custom-call(bf16[512,2048]{1,0:T(8,128)(2,1)} %w_hbm.3), custom_call_target="tpu_custom_call" | custom-call | tf_op jit(solution)/shard_map/own_rows/pallas_call | solution.py:375
  1.3 3.6 %collective-permute-start.16 = (bf16[2,128,2048]{2,1,0:T(8,128)(2,1)S(1)}, bf16[2,128,2048]{2,1,0:T(8,128)(2,1)S(1)}, u32[]{:S(2)}, u32[]{:S(2)}) collective-permute-start(bf16[2,128,2048]{2,1,0:T(8,128)(2,1)S(1)} %own_rows.1.refs_4_), channel_id=1, source_target_pairs={{0,3},{1,0},{2,1},{3,2},{4,7},{5,4},{6,5},{7,6},{8,11},{9,8},{10,9... | collective-permute-start | bytes 3145736 | tf_op jit(solution)/shard_map/ppermute | solution.py:410
  4.9 0.3 collective-permute-start.15
  5.3 0.7 collective-permute-start.14
  6.0 4.6 %project.1 = (bf16[3,256,512]{2,1,0:T(8,128)(2,1)S(1)}, bf16[3,16,512]{2,1,0:T(8,128)(2,1)S(1)}, f32[256,4]{1,0:T(8,128)S(1)}) custom-call(bf16[256,2048]{1,0:T(8,128)(2,1)} %tokens_hbm.1, bf16[3,2048,512]{2,1,0:T(8,128)(2,1)} %w_hbm.2, bf16[4,2048]{1,0:T(4,128)(2,1)} %beta_w_hbm.1), custom_call_target="tpu_custom_call" | custom-call | tf_op jit(solution)/shard_map/project/pallas_call | solution.py:70
  10.6 3.1 %collective-permute-start = (bf16[3,16,512]{2,1,0:T(8,128)(2,1)S(1)}, bf16[3,16,512]{2,1,0:T(8,128)(2,1)S(1)}, u32[]{:S(2)}, u32[]{:S(2)}) collective-permute-start(bf16[3,16,512]{2,1,0:T(8,128)(2,1)S(1)} %get-tuple-element.32), channel_id=1, source_target_pairs={{0,4},{4,8},{8,12},{12,16},{16,20},{20,24},{24,28},{28,32},{32,36}... | collective-permute-start | bytes 147464 | tf_op jit(solution)/shard_map/ppermute | solution.py:410
  13.7 1.2 %collective-permute-done.edge_ref = bf16[3,16,512]{2,1,0:T(8,128)(2,1)S(1)} collective-permute-done((bf16[3,16,512]{2,1,0:T(8,128)(2,1)S(1)}, bf16[3,16,512]{2,1,0:T(8,128)(2,1)S(1)}, u32[]{:S(2)}, u32[]{:S(2)}) %collective-permute-start) | collective-permute-done | bytes 49184 | tf_op jit(solution)/shard_map/ppermute | solution.py:410
  14.9 0.0 copy-done.2
  14.9 0.0 copy-done
  14.9 4.0 %local_maps.1 = (bf16[4,256,128]{2,1,0:T(8,128)(2,1)S(1)}, bf16[4,128,256]{2,1,0:T(8,128)(2,1)S(1)}, bf16[4,256,256]{2,1,0:T(8,128)(2,1)S(1)}, bf16[2,128,256]{2,1,0:T(8,128)(2,1)S(1)}, bf16[2,128,256]{2,1,0:T(8,128)(2,1)S(1)}) custom-call(bf16[3,256,512]{2,1,0:T(8,128)(2,1)S(1)} %get-tuple-element.31.proj_ref, ...), custom_call_target="tpu_custom_call" | custom-call | tf_op jit(solution)/shard_map/local_maps/pallas_call | solution.py:196
  18.8 5.8 %collective-permute-start.1 = (bf16[2,128,256]{2,1,0:T(8,128)(2,1)S(1)}, bf16[2,128,256]{2,1,0:T(8,128)(2,1)S(1)}, u32[]{:S(2)}, u32[]{:S(2)}) collective-permute-start(bf16[2,128,256]{2,1,0:T(8,128)(2,1)S(1)} %get-tuple-element.35), channel_id=1, source_target_pairs={{0,4},{4,0},{8,12},{12,8},{16,20},{20,16},{24,28},{28,24},{32,36},... | collective-permute-start | bytes 393224 | tf_op jit(solution)/shard_map/ppermute | solution.py:405
  24.6 1.0 %collective-permute-done.1.other_ref.other_maps = bf16[2,128,256]{2,1,0:T(8,128)(2,1)S(1)} collective-permute-done((bf16[2,128,256]{2,1,0:T(8,128)(2,1)S(1)}, bf16[2,128,256]{2,1,0:T(8,128)(2,1)S(1)}, u32[]{:S(2)}, u32[]{:S(2)}) %collective-permute-start.1) | collective-permute-done | bytes 131104 | tf_op jit(solution)/shard_map/ppermute | solution.py:405
  25.6 0.2 chip_map.1
  25.9 0.3 collective-permute-start.4
  26.1 0.0 collective-permute-start.2
  26.2 5.0 %collective-permute-done.4.diagonal_ref = bf16[128,256]{1,0:T(8,128)(2,1)S(1)} collective-permute-done((bf16[128,256]{1,0:T(8,128)(2,1)S(1)}, bf16[128,256]{1,0:T(8,128)(2,1)S(1)}, u32[]{:S(2)}, u32[]{:S(2)}) %collective-permute-start.4) | collective-permute-done | bytes 65568 | tf_op jit(solution)/shard_map/ppermute | solution.py:405
  31.2 0.0 collective-permute-start.3
  31.2 0.0 collective-permute-done.2.pair_ref.other_ref
  31.2 4.7 %collective-permute-done.3.across_ref = bf16[128,256]{1,0:T(8,128)(2,1)S(1)} collective-permute-done((bf16[128,256]{1,0:T(8,128)(2,1)S(1)}, bf16[128,256]{1,0:T(8,128)(2,1)S(1)}, u32[]{:S(2)}, u32[]{:S(2)}) %collective-permute-start.3) | collective-permute-done | bytes 65568 | tf_op jit(solution)/shard_map/ppermute | solution.py:405
  35.9 0.4 four_map.1
  36.2 0.8 %collective-permute-start.5 = (bf16[128,256]{1,0:T(8,128)(2,1)S(1)}, bf16[128,256]{1,0:T(8,128)(2,1)S(1)}, u32[]{:S(2)}, u32[]{:S(2)}) collective-permute-start(bf16[128,256]{1,0:T(8,128)(2,1)S(1)} %get-tuple-element.38.own_ref), channel_id=1, source_target_pairs={{0,48},{4,52},{8,56},{12,60},{16,32},{20,36},{24,40},{28,44},{32,1... | collective-permute-start | bytes 196616 | tf_op jit(solution)/shard_map/ppermute | solution.py:405
  37.1 4.5 %collective-permute-done.5.other_ref = bf16[128,256]{1,0:T(8,128)(2,1)S(1)} collective-permute-done((bf16[128,256]{1,0:T(8,128)(2,1)S(1)}, bf16[128,256]{1,0:T(8,128)(2,1)S(1)}, u32[]{:S(2)}, u32[]{:S(2)}) %collective-permute-start.5) | collective-permute-done | bytes 65568 | tf_op jit(solution)/shard_map/ppermute | solution.py:405
  41.6 0.2 far_map.1
  41.8 0.3 collective-permute-start.6
  42.0 0.5 inner_outputs.1
  42.6 3.5 %collective-permute-start.9 = (f32[2,256,128]{2,1,0:T(8,128)S(1)}, f32[2,256,128]{2,1,0:T(8,128)S(1)}, u32[]{:S(2)}, u32[]{:S(2)}) collective-permute-start(f32[2,256,128]{2,1,0:T(8,128)S(1)} %get-tuple-element.49), channel_id=1, source_target_pairs={{0,4},{4,0},{8,12},{12,8},{16,20},{20,16},{24,28},{28,24},{32,36},... | collective-permute-start | bytes 786440 | tf_op jit(solution)/shard_map/ppermute | solution.py:405
  46.1 0.0 collective-permute-done.6.other_ref.row_ref
  46.1 0.2 rows_state.1
  46.2 1.5 %collective-permute-start.7 = (bf16[128,128]{1,0:T(8,128)(2,1)S(1)}, bf16[128,128]{1,0:T(8,128)(2,1)S(1)}, u32[]{:S(2)}, u32[]{:S(2)}) collective-permute-start(bf16[128,128]{1,0:T(8,128)(2,1)S(1)} %rows_state.1), channel_id=1, source_target_pairs={{0,192},{4,196},{8,200},{12,204},{16,208},{20,212},{24,216},{28,22... | collective-permute-start | bytes 98312 | tf_op jit(solution)/shard_map/ppermute | solution.py:405
  47.8 2.8 %collective-permute-done.7.rows_ref = bf16[128,128]{1,0:T(8,128)(2,1)S(1)} collective-permute-done((bf16[128,128]{1,0:T(8,128)(2,1)S(1)}, bf16[128,128]{1,0:T(8,128)(2,1)S(1)}, u32[]{:S(2)}, u32[]{:S(2)}) %collective-permute-start.7) | collective-permute-done | bytes 32800 | tf_op jit(solution)/shard_map/ppermute | solution.py:405
  50.5 4.5 %collective-permute-start.10 = (bf16[2,256,128]{2,1,0:T(8,128)(2,1)S(1)}, bf16[2,256,128]{2,1,0:T(8,128)(2,1)S(1)}, u32[]{:S(2)}, u32[]{:S(2)}) collective-permute-start(bf16[2,256,128]{2,1,0:T(8,128)(2,1)S(1)} %get-tuple-element.50), channel_id=1, source_target_pairs={{0,4},{4,0},{8,12},{12,8},{16,20},{20,16},{24,28},{28,24},{32,36},... | collective-permute-start | bytes 393224 | tf_op jit(solution)/shard_map/ppermute | solution.py:405
  55.0 0.4 pair_start.1
  55.4 0.6 collective-permute-done.10.gate_in
  56.0 0.0 collective-permute-start.8
  56.0 0.0 collective-permute-done.9.base_in
  56.0 2.8 %collective-permute-done.8.other_state = bf16[128,128]{1,0:T(8,128)(2,1)S(1)} collective-permute-done((bf16[128,128]{1,0:T(8,128)(2,1)S(1)}, bf16[128,128]{1,0:T(8,128)(2,1)S(1)}, u32[]{:S(2)}, u32[]{:S(2)}) %collective-permute-start.8) | collective-permute-done | bytes 32800 | tf_op jit(solution)/shard_map/ppermute | solution.py:405
  58.8 0.0 copy-done.1
  58.8 0.6 finish.1
  59.4 1.7 %collective-permute-start.11 = (bf16[2,64,256]{2,1,0:T(8,128)(2,1)S(1)}, bf16[2,64,256]{2,1,0:T(8,128)(2,1)S(1)}, u32[]{:S(2)}, u32[]{:S(2)}) collective-permute-start(bf16[2,64,256]{2,1,0:T(8,128)(2,1)S(1)} %get-tuple-element.52), channel_id=1, source_target_pairs={{0,1},{1,2},{2,3},{3,0},{4,5},{5,6},{6,7},{7,4},{8,9},{9,10},{10,1... | collective-permute-start | bytes 196616 | tf_op jit(solution)/shard_map/ppermute | solution.py:410
  61.1 1.6 %collective-permute-start.12 = (bf16[2,64,256]{2,1,0:T(8,128)(2,1)S(1)}, bf16[2,64,256]{2,1,0:T(8,128)(2,1)S(1)}, u32[]{:S(2)}, u32[]{:S(2)}) collective-permute-start(bf16[2,64,256]{2,1,0:T(8,128)(2,1)S(1)} %get-tuple-element.53), channel_id=1, source_target_pairs={{0,2},{1,3},{2,0},{3,1},{4,6},{5,7},{6,4},{7,5},{8,10},{9,11},{10,... | collective-permute-start | bytes 196616 | tf_op jit(solution)/shard_map/ppermute | solution.py:410
  62.7 1.2 %collective-permute-done.11.refs_1_ = bf16[2,64,256]{2,1,0:T(8,128)(2,1)S(1)} collective-permute-done((bf16[2,64,256]{2,1,0:T(8,128)(2,1)S(1)}, bf16[2,64,256]{2,1,0:T(8,128)(2,1)S(1)}, u32[]{:S(2)}, u32[]{:S(2)}) %collective-permute-start.11) | collective-permute-done | bytes 65568 | tf_op jit(solution)/shard_map/ppermute | solution.py:410
  63.8 0.8 %collective-permute-start.13 = (bf16[2,64,256]{2,1,0:T(8,128)(2,1)S(1)}, bf16[2,64,256]{2,1,0:T(8,128)(2,1)S(1)}, u32[]{:S(2)}, u32[]{:S(2)}) collective-permute-start(bf16[2,64,256]{2,1,0:T(8,128)(2,1)S(1)} %get-tuple-element.54), channel_id=1, source_target_pairs={{0,3},{1,0},{2,1},{3,2},{4,7},{5,4},{6,5},{7,6},{8,11},{9,8},{10,9... | collective-permute-start | bytes 196616 | tf_op jit(solution)/shard_map/ppermute | solution.py:410
  64.6 1.3 %collective-permute-done.12.refs_2_ = bf16[2,64,256]{2,1,0:T(8,128)(2,1)S(1)} collective-permute-done((bf16[2,64,256]{2,1,0:T(8,128)(2,1)S(1)}, bf16[2,64,256]{2,1,0:T(8,128)(2,1)S(1)}, u32[]{:S(2)}, u32[]{:S(2)}) %collective-permute-start.12) | collective-permute-done | bytes 65568 | tf_op jit(solution)/shard_map/ppermute | solution.py:410
  65.9 1.7 %collective-permute-done.13.refs_3_ = bf16[2,64,256]{2,1,0:T(8,128)(2,1)S(1)} collective-permute-done((bf16[2,64,256]{2,1,0:T(8,128)(2,1)S(1)}, bf16[2,64,256]{2,1,0:T(8,128)(2,1)S(1)}, u32[]{:S(2)}, u32[]{:S(2)}) %collective-permute-start.13) | collective-permute-done | bytes 65568 | tf_op jit(solution)/shard_map/ppermute | solution.py:410
  67.6 0.0 collective-permute-done.16.refs_7_
  67.6 0.0 collective-permute-done.15.refs_6_
  67.6 0.0 collective-permute-done.14.refs_5_
  67.7 0.7 merge.1
  68.4 3.8 %collective-permute-start.17 = (bf16[64,2048]{1,0:T(8,128)(2,1)S(1)}, bf16[64,2048]{1,0:T(8,128)(2,1)S(1)}, u32[]{:S(2)}, u32[]{:S(2)}) collective-permute-start(bf16[64,2048]{1,0:T(8,128)(2,1)S(1)} %get-tuple-element.56), channel_id=1, source_target_pairs={{0,4},{4,0},{8,12},{12,8},{16,20},{20,16},{24,28},{28,24},{32,36},... | collective-permute-start | bytes 786440 | tf_op jit(solution)/shard_map/ppermute | solution.py:405
  72.2 1.2 %collective-permute-done.17 = bf16[64,2048]{1,0:T(8,128)(2,1)S(1)} collective-permute-done((bf16[64,2048]{1,0:T(8,128)(2,1)S(1)}, bf16[64,2048]{1,0:T(8,128)(2,1)S(1)}, u32[]{:S(2)}, u32[]{:S(2)}) %collective-permute-start.17) | collective-permute-done | bytes 262176 | tf_op jit(solution)/shard_map/ppermute | solution.py:405
  73.4 0.8 %add_convert_fusion = bf16[64,2048]{1,0:T(8,128)(2,1)} fusion(f32[64,2048]{1,0:T(8,128)S(1)} %get-tuple-element.55, bf16[64,2048]{1,0:T(8,128)(2,1)S(1)} %collective-permute-done.17), kind=kLoop, calls=%fused_computation | loop fusion | flops 393216 | bytes 1048576 | tf_op jit(solution)/shard_map/convert_element_type | solution.py:440
Async XLA Ops:
  0.0 14.9 %copy-start.2 = (f32[4]{0:T(128)S(1)}, f32[4]{0:T(128)}, u32[]{:S(2)}) copy-start(f32[4]{0:T(128)} %param.11) | copy-start | bytes 52
  0.0 14.9 %copy-start = (f32[3,4,512]{2,1,0:T(4,128)S(1)}, f32[3,4,512]{2,1,0:T(4,128)}, u32[]{:S(2)}) copy-start(f32[3,4,512]{2,1,0:T(4,128)} %conv_ref.1) | copy-start | bytes 73732
  0.0 58.8 %copy-start.1 = (f32[512]{0:T(512)S(1)}, f32[512]{0:T(512)}, u32[]{:S(2)}) copy-start(f32[512]{0:T(512)} %param.12) | copy-start | bytes 6148
  1.3 66.4 %collective-permute-start.16 = (bf16[2,128,2048]{2,1,0:T(8,128)(2,1)S(1)}, bf16[2,128,2048]{2,1,0:T(8,128)(2,1)S(1)}, u32[]{:S(2)}, u32[]{:S(2)}) collective-permute-start(bf16[2,128,2048]{2,1,0:T(8,128)(2,1)S(1)} %own_rows.1.refs_4_), channel_id=1, source_target_pairs={{0,3},{1,0},{2,1},{3,2},{4,7},{5,4},{6,5},{7,6},{8,11},{9,8},{10,9... | collective-permute-start | bytes 3145736 | tf_op jit(solution)/shard_map/ppermute | solution.py:410
  4.9 62.7 %collective-permute-start.15 = (bf16[2,128,2048]{2,1,0:T(8,128)(2,1)S(1)}, bf16[2,128,2048]{2,1,0:T(8,128)(2,1)S(1)}, u32[]{:S(2)}, u32[]{:S(2)}) collective-permute-start(bf16[2,128,2048]{2,1,0:T(8,128)(2,1)S(1)} %own_rows.1.refs_4_), channel_id=1, source_target_pairs={{0,2},{1,3},{2,0},{3,1},{4,6},{5,7},{6,4},{7,5},{8,10},{9,11},{10,... | collective-permute-start | bytes 3145736 | tf_op jit(solution)/shard_map/ppermute | solution.py:410
  5.3 62.4 %collective-permute-start.14 = (bf16[2,128,2048]{2,1,0:T(8,128)(2,1)S(1)}, bf16[2,128,2048]{2,1,0:T(8,128)(2,1)S(1)}, u32[]{:S(2)}, u32[]{:S(2)}) collective-permute-start(bf16[2,128,2048]{2,1,0:T(8,128)(2,1)S(1)} %own_rows.1.refs_4_), channel_id=1, source_target_pairs={{0,1},{1,2},{2,3},{3,0},{4,5},{5,6},{6,7},{7,4},{8,9},{9,10},{10,1... | collective-permute-start | bytes 3145736 | tf_op jit(solution)/shard_map/ppermute | solution.py:410
  10.6 4.3 %collective-permute-start = (bf16[3,16,512]{2,1,0:T(8,128)(2,1)S(1)}, bf16[3,16,512]{2,1,0:T(8,128)(2,1)S(1)}, u32[]{:S(2)}, u32[]{:S(2)}) collective-permute-start(bf16[3,16,512]{2,1,0:T(8,128)(2,1)S(1)} %get-tuple-element.32), channel_id=1, source_target_pairs={{0,4},{4,8},{8,12},{12,16},{16,20},{20,24},{24,28},{28,32},{32,36}... | collective-permute-start | bytes 147464 | tf_op jit(solution)/shard_map/ppermute | solution.py:410
  18.8 6.8 %collective-permute-start.1 = (bf16[2,128,256]{2,1,0:T(8,128)(2,1)S(1)}, bf16[2,128,256]{2,1,0:T(8,128)(2,1)S(1)}, u32[]{:S(2)}, u32[]{:S(2)}) collective-permute-start(bf16[2,128,256]{2,1,0:T(8,128)(2,1)S(1)} %get-tuple-element.35), channel_id=1, source_target_pairs={{0,4},{4,0},{8,12},{12,8},{16,20},{20,16},{24,28},{28,24},{32,36},... | collective-permute-start | bytes 393224 | tf_op jit(solution)/shard_map/ppermute | solution.py:405
  25.9 5.3 %collective-permute-start.4 = (bf16[128,256]{1,0:T(8,128)(2,1)S(1)}, bf16[128,256]{1,0:T(8,128)(2,1)S(1)}, u32[]{:S(2)}, u32[]{:S(2)}) collective-permute-start(bf16[128,256]{1,0:T(8,128)(2,1)S(1)} %get-tuple-element.37), channel_id=1, source_target_pairs={{0,24},{4,28},{8,16},{12,20},{16,8},{20,12},{24,0},{28,4},{32,56},... | collective-permute-start | bytes 196616 | tf_op jit(solution)/shard_map/ppermute | solution.py:405
  26.1 5.0 %collective-permute-start.2 = (bf16[128,256]{1,0:T(8,128)(2,1)S(1)}, bf16[128,256]{1,0:T(8,128)(2,1)S(1)}, u32[]{:S(2)}, u32[]{:S(2)}) collective-permute-start(bf16[128,256]{1,0:T(8,128)(2,1)S(1)} %get-tuple-element.37), channel_id=1, source_target_pairs={{0,8},{4,12},{8,0},{12,4},{16,24},{20,28},{24,16},{28,20},{32,40},... | collective-permute-start | bytes 196616 | tf_op jit(solution)/shard_map/ppermute | solution.py:405
  31.2 4.7 %collective-permute-start.3 = (bf16[128,256]{1,0:T(8,128)(2,1)S(1)}, bf16[128,256]{1,0:T(8,128)(2,1)S(1)}, u32[]{:S(2)}, u32[]{:S(2)}) collective-permute-start(bf16[128,256]{1,0:T(8,128)(2,1)S(1)} %get-tuple-element.36.own_ref), channel_id=1, source_target_pairs={{0,16},{4,20},{8,24},{12,28},{16,0},{20,4},{24,8},{28,12},{32,48},... | collective-permute-start | bytes 196616 | tf_op jit(solution)/shard_map/ppermute | solution.py:405
  36.2 5.3 %collective-permute-start.5 = (bf16[128,256]{1,0:T(8,128)(2,1)S(1)}, bf16[128,256]{1,0:T(8,128)(2,1)S(1)}, u32[]{:S(2)}, u32[]{:S(2)}) collective-permute-start(bf16[128,256]{1,0:T(8,128)(2,1)S(1)} %get-tuple-element.38.own_ref), channel_id=1, source_target_pairs={{0,48},{4,52},{8,56},{12,60},{16,32},{20,36},{24,40},{28,44},{32,1... | collective-permute-start | bytes 196616 | tf_op jit(solution)/shard_map/ppermute | solution.py:405
  41.8 4.3 %collective-permute-start.6 = (bf16[128,256]{1,0:T(8,128)(2,1)S(1)}, bf16[128,256]{1,0:T(8,128)(2,1)S(1)}, u32[]{:S(2)}, u32[]{:S(2)}) collective-permute-start(bf16[128,256]{1,0:T(8,128)(2,1)S(1)} %get-tuple-element.40.own_ref), channel_id=1, source_target_pairs={{0,64},{4,68},{8,72},{12,76},{16,80},{20,84},{24,88},{28,92},{32,9... | collective-permute-start | bytes 196616 | tf_op jit(solution)/shard_map/ppermute | solution.py:405
  42.6 13.4 %collective-permute-start.9 = (f32[2,256,128]{2,1,0:T(8,128)S(1)}, f32[2,256,128]{2,1,0:T(8,128)S(1)}, u32[]{:S(2)}, u32[]{:S(2)}) collective-permute-start(f32[2,256,128]{2,1,0:T(8,128)S(1)} %get-tuple-element.49), channel_id=1, source_target_pairs={{0,4},{4,0},{8,12},{12,8},{16,20},{20,16},{24,28},{28,24},{32,36},... | collective-permute-start | bytes 786440 | tf_op jit(solution)/shard_map/ppermute | solution.py:405
  46.2 4.3 %collective-permute-start.7 = (bf16[128,128]{1,0:T(8,128)(2,1)S(1)}, bf16[128,128]{1,0:T(8,128)(2,1)S(1)}, u32[]{:S(2)}, u32[]{:S(2)}) collective-permute-start(bf16[128,128]{1,0:T(8,128)(2,1)S(1)} %rows_state.1), channel_id=1, source_target_pairs={{0,192},{4,196},{8,200},{12,204},{16,208},{20,212},{24,216},{28,22... | collective-permute-start | bytes 98312 | tf_op jit(solution)/shard_map/ppermute | solution.py:405
  50.5 5.4 %collective-permute-start.10 = (bf16[2,256,128]{2,1,0:T(8,128)(2,1)S(1)}, bf16[2,256,128]{2,1,0:T(8,128)(2,1)S(1)}, u32[]{:S(2)}, u32[]{:S(2)}) collective-permute-start(bf16[2,256,128]{2,1,0:T(8,128)(2,1)S(1)} %get-tuple-element.50), channel_id=1, source_target_pairs={{0,4},{4,0},{8,12},{12,8},{16,20},{20,16},{24,28},{28,24},{32,36},... | collective-permute-start | bytes 393224 | tf_op jit(solution)/shard_map/ppermute | solution.py:405
  56.0 2.8 %collective-permute-start.8 = (bf16[128,128]{1,0:T(8,128)(2,1)S(1)}, bf16[128,128]{1,0:T(8,128)(2,1)S(1)}, u32[]{:S(2)}, u32[]{:S(2)}) collective-permute-start(bf16[128,128]{1,0:T(8,128)(2,1)S(1)} %get-tuple-element.43), channel_id=1, source_target_pairs={{0,8},{4,12},{8,0},{12,4},{16,24},{20,28},{24,16},{28,20},{32,40},... | collective-permute-start | bytes 98312 | tf_op jit(solution)/shard_map/ppermute | solution.py:405
  59.4 4.4 %collective-permute-start.11 = (bf16[2,64,256]{2,1,0:T(8,128)(2,1)S(1)}, bf16[2,64,256]{2,1,0:T(8,128)(2,1)S(1)}, u32[]{:S(2)}, u32[]{:S(2)}) collective-permute-start(bf16[2,64,256]{2,1,0:T(8,128)(2,1)S(1)} %get-tuple-element.52), channel_id=1, source_target_pairs={{0,1},{1,2},{2,3},{3,0},{4,5},{5,6},{6,7},{7,4},{8,9},{9,10},{10,1... | collective-permute-start | bytes 196616 | tf_op jit(solution)/shard_map/ppermute | solution.py:410
  61.1 4.8 %collective-permute-start.12 = (bf16[2,64,256]{2,1,0:T(8,128)(2,1)S(1)}, bf16[2,64,256]{2,1,0:T(8,128)(2,1)S(1)}, u32[]{:S(2)}, u32[]{:S(2)}) collective-permute-start(bf16[2,64,256]{2,1,0:T(8,128)(2,1)S(1)} %get-tuple-element.53), channel_id=1, source_target_pairs={{0,2},{1,3},{2,0},{3,1},{4,6},{5,7},{6,4},{7,5},{8,10},{9,11},{10,... | collective-permute-start | bytes 196616 | tf_op jit(solution)/shard_map/ppermute | solution.py:410
  63.8 3.8 %collective-permute-start.13 = (bf16[2,64,256]{2,1,0:T(8,128)(2,1)S(1)}, bf16[2,64,256]{2,1,0:T(8,128)(2,1)S(1)}, u32[]{:S(2)}, u32[]{:S(2)}) collective-permute-start(bf16[2,64,256]{2,1,0:T(8,128)(2,1)S(1)} %get-tuple-element.54), channel_id=1, source_target_pairs={{0,3},{1,0},{2,1},{3,2},{4,7},{5,4},{6,5},{7,6},{8,11},{9,8},{10,9... | collective-permute-start | bytes 196616 | tf_op jit(solution)/shard_map/ppermute | solution.py:410
  68.4 5.0 %collective-permute-start.17 = (bf16[64,2048]{1,0:T(8,128)(2,1)S(1)}, bf16[64,2048]{1,0:T(8,128)(2,1)S(1)}, u32[]{:S(2)}, u32[]{:S(2)}) collective-permute-start(bf16[64,2048]{1,0:T(8,128)(2,1)S(1)} %get-tuple-element.56), channel_id=1, source_target_pairs={{0,4},{4,0},{8,12},{12,8},{16,20},{20,16},{24,28},{28,24},{32,36},... | collective-permute-start | bytes 786440 | tf_op jit(solution)/shard_map/ppermute | solution.py:405

commit v5 on v4

--- a/solution.py
+++ b/solution.py
@@ -37,13 +37,21 @@
 
 
 def project_kernel(
-    tokens_hbm, w_hbm, beta_w_hbm, out_ref, edge_ref, logits_ref,
+    tokens_hbm, w_hbm, beta_w_hbm, w_out_hbm, out_ref, edge_ref, logits_ref, w_own_ref,
     tokens_ref, w_ref, beta_w_ref, small_sems, w_sems
 ):
     length = tokens_ref.shape[0]
     first = pltpu.make_async_copy(tokens_hbm, tokens_ref, small_sems.at[0])
     last = pltpu.make_async_copy(beta_w_hbm, beta_w_ref, small_sems.at[1])
     copies = [pltpu.make_async_copy(w_hbm.at[s], w_ref.at[s], w_sems.at[s]) for s in range(3)]
+    rows = [
+        pltpu.make_async_copy(
+            w_out_hbm.at[pl.ds(pl.multiple_of((2 * j + bit(1)) * DK, DK), DK)],
+            w_own_ref.at[j],
+            small_sems.at[2 + j],
+        )
+        for j in range(2)
+    ]
     first.start()
     last.start()
     copies[0].start()
@@ -55,32 +63,38 @@
         copies[s].wait()
         if s == 0:
             copies[2].start()
+        if s == 1:
+            rows[0].start()
+            rows[1].start()
         result = dot(tokens_ref[...], w_ref[s]).astype(bf16)
         out_ref[s] = result
         edge_ref[s] = result[length - EDGE :]
-
-
-def project(tokens, w_qkv, beta_weight):
+    rows[0].wait()
+    rows[1].wait()
+
+
+def project(tokens, w_qkv, beta_weight, w_out):
     length, depth = tokens.shape
     columns = w_qkv.shape[2]
     heads = beta_weight.shape[0]
     operands = [
-        pltpu.with_memory_space_constraint(x, pltpu.HBM) for x in (tokens, w_qkv, beta_weight)
+        pltpu.with_memory_space_constraint(x, pltpu.HBM) for x in (tokens, w_qkv, beta_weight, w_out)
     ]
     return pl.pallas_call(
         project_kernel,
-        in_specs=[pl.BlockSpec(memory_space=pltpu.HBM)] * 3,
-        out_specs=whole(3),
+        in_specs=[pl.BlockSpec(memory_space=pltpu.HBM)] * 4,
+        out_specs=whole(4),
         out_shape=[
             shape((3, length, columns), bf16),
             shape((3, EDGE, columns), bf16),
             shape((length, heads), f32),
+            shape((2, DK, w_out.shape[1]), bf16),
         ],
         scratch_shapes=[
             pltpu.VMEM(tokens.shape, bf16),
             pltpu.VMEM(w_qkv.shape, bf16),
             pltpu.VMEM(beta_weight.shape, bf16),
-            pltpu.SemaphoreType.DMA((2,)),
+            pltpu.SemaphoreType.DMA((4,)),
             pltpu.SemaphoreType.DMA((3,)),
         ],
         compiler_params=params(),
@@ -212,30 +226,31 @@
     )(projected, edge, conv_weight, logits, beta_bias[None, :])
 
 
-def inner_kernel(queries_ref, keys_t_ref, uw_ref, base_ref, gate_ref, base_out, gate_out):
+def inner_kernel(queries_ref, keys_t_ref, uw_ref, base_ref, gate_ref, both_out):
     length = queries_ref.shape[1]
     row, column = grid_index(length, length)
     core = bit(1)
     for j in range(2):
         for h, base, gate in (
-            (2 * j + core, base_ref, gate_ref),
-            (2 * j + 1 - core, base_out, gate_out),
+            (2 * j + core, base_ref.at[j], gate_ref.at[j]),
+            (2 * j + 1 - core, both_out.at[0, j], both_out.at[1, j]),
         ):
             query = queries_ref[h]
             scores = jnp.where(row >= column, dot(query, keys_t_ref[h]), 0.0).astype(bf16)
             both = dot(scores, uw_ref[h])
-            base[j] = both[:, :DK]
-            gate[j] = (query.astype(f32) - both[:, DK:]).astype(bf16)
+            base[...] = both[:, :DK].astype(base.dtype)
+            gate[...] = (query.astype(f32) - both[:, DK:]).astype(bf16)
 
 
 def inner_outputs(queries, keys_t, uw):
     heads, length, _ = queries.shape
     outs = [shape((2, length, DK), f32), shape((2, length, DK), bf16)]
+    outs.append(shape((2, 2, length, DK), bf16))
     return pl.pallas_call(
         inner_kernel,
         in_specs=whole(3),
-        out_specs=whole(4),
-        out_shape=outs + outs,
+        out_specs=whole(3),
+        out_shape=outs,
         compiler_params=params(),
         cost_estimate=pl.CostEstimate(
             flops=2 * heads * length * length * 3 * DK, bytes_accessed=2 << 20, transcendentals=0
@@ -325,7 +340,7 @@
 
 
 def finish_kernel(
-    own_state, other_state, own_maps, other_maps, base_ref, gate_ref, base_in, gate_in, gain_ref,
+    own_state, other_state, own_maps, other_maps, base_ref, gate_ref, both_in, gain_ref,
     mine_ref, one, two, three, normed
 ):
     late, upper = bit(1) == 1, bit(2) == 1
@@ -337,10 +352,10 @@
         after = advance(state, first)
         gain = gain_ref[2 * j + core]
         for slot, start, base, gate in (
-            (0, jnp.where(late, after, state), base_ref, gate_ref),
-            (1, jnp.where(late, state, after), base_in, gate_in),
+            (0, jnp.where(late, after, state), base_ref.at[j], gate_ref.at[j]),
+            (1, jnp.where(late, state, after), both_in.at[0, j], both_in.at[1, j]),
         ):
-            heads_out = base[j] + dot(gate[j], start.astype(bf16))
+            heads_out = base[...].astype(f32) + dot(gate[...], start.astype(bf16))
             scale = lax.rsqrt(jnp.mean(heads_out * heads_out, axis=-1, keepdims=True) + EPS)
             normed[slot, :, j * DK : (j + 1) * DK] = (heads_out * scale * gain).astype(bf16)
     rows = mine_ref.shape[1]
@@ -355,32 +370,7 @@
     part = shape((2, length // 4, 2 * DK), bf16)
     return small_call(
         finish_kernel, [part] * 4, "finish", [pltpu.VMEM((2, length, 2 * DK), bf16)]
-    )(*states, *maps, *inner, *inner_in, norm_gain.reshape(4, 1, DK))
-
-
-def rows_kernel_of(w_hbm, out_ref, sems):
-    copies = [
-        pltpu.make_async_copy(
-            w_hbm.at[pl.ds(pl.multiple_of((2 * j + bit(1)) * DK, DK), DK)], out_ref.at[j], sems.at[j]
-        )
-        for j in range(2)
-    ]
-    for copy in copies:
-        copy.start()
-    for copy in copies:
-        copy.wait()
-
-
-def own_rows(w_out):
-    return pl.pallas_call(
-        rows_kernel_of,
-        in_specs=[pl.BlockSpec(memory_space=pltpu.HBM)],
-        out_specs=pl.BlockSpec(memory_space=pltpu.VMEM),
-        out_shape=shape((2, DK, w_out.shape[1]), bf16),
-        scratch_shapes=[pltpu.SemaphoreType.DMA((2,))],
-        compiler_params=params(),
-        name="own_rows",
-    )(pltpu.with_memory_space_constraint(w_out, pltpu.HBM))
+    )(*states, *maps, *inner, inner_in, norm_gain.reshape(4, 1, DK))
 
 
 def merge_kernel(*refs):
@@ -411,21 +401,23 @@
 
 
 def per_device(tokens_in, w_qkv, conv_weight, beta_weight, beta_bias, norm_gain, w_out):
-    w_own = own_rows(w_out)
-    w_one, w_three, w_two = (turned(w_own, "head", s) for s in (1, 3, 2))
-    projected, edge, logits = project(tokens_in, w_qkv, beta_weight)
+    projected, edge, logits, w_own = project(tokens_in, w_qkv, beta_weight, w_out)
     edge = turned(edge, "ctx", 1)
+    w_one, w_three = turned(w_own, "head", 1), turned(w_own, "head", 3)
     queries, keys_t, uw, maps, send = local_maps(projected, edge, conv_weight, logits, beta_bias)
     sibling = swapped(send, 1)
-    base, gate, *sent = inner_outputs(queries, keys_t, uw)
-    inner_in = [swapped(x, 1) for x in sent]
     chip, send = small_call(
         chip_kernel, [MAP, MAP], "chip_map", [pltpu.VMEM((2, DK, 2 * DK), bf16)]
     )(maps, sibling)
     pair, across, diagonal = swapped(send, 2), swapped(chip, 4), swapped(send, 6)
     four, near = small_call(four_kernel, [MAP, MAP], "four_map")(chip, pair, across, diagonal)
+    near, w_own, w_one, w_three = lax.optimization_barrier((near, w_own, w_one, w_three))
+    w_two = turned(w_own, "head", 2)
     row, before = small_call(far_kernel, [MAP, MAP], "far_map")(four, swapped(four, 12), near)
     other_row = swapped(row, 16)
+    before, queries = lax.optimization_barrier((before, queries))
+    base, gate, both = inner_outputs(queries, keys_t, uw)
+    inner_in = swapped(both, 1)
     (two_rows,) = small_call(rows_kernel, [STATE], "rows_state")(row, other_row)
     rows = swapped(two_rows, 48)
     state, send = small_call(pair_start_kernel, [STATE, STATE], "pair_start")(

time: 74.3 us -> 69.9 us (0.941)
  waiting for transfers between devices: 27.8 us -> 16.6 us
  starting transfers between devices: 32.3 us -> 40.5 us
  Pallas kernels: 13.1 us -> 11.9 us
    ppermute x11 -> x10, waiting for transfers between devices: 22.4 us -> 12.8 us  [swapped(): lax.ppermute(x, 'ctx', [(i, i ^ by) for i in range(lax.axis_size('ctx'))])]
    ppermute x11 -> x10, starting transfers between devices: 20.5 us -> 28.3 us  [swapped(): lax.ppermute(x, 'ctx', [(i, i ^ by) for i in range(lax.axis_size('ctx'))])]
    ppermute x7, waiting for transfers between devices: 5.4 us -> 3.75 us  [turned(): return lax.ppermute(x, axis, [(i, (i + by) % count) for i in range(count)])]
    pallas_call x2 -> x1, Pallas kernels: 1.8 us -> 0.54 us  [inner_outputs(): pl.pallas_call(inner_kernel, in_specs=whole(3), out_specs=whole(3), out_s...]
  transfers between devices with their start and end apart: 18 -> 17, of which waited for: 12 -> 12; matrix products, arithmetic and copies ran while one was open for 0% -> 0% of each run, Pallas kernels for 15% -> 9%
where the time goes in v5:
time: 69.9 us; the launch traced here: 69.8 us
  starting transfers between devices  40.5 us (58%)
  waiting for transfers between devices  16.6 us (24%)
  Pallas kernels  11.9 us (17%)
  other arithmetic  0.76 us (1%)
    ppermute x10, starting transfers between devices, swapped(): lax.ppermute(x, 'ctx', [(i, i ^ by) for i in range(lax.axis_size('ctx'))])  28.3 us
    ppermute x10, waiting for transfers between devices, swapped(): lax.ppermute(x, 'ctx', [(i, i ^ by) for i in range(lax.axis_size('ctx'))])  12.8 us
    ppermute x7, starting transfers between devices, turned(): return lax.ppermute(x, axis, [(i, (i + by) % count) for i in range(count)])  12.2 us
    pallas_call x1, Pallas kernels, project(): pl.pallas_call(project_kernel, in_specs=[pl.BlockSpec(memory_space=pltpu....  4.63 us
    pallas_call x1, Pallas kernels, local_maps(): pl.pallas_call(local_kernel, in_specs=whole(5), out_specs=whole(5), out_s...  3.96 us
    ppermute x7, waiting for transfers between devices, turned(): return lax.ppermute(x, axis, [(i, (i + by) % count) for i in range(count)])  3.75 us
  transfers between devices with their start and end apart: 17, of which 12 were waited for; matrix products, arithmetic and copies ran while one was open for 0% of the time, Pallas kernels for 9%

profile of v5, /device:TPU:1, one launch (start us, length us, event | category | flops | bytes accessed | tf_op | source)
XLA Modules:
  0.0 69.8 jit_solution(6220868994920064821)
XLA Ops:
  0.0 0.0 copy-start
  0.0 0.0 copy-start.2
  0.0 0.0 copy-start.1
  0.0 4.6 %project.1 = (bf16[3,256,512]{2,1,0:T(8,128)(2,1)S(1)}, bf16[3,16,512]{2,1,0:T(8,128)(2,1)S(1)}, f32[256,4]{1,0:T(8,128)S(1)}, bf16[2,128,2048]{2,1,0:T(8,128)(2,1)S(1)}) custom-call(bf16[256,2048]{1,0:T(8,128)(2,1)} %tokens_hbm.1, bf16[3,2048,512]{2,1,0:T(8,128)(2,1)} %w_hbm.1, bf16[4,2048]{1,0:T(4,128)(2,1)} %beta_w_hbm.1, bf16[512,2048]{1,0:T(8,128)(2,1)} %w_out_hbm.1), custom_call_target="tpu_custom_call" | custom-call | tf_op jit(solution)/shard_map/project/pallas_call | solution.py:83
  4.6 2.2 %collective-permute-start.6 = (bf16[2,128,2048]{2,1,0:T(8,128)(2,1)S(1)}, bf16[2,128,2048]{2,1,0:T(8,128)(2,1)S(1)}, u32[]{:S(2)}, u32[]{:S(2)}) collective-permute-start(bf16[2,128,2048]{2,1,0:T(8,128)(2,1)S(1)} %get-tuple-element.64.refs_4_), channel_id=1, source_target_pairs={{0,1},{1,2},{2,3},{3,0},{4,5},{5,6},{6,7},{7,4},{8,9},{9,10},{10,1... | collective-permute-start | bytes 3145736 | tf_op jit(solution)/shard_map/ppermute | solution.py:400
  6.8 1.5 %collective-permute-start.7 = (bf16[2,128,2048]{2,1,0:T(8,128)(2,1)S(1)}, bf16[2,128,2048]{2,1,0:T(8,128)(2,1)S(1)}, u32[]{:S(2)}, u32[]{:S(2)}) collective-permute-start(bf16[2,128,2048]{2,1,0:T(8,128)(2,1)S(1)} %get-tuple-element.64.refs_4_), channel_id=1, source_target_pairs={{0,3},{1,0},{2,1},{3,2},{4,7},{5,4},{6,5},{7,6},{8,11},{9,8},{10,9... | collective-permute-start | bytes 3145736 | tf_op jit(solution)/shard_map/ppermute | solution.py:400
  8.4 2.6 %collective-permute-start = (bf16[3,16,512]{2,1,0:T(8,128)(2,1)S(1)}, bf16[3,16,512]{2,1,0:T(8,128)(2,1)S(1)}, u32[]{:S(2)}, u32[]{:S(2)}) collective-permute-start(bf16[3,16,512]{2,1,0:T(8,128)(2,1)S(1)} %get-tuple-element.38), channel_id=1, source_target_pairs={{0,4},{4,8},{8,12},{12,16},{16,20},{20,24},{24,28},{28,32},{32,36}... | collective-permute-start | bytes 147464 | tf_op jit(solution)/shard_map/ppermute | solution.py:400
  11.0 1.2 %collective-permute-done.edge_ref = bf16[3,16,512]{2,1,0:T(8,128)(2,1)S(1)} collective-permute-done((bf16[3,16,512]{2,1,0:T(8,128)(2,1)S(1)}, bf16[3,16,512]{2,1,0:T(8,128)(2,1)S(1)}, u32[]{:S(2)}, u32[]{:S(2)}) %collective-permute-start) | collective-permute-done | bytes 49184 | tf_op jit(solution)/shard_map/ppermute | solution.py:400
  12.2 0.0 copy-done
  12.2 0.0 copy-done.2
  12.2 4.0 %local_maps.1 = (bf16[4,256,128]{2,1,0:T(8,128)(2,1)S(1)}, bf16[4,128,256]{2,1,0:T(8,128)(2,1)S(1)}, bf16[4,256,256]{2,1,0:T(8,128)(2,1)S(1)}, bf16[2,128,256]{2,1,0:T(8,128)(2,1)S(1)}, bf16[2,128,256]{2,1,0:T(8,128)(2,1)S(1)}) custom-call(bf16[3,256,512]{2,1,0:T(8,128)(2,1)S(1)} %get-tuple-element.37.proj_ref, ...), custom_call_target="tpu_custom_call" | custom-call | tf_op jit(solution)/shard_map/local_maps/pallas_call | solution.py:210
  16.1 6.2 %collective-permute-start.1 = (bf16[2,128,256]{2,1,0:T(8,128)(2,1)S(1)}, bf16[2,128,256]{2,1,0:T(8,128)(2,1)S(1)}, u32[]{:S(2)}, u32[]{:S(2)}) collective-permute-start(bf16[2,128,256]{2,1,0:T(8,128)(2,1)S(1)} %get-tuple-element.41), channel_id=1, source_target_pairs={{0,4},{4,0},{8,12},{12,8},{16,20},{20,16},{24,28},{28,24},{32,36},... | collective-permute-start | bytes 393224 | tf_op jit(solution)/shard_map/ppermute | solution.py:395
  22.4 1.0 %collective-permute-done.1.other_ref.other_maps = bf16[2,128,256]{2,1,0:T(8,128)(2,1)S(1)} collective-permute-done((bf16[2,128,256]{2,1,0:T(8,128)(2,1)S(1)}, bf16[2,128,256]{2,1,0:T(8,128)(2,1)S(1)}, u32[]{:S(2)}, u32[]{:S(2)}) %collective-permute-start.1) | collective-permute-done | bytes 131104 | tf_op jit(solution)/shard_map/ppermute | solution.py:395
  23.4 0.2 chip_map.1
  23.6 0.1 collective-permute-start.2
  23.7 0.1 collective-permute-start.3
  23.8 3.4 %collective-permute-start.4 = (bf16[128,256]{1,0:T(8,128)(2,1)S(1)}, bf16[128,256]{1,0:T(8,128)(2,1)S(1)}, u32[]{:S(2)}, u32[]{:S(2)}) collective-permute-start(bf16[128,256]{1,0:T(8,128)(2,1)S(1)} %get-tuple-element.43), channel_id=1, source_target_pairs={{0,24},{4,28},{8,16},{12,20},{16,8},{20,12},{24,0},{28,4},{32,56},... | collective-permute-start | bytes 196616 | tf_op jit(solution)/shard_map/ppermute | solution.py:395
  27.2 0.0 collective-permute-done.2.pair_ref.other_ref
  27.2 0.9 %collective-permute-done.3.across_ref = bf16[128,256]{1,0:T(8,128)(2,1)S(1)} collective-permute-done((bf16[128,256]{1,0:T(8,128)(2,1)S(1)}, bf16[128,256]{1,0:T(8,128)(2,1)S(1)}, u32[]{:S(2)}, u32[]{:S(2)}) %collective-permute-start.3) | collective-permute-done | bytes 65568 | tf_op jit(solution)/shard_map/ppermute | solution.py:395
  28.1 1.9 %collective-permute-done.4.diagonal_ref = bf16[128,256]{1,0:T(8,128)(2,1)S(1)} collective-permute-done((bf16[128,256]{1,0:T(8,128)(2,1)S(1)}, bf16[128,256]{1,0:T(8,128)(2,1)S(1)}, u32[]{:S(2)}, u32[]{:S(2)}) %collective-permute-start.4) | collective-permute-done | bytes 65568 | tf_op jit(solution)/shard_map/ppermute | solution.py:395
  30.0 0.4 four_map.1
  30.4 0.0 collective-permute-done.6.refs_5_
  30.4 0.0 collective-permute-done.7.refs_7_
  30.4 2.8 %collective-permute-start.15 = (bf16[2,128,2048]{2,1,0:T(8,128)(2,1)S(1)}, bf16[2,128,2048]{2,1,0:T(8,128)(2,1)S(1)}, u32[]{:S(2)}, u32[]{:S(2)}) collective-permute-start(bf16[2,128,2048]{2,1,0:T(8,128)(2,1)S(1)} %get-tuple-element.64.refs_4_), channel_id=1, source_target_pairs={{0,2},{1,3},{2,0},{3,1},{4,6},{5,7},{6,4},{7,5},{8,10},{9,11},{10,... | collective-permute-start | bytes 3145736 | tf_op jit(solution)/shard_map/ppermute | solution.py:400
  33.2 6.0 %collective-permute-start.5 = (bf16[128,256]{1,0:T(8,128)(2,1)S(1)}, bf16[128,256]{1,0:T(8,128)(2,1)S(1)}, u32[]{:S(2)}, u32[]{:S(2)}) collective-permute-start(bf16[128,256]{1,0:T(8,128)(2,1)S(1)} %get-tuple-element.44.own_ref), channel_id=1, source_target_pairs={{0,48},{4,52},{8,56},{12,60},{16,32},{20,36},{24,40},{28,44},{32,1... | collective-permute-start | bytes 196616 | tf_op jit(solution)/shard_map/ppermute | solution.py:395
  39.2 1.9 %collective-permute-done.5.other_ref = bf16[128,256]{1,0:T(8,128)(2,1)S(1)} collective-permute-done((bf16[128,256]{1,0:T(8,128)(2,1)S(1)}, bf16[128,256]{1,0:T(8,128)(2,1)S(1)}, u32[]{:S(2)}, u32[]{:S(2)}) %collective-permute-start.5) | collective-permute-done | bytes 65568 | tf_op jit(solution)/shard_map/ppermute | solution.py:395
  41.1 0.2 far_map.1
  41.3 0.5 inner_outputs.1
  41.9 3.1 %collective-permute-start.11 = (bf16[2,2,256,128]{3,2,1,0:T(8,128)(2,1)S(1)}, bf16[2,2,256,128]{3,2,1,0:T(8,128)(2,1)S(1)}, u32[]{:S(2)}, u32[]{:S(2)}) collective-permute-start(bf16[2,2,256,128]{3,2,1,0:T(8,128)(2,1)S(1)} %get-tuple-element.59), channel_id=1, source_target_pairs={{0,4},{4,0},{8,12},{12,8},{16,20},{20,16},{24,28},{28,24},{32,36},... | collective-permute-start | bytes 786440 | tf_op jit(solution)/shard_map/ppermute | solution.py:395
  45.0 1.2 %collective-permute-start.8 = (bf16[128,256]{1,0:T(8,128)(2,1)S(1)}, bf16[128,256]{1,0:T(8,128)(2,1)S(1)}, u32[]{:S(2)}, u32[]{:S(2)}) collective-permute-start(bf16[128,256]{1,0:T(8,128)(2,1)S(1)} %get-tuple-element.48.own_ref), channel_id=1, source_target_pairs={{0,64},{4,68},{8,72},{12,76},{16,80},{20,84},{24,88},{28,92},{32,9... | collective-permute-start | bytes 196616 | tf_op jit(solution)/shard_map/ppermute | solution.py:395
  46.2 2.4 %collective-permute-done.8.other_ref.row_ref = bf16[128,256]{1,0:T(8,128)(2,1)S(1)} collective-permute-done((bf16[128,256]{1,0:T(8,128)(2,1)S(1)}, bf16[128,256]{1,0:T(8,128)(2,1)S(1)}, u32[]{:S(2)}, u32[]{:S(2)}) %collective-permute-start.8) | collective-permute-done | bytes 65568 | tf_op jit(solution)/shard_map/ppermute | solution.py:395
  48.6 0.1 rows_state.1
  48.8 2.5 %collective-permute-start.9 = (bf16[128,128]{1,0:T(8,128)(2,1)S(1)}, bf16[128,128]{1,0:T(8,128)(2,1)S(1)}, u32[]{:S(2)}, u32[]{:S(2)}) collective-permute-start(bf16[128,128]{1,0:T(8,128)(2,1)S(1)} %rows_state.1), channel_id=1, source_target_pairs={{0,192},{4,196},{8,200},{12,204},{16,208},{20,212},{24,216},{28,22... | collective-permute-start | bytes 98312 | tf_op jit(solution)/shard_map/ppermute | solution.py:395
  51.3 1.8 %collective-permute-done.9.rows_ref = bf16[128,128]{1,0:T(8,128)(2,1)S(1)} collective-permute-done((bf16[128,128]{1,0:T(8,128)(2,1)S(1)}, bf16[128,128]{1,0:T(8,128)(2,1)S(1)}, u32[]{:S(2)}, u32[]{:S(2)}) %collective-permute-start.9) | collective-permute-done | bytes 32800 | tf_op jit(solution)/shard_map/ppermute | solution.py:395
  53.1 0.4 pair_start.1
  53.5 1.4 %collective-permute-start.10 = (bf16[128,128]{1,0:T(8,128)(2,1)S(1)}, bf16[128,128]{1,0:T(8,128)(2,1)S(1)}, u32[]{:S(2)}, u32[]{:S(2)}) collective-permute-start(bf16[128,128]{1,0:T(8,128)(2,1)S(1)} %get-tuple-element.53), channel_id=1, source_target_pairs={{0,8},{4,12},{8,0},{12,4},{16,24},{20,28},{24,16},{28,20},{32,40},... | collective-permute-start | bytes 98312 | tf_op jit(solution)/shard_map/ppermute | solution.py:395
  55.0 1.7 %collective-permute-done.10.other_state = bf16[128,128]{1,0:T(8,128)(2,1)S(1)} collective-permute-done((bf16[128,128]{1,0:T(8,128)(2,1)S(1)}, bf16[128,128]{1,0:T(8,128)(2,1)S(1)}, u32[]{:S(2)}, u32[]{:S(2)}) %collective-permute-start.10) | collective-permute-done | bytes 32800 | tf_op jit(solution)/shard_map/ppermute | solution.py:395
  56.7 0.0 collective-permute-done.11.both_in
  56.7 0.0 copy-done.1
  56.7 0.7 finish.1
  57.3 0.6 collective-permute-start.12
  58.0 1.7 %collective-permute-start.13 = (bf16[2,64,256]{2,1,0:T(8,128)(2,1)S(1)}, bf16[2,64,256]{2,1,0:T(8,128)(2,1)S(1)}, u32[]{:S(2)}, u32[]{:S(2)}) collective-permute-start(bf16[2,64,256]{2,1,0:T(8,128)(2,1)S(1)} %get-tuple-element.62), channel_id=1, source_target_pairs={{0,2},{1,3},{2,0},{3,1},{4,6},{5,7},{6,4},{7,5},{8,10},{9,11},{10,... | collective-permute-start | bytes 196616 | tf_op jit(solution)/shard_map/ppermute | solution.py:400
  59.7 0.8 %collective-permute-start.14 = (bf16[2,64,256]{2,1,0:T(8,128)(2,1)S(1)}, bf16[2,64,256]{2,1,0:T(8,128)(2,1)S(1)}, u32[]{:S(2)}, u32[]{:S(2)}) collective-permute-start(bf16[2,64,256]{2,1,0:T(8,128)(2,1)S(1)} %get-tuple-element.63), channel_id=1, source_target_pairs={{0,3},{1,0},{2,1},{3,2},{4,7},{5,4},{6,5},{7,6},{8,11},{9,8},{10,9... | collective-permute-start | bytes 196616 | tf_op jit(solution)/shard_map/ppermute | solution.py:400
  60.5 1.3 %collective-permute-done.12.refs_1_ = bf16[2,64,256]{2,1,0:T(8,128)(2,1)S(1)} collective-permute-done((bf16[2,64,256]{2,1,0:T(8,128)(2,1)S(1)}, bf16[2,64,256]{2,1,0:T(8,128)(2,1)S(1)}, u32[]{:S(2)}, u32[]{:S(2)}) %collective-permute-start.12) | collective-permute-done | bytes 65568 | tf_op jit(solution)/shard_map/ppermute | solution.py:400
  61.7 0.8 %collective-permute-done.13.refs_2_ = bf16[2,64,256]{2,1,0:T(8,128)(2,1)S(1)} collective-permute-done((bf16[2,64,256]{2,1,0:T(8,128)(2,1)S(1)}, bf16[2,64,256]{2,1,0:T(8,128)(2,1)S(1)}, u32[]{:S(2)}, u32[]{:S(2)}) %collective-permute-start.13) | collective-permute-done | bytes 65568 | tf_op jit(solution)/shard_map/ppermute | solution.py:400
  62.6 0.4 collective-permute-done.14.refs_3_
  63.0 0.0 collective-permute-done.15.refs_6_
  63.0 0.7 %merge.1 = (f32[64,2048]{1,0:T(8,128)S(1)}, bf16[64,2048]{1,0:T(8,128)(2,1)S(1)}) custom-call(bf16[2,64,256]{2,1,0:T(8,128)(2,1)S(1)} %get-tuple-element.60.refs_0_, bf16[2,64,256]{2,1,0:T(8,128)(2,1)S(1)} %collective-permute-done.12.refs_1_, bf16[2,64,256]{2,1,0:T(8,128)(2,1)S(1)} %collective-permute-done.13.refs_2_, ...), custom_call_target="tpu_custom_call" | custom-call | tf_op jit(solution)/shard_map/merge/pallas_call | solution.py:389
  63.8 4.2 %collective-permute-start.16 = (bf16[64,2048]{1,0:T(8,128)(2,1)S(1)}, bf16[64,2048]{1,0:T(8,128)(2,1)S(1)}, u32[]{:S(2)}, u32[]{:S(2)}) collective-permute-start(bf16[64,2048]{1,0:T(8,128)(2,1)S(1)} %get-tuple-element.68), channel_id=1, source_target_pairs={{0,4},{4,0},{8,12},{12,8},{16,20},{20,16},{24,28},{28,24},{32,36},... | collective-permute-start | bytes 786440 | tf_op jit(solution)/shard_map/ppermute | solution.py:395
  67.9 1.2 %collective-permute-done.16 = bf16[64,2048]{1,0:T(8,128)(2,1)S(1)} collective-permute-done((bf16[64,2048]{1,0:T(8,128)(2,1)S(1)}, bf16[64,2048]{1,0:T(8,128)(2,1)S(1)}, u32[]{:S(2)}, u32[]{:S(2)}) %collective-permute-start.16) | collective-permute-done | bytes 262176 | tf_op jit(solution)/shard_map/ppermute | solution.py:395
  69.1 0.8 %add_convert_fusion = bf16[64,2048]{1,0:T(8,128)(2,1)} fusion(f32[64,2048]{1,0:T(8,128)S(1)} %get-tuple-element.67, bf16[64,2048]{1,0:T(8,128)(2,1)S(1)} %collective-permute-done.16), kind=kLoop, calls=%fused_computation | loop fusion | flops 393216 | bytes 1048576 | tf_op jit(solution)/shard_map/convert_element_type | solution.py:432
Async XLA Ops:
  0.0 12.2 %copy-start = (f32[3,4,512]{2,1,0:T(4,128)S(1)}, f32[3,4,512]{2,1,0:T(4,128)}, u32[]{:S(2)}) copy-start(f32[3,4,512]{2,1,0:T(4,128)} %conv_ref.1) | copy-start | bytes 73732
  0.0 12.2 %copy-start.2 = (f32[4]{0:T(128)S(1)}, f32[4]{0:T(128)}, u32[]{:S(2)}) copy-start(f32[4]{0:T(128)} %param.11) | copy-start | bytes 52
  0.0 56.7 %copy-start.1 = (f32[512]{0:T(512)S(1)}, f32[512]{0:T(512)}, u32[]{:S(2)}) copy-start(f32[512]{0:T(512)} %param.12) | copy-start | bytes 6148
  4.6 25.8 %collective-permute-start.6 = (bf16[2,128,2048]{2,1,0:T(8,128)(2,1)S(1)}, bf16[2,128,2048]{2,1,0:T(8,128)(2,1)S(1)}, u32[]{:S(2)}, u32[]{:S(2)}) collective-permute-start(bf16[2,128,2048]{2,1,0:T(8,128)(2,1)S(1)} %get-tuple-element.64.refs_4_), channel_id=1, source_target_pairs={{0,1},{1,2},{2,3},{3,0},{4,5},{5,6},{6,7},{7,4},{8,9},{9,10},{10,1... | collective-permute-start | bytes 3145736 | tf_op jit(solution)/shard_map/ppermute | solution.py:400
  6.8 23.6 %collective-permute-start.7 = (bf16[2,128,2048]{2,1,0:T(8,128)(2,1)S(1)}, bf16[2,128,2048]{2,1,0:T(8,128)(2,1)S(1)}, u32[]{:S(2)}, u32[]{:S(2)}) collective-permute-start(bf16[2,128,2048]{2,1,0:T(8,128)(2,1)S(1)} %get-tuple-element.64.refs_4_), channel_id=1, source_target_pairs={{0,3},{1,0},{2,1},{3,2},{4,7},{5,4},{6,5},{7,6},{8,11},{9,8},{10,9... | collective-permute-start | bytes 3145736 | tf_op jit(solution)/shard_map/ppermute | solution.py:400
  8.4 3.8 %collective-permute-start = (bf16[3,16,512]{2,1,0:T(8,128)(2,1)S(1)}, bf16[3,16,512]{2,1,0:T(8,128)(2,1)S(1)}, u32[]{:S(2)}, u32[]{:S(2)}) collective-permute-start(bf16[3,16,512]{2,1,0:T(8,128)(2,1)S(1)} %get-tuple-element.38), channel_id=1, source_target_pairs={{0,4},{4,8},{8,12},{12,16},{16,20},{20,24},{24,28},{28,32},{32,36}... | collective-permute-start | bytes 147464 | tf_op jit(solution)/shard_map/ppermute | solution.py:400
  16.1 7.2 %collective-permute-start.1 = (bf16[2,128,256]{2,1,0:T(8,128)(2,1)S(1)}, bf16[2,128,256]{2,1,0:T(8,128)(2,1)S(1)}, u32[]{:S(2)}, u32[]{:S(2)}) collective-permute-start(bf16[2,128,256]{2,1,0:T(8,128)(2,1)S(1)} %get-tuple-element.41), channel_id=1, source_target_pairs={{0,4},{4,0},{8,12},{12,8},{16,20},{20,16},{24,28},{28,24},{32,36},... | collective-permute-start | bytes 393224 | tf_op jit(solution)/shard_map/ppermute | solution.py:395
  23.6 3.6 %collective-permute-start.2 = (bf16[128,256]{1,0:T(8,128)(2,1)S(1)}, bf16[128,256]{1,0:T(8,128)(2,1)S(1)}, u32[]{:S(2)}, u32[]{:S(2)}) collective-permute-start(bf16[128,256]{1,0:T(8,128)(2,1)S(1)} %get-tuple-element.43), channel_id=1, source_target_pairs={{0,8},{4,12},{8,0},{12,4},{16,24},{20,28},{24,16},{28,20},{32,40},... | collective-permute-start | bytes 196616 | tf_op jit(solution)/shard_map/ppermute | solution.py:395
  23.7 4.4 %collective-permute-start.3 = (bf16[128,256]{1,0:T(8,128)(2,1)S(1)}, bf16[128,256]{1,0:T(8,128)(2,1)S(1)}, u32[]{:S(2)}, u32[]{:S(2)}) collective-permute-start(bf16[128,256]{1,0:T(8,128)(2,1)S(1)} %get-tuple-element.42.own_ref), channel_id=1, source_target_pairs={{0,16},{4,20},{8,24},{12,28},{16,0},{20,4},{24,8},{28,12},{32,48},... | collective-permute-start | bytes 196616 | tf_op jit(solution)/shard_map/ppermute | solution.py:395
  23.8 6.2 %collective-permute-start.4 = (bf16[128,256]{1,0:T(8,128)(2,1)S(1)}, bf16[128,256]{1,0:T(8,128)(2,1)S(1)}, u32[]{:S(2)}, u32[]{:S(2)}) collective-permute-start(bf16[128,256]{1,0:T(8,128)(2,1)S(1)} %get-tuple-element.43), channel_id=1, source_target_pairs={{0,24},{4,28},{8,16},{12,20},{16,8},{20,12},{24,0},{28,4},{32,56},... | collective-permute-start | bytes 196616 | tf_op jit(solution)/shard_map/ppermute | solution.py:395
  30.4 32.6 %collective-permute-start.15 = (bf16[2,128,2048]{2,1,0:T(8,128)(2,1)S(1)}, bf16[2,128,2048]{2,1,0:T(8,128)(2,1)S(1)}, u32[]{:S(2)}, u32[]{:S(2)}) collective-permute-start(bf16[2,128,2048]{2,1,0:T(8,128)(2,1)S(1)} %get-tuple-element.64.refs_4_), channel_id=1, source_target_pairs={{0,2},{1,3},{2,0},{3,1},{4,6},{5,7},{6,4},{7,5},{8,10},{9,11},{10,... | collective-permute-start | bytes 3145736 | tf_op jit(solution)/shard_map/ppermute | solution.py:400
  33.2 8.0 %collective-permute-start.5 = (bf16[128,256]{1,0:T(8,128)(2,1)S(1)}, bf16[128,256]{1,0:T(8,128)(2,1)S(1)}, u32[]{:S(2)}, u32[]{:S(2)}) collective-permute-start(bf16[128,256]{1,0:T(8,128)(2,1)S(1)} %get-tuple-element.44.own_ref), channel_id=1, source_target_pairs={{0,48},{4,52},{8,56},{12,60},{16,32},{20,36},{24,40},{28,44},{32,1... | collective-permute-start | bytes 196616 | tf_op jit(solution)/shard_map/ppermute | solution.py:395
  41.9 14.8 %collective-permute-start.11 = (bf16[2,2,256,128]{3,2,1,0:T(8,128)(2,1)S(1)}, bf16[2,2,256,128]{3,2,1,0:T(8,128)(2,1)S(1)}, u32[]{:S(2)}, u32[]{:S(2)}) collective-permute-start(bf16[2,2,256,128]{3,2,1,0:T(8,128)(2,1)S(1)} %get-tuple-element.59), channel_id=1, source_target_pairs={{0,4},{4,0},{8,12},{12,8},{16,20},{20,16},{24,28},{28,24},{32,36},... | collective-permute-start | bytes 786440 | tf_op jit(solution)/shard_map/ppermute | solution.py:395
  45.0 3.7 %collective-permute-start.8 = (bf16[128,256]{1,0:T(8,128)(2,1)S(1)}, bf16[128,256]{1,0:T(8,128)(2,1)S(1)}, u32[]{:S(2)}, u32[]{:S(2)}) collective-permute-start(bf16[128,256]{1,0:T(8,128)(2,1)S(1)} %get-tuple-element.48.own_ref), channel_id=1, source_target_pairs={{0,64},{4,68},{8,72},{12,76},{16,80},{20,84},{24,88},{28,92},{32,9... | collective-permute-start | bytes 196616 | tf_op jit(solution)/shard_map/ppermute | solution.py:395
  48.8 4.3 %collective-permute-start.9 = (bf16[128,128]{1,0:T(8,128)(2,1)S(1)}, bf16[128,128]{1,0:T(8,128)(2,1)S(1)}, u32[]{:S(2)}, u32[]{:S(2)}) collective-permute-start(bf16[128,128]{1,0:T(8,128)(2,1)S(1)} %rows_state.1), channel_id=1, source_target_pairs={{0,192},{4,196},{8,200},{12,204},{16,208},{20,212},{24,216},{28,22... | collective-permute-start | bytes 98312 | tf_op jit(solution)/shard_map/ppermute | solution.py:395
  53.5 3.1 %collective-permute-start.10 = (bf16[128,128]{1,0:T(8,128)(2,1)S(1)}, bf16[128,128]{1,0:T(8,128)(2,1)S(1)}, u32[]{:S(2)}, u32[]{:S(2)}) collective-permute-start(bf16[128,128]{1,0:T(8,128)(2,1)S(1)} %get-tuple-element.53), channel_id=1, source_target_pairs={{0,8},{4,12},{8,0},{12,4},{16,24},{20,28},{24,16},{28,20},{32,40},... | collective-permute-start | bytes 98312 | tf_op jit(solution)/shard_map/ppermute | solution.py:395
  57.3 4.4 %collective-permute-start.12 = (bf16[2,64,256]{2,1,0:T(8,128)(2,1)S(1)}, bf16[2,64,256]{2,1,0:T(8,128)(2,1)S(1)}, u32[]{:S(2)}, u32[]{:S(2)}) collective-permute-start(bf16[2,64,256]{2,1,0:T(8,128)(2,1)S(1)} %get-tuple-element.61), channel_id=1, source_target_pairs={{0,1},{1,2},{2,3},{3,0},{4,5},{5,6},{6,7},{7,4},{8,9},{9,10},{10,1... | collective-permute-start | bytes 196616 | tf_op jit(solution)/shard_map/ppermute | solution.py:400
  58.0 4.6 %collective-permute-start.13 = (bf16[2,64,256]{2,1,0:T(8,128)(2,1)S(1)}, bf16[2,64,256]{2,1,0:T(8,128)(2,1)S(1)}, u32[]{:S(2)}, u32[]{:S(2)}) collective-permute-start(bf16[2,64,256]{2,1,0:T(8,128)(2,1)S(1)} %get-tuple-element.62), channel_id=1, source_target_pairs={{0,2},{1,3},{2,0},{3,1},{4,6},{5,7},{6,4},{7,5},{8,10},{9,11},{10,... | collective-permute-start | bytes 196616 | tf_op jit(solution)/shard_map/ppermute | solution.py:400
  59.7 3.4 %collective-permute-start.14 = (bf16[2,64,256]{2,1,0:T(8,128)(2,1)S(1)}, bf16[2,64,256]{2,1,0:T(8,128)(2,1)S(1)}, u32[]{:S(2)}, u32[]{:S(2)}) collective-permute-start(bf16[2,64,256]{2,1,0:T(8,128)(2,1)S(1)} %get-tuple-element.63), channel_id=1, source_target_pairs={{0,3},{1,0},{2,1},{3,2},{4,7},{5,4},{6,5},{7,6},{8,11},{9,8},{10,9... | collective-permute-start | bytes 196616 | tf_op jit(solution)/shard_map/ppermute | solution.py:400
  63.8 5.3 %collective-permute-start.16 = (bf16[64,2048]{1,0:T(8,128)(2,1)S(1)}, bf16[64,2048]{1,0:T(8,128)(2,1)S(1)}, u32[]{:S(2)}, u32[]{:S(2)}) collective-permute-start(bf16[64,2048]{1,0:T(8,128)(2,1)S(1)} %get-tuple-element.68), channel_id=1, source_target_pairs={{0,4},{4,0},{8,12},{12,8},{16,20},{20,16},{24,28},{28,24},{32,36},... | collective-permute-start | bytes 786440 | tf_op jit(solution)/shard_map/ppermute | solution.py:395

commit v6 on v5

--- a/solution.py
+++ b/solution.py
@@ -8,7 +8,7 @@
 DK = 128
 BLOCK = 128
 WIDTH = 2 * BLOCK
-EDGE = 16
+EDGE = 8
 EPS = 1e-06
 FAN = 4
 
@@ -24,7 +24,7 @@
     return lax.dot_general(a, b, (((1,), (1,)), ((), ())), preferred_element_type=f32)
 
 
-def params(megabytes=48):
+def params(megabytes=24):
     return pltpu.CompilerParams(vmem_limit_bytes=megabytes << 20)
 
 
@@ -37,10 +37,9 @@
 
 
 def project_kernel(
-    tokens_hbm, w_hbm, beta_w_hbm, w_out_hbm, out_ref, edge_ref, logits_ref, w_own_ref,
-    tokens_ref, w_ref, beta_w_ref, small_sems, w_sems
+    tokens_hbm, w_hbm, beta_w_hbm, w_out_hbm, out_ref, w_ref, logits_ref, w_own_ref,
+    tokens_ref, beta_w_ref, small_sems, w_sems
 ):
-    length = tokens_ref.shape[0]
     first = pltpu.make_async_copy(tokens_hbm, tokens_ref, small_sems.at[0])
     last = pltpu.make_async_copy(beta_w_hbm, beta_w_ref, small_sems.at[1])
     copies = [pltpu.make_async_copy(w_hbm.at[s], w_ref.at[s], w_sems.at[s]) for s in range(3)]
@@ -66,9 +65,7 @@
         if s == 1:
             rows[0].start()
             rows[1].start()
-        result = dot(tokens_ref[...], w_ref[s]).astype(bf16)
-        out_ref[s] = result
-        edge_ref[s] = result[length - EDGE :]
+        out_ref[s] = dot(tokens_ref[...], w_ref[s]).astype(bf16)
     rows[0].wait()
     rows[1].wait()
 
@@ -86,13 +83,12 @@
         out_specs=whole(4),
         out_shape=[
             shape((3, length, columns), bf16),
-            shape((3, EDGE, columns), bf16),
+            shape(w_qkv.shape, bf16),
             shape((length, heads), f32),
             shape((2, DK, w_out.shape[1]), bf16),
         ],
         scratch_shapes=[
             pltpu.VMEM(tokens.shape, bf16),
-            pltpu.VMEM(w_qkv.shape, bf16),
             pltpu.VMEM(beta_weight.shape, bf16),
             pltpu.SemaphoreType.DMA((4,)),
             pltpu.SemaphoreType.DMA((3,)),
@@ -148,7 +144,7 @@
 
 
 def local_kernel(
-    proj_ref, edge_ref, conv_ref, logits_ref, bias_ref,
+    proj_ref, w_ref, edge_ref, conv_ref, logits_ref, bias_ref,
     queries_ref, keys_t_ref, uw_ref, keep_ref, send_ref, padded, maps
 ):
     length = proj_ref.shape[1]
@@ -157,7 +153,7 @@
     core = lax.axis_index("ctx") % 2
     first = lax.axis_index("ctx") == 0
     for s in range(3):
-        edge = edge_ref[s].astype(f32)
+        edge = dot(edge_ref[...], w_ref[s]).astype(bf16).astype(f32)
         padded[s, :EDGE] = jnp.where(first, jnp.zeros_like(edge), edge)
         padded[s, EDGE:] = proj_ref[s].astype(f32)
     row, column = grid_index(length, length)
@@ -203,13 +199,13 @@
         send_ref[j] = maps[2 * j + 1 - core]
 
 
-def local_maps(projected, edge, conv_weight, logits, beta_bias):
+def local_maps(projected, weights, edge, conv_weight, logits, beta_bias):
     length, columns = projected.shape[1:]
     heads = logits.shape[1]
     two = shape((heads // 2, DK, 2 * DK), bf16)
     return pl.pallas_call(
         local_kernel,
-        in_specs=whole(5),
+        in_specs=whole(6),
         out_specs=whole(5),
         out_shape=[
             shape((heads, length, DK), bf16),
@@ -223,7 +219,7 @@
         ],
         compiler_params=params(),
         name="local_maps",
-    )(projected, edge, conv_weight, logits, beta_bias[None, :])
+    )(projected, weights, edge, conv_weight, logits, beta_bias[None, :])
 
 
 def inner_kernel(queries_ref, keys_t_ref, uw_ref, base_ref, gate_ref, both_out):
@@ -373,13 +369,16 @@
     )(*states, *maps, *inner, inner_in, norm_gain.reshape(4, 1, DK))
 
 
-def merge_kernel(*refs):
-    parts, weights, (keep_ref, send_ref) = refs[:4], refs[4:8], refs[8:]
-    _, rows, width = parts[0].shape
+def merge_kernel(
+    mine_ref, one, two, three, w_own, w_one, w_two0, w_two1, w_three, keep_ref, send_ref
+):
+    _, rows, width = mine_ref.shape
     total = None
-    for ref, weight in zip(parts, weights):
+    for ref, weight in ((mine_ref, w_own), (one, w_one), (three, w_three)):
         term = dot(ref[...].reshape(2 * rows, width), weight[...].reshape(width, -1))
         total = term if total is None else total + term
+    both = jnp.concatenate([w_two0[...], w_two1[...]], axis=0)
+    total = total + dot(two[...].reshape(2 * rows, width), both)
     keep_ref[...] = total[:rows]
     send_ref[...] = total[rows:].astype(bf16)
 
@@ -401,24 +400,26 @@
 
 
 def per_device(tokens_in, w_qkv, conv_weight, beta_weight, beta_bias, norm_gain, w_out):
-    projected, edge, logits, w_own = project(tokens_in, w_qkv, beta_weight, w_out)
-    edge = turned(edge, "ctx", 1)
+    edge = turned(tokens_in[-EDGE:], "ctx", 1)
+    projected, weights, logits, w_own = project(tokens_in, w_qkv, beta_weight, w_out)
+    queries, keys_t, uw, maps, send = local_maps(
+        projected, weights, edge, conv_weight, logits, beta_bias
+    )
+    send, w_own = lax.optimization_barrier((send, w_own))
     w_one, w_three = turned(w_own, "head", 1), turned(w_own, "head", 3)
-    queries, keys_t, uw, maps, send = local_maps(projected, edge, conv_weight, logits, beta_bias)
     sibling = swapped(send, 1)
     chip, send = small_call(
         chip_kernel, [MAP, MAP], "chip_map", [pltpu.VMEM((2, DK, 2 * DK), bf16)]
     )(maps, sibling)
     pair, across, diagonal = swapped(send, 2), swapped(chip, 4), swapped(send, 6)
     four, near = small_call(four_kernel, [MAP, MAP], "four_map")(chip, pair, across, diagonal)
-    near, w_own, w_one, w_three = lax.optimization_barrier((near, w_own, w_one, w_three))
-    w_two = turned(w_own, "head", 2)
     row, before = small_call(far_kernel, [MAP, MAP], "far_map")(four, swapped(four, 12), near)
     other_row = swapped(row, 16)
-    before, queries = lax.optimization_barrier((before, queries))
     base, gate, both = inner_outputs(queries, keys_t, uw)
     inner_in = swapped(both, 1)
     (two_rows,) = small_call(rows_kernel, [STATE], "rows_state")(row, other_row)
+    two_rows, w_one, w_three = lax.optimization_barrier((two_rows, w_one, w_three))
+    w_two = turned(w_one[0], "head", 1), turned(w_three[1], "head", 3)
     rows = swapped(two_rows, 48)
     state, send = small_call(pair_start_kernel, [STATE, STATE], "pair_start")(
         rows, other_row, before, chip, pair
@@ -428,7 +429,7 @@
         (state, back), (maps, sibling), (base, gate), inner_in, norm_gain
     )
     one, three, two = turned(one, "head", 1), turned(three, "head", 3), turned(two, "head", 2)
-    keep, send = merge([mine, one, two, three], [w_own, w_one, w_two, w_three])
+    keep, send = merge([mine, one, two, three], [w_own, w_one, *w_two, w_three])
     return (keep + swapped(send, 1).astype(f32)).astype(bf16)
 
 

time: 69.9 us -> 67.9 us (0.971)
  starting transfers between devices: 40.5 us -> 31.5 us
  waiting for transfers between devices: 16.6 us -> 22.1 us
  local copies, waits for them, and re-layouts: 0.01 us -> 0.87 us
    ppermute x10, starting transfers between devices: 28.3 us -> 19.2 us  [swapped(): lax.ppermute(x, 'ctx', [(i, i ^ by) for i in range(lax.axis_size('ctx'))])]
    ppermute x10, waiting for transfers between devices: 12.8 us -> 18.2 us  [swapped(): lax.ppermute(x, 'ctx', [(i, i ^ by) for i in range(lax.axis_size('ctx'))])]
    slice x0 -> x1, local copies, waits for them, and re-layouts: none -> 0.78 us  [per_device(): edge = turned(tokens_in[-EDGE:], 'ctx', 1)]
    ppermute x7 -> x8, waiting for transfers between devices: 3.75 us -> 3.91 us  [turned(): return lax.ppermute(x, axis, [(i, (i + by) % count) for i in range(count)])]
    ppermute x7 -> x8, starting transfers between devices: 12.2 us -> 12.2 us  [turned(): return lax.ppermute(x, axis, [(i, (i + by) % count) for i in range(count)])]
  transfers between devices with their start and end apart: 17 -> 18, of which waited for: 12 -> 12; matrix products, arithmetic and copies ran while one was open for 0% -> 0% of each run, Pallas kernels for 9% -> 11%
where the time goes in v6:
time: 67.9 us; the launch traced here: 67.8 us
  starting transfers between devices  31.5 us (46%)
  waiting for transfers between devices  22.1 us (33%)
  Pallas kernels  12.4 us (18%)
  local copies, waits for them, and re-layouts  0.87 us (1%)
  other arithmetic  0.76 us (1%)
    ppermute x10, starting transfers between devices, swapped(): lax.ppermute(x, 'ctx', [(i, i ^ by) for i in range(lax.axis_size('ctx'))])  19.2 us
    ppermute x10, waiting for transfers between devices, swapped(): lax.ppermute(x, 'ctx', [(i, i ^ by) for i in range(lax.axis_size('ctx'))])  18.2 us
    ppermute x8, starting transfers between devices, turned(): return lax.ppermute(x, axis, [(i, (i + by) % count) for i in range(count)])  12.2 us
    pallas_call x1, Pallas kernels, project(): pl.pallas_call(project_kernel, in_specs=[pl.BlockSpec(memory_space=pltpu....  4.62 us
    pallas_call x1, Pallas kernels, local_maps(): pl.pallas_call(local_kernel, in_specs=whole(6), out_specs=whole(5), out_s...  4.53 us
    ppermute x8, waiting for transfers between devices, turned(): return lax.ppermute(x, axis, [(i, (i + by) % count) for i in range(count)])  3.91 us
  transfers between devices with their start and end apart: 18, of which 12 were waited for; matrix products, arithmetic and copies ran while one was open for 0% of the time, Pallas kernels for 11%

profile of v6, /device:TPU:1, one launch (start us, length us, event | category | flops | bytes accessed | tf_op | source)
XLA Modules:
  0.0 67.8 jit_solution(12132471276132276471)
XLA Ops:
  0.0 0.0 copy-start.2
  0.0 0.0 copy-start
  0.0 0.8 %slice.9 = bf16[8,2048]{1,0:T(8,128)(2,1)S(1)} slice(bf16[256,2048]{1,0:T(8,128)(2,1)} %tokens_hbm.1), slice={[248:256], [0:2048]} | slice | bytes 65536 | tf_op jit(solution)/shard_map/slice | solution.py:403
  0.8 3.0 %collective-permute-start = (bf16[8,2048]{1,0:T(8,128)(2,1)S(1)}, bf16[8,2048]{1,0:T(8,128)(2,1)S(1)}, u32[]{:S(2)}, u32[]{:S(2)}) collective-permute-start(bf16[8,2048]{1,0:T(8,128)(2,1)S(1)} %slice.9), channel_id=1, source_target_pairs={{0,4},{4,8},{8,12},{12,16},{16,20},{20,24},{24,28},{28,32},{32,36}... | collective-permute-start | bytes 98312 | tf_op jit(solution)/shard_map/ppermute | solution.py:399
  3.8 4.6 %project.1 = (bf16[3,256,512]{2,1,0:T(8,128)(2,1)S(1)}, bf16[3,2048,512]{2,1,0:T(8,128)(2,1)S(1)}, f32[256,4]{1,0:T(8,128)S(1)}, bf16[2,128,2048]{2,1,0:T(8,128)(2,1)S(1)}) custom-call(bf16[256,2048]{1,0:T(8,128)(2,1)} %tokens_hbm.1, bf16[3,2048,512]{2,1,0:T(8,128)(2,1)} %w_hbm.1, bf16[4,2048]{1,0:T(4,128)(2,1)} %beta_w_hbm.1, bf16[512,2048]{1,0:T(8,128)(2,1)} %w_out_hbm.1), custom_call_target="tpu_custom_call" | custom-call | tf_op jit(solution)/shard_map/project/pallas_call | solution.py:80
  8.4 0.0 copy-start.1
  8.4 0.0 collective-permute-done.edge_ref
  8.5 0.0 copy-done.2
  8.5 0.0 copy-done
  8.5 4.5 %local_maps.1 = (bf16[4,256,128]{2,1,0:T(8,128)(2,1)S(1)}, bf16[4,128,256]{2,1,0:T(8,128)(2,1)S(1)}, bf16[4,256,256]{2,1,0:T(8,128)(2,1)S(1)}, bf16[2,128,256]{2,1,0:T(8,128)(2,1)S(1)}, bf16[2,128,256]{2,1,0:T(8,128)(2,1)S(1)}) custom-call(bf16[3,256,512]{2,1,0:T(8,128)(2,1)S(1)} %get-tuple-element.36.proj_ref, ...), custom_call_target="tpu_custom_call" | custom-call | tf_op jit(solution)/shard_map/local_maps/pallas_call | solution.py:206
  13.0 2.8 %collective-permute-start.8 = (bf16[2,128,2048]{2,1,0:T(8,128)(2,1)S(1)}, bf16[2,128,2048]{2,1,0:T(8,128)(2,1)S(1)}, u32[]{:S(2)}, u32[]{:S(2)}) collective-permute-start(bf16[2,128,2048]{2,1,0:T(8,128)(2,1)S(1)} %get-tuple-element.48.w_own), channel_id=1, source_target_pairs={{0,3},{1,0},{2,1},{3,2},{4,7},{5,4},{6,5},{7,6},{8,11},{9,8},{10,9... | collective-permute-start | bytes 3145736 | tf_op jit(solution)/shard_map/ppermute | solution.py:399
  15.8 0.0 collective-permute-start.7
  15.8 3.2 %collective-permute-start.1 = (bf16[2,128,256]{2,1,0:T(8,128)(2,1)S(1)}, bf16[2,128,256]{2,1,0:T(8,128)(2,1)S(1)}, u32[]{:S(2)}, u32[]{:S(2)}) collective-permute-start(bf16[2,128,256]{2,1,0:T(8,128)(2,1)S(1)} %get-tuple-element.42), channel_id=1, source_target_pairs={{0,4},{4,0},{8,12},{12,8},{16,20},{20,16},{24,28},{28,24},{32,36},... | collective-permute-start | bytes 393224 | tf_op jit(solution)/shard_map/ppermute | solution.py:394
  19.0 1.0 %collective-permute-done.1.other_ref.other_maps = bf16[2,128,256]{2,1,0:T(8,128)(2,1)S(1)} collective-permute-done((bf16[2,128,256]{2,1,0:T(8,128)(2,1)S(1)}, bf16[2,128,256]{2,1,0:T(8,128)(2,1)S(1)}, u32[]{:S(2)}, u32[]{:S(2)}) %collective-permute-start.1) | collective-permute-done | bytes 131104 | tf_op jit(solution)/shard_map/ppermute | solution.py:394
  20.0 0.2 chip_map.1
  20.2 2.8 %collective-permute-start.4 = (bf16[128,256]{1,0:T(8,128)(2,1)S(1)}, bf16[128,256]{1,0:T(8,128)(2,1)S(1)}, u32[]{:S(2)}, u32[]{:S(2)}) collective-permute-start(bf16[128,256]{1,0:T(8,128)(2,1)S(1)} %get-tuple-element.44), channel_id=1, source_target_pairs={{0,24},{4,28},{8,16},{12,20},{16,8},{20,12},{24,0},{28,4},{32,56},... | collective-permute-start | bytes 196616 | tf_op jit(solution)/shard_map/ppermute | solution.py:394
  23.1 0.0 collective-permute-start.2
  23.1 0.8 %collective-permute-start.3 = (bf16[128,256]{1,0:T(8,128)(2,1)S(1)}, bf16[128,256]{1,0:T(8,128)(2,1)S(1)}, u32[]{:S(2)}, u32[]{:S(2)}) collective-permute-start(bf16[128,256]{1,0:T(8,128)(2,1)S(1)} %get-tuple-element.43.own_ref), channel_id=1, source_target_pairs={{0,16},{4,20},{8,24},{12,28},{16,0},{20,4},{24,8},{28,12},{32,48},... | collective-permute-start | bytes 196616 | tf_op jit(solution)/shard_map/ppermute | solution.py:394
  23.9 1.4 %collective-permute-done.4.diagonal_ref = bf16[128,256]{1,0:T(8,128)(2,1)S(1)} collective-permute-done((bf16[128,256]{1,0:T(8,128)(2,1)S(1)}, bf16[128,256]{1,0:T(8,128)(2,1)S(1)}, u32[]{:S(2)}, u32[]{:S(2)}) %collective-permute-start.4) | collective-permute-done | bytes 65568 | tf_op jit(solution)/shard_map/ppermute | solution.py:394
  25.2 3.2 %collective-permute-done.2.pair_ref.other_ref = bf16[128,256]{1,0:T(8,128)(2,1)S(1)} collective-permute-done((bf16[128,256]{1,0:T(8,128)(2,1)S(1)}, bf16[128,256]{1,0:T(8,128)(2,1)S(1)}, u32[]{:S(2)}, u32[]{:S(2)}) %collective-permute-start.2) | collective-permute-done | bytes 65568 | tf_op jit(solution)/shard_map/ppermute | solution.py:394
  28.4 0.0 collective-permute-done.3.across_ref
  28.4 0.4 four_map.1
  28.8 1.1 %collective-permute-start.5 = (bf16[128,256]{1,0:T(8,128)(2,1)S(1)}, bf16[128,256]{1,0:T(8,128)(2,1)S(1)}, u32[]{:S(2)}, u32[]{:S(2)}) collective-permute-start(bf16[128,256]{1,0:T(8,128)(2,1)S(1)} %get-tuple-element.45.own_ref), channel_id=1, source_target_pairs={{0,48},{4,52},{8,56},{12,60},{16,32},{20,36},{24,40},{28,44},{32,1... | collective-permute-start | bytes 196616 | tf_op jit(solution)/shard_map/ppermute | solution.py:394
  30.0 4.2 %collective-permute-done.5.other_ref = bf16[128,256]{1,0:T(8,128)(2,1)S(1)} collective-permute-done((bf16[128,256]{1,0:T(8,128)(2,1)S(1)}, bf16[128,256]{1,0:T(8,128)(2,1)S(1)}, u32[]{:S(2)}, u32[]{:S(2)}) %collective-permute-start.5) | collective-permute-done | bytes 65568 | tf_op jit(solution)/shard_map/ppermute | solution.py:394
  34.1 0.2 far_map.1
  34.3 0.3 collective-permute-start.6
  34.6 3.2 %collective-permute-done.6.other_ref.row_ref = bf16[128,256]{1,0:T(8,128)(2,1)S(1)} collective-permute-done((bf16[128,256]{1,0:T(8,128)(2,1)S(1)}, bf16[128,256]{1,0:T(8,128)(2,1)S(1)}, u32[]{:S(2)}, u32[]{:S(2)}) %collective-permute-start.6) | collective-permute-done | bytes 65568 | tf_op jit(solution)/shard_map/ppermute | solution.py:394
  37.8 0.1 rows_state.1
  38.0 0.0 collective-permute-done.8.w_three
  38.0 0.6 collective-permute-done.7.w_one
  38.6 2.4 %collective-permute-start.16 = (bf16[128,2048]{1,0:T(8,128)(2,1)S(1)}, bf16[128,2048]{1,0:T(8,128)(2,1)S(1)}, u32[]{:S(2)}, u32[]{:S(2)}) collective-permute-start(bf16[128,2048]{1,0:T(8,128)(2,1)S(1)} %slice_bitcast_fusion), channel_id=1, source_target_pairs={{0,3},{1,0},{2,1},{3,2},{4,7},{5,4},{6,5},{7,6},{8,11},{9,8},{10,9... | collective-permute-start | bytes 1572872 | tf_op jit(solution)/shard_map/ppermute | solution.py:399
  41.1 0.0 collective-permute-start.15
  41.1 0.5 inner_outputs.1
  41.6 4.1 %collective-permute-start.11 = (bf16[2,2,256,128]{3,2,1,0:T(8,128)(2,1)S(1)}, bf16[2,2,256,128]{3,2,1,0:T(8,128)(2,1)S(1)}, u32[]{:S(2)}, u32[]{:S(2)}) collective-permute-start(bf16[2,2,256,128]{3,2,1,0:T(8,128)(2,1)S(1)} %get-tuple-element.58), channel_id=1, source_target_pairs={{0,4},{4,0},{8,12},{12,8},{16,20},{20,16},{24,28},{28,24},{32,36},... | collective-permute-start | bytes 786440 | tf_op jit(solution)/shard_map/ppermute | solution.py:394
  45.7 2.4 %collective-permute-start.9 = (bf16[128,128]{1,0:T(8,128)(2,1)S(1)}, bf16[128,128]{1,0:T(8,128)(2,1)S(1)}, u32[]{:S(2)}, u32[]{:S(2)}) collective-permute-start(bf16[128,128]{1,0:T(8,128)(2,1)S(1)} %rows_state.1), channel_id=1, source_target_pairs={{0,192},{4,196},{8,200},{12,204},{16,208},{20,212},{24,216},{28,22... | collective-permute-start | bytes 98312 | tf_op jit(solution)/shard_map/ppermute | solution.py:394
  48.1 1.8 %collective-permute-done.9.rows_ref = bf16[128,128]{1,0:T(8,128)(2,1)S(1)} collective-permute-done((bf16[128,128]{1,0:T(8,128)(2,1)S(1)}, bf16[128,128]{1,0:T(8,128)(2,1)S(1)}, u32[]{:S(2)}, u32[]{:S(2)}) %collective-permute-start.9) | collective-permute-done | bytes 32800 | tf_op jit(solution)/shard_map/ppermute | solution.py:394
  50.0 0.4 pair_start.1
  50.4 0.9 %collective-permute-start.10 = (bf16[128,128]{1,0:T(8,128)(2,1)S(1)}, bf16[128,128]{1,0:T(8,128)(2,1)S(1)}, u32[]{:S(2)}, u32[]{:S(2)}) collective-permute-start(bf16[128,128]{1,0:T(8,128)(2,1)S(1)} %get-tuple-element.52), channel_id=1, source_target_pairs={{0,8},{4,12},{8,0},{12,4},{16,24},{20,28},{24,16},{28,20},{32,40},... | collective-permute-start | bytes 98312 | tf_op jit(solution)/shard_map/ppermute | solution.py:394
  51.2 0.0 collective-permute-done.11.both_in
  51.2 2.3 %collective-permute-done.10.other_state = bf16[128,128]{1,0:T(8,128)(2,1)S(1)} collective-permute-done((bf16[128,128]{1,0:T(8,128)(2,1)S(1)}, bf16[128,128]{1,0:T(8,128)(2,1)S(1)}, u32[]{:S(2)}, u32[]{:S(2)}) %collective-permute-start.10) | collective-permute-done | bytes 32800 | tf_op jit(solution)/shard_map/ppermute | solution.py:394
  53.5 0.0 copy-done.1
  53.5 0.6 finish.1
  54.2 0.1 collective-permute-start.12
  54.3 3.9 %collective-permute-start.13 = (bf16[2,64,256]{2,1,0:T(8,128)(2,1)S(1)}, bf16[2,64,256]{2,1,0:T(8,128)(2,1)S(1)}, u32[]{:S(2)}, u32[]{:S(2)}) collective-permute-start(bf16[2,64,256]{2,1,0:T(8,128)(2,1)S(1)} %get-tuple-element.61), channel_id=1, source_target_pairs={{0,2},{1,3},{2,0},{3,1},{4,6},{5,7},{6,4},{7,5},{8,10},{9,11},{10,... | collective-permute-start | bytes 196616 | tf_op jit(solution)/shard_map/ppermute | solution.py:399
  58.1 0.0 collective-permute-start.14
  58.1 0.5 collective-permute-done.12.one
  58.6 1.9 %collective-permute-done.13.two = bf16[2,64,256]{2,1,0:T(8,128)(2,1)S(1)} collective-permute-done((bf16[2,64,256]{2,1,0:T(8,128)(2,1)S(1)}, bf16[2,64,256]{2,1,0:T(8,128)(2,1)S(1)}, u32[]{:S(2)}, u32[]{:S(2)}) %collective-permute-start.13) | collective-permute-done | bytes 65568 | tf_op jit(solution)/shard_map/ppermute | solution.py:399
  60.5 1.0 %collective-permute-done.14.three = bf16[2,64,256]{2,1,0:T(8,128)(2,1)S(1)} collective-permute-done((bf16[2,64,256]{2,1,0:T(8,128)(2,1)S(1)}, bf16[2,64,256]{2,1,0:T(8,128)(2,1)S(1)}, u32[]{:S(2)}, u32[]{:S(2)}) %collective-permute-start.14) | collective-permute-done | bytes 65568 | tf_op jit(solution)/shard_map/ppermute | solution.py:399
  61.5 0.0 collective-permute-done.16.w_two1
  61.5 0.0 collective-permute-done.15.w_two0
  61.5 0.7 %merge.1 = (f32[64,2048]{1,0:T(8,128)S(1)}, bf16[64,2048]{1,0:T(8,128)(2,1)S(1)}) custom-call(bf16[2,64,256]{2,1,0:T(8,128)(2,1)S(1)} %get-tuple-element.59.mine_ref, bf16[2,64,256]{2,1,0:T(8,128)(2,1)S(1)} %collective-permute-done.12.one, bf16[2,64,256]{2,1,0:T(8,128)(2,1)S(1)} %collective-permute-done.13.two, ...), custom_call_target="tpu_custom_call" | custom-call | tf_op jit(solution)/shard_map/merge/pallas_call | solution.py:388
  62.2 3.6 %collective-permute-start.17 = (bf16[64,2048]{1,0:T(8,128)(2,1)S(1)}, bf16[64,2048]{1,0:T(8,128)(2,1)S(1)}, u32[]{:S(2)}, u32[]{:S(2)}) collective-permute-start(bf16[64,2048]{1,0:T(8,128)(2,1)S(1)} %get-tuple-element.66), channel_id=1, source_target_pairs={{0,4},{4,0},{8,12},{12,8},{16,20},{20,16},{24,28},{28,24},{32,36},... | collective-permute-start | bytes 786440 | tf_op jit(solution)/shard_map/ppermute | solution.py:394
  65.9 1.2 %collective-permute-done.17 = bf16[64,2048]{1,0:T(8,128)(2,1)S(1)} collective-permute-done((bf16[64,2048]{1,0:T(8,128)(2,1)S(1)}, bf16[64,2048]{1,0:T(8,128)(2,1)S(1)}, u32[]{:S(2)}, u32[]{:S(2)}) %collective-permute-start.17) | collective-permute-done | bytes 262176 | tf_op jit(solution)/shard_map/ppermute | solution.py:394
  67.0 0.8 %add_convert_fusion = bf16[64,2048]{1,0:T(8,128)(2,1)} fusion(f32[64,2048]{1,0:T(8,128)S(1)} %get-tuple-element.65, bf16[64,2048]{1,0:T(8,128)(2,1)S(1)} %collective-permute-done.17), kind=kLoop, calls=%fused_computation | loop fusion | flops 393216 | bytes 1048576 | tf_op jit(solution)/shard_map/convert_element_type | solution.py:433
  (2 shorter events, 0.1 us)
Async XLA Ops:
  0.0 8.5 %copy-start.2 = (f32[4]{0:T(128)S(1)}, f32[4]{0:T(128)}, u32[]{:S(2)}) copy-start(f32[4]{0:T(128)} %param.11) | copy-start | bytes 52
  0.0 8.5 %copy-start = (f32[3,4,512]{2,1,0:T(4,128)S(1)}, f32[3,4,512]{2,1,0:T(4,128)}, u32[]{:S(2)}) copy-start(f32[3,4,512]{2,1,0:T(4,128)} %conv_ref.1) | copy-start | bytes 73732
  0.8 7.7 %collective-permute-start = (bf16[8,2048]{1,0:T(8,128)(2,1)S(1)}, bf16[8,2048]{1,0:T(8,128)(2,1)S(1)}, u32[]{:S(2)}, u32[]{:S(2)}) collective-permute-start(bf16[8,2048]{1,0:T(8,128)(2,1)S(1)} %slice.9), channel_id=1, source_target_pairs={{0,4},{4,8},{8,12},{12,16},{16,20},{20,24},{24,28},{28,32},{32,36}... | collective-permute-start | bytes 98312 | tf_op jit(solution)/shard_map/ppermute | solution.py:399
  8.4 45.1 %copy-start.1 = (f32[512]{0:T(512)S(1)}, f32[512]{0:T(512)}, u32[]{:S(2)}) copy-start(f32[512]{0:T(512)} %param.12) | copy-start | bytes 6148
  13.0 24.9 %collective-permute-start.8 = (bf16[2,128,2048]{2,1,0:T(8,128)(2,1)S(1)}, bf16[2,128,2048]{2,1,0:T(8,128)(2,1)S(1)}, u32[]{:S(2)}, u32[]{:S(2)}) collective-permute-start(bf16[2,128,2048]{2,1,0:T(8,128)(2,1)S(1)} %get-tuple-element.48.w_own), channel_id=1, source_target_pairs={{0,3},{1,0},{2,1},{3,2},{4,7},{5,4},{6,5},{7,6},{8,11},{9,8},{10,9... | collective-permute-start | bytes 3145736 | tf_op jit(solution)/shard_map/ppermute | solution.py:399
  15.8 22.7 %collective-permute-start.7 = (bf16[2,128,2048]{2,1,0:T(8,128)(2,1)S(1)}, bf16[2,128,2048]{2,1,0:T(8,128)(2,1)S(1)}, u32[]{:S(2)}, u32[]{:S(2)}) collective-permute-start(bf16[2,128,2048]{2,1,0:T(8,128)(2,1)S(1)} %get-tuple-element.48.w_own), channel_id=1, source_target_pairs={{0,1},{1,2},{2,3},{3,0},{4,5},{5,6},{6,7},{7,4},{8,9},{9,10},{10,1... | collective-permute-start | bytes 3145736 | tf_op jit(solution)/shard_map/ppermute | solution.py:399
  15.8 4.2 %collective-permute-start.1 = (bf16[2,128,256]{2,1,0:T(8,128)(2,1)S(1)}, bf16[2,128,256]{2,1,0:T(8,128)(2,1)S(1)}, u32[]{:S(2)}, u32[]{:S(2)}) collective-permute-start(bf16[2,128,256]{2,1,0:T(8,128)(2,1)S(1)} %get-tuple-element.42), channel_id=1, source_target_pairs={{0,4},{4,0},{8,12},{12,8},{16,20},{20,16},{24,28},{28,24},{32,36},... | collective-permute-start | bytes 393224 | tf_op jit(solution)/shard_map/ppermute | solution.py:394
  20.2 5.0 %collective-permute-start.4 = (bf16[128,256]{1,0:T(8,128)(2,1)S(1)}, bf16[128,256]{1,0:T(8,128)(2,1)S(1)}, u32[]{:S(2)}, u32[]{:S(2)}) collective-permute-start(bf16[128,256]{1,0:T(8,128)(2,1)S(1)} %get-tuple-element.44), channel_id=1, source_target_pairs={{0,24},{4,28},{8,16},{12,20},{16,8},{20,12},{24,0},{28,4},{32,56},... | collective-permute-start | bytes 196616 | tf_op jit(solution)/shard_map/ppermute | solution.py:394
  23.1 5.4 %collective-permute-start.2 = (bf16[128,256]{1,0:T(8,128)(2,1)S(1)}, bf16[128,256]{1,0:T(8,128)(2,1)S(1)}, u32[]{:S(2)}, u32[]{:S(2)}) collective-permute-start(bf16[128,256]{1,0:T(8,128)(2,1)S(1)} %get-tuple-element.44), channel_id=1, source_target_pairs={{0,8},{4,12},{8,0},{12,4},{16,24},{20,28},{24,16},{28,20},{32,40},... | collective-permute-start | bytes 196616 | tf_op jit(solution)/shard_map/ppermute | solution.py:394
  23.1 5.4 %collective-permute-start.3 = (bf16[128,256]{1,0:T(8,128)(2,1)S(1)}, bf16[128,256]{1,0:T(8,128)(2,1)S(1)}, u32[]{:S(2)}, u32[]{:S(2)}) collective-permute-start(bf16[128,256]{1,0:T(8,128)(2,1)S(1)} %get-tuple-element.43.own_ref), channel_id=1, source_target_pairs={{0,16},{4,20},{8,24},{12,28},{16,0},{20,4},{24,8},{28,12},{32,48},... | collective-permute-start | bytes 196616 | tf_op jit(solution)/shard_map/ppermute | solution.py:394
  28.8 5.3 %collective-permute-start.5 = (bf16[128,256]{1,0:T(8,128)(2,1)S(1)}, bf16[128,256]{1,0:T(8,128)(2,1)S(1)}, u32[]{:S(2)}, u32[]{:S(2)}) collective-permute-start(bf16[128,256]{1,0:T(8,128)(2,1)S(1)} %get-tuple-element.45.own_ref), channel_id=1, source_target_pairs={{0,48},{4,52},{8,56},{12,60},{16,32},{20,36},{24,40},{28,44},{32,1... | collective-permute-start | bytes 196616 | tf_op jit(solution)/shard_map/ppermute | solution.py:394
  34.3 3.5 %collective-permute-start.6 = (bf16[128,256]{1,0:T(8,128)(2,1)S(1)}, bf16[128,256]{1,0:T(8,128)(2,1)S(1)}, u32[]{:S(2)}, u32[]{:S(2)}) collective-permute-start(bf16[128,256]{1,0:T(8,128)(2,1)S(1)} %get-tuple-element.47.own_ref), channel_id=1, source_target_pairs={{0,64},{4,68},{8,72},{12,76},{16,80},{20,84},{24,88},{28,92},{32,9... | collective-permute-start | bytes 196616 | tf_op jit(solution)/shard_map/ppermute | solution.py:394
  38.6 22.9 %collective-permute-start.16 = (bf16[128,2048]{1,0:T(8,128)(2,1)S(1)}, bf16[128,2048]{1,0:T(8,128)(2,1)S(1)}, u32[]{:S(2)}, u32[]{:S(2)}) collective-permute-start(bf16[128,2048]{1,0:T(8,128)(2,1)S(1)} %slice_bitcast_fusion), channel_id=1, source_target_pairs={{0,3},{1,0},{2,1},{3,2},{4,7},{5,4},{6,5},{7,6},{8,11},{9,8},{10,9... | collective-permute-start | bytes 1572872 | tf_op jit(solution)/shard_map/ppermute | solution.py:399
  41.1 20.4 %collective-permute-start.15 = (bf16[128,2048]{1,0:T(8,128)(2,1)S(1)}, bf16[128,2048]{1,0:T(8,128)(2,1)S(1)}, u32[]{:S(2)}, u32[]{:S(2)}) collective-permute-start(bf16[128,2048]{1,0:T(8,128)(2,1)S(1)} %slice_bitcast_fusion.1), channel_id=1, source_target_pairs={{0,1},{1,2},{2,3},{3,0},{4,5},{5,6},{6,7},{7,4},{8,9},{9,10},{10,1... | collective-permute-start | bytes 1572872 | tf_op jit(solution)/shard_map/ppermute | solution.py:399
  41.6 9.6 %collective-permute-start.11 = (bf16[2,2,256,128]{3,2,1,0:T(8,128)(2,1)S(1)}, bf16[2,2,256,128]{3,2,1,0:T(8,128)(2,1)S(1)}, u32[]{:S(2)}, u32[]{:S(2)}) collective-permute-start(bf16[2,2,256,128]{3,2,1,0:T(8,128)(2,1)S(1)} %get-tuple-element.58), channel_id=1, source_target_pairs={{0,4},{4,0},{8,12},{12,8},{16,20},{20,16},{24,28},{28,24},{32,36},... | collective-permute-start | bytes 786440 | tf_op jit(solution)/shard_map/ppermute | solution.py:394
  45.7 4.3 %collective-permute-start.9 = (bf16[128,128]{1,0:T(8,128)(2,1)S(1)}, bf16[128,128]{1,0:T(8,128)(2,1)S(1)}, u32[]{:S(2)}, u32[]{:S(2)}) collective-permute-start(bf16[128,128]{1,0:T(8,128)(2,1)S(1)} %rows_state.1), channel_id=1, source_target_pairs={{0,192},{4,196},{8,200},{12,204},{16,208},{20,212},{24,216},{28,22... | collective-permute-start | bytes 98312 | tf_op jit(solution)/shard_map/ppermute | solution.py:394
  50.4 3.1 %collective-permute-start.10 = (bf16[128,128]{1,0:T(8,128)(2,1)S(1)}, bf16[128,128]{1,0:T(8,128)(2,1)S(1)}, u32[]{:S(2)}, u32[]{:S(2)}) collective-permute-start(bf16[128,128]{1,0:T(8,128)(2,1)S(1)} %get-tuple-element.52), channel_id=1, source_target_pairs={{0,8},{4,12},{8,0},{12,4},{16,24},{20,28},{24,16},{28,20},{32,40},... | collective-permute-start | bytes 98312 | tf_op jit(solution)/shard_map/ppermute | solution.py:394
  54.2 4.4 %collective-permute-start.12 = (bf16[2,64,256]{2,1,0:T(8,128)(2,1)S(1)}, bf16[2,64,256]{2,1,0:T(8,128)(2,1)S(1)}, u32[]{:S(2)}, u32[]{:S(2)}) collective-permute-start(bf16[2,64,256]{2,1,0:T(8,128)(2,1)S(1)} %get-tuple-element.60), channel_id=1, source_target_pairs={{0,1},{1,2},{2,3},{3,0},{4,5},{5,6},{6,7},{7,4},{8,9},{9,10},{10,1... | collective-permute-start | bytes 196616 | tf_op jit(solution)/shard_map/ppermute | solution.py:399
  54.3 6.2 %collective-permute-start.13 = (bf16[2,64,256]{2,1,0:T(8,128)(2,1)S(1)}, bf16[2,64,256]{2,1,0:T(8,128)(2,1)S(1)}, u32[]{:S(2)}, u32[]{:S(2)}) collective-permute-start(bf16[2,64,256]{2,1,0:T(8,128)(2,1)S(1)} %get-tuple-element.61), channel_id=1, source_target_pairs={{0,2},{1,3},{2,0},{3,1},{4,6},{5,7},{6,4},{7,5},{8,10},{9,11},{10,... | collective-permute-start | bytes 196616 | tf_op jit(solution)/shard_map/ppermute | solution.py:399
  58.1 3.3 %collective-permute-start.14 = (bf16[2,64,256]{2,1,0:T(8,128)(2,1)S(1)}, bf16[2,64,256]{2,1,0:T(8,128)(2,1)S(1)}, u32[]{:S(2)}, u32[]{:S(2)}) collective-permute-start(bf16[2,64,256]{2,1,0:T(8,128)(2,1)S(1)} %get-tuple-element.62), channel_id=1, source_target_pairs={{0,3},{1,0},{2,1},{3,2},{4,7},{5,4},{6,5},{7,6},{8,11},{9,8},{10,9... | collective-permute-start | bytes 196616 | tf_op jit(solution)/shard_map/ppermute | solution.py:399
  62.2 4.8 %collective-permute-start.17 = (bf16[64,2048]{1,0:T(8,128)(2,1)S(1)}, bf16[64,2048]{1,0:T(8,128)(2,1)S(1)}, u32[]{:S(2)}, u32[]{:S(2)}) collective-permute-start(bf16[64,2048]{1,0:T(8,128)(2,1)S(1)} %get-tuple-element.66), channel_id=1, source_target_pairs={{0,4},{4,0},{8,12},{12,8},{16,20},{20,16},{24,28},{28,24},{32,36},... | collective-permute-start | bytes 786440 | tf_op jit(solution)/shard_map/ppermute | solution.py:394

commit v7 on v6

--- a/solution.py
+++ b/solution.py
@@ -37,20 +37,12 @@
 
 
 def project_kernel(
-    tokens_hbm, w_hbm, beta_w_hbm, w_out_hbm, out_ref, w_ref, logits_ref, w_own_ref,
+    tokens_hbm, w_hbm, beta_w_hbm, out_ref, w_ref, logits_ref,
     tokens_ref, beta_w_ref, small_sems, w_sems
 ):
     first = pltpu.make_async_copy(tokens_hbm, tokens_ref, small_sems.at[0])
     last = pltpu.make_async_copy(beta_w_hbm, beta_w_ref, small_sems.at[1])
     copies = [pltpu.make_async_copy(w_hbm.at[s], w_ref.at[s], w_sems.at[s]) for s in range(3)]
-    rows = [
-        pltpu.make_async_copy(
-            w_out_hbm.at[pl.ds(pl.multiple_of((2 * j + bit(1)) * DK, DK), DK)],
-            w_own_ref.at[j],
-            small_sems.at[2 + j],
-        )
-        for j in range(2)
-    ]
     first.start()
     last.start()
     copies[0].start()
@@ -62,35 +54,29 @@
         copies[s].wait()
         if s == 0:
             copies[2].start()
-        if s == 1:
-            rows[0].start()
-            rows[1].start()
         out_ref[s] = dot(tokens_ref[...], w_ref[s]).astype(bf16)
-    rows[0].wait()
-    rows[1].wait()
-
-
-def project(tokens, w_qkv, beta_weight, w_out):
+
+
+def project(tokens, w_qkv, beta_weight):
     length, depth = tokens.shape
     columns = w_qkv.shape[2]
     heads = beta_weight.shape[0]
     operands = [
-        pltpu.with_memory_space_constraint(x, pltpu.HBM) for x in (tokens, w_qkv, beta_weight, w_out)
+        pltpu.with_memory_space_constraint(x, pltpu.HBM) for x in (tokens, w_qkv, beta_weight)
     ]
     return pl.pallas_call(
         project_kernel,
-        in_specs=[pl.BlockSpec(memory_space=pltpu.HBM)] * 4,
-        out_specs=whole(4),
+        in_specs=[pl.BlockSpec(memory_space=pltpu.HBM)] * 3,
+        out_specs=whole(3),
         out_shape=[
             shape((3, length, columns), bf16),
             shape(w_qkv.shape, bf16),
             shape((length, heads), f32),
-            shape((2, DK, w_out.shape[1]), bf16),
         ],
         scratch_shapes=[
             pltpu.VMEM(tokens.shape, bf16),
             pltpu.VMEM(beta_weight.shape, bf16),
-            pltpu.SemaphoreType.DMA((4,)),
+            pltpu.SemaphoreType.DMA((2,)),
             pltpu.SemaphoreType.DMA((3,)),
         ],
         compiler_params=params(),
@@ -144,9 +130,19 @@
 
 
 def local_kernel(
-    proj_ref, w_ref, edge_ref, conv_ref, logits_ref, bias_ref,
-    queries_ref, keys_t_ref, uw_ref, keep_ref, send_ref, padded, maps
+    proj_ref, w_ref, edge_ref, conv_ref, logits_ref, bias_ref, w_out_hbm,
+    queries_ref, keys_t_ref, uw_ref, keep_ref, send_ref, w_own_ref, padded, maps, sems
 ):
+    rows = [
+        pltpu.make_async_copy(
+            w_out_hbm.at[pl.ds(pl.multiple_of((2 * j + bit(1)) * DK, DK), DK)],
+            w_own_ref.at[j],
+            sems.at[j],
+        )
+        for j in range(2)
+    ]
+    rows[0].start()
+    rows[1].start()
     length = proj_ref.shape[1]
     heads = logits_ref.shape[1]
     betas = 1.0 / (1.0 + jnp.exp(-(logits_ref[...] + bias_ref[...])))
@@ -197,29 +193,36 @@
     for j in range(heads // 2):
         keep_ref[j] = maps[2 * j + core]
         send_ref[j] = maps[2 * j + 1 - core]
-
-
-def local_maps(projected, weights, edge, conv_weight, logits, beta_bias):
+    rows[0].wait()
+    rows[1].wait()
+
+
+def local_maps(projected, weights, edge, conv_weight, logits, beta_bias, w_out):
     length, columns = projected.shape[1:]
     heads = logits.shape[1]
     two = shape((heads // 2, DK, 2 * DK), bf16)
     return pl.pallas_call(
         local_kernel,
-        in_specs=whole(6),
-        out_specs=whole(5),
+        in_specs=whole(6) + [pl.BlockSpec(memory_space=pltpu.HBM)],
+        out_specs=whole(6),
         out_shape=[
             shape((heads, length, DK), bf16),
             shape((heads, DK, length), bf16),
             shape((heads, length, 2 * DK), bf16),
             two, two,
+            shape((2, DK, w_out.shape[1]), bf16),
         ],
         scratch_shapes=[
             pltpu.VMEM((3, EDGE + length, columns), f32),
             pltpu.VMEM((heads, DK, 2 * DK), bf16),
+            pltpu.SemaphoreType.DMA((2,)),
         ],
         compiler_params=params(),
         name="local_maps",
-    )(projected, weights, edge, conv_weight, logits, beta_bias[None, :])
+    )(
+        projected, weights, edge, conv_weight, logits, beta_bias[None, :],
+        pltpu.with_memory_space_constraint(w_out, pltpu.HBM),
+    )
 
 
 def inner_kernel(queries_ref, keys_t_ref, uw_ref, base_ref, gate_ref, both_out):
@@ -267,13 +270,17 @@
 STATE = shape((DK, DK), bf16)
 
 
-def small_call(kernel, outs, name, scratch=()):
+LONG = pl.CostEstimate(flops=60_000_000_000, bytes_accessed=1 << 20, transcendentals=0)
+
+
+def small_call(kernel, outs, name, scratch=(), cost=None):
     return pl.pallas_call(
         kernel,
         out_specs=whole(len(outs)),
         out_shape=list(outs),
         scratch_shapes=list(scratch),
         compiler_params=params(),
+        cost_estimate=cost,
         name=name,
     )
 
@@ -401,15 +408,14 @@
 
 def per_device(tokens_in, w_qkv, conv_weight, beta_weight, beta_bias, norm_gain, w_out):
     edge = turned(tokens_in[-EDGE:], "ctx", 1)
-    projected, weights, logits, w_own = project(tokens_in, w_qkv, beta_weight, w_out)
-    queries, keys_t, uw, maps, send = local_maps(
-        projected, weights, edge, conv_weight, logits, beta_bias
-    )
-    send, w_own = lax.optimization_barrier((send, w_own))
+    projected, weights, logits = project(tokens_in, w_qkv, beta_weight)
+    queries, keys_t, uw, maps, send, w_own = local_maps(
+        projected, weights, edge, conv_weight, logits, beta_bias, w_out
+    )
     w_one, w_three = turned(w_own, "head", 1), turned(w_own, "head", 3)
     sibling = swapped(send, 1)
     chip, send = small_call(
-        chip_kernel, [MAP, MAP], "chip_map", [pltpu.VMEM((2, DK, 2 * DK), bf16)]
+        chip_kernel, [MAP, MAP], "chip_map", [pltpu.VMEM((2, DK, 2 * DK), bf16)], LONG
     )(maps, sibling)
     pair, across, diagonal = swapped(send, 2), swapped(chip, 4), swapped(send, 6)
     four, near = small_call(four_kernel, [MAP, MAP], "four_map")(chip, pair, across, diagonal)
@@ -418,10 +424,10 @@
     base, gate, both = inner_outputs(queries, keys_t, uw)
     inner_in = swapped(both, 1)
     (two_rows,) = small_call(rows_kernel, [STATE], "rows_state")(row, other_row)
-    two_rows, w_one, w_three = lax.optimization_barrier((two_rows, w_one, w_three))
+    _, w_one, w_three = lax.optimization_barrier((two_rows, w_one, w_three))
     w_two = turned(w_one[0], "head", 1), turned(w_three[1], "head", 3)
     rows = swapped(two_rows, 48)
-    state, send = small_call(pair_start_kernel, [STATE, STATE], "pair_start")(
+    state, send = small_call(pair_start_kernel, [STATE, STATE], "pair_start", (), LONG)(
         rows, other_row, before, chip, pair
     )
     back = swapped(send, 2)

time: 67.9 us -> 67 us (0.987)
  starting transfers between devices: 31.5 us -> 28 us
  waiting for transfers between devices: 22.1 us -> 23.8 us
  Pallas kernels: 12.4 us -> 13.2 us
    ppermute x8, waiting for transfers between devices: 3.91 us -> 11.8 us  [turned(): return lax.ppermute(x, axis, [(i, (i + by) % count) for i in range(count)])]
    ppermute x10, waiting for transfers between devices: 18.2 us -> 12 us  [swapped(): lax.ppermute(x, 'ctx', [(i, i ^ by) for i in range(lax.axis_size('ctx'))])]
    ppermute x8, starting transfers between devices: 12.2 us -> 10.1 us  [turned(): return lax.ppermute(x, axis, [(i, (i + by) % count) for i in range(count)])]
    ppermute x10, starting transfers between devices: 19.2 us -> 17.9 us  [swapped(): lax.ppermute(x, 'ctx', [(i, i ^ by) for i in range(lax.axis_size('ctx'))])]
    pallas_call x2, Pallas kernels: 4.94 us -> 5.78 us  [the longest x1 5.36 us: local_maps(): pl.pallas_call(local_kernel, in_specs=whole(6) + [pl.BlockSpec(memory_spa...]
  transfers between devices with their start and end apart: 18 -> 18, of which waited for: 12 -> 8; matrix products, arithmetic and copies ran while one was open for 0% -> 0% of each run, Pallas kernels for 11% -> 11%
where the time goes in v7:
time: 67 us; the launch traced here: 66.8 us
  starting transfers between devices  28 us (42%)
  waiting for transfers between devices  23.8 us (36%)
  Pallas kernels  13.2 us (20%)
  local copies, waits for them, and re-layouts  0.87 us (1%)
  other arithmetic  0.76 us (1%)
    ppermute x10, starting transfers between devices, swapped(): lax.ppermute(x, 'ctx', [(i, i ^ by) for i in range(lax.axis_size('ctx'))])  17.9 us
    ppermute x10, waiting for transfers between devices, swapped(): lax.ppermute(x, 'ctx', [(i, i ^ by) for i in range(lax.axis_size('ctx'))])  12 us
    ppermute x8, waiting for transfers between devices, turned(): return lax.ppermute(x, axis, [(i, (i + by) % count) for i in range(count)])  11.8 us
    ppermute x8, starting transfers between devices, turned(): return lax.ppermute(x, axis, [(i, (i + by) % count) for i in range(count)])  10.1 us
    pallas_call x1, Pallas kernels, local_maps(): pl.pallas_call(local_kernel, in_specs=whole(6) + [pl.BlockSpec(memory_spa...  5.36 us
    pallas_call x1, Pallas kernels, project(): pl.pallas_call(project_kernel, in_specs=[pl.BlockSpec(memory_space=pltpu....  4.59 us
  transfers between devices with their start and end apart: 18, of which 8 were waited for; matrix products, arithmetic and copies ran while one was open for 0% of the time, Pallas kernels for 11%

profile of v7, /device:TPU:1, one launch (start us, length us, event | category | flops | bytes accessed | tf_op | source)
XLA Modules:
  0.0 66.8 jit_solution(18089520862605567460)
XLA Ops:
  0.0 0.0 copy-start.2
  0.0 0.0 copy-start
  0.0 0.8 %slice.9 = bf16[8,2048]{1,0:T(8,128)(2,1)S(1)} slice(bf16[256,2048]{1,0:T(8,128)(2,1)} %tokens_hbm.1), slice={[248:256], [0:2048]} | slice | bytes 65536 | tf_op jit(solution)/shard_map/slice | solution.py:410
  0.8 3.0 %collective-permute-start = (bf16[8,2048]{1,0:T(8,128)(2,1)S(1)}, bf16[8,2048]{1,0:T(8,128)(2,1)S(1)}, u32[]{:S(2)}, u32[]{:S(2)}) collective-permute-start(bf16[8,2048]{1,0:T(8,128)(2,1)S(1)} %slice.9), channel_id=1, source_target_pairs={{0,4},{4,8},{8,12},{12,16},{16,20},{20,24},{24,28},{28,32},{32,36}... | collective-permute-start | bytes 98312 | tf_op jit(solution)/shard_map/ppermute | solution.py:406
  3.8 4.6 %project.1 = (bf16[3,256,512]{2,1,0:T(8,128)(2,1)S(1)}, bf16[3,2048,512]{2,1,0:T(8,128)(2,1)S(1)}, f32[256,4]{1,0:T(8,128)S(1)}) custom-call(bf16[256,2048]{1,0:T(8,128)(2,1)} %tokens_hbm.1, bf16[3,2048,512]{2,1,0:T(8,128)(2,1)} %w_hbm.1, bf16[4,2048]{1,0:T(4,128)(2,1)} %beta_w_hbm.1), custom_call_target="tpu_custom_call" | custom-call | tf_op jit(solution)/shard_map/project/pallas_call | solution.py:67
  8.4 0.0 collective-permute-done.edge_ref
  8.4 0.0 copy-done.2
  8.4 0.0 copy-done
  8.4 5.4 %local_maps.1 = (bf16[4,256,128]{2,1,0:T(8,128)(2,1)S(1)}, bf16[4,128,256]{2,1,0:T(8,128)(2,1)S(1)}, bf16[4,256,256]{2,1,0:T(8,128)(2,1)S(1)}, bf16[2,128,256]{2...) custom-call(bf16[3,256,512]{2,1,0:T(8,128)(2,1)S(1)} %get-tuple-element.33.proj_ref, ...), custom_call_target="tpu_custom_call" | custom-call | tf_op jit(solution)/shard_map/local_maps/pallas_call | solution.py:204
  13.8 3.0 %collective-permute-start.1 = (bf16[2,128,256]{2,1,0:T(8,128)(2,1)S(1)}, bf16[2,128,256]{2,1,0:T(8,128)(2,1)S(1)}, u32[]{:S(2)}, u32[]{:S(2)}) collective-permute-start(bf16[2,128,256]{2,1,0:T(8,128)(2,1)S(1)} %get-tuple-element.37), channel_id=1, source_target_pairs={{0,4},{4,0},{8,12},{12,8},{16,20},{20,16},{24,28},{28,24},{32,36},... | collective-permute-start | bytes 393224 | tf_op jit(solution)/shard_map/ppermute | solution.py:401
  16.8 2.7 %collective-permute-start.14 = (bf16[2,128,2048]{2,1,0:T(8,128)(2,1)S(1)}, bf16[2,128,2048]{2,1,0:T(8,128)(2,1)S(1)}, u32[]{:S(2)}, u32[]{:S(2)}) collective-permute-start(bf16[2,128,2048]{2,1,0:T(8,128)(2,1)S(1)} %get-tuple-element.56.w_own), channel_id=1, source_target_pairs={{0,3},{1,0},{2,1},{3,2},{4,7},{5,4},{6,5},{7,6},{8,11},{9,8},{10,9... | collective-permute-start | bytes 3145736 | tf_op jit(solution)/shard_map/ppermute | solution.py:406
  19.6 0.0 collective-permute-start.13
  19.6 0.0 collective-permute-done.1.other_ref.other_maps
  19.6 0.2 chip_map.1
  19.8 2.8 %collective-permute-start.4 = (bf16[128,256]{1,0:T(8,128)(2,1)S(1)}, bf16[128,256]{1,0:T(8,128)(2,1)S(1)}, u32[]{:S(2)}, u32[]{:S(2)}) collective-permute-start(bf16[128,256]{1,0:T(8,128)(2,1)S(1)} %get-tuple-element.39), channel_id=1, source_target_pairs={{0,24},{4,28},{8,16},{12,20},{16,8},{20,12},{24,0},{28,4},{32,56},... | collective-permute-start | bytes 196616 | tf_op jit(solution)/shard_map/ppermute | solution.py:401
  22.6 0.0 collective-permute-start.2
  22.6 0.8 %collective-permute-start.3 = (bf16[128,256]{1,0:T(8,128)(2,1)S(1)}, bf16[128,256]{1,0:T(8,128)(2,1)S(1)}, u32[]{:S(2)}, u32[]{:S(2)}) collective-permute-start(bf16[128,256]{1,0:T(8,128)(2,1)S(1)} %get-tuple-element.38.own_ref), channel_id=1, source_target_pairs={{0,16},{4,20},{8,24},{12,28},{16,0},{20,4},{24,8},{28,12},{32,48},... | collective-permute-start | bytes 196616 | tf_op jit(solution)/shard_map/ppermute | solution.py:401
  23.5 1.4 %collective-permute-done.4.diagonal_ref = bf16[128,256]{1,0:T(8,128)(2,1)S(1)} collective-permute-done((bf16[128,256]{1,0:T(8,128)(2,1)S(1)}, bf16[128,256]{1,0:T(8,128)(2,1)S(1)}, u32[]{:S(2)}, u32[]{:S(2)}) %collective-permute-start.4) | collective-permute-done | bytes 65568 | tf_op jit(solution)/shard_map/ppermute | solution.py:401
  24.8 2.6 %collective-permute-done.2.pair_ref.other_ref = bf16[128,256]{1,0:T(8,128)(2,1)S(1)} collective-permute-done((bf16[128,256]{1,0:T(8,128)(2,1)S(1)}, bf16[128,256]{1,0:T(8,128)(2,1)S(1)}, u32[]{:S(2)}, u32[]{:S(2)}) %collective-permute-start.2) | collective-permute-done | bytes 65568 | tf_op jit(solution)/shard_map/ppermute | solution.py:401
  27.5 0.0 collective-permute-done.3.across_ref
  27.5 0.4 four_map.1
  27.8 1.7 %collective-permute-start.5 = (bf16[128,256]{1,0:T(8,128)(2,1)S(1)}, bf16[128,256]{1,0:T(8,128)(2,1)S(1)}, u32[]{:S(2)}, u32[]{:S(2)}) collective-permute-start(bf16[128,256]{1,0:T(8,128)(2,1)S(1)} %get-tuple-element.40.own_ref), channel_id=1, source_target_pairs={{0,48},{4,52},{8,56},{12,60},{16,32},{20,36},{24,40},{28,44},{32,1... | collective-permute-start | bytes 196616 | tf_op jit(solution)/shard_map/ppermute | solution.py:401
  29.5 3.8 %collective-permute-done.5.other_ref = bf16[128,256]{1,0:T(8,128)(2,1)S(1)} collective-permute-done((bf16[128,256]{1,0:T(8,128)(2,1)S(1)}, bf16[128,256]{1,0:T(8,128)(2,1)S(1)}, u32[]{:S(2)}, u32[]{:S(2)}) %collective-permute-start.5) | collective-permute-done | bytes 65568 | tf_op jit(solution)/shard_map/ppermute | solution.py:401
  33.3 0.2 far_map.1
  33.5 1.2 %collective-permute-start.6 = (bf16[128,256]{1,0:T(8,128)(2,1)S(1)}, bf16[128,256]{1,0:T(8,128)(2,1)S(1)}, u32[]{:S(2)}, u32[]{:S(2)}) collective-permute-start(bf16[128,256]{1,0:T(8,128)(2,1)S(1)} %get-tuple-element.42.own_ref), channel_id=1, source_target_pairs={{0,64},{4,68},{8,72},{12,76},{16,80},{20,84},{24,88},{28,92},{32,9... | collective-permute-start | bytes 196616 | tf_op jit(solution)/shard_map/ppermute | solution.py:401
  34.7 0.5 inner_outputs.1
  35.2 3.4 %collective-permute-start.9 = (bf16[2,2,256,128]{3,2,1,0:T(8,128)(2,1)S(1)}, bf16[2,2,256,128]{3,2,1,0:T(8,128)(2,1)S(1)}, u32[]{:S(2)}, u32[]{:S(2)}) collective-permute-start(bf16[2,2,256,128]{3,2,1,0:T(8,128)(2,1)S(1)} %get-tuple-element.51), channel_id=1, source_target_pairs={{0,4},{4,0},{8,12},{12,8},{16,20},{20,16},{24,28},{28,24},{32,36},... | collective-permute-start | bytes 786440 | tf_op jit(solution)/shard_map/ppermute | solution.py:401
  38.7 0.0 collective-permute-done.6.other_ref.row_ref
  38.7 0.2 rows_state.1
  38.8 1.9 %collective-permute-start.7 = (bf16[128,128]{1,0:T(8,128)(2,1)S(1)}, bf16[128,128]{1,0:T(8,128)(2,1)S(1)}, u32[]{:S(2)}, u32[]{:S(2)}) collective-permute-start(bf16[128,128]{1,0:T(8,128)(2,1)S(1)} %rows_state.1), channel_id=1, source_target_pairs={{0,192},{4,196},{8,200},{12,204},{16,208},{20,212},{24,216},{28,22... | collective-permute-start | bytes 98312 | tf_op jit(solution)/shard_map/ppermute | solution.py:401
  40.7 1.4 %collective-permute-done.14.w_three = bf16[2,128,2048]{2,1,0:T(8,128)(2,1)S(1)} collective-permute-done((bf16[2,128,2048]{2,1,0:T(8,128)(2,1)S(1)}, bf16[2,128,2048]{2,1,0:T(8,128)(2,1)S(1)}, u32[]{:S(2)}, u32[]{:S(2)}) %collective-permute-start.14) | collective-permute-done | bytes 1048608 | tf_op jit(solution)/shard_map/ppermute | solution.py:406
  42.1 3.1 %collective-permute-done.13.w_one = bf16[2,128,2048]{2,1,0:T(8,128)(2,1)S(1)} collective-permute-done((bf16[2,128,2048]{2,1,0:T(8,128)(2,1)S(1)}, bf16[2,128,2048]{2,1,0:T(8,128)(2,1)S(1)}, u32[]{:S(2)}, u32[]{:S(2)}) %collective-permute-start.13) | collective-permute-done | bytes 1048608 | tf_op jit(solution)/shard_map/ppermute | solution.py:406
  45.3 0.4 collective-permute-start.16
  45.7 1.1 %collective-permute-start.15 = (bf16[128,2048]{1,0:T(8,128)(2,1)S(1)}, bf16[128,2048]{1,0:T(8,128)(2,1)S(1)}, u32[]{:S(2)}, u32[]{:S(2)}) collective-permute-start(bf16[128,2048]{1,0:T(8,128)(2,1)S(1)} %slice_bitcast_fusion.1), channel_id=1, source_target_pairs={{0,1},{1,2},{2,3},{3,0},{4,5},{5,6},{6,7},{7,4},{8,9},{9,10},{10,1... | collective-permute-start | bytes 1572872 | tf_op jit(solution)/shard_map/ppermute | solution.py:406
  46.8 0.0 collective-permute-done.7.rows_ref
  46.8 0.0 copy-start.1
  46.8 0.4 pair_start.1
  47.3 0.1 collective-permute-start.8
  47.4 0.0 collective-permute-done.9.both_in
  47.4 3.0 %collective-permute-done.8.other_state = bf16[128,128]{1,0:T(8,128)(2,1)S(1)} collective-permute-done((bf16[128,128]{1,0:T(8,128)(2,1)S(1)}, bf16[128,128]{1,0:T(8,128)(2,1)S(1)}, u32[]{:S(2)}, u32[]{:S(2)}) %collective-permute-start.8) | collective-permute-done | bytes 32800 | tf_op jit(solution)/shard_map/ppermute | solution.py:401
  50.4 0.0 copy-done.1
  50.4 0.6 finish.1
  51.1 0.1 collective-permute-start.10
  51.2 2.7 %collective-permute-start.11 = (bf16[2,64,256]{2,1,0:T(8,128)(2,1)S(1)}, bf16[2,64,256]{2,1,0:T(8,128)(2,1)S(1)}, u32[]{:S(2)}, u32[]{:S(2)}) collective-permute-start(bf16[2,64,256]{2,1,0:T(8,128)(2,1)S(1)} %get-tuple-element.54), channel_id=1, source_target_pairs={{0,2},{1,3},{2,0},{3,1},{4,6},{5,7},{6,4},{7,5},{8,10},{9,11},{10,... | collective-permute-start | bytes 196616 | tf_op jit(solution)/shard_map/ppermute | solution.py:406
  53.9 0.0 collective-permute-start.12
  53.9 7.3 %collective-permute-done.10.one = bf16[2,64,256]{2,1,0:T(8,128)(2,1)S(1)} collective-permute-done((bf16[2,64,256]{2,1,0:T(8,128)(2,1)S(1)}, bf16[2,64,256]{2,1,0:T(8,128)(2,1)S(1)}, u32[]{:S(2)}, u32[]{:S(2)}) %collective-permute-start.10) | collective-permute-done | bytes 65568 | tf_op jit(solution)/shard_map/ppermute | solution.py:406
  61.2 0.0 collective-permute-done.11.two
  61.2 0.0 collective-permute-done.12.three
  61.2 0.0 collective-permute-done.16.w_two1
  61.2 0.0 collective-permute-done.15.w_two0
  61.2 0.7 %merge.1 = (f32[64,2048]{1,0:T(8,128)S(1)}, bf16[64,2048]{1,0:T(8,128)(2,1)S(1)}) custom-call(bf16[2,64,256]{2,1,0:T(8,128)(2,1)S(1)} %get-tuple-element.52.mine_ref, bf16[2,64,256]{2,1,0:T(8,128)(2,1)S(1)} %collective-permute-done.10.one, bf16[2,64,256]{2,1,0:T(8,128)(2,1)S(1)} %collective-permute-done.11.two, ...), custom_call_target="tpu_custom_call" | custom-call | tf_op jit(solution)/shard_map/merge/pallas_call | solution.py:395
  62.0 2.9 %collective-permute-start.17 = (bf16[64,2048]{1,0:T(8,128)(2,1)S(1)}, bf16[64,2048]{1,0:T(8,128)(2,1)S(1)}, u32[]{:S(2)}, u32[]{:S(2)}) collective-permute-start(bf16[64,2048]{1,0:T(8,128)(2,1)S(1)} %get-tuple-element.60), channel_id=1, source_target_pairs={{0,4},{4,0},{8,12},{12,8},{16,20},{20,16},{24,28},{28,24},{32,36},... | collective-permute-start | bytes 786440 | tf_op jit(solution)/shard_map/ppermute | solution.py:401
  64.9 1.2 %collective-permute-done.17 = bf16[64,2048]{1,0:T(8,128)(2,1)S(1)} collective-permute-done((bf16[64,2048]{1,0:T(8,128)(2,1)S(1)}, bf16[64,2048]{1,0:T(8,128)(2,1)S(1)}, u32[]{:S(2)}, u32[]{:S(2)}) %collective-permute-start.17) | collective-permute-done | bytes 262176 | tf_op jit(solution)/shard_map/ppermute | solution.py:401
  66.1 0.8 %add_convert_fusion = bf16[64,2048]{1,0:T(8,128)(2,1)} fusion(f32[64,2048]{1,0:T(8,128)S(1)} %get-tuple-element.59, bf16[64,2048]{1,0:T(8,128)(2,1)S(1)} %collective-permute-done.17), kind=kLoop, calls=%fused_computation | loop fusion | flops 393216 | bytes 1048576 | tf_op jit(solution)/shard_map/convert_element_type | solution.py:439
  (2 shorter events, 0.1 us)
Async XLA Ops:
  0.0 8.4 %copy-start.2 = (f32[4]{0:T(128)S(1)}, f32[4]{0:T(128)}, u32[]{:S(2)}) copy-start(f32[4]{0:T(128)} %param.11) | copy-start | bytes 52
  0.0 8.4 %copy-start = (f32[3,4,512]{2,1,0:T(4,128)S(1)}, f32[3,4,512]{2,1,0:T(4,128)}, u32[]{:S(2)}) copy-start(f32[3,4,512]{2,1,0:T(4,128)} %conv_ref.1) | copy-start | bytes 73732
  0.8 7.6 %collective-permute-start = (bf16[8,2048]{1,0:T(8,128)(2,1)S(1)}, bf16[8,2048]{1,0:T(8,128)(2,1)S(1)}, u32[]{:S(2)}, u32[]{:S(2)}) collective-permute-start(bf16[8,2048]{1,0:T(8,128)(2,1)S(1)} %slice.9), channel_id=1, source_target_pairs={{0,4},{4,8},{8,12},{12,16},{16,20},{20,24},{24,28},{28,32},{32,36}... | collective-permute-start | bytes 98312 | tf_op jit(solution)/shard_map/ppermute | solution.py:406
  13.8 5.8 %collective-permute-start.1 = (bf16[2,128,256]{2,1,0:T(8,128)(2,1)S(1)}, bf16[2,128,256]{2,1,0:T(8,128)(2,1)S(1)}, u32[]{:S(2)}, u32[]{:S(2)}) collective-permute-start(bf16[2,128,256]{2,1,0:T(8,128)(2,1)S(1)} %get-tuple-element.37), channel_id=1, source_target_pairs={{0,4},{4,0},{8,12},{12,8},{16,20},{20,16},{24,28},{28,24},{32,36},... | collective-permute-start | bytes 393224 | tf_op jit(solution)/shard_map/ppermute | solution.py:401
  16.8 25.3 %collective-permute-start.14 = (bf16[2,128,2048]{2,1,0:T(8,128)(2,1)S(1)}, bf16[2,128,2048]{2,1,0:T(8,128)(2,1)S(1)}, u32[]{:S(2)}, u32[]{:S(2)}) collective-permute-start(bf16[2,128,2048]{2,1,0:T(8,128)(2,1)S(1)} %get-tuple-element.56.w_own), channel_id=1, source_target_pairs={{0,3},{1,0},{2,1},{3,2},{4,7},{5,4},{6,5},{7,6},{8,11},{9,8},{10,9... | collective-permute-start | bytes 3145736 | tf_op jit(solution)/shard_map/ppermute | solution.py:406
  19.6 25.6 %collective-permute-start.13 = (bf16[2,128,2048]{2,1,0:T(8,128)(2,1)S(1)}, bf16[2,128,2048]{2,1,0:T(8,128)(2,1)S(1)}, u32[]{:S(2)}, u32[]{:S(2)}) collective-permute-start(bf16[2,128,2048]{2,1,0:T(8,128)(2,1)S(1)} %get-tuple-element.56.w_own), channel_id=1, source_target_pairs={{0,1},{1,2},{2,3},{3,0},{4,5},{5,6},{6,7},{7,4},{8,9},{9,10},{10,1... | collective-permute-start | bytes 3145736 | tf_op jit(solution)/shard_map/ppermute | solution.py:406
  19.8 5.0 %collective-permute-start.4 = (bf16[128,256]{1,0:T(8,128)(2,1)S(1)}, bf16[128,256]{1,0:T(8,128)(2,1)S(1)}, u32[]{:S(2)}, u32[]{:S(2)}) collective-permute-start(bf16[128,256]{1,0:T(8,128)(2,1)S(1)} %get-tuple-element.39), channel_id=1, source_target_pairs={{0,24},{4,28},{8,16},{12,20},{16,8},{20,12},{24,0},{28,4},{32,56},... | collective-permute-start | bytes 196616 | tf_op jit(solution)/shard_map/ppermute | solution.py:401
  22.6 4.9 %collective-permute-start.2 = (bf16[128,256]{1,0:T(8,128)(2,1)S(1)}, bf16[128,256]{1,0:T(8,128)(2,1)S(1)}, u32[]{:S(2)}, u32[]{:S(2)}) collective-permute-start(bf16[128,256]{1,0:T(8,128)(2,1)S(1)} %get-tuple-element.39), channel_id=1, source_target_pairs={{0,8},{4,12},{8,0},{12,4},{16,24},{20,28},{24,16},{28,20},{32,40},... | collective-permute-start | bytes 196616 | tf_op jit(solution)/shard_map/ppermute | solution.py:401
  22.6 4.9 %collective-permute-start.3 = (bf16[128,256]{1,0:T(8,128)(2,1)S(1)}, bf16[128,256]{1,0:T(8,128)(2,1)S(1)}, u32[]{:S(2)}, u32[]{:S(2)}) collective-permute-start(bf16[128,256]{1,0:T(8,128)(2,1)S(1)} %get-tuple-element.38.own_ref), channel_id=1, source_target_pairs={{0,16},{4,20},{8,24},{12,28},{16,0},{20,4},{24,8},{28,12},{32,48},... | collective-permute-start | bytes 196616 | tf_op jit(solution)/shard_map/ppermute | solution.py:401
  27.8 5.4 %collective-permute-start.5 = (bf16[128,256]{1,0:T(8,128)(2,1)S(1)}, bf16[128,256]{1,0:T(8,128)(2,1)S(1)}, u32[]{:S(2)}, u32[]{:S(2)}) collective-permute-start(bf16[128,256]{1,0:T(8,128)(2,1)S(1)} %get-tuple-element.40.own_ref), channel_id=1, source_target_pairs={{0,48},{4,52},{8,56},{12,60},{16,32},{20,36},{24,40},{28,44},{32,1... | collective-permute-start | bytes 196616 | tf_op jit(solution)/shard_map/ppermute | solution.py:401
  33.5 5.2 %collective-permute-start.6 = (bf16[128,256]{1,0:T(8,128)(2,1)S(1)}, bf16[128,256]{1,0:T(8,128)(2,1)S(1)}, u32[]{:S(2)}, u32[]{:S(2)}) collective-permute-start(bf16[128,256]{1,0:T(8,128)(2,1)S(1)} %get-tuple-element.42.own_ref), channel_id=1, source_target_pairs={{0,64},{4,68},{8,72},{12,76},{16,80},{20,84},{24,88},{28,92},{32,9... | collective-permute-start | bytes 196616 | tf_op jit(solution)/shard_map/ppermute | solution.py:401
  35.2 12.1 %collective-permute-start.9 = (bf16[2,2,256,128]{3,2,1,0:T(8,128)(2,1)S(1)}, bf16[2,2,256,128]{3,2,1,0:T(8,128)(2,1)S(1)}, u32[]{:S(2)}, u32[]{:S(2)}) collective-permute-start(bf16[2,2,256,128]{3,2,1,0:T(8,128)(2,1)S(1)} %get-tuple-element.51), channel_id=1, source_target_pairs={{0,4},{4,0},{8,12},{12,8},{16,20},{20,16},{24,28},{28,24},{32,36},... | collective-permute-start | bytes 786440 | tf_op jit(solution)/shard_map/ppermute | solution.py:401
  38.8 8.0 %collective-permute-start.7 = (bf16[128,128]{1,0:T(8,128)(2,1)S(1)}, bf16[128,128]{1,0:T(8,128)(2,1)S(1)}, u32[]{:S(2)}, u32[]{:S(2)}) collective-permute-start(bf16[128,128]{1,0:T(8,128)(2,1)S(1)} %rows_state.1), channel_id=1, source_target_pairs={{0,192},{4,196},{8,200},{12,204},{16,208},{20,212},{24,216},{28,22... | collective-permute-start | bytes 98312 | tf_op jit(solution)/shard_map/ppermute | solution.py:401
  45.3 15.9 %collective-permute-start.16 = (bf16[128,2048]{1,0:T(8,128)(2,1)S(1)}, bf16[128,2048]{1,0:T(8,128)(2,1)S(1)}, u32[]{:S(2)}, u32[]{:S(2)}) collective-permute-start(bf16[128,2048]{1,0:T(8,128)(2,1)S(1)} %slice_bitcast_fusion), channel_id=1, source_target_pairs={{0,3},{1,0},{2,1},{3,2},{4,7},{5,4},{6,5},{7,6},{8,11},{9,8},{10,9... | collective-permute-start | bytes 1572872 | tf_op jit(solution)/shard_map/ppermute | solution.py:406
  45.7 15.5 %collective-permute-start.15 = (bf16[128,2048]{1,0:T(8,128)(2,1)S(1)}, bf16[128,2048]{1,0:T(8,128)(2,1)S(1)}, u32[]{:S(2)}, u32[]{:S(2)}) collective-permute-start(bf16[128,2048]{1,0:T(8,128)(2,1)S(1)} %slice_bitcast_fusion.1), channel_id=1, source_target_pairs={{0,1},{1,2},{2,3},{3,0},{4,5},{5,6},{6,7},{7,4},{8,9},{9,10},{10,1... | collective-permute-start | bytes 1572872 | tf_op jit(solution)/shard_map/ppermute | solution.py:406
  46.8 3.6 %copy-start.1 = (f32[512]{0:T(512)S(1)}, f32[512]{0:T(512)}, u32[]{:S(2)}) copy-start(f32[512]{0:T(512)} %param.12) | copy-start | bytes 6148
  47.3 3.1 %collective-permute-start.8 = (bf16[128,128]{1,0:T(8,128)(2,1)S(1)}, bf16[128,128]{1,0:T(8,128)(2,1)S(1)}, u32[]{:S(2)}, u32[]{:S(2)}) collective-permute-start(bf16[128,128]{1,0:T(8,128)(2,1)S(1)} %get-tuple-element.45), channel_id=1, source_target_pairs={{0,8},{4,12},{8,0},{12,4},{16,24},{20,28},{24,16},{28,20},{32,40},... | collective-permute-start | bytes 98312 | tf_op jit(solution)/shard_map/ppermute | solution.py:401
  51.1 10.1 %collective-permute-start.10 = (bf16[2,64,256]{2,1,0:T(8,128)(2,1)S(1)}, bf16[2,64,256]{2,1,0:T(8,128)(2,1)S(1)}, u32[]{:S(2)}, u32[]{:S(2)}) collective-permute-start(bf16[2,64,256]{2,1,0:T(8,128)(2,1)S(1)} %get-tuple-element.53), channel_id=1, source_target_pairs={{0,1},{1,2},{2,3},{3,0},{4,5},{5,6},{6,7},{7,4},{8,9},{9,10},{10,1... | collective-permute-start | bytes 196616 | tf_op jit(solution)/shard_map/ppermute | solution.py:406
  51.2 10.1 %collective-permute-start.11 = (bf16[2,64,256]{2,1,0:T(8,128)(2,1)S(1)}, bf16[2,64,256]{2,1,0:T(8,128)(2,1)S(1)}, u32[]{:S(2)}, u32[]{:S(2)}) collective-permute-start(bf16[2,64,256]{2,1,0:T(8,128)(2,1)S(1)} %get-tuple-element.54), channel_id=1, source_target_pairs={{0,2},{1,3},{2,0},{3,1},{4,6},{5,7},{6,4},{7,5},{8,10},{9,11},{10,... | collective-permute-start | bytes 196616 | tf_op jit(solution)/shard_map/ppermute | solution.py:406
  53.9 7.4 %collective-permute-start.12 = (bf16[2,64,256]{2,1,0:T(8,128)(2,1)S(1)}, bf16[2,64,256]{2,1,0:T(8,128)(2,1)S(1)}, u32[]{:S(2)}, u32[]{:S(2)}) collective-permute-start(bf16[2,64,256]{2,1,0:T(8,128)(2,1)S(1)} %get-tuple-element.55), channel_id=1, source_target_pairs={{0,3},{1,0},{2,1},{3,2},{4,7},{5,4},{6,5},{7,6},{8,11},{9,8},{10,9... | collective-permute-start | bytes 196616 | tf_op jit(solution)/shard_map/ppermute | solution.py:406
  62.0 4.1 %collective-permute-start.17 = (bf16[64,2048]{1,0:T(8,128)(2,1)S(1)}, bf16[64,2048]{1,0:T(8,128)(2,1)S(1)}, u32[]{:S(2)}, u32[]{:S(2)}) collective-permute-start(bf16[64,2048]{1,0:T(8,128)(2,1)S(1)} %get-tuple-element.60), channel_id=1, source_target_pairs={{0,4},{4,0},{8,12},{12,8},{16,20},{20,16},{24,28},{28,24},{32,36},... | collective-permute-start | bytes 786440 | tf_op jit(solution)/shard_map/ppermute | solution.py:401

commit v8 on v6

--- a/solution.py
+++ b/solution.py
@@ -34,6 +34,9 @@
 
 def shape(dims, kind):
     return jax.ShapeDtypeStruct(dims, kind)
+
+
+LONG = pl.CostEstimate(flops=60_000_000_000, bytes_accessed=1 << 20, transcendentals=0)
 
 
 def project_kernel(
@@ -94,6 +97,7 @@
             pltpu.SemaphoreType.DMA((3,)),
         ],
         compiler_params=params(),
+        cost_estimate=LONG,
         name="project",
     )(*operands)
 
@@ -218,6 +222,7 @@
             pltpu.VMEM((heads, DK, 2 * DK), bf16),
         ],
         compiler_params=params(),
+        cost_estimate=LONG,
         name="local_maps",
     )(projected, weights, edge, conv_weight, logits, beta_bias[None, :])
 
@@ -267,13 +272,14 @@
 STATE = shape((DK, DK), bf16)
 
 
-def small_call(kernel, outs, name, scratch=()):
+def small_call(kernel, outs, name, scratch=(), cost=None):
     return pl.pallas_call(
         kernel,
         out_specs=whole(len(outs)),
         out_shape=list(outs),
         scratch_shapes=list(scratch),
         compiler_params=params(),
+        cost_estimate=cost,
         name=name,
     )
 
@@ -402,12 +408,13 @@
 def per_device(tokens_in, w_qkv, conv_weight, beta_weight, beta_bias, norm_gain, w_out):
     edge = turned(tokens_in[-EDGE:], "ctx", 1)
     projected, weights, logits, w_own = project(tokens_in, w_qkv, beta_weight, w_out)
+    w_one, w_three = turned(w_own, "head", 1), turned(w_own, "head", 3)
     queries, keys_t, uw, maps, send = local_maps(
         projected, weights, edge, conv_weight, logits, beta_bias
     )
-    send, w_own = lax.optimization_barrier((send, w_own))
-    w_one, w_three = turned(w_own, "head", 1), turned(w_own, "head", 3)
     sibling = swapped(send, 1)
+    base, gate, both = inner_outputs(queries, keys_t, uw)
+    inner_in = swapped(both, 1)
     chip, send = small_call(
         chip_kernel, [MAP, MAP], "chip_map", [pltpu.VMEM((2, DK, 2 * DK), bf16)]
     )(maps, sibling)
@@ -415,13 +422,11 @@
     four, near = small_call(four_kernel, [MAP, MAP], "four_map")(chip, pair, across, diagonal)
     row, before = small_call(far_kernel, [MAP, MAP], "far_map")(four, swapped(four, 12), near)
     other_row = swapped(row, 16)
-    base, gate, both = inner_outputs(queries, keys_t, uw)
-    inner_in = swapped(both, 1)
     (two_rows,) = small_call(rows_kernel, [STATE], "rows_state")(row, other_row)
-    two_rows, w_one, w_three = lax.optimization_barrier((two_rows, w_one, w_three))
+    _, w_one, w_three = lax.optimization_barrier((two_rows, w_one, w_three))
     w_two = turned(w_one[0], "head", 1), turned(w_three[1], "head", 3)
     rows = swapped(two_rows, 48)
-    state, send = small_call(pair_start_kernel, [STATE, STATE], "pair_start")(
+    state, send = small_call(pair_start_kernel, [STATE, STATE], "pair_start", (), LONG)(
         rows, other_row, before, chip, pair
     )
     back = swapped(send, 2)

time: 67.9 us -> 65.1 us (0.959)
  waiting for transfers between devices: 22.1 us -> 16.1 us
  starting transfers between devices: 31.5 us -> 34.7 us
    ppermute x10, waiting for transfers between devices: 18.2 us -> 11.1 us  [swapped(): lax.ppermute(x, 'ctx', [(i, i ^ by) for i in range(lax.axis_size('ctx'))])]
    ppermute x10, starting transfers between devices: 19.2 us -> 22.2 us  [swapped(): lax.ppermute(x, 'ctx', [(i, i ^ by) for i in range(lax.axis_size('ctx'))])]
    ppermute x8, waiting for transfers between devices: 3.91 us -> 5.02 us  [turned(): return lax.ppermute(x, axis, [(i, (i + by) % count) for i in range(count)])]
  transfers between devices with their start and end apart: 18 -> 18, of which waited for: 12 -> 8; matrix products, arithmetic and copies ran while one was open for 0% -> 0% of each run, Pallas kernels for 11% -> 18%
where the time goes in v8:
time: 65.1 us; the launch traced here: 64.9 us
  starting transfers between devices  34.7 us (53%)
  waiting for transfers between devices  16.1 us (25%)
  Pallas kernels  12.4 us (19%)
  local copies, waits for them, and re-layouts  0.85 us (1%)
  other arithmetic  0.76 us (1%)
    ppermute x10, starting transfers between devices, swapped(): lax.ppermute(x, 'ctx', [(i, i ^ by) for i in range(lax.axis_size('ctx'))])  22.2 us
    ppermute x8, starting transfers between devices, turned(): return lax.ppermute(x, axis, [(i, (i + by) % count) for i in range(count)])  12.5 us
    ppermute x10, waiting for transfers between devices, swapped(): lax.ppermute(x, 'ctx', [(i, i ^ by) for i in range(lax.axis_size('ctx'))])  11.1 us
    ppermute x8, waiting for transfers between devices, turned(): return lax.ppermute(x, axis, [(i, (i + by) % count) for i in range(count)])  5.02 us
    pallas_call x1, Pallas kernels, project(): pl.pallas_call(project_kernel, in_specs=[pl.BlockSpec(memory_space=pltpu....  4.62 us
    pallas_call x1, Pallas kernels, local_maps(): pl.pallas_call(local_kernel, in_specs=whole(6), out_specs=whole(5), out_s...  4.53 us
  transfers between devices with their start and end apart: 18, of which 8 were waited for; matrix products, arithmetic and copies ran while one was open for 0% of the time, Pallas kernels for 18%

profile of v8, /device:TPU:1, one launch (start us, length us, event | category | flops | bytes accessed | tf_op | source)
XLA Modules:
  0.0 64.9 jit_solution(14871989179028031916)
XLA Ops:
  0.0 0.8 %slice.9 = bf16[8,2048]{1,0:T(8,128)(2,1)S(1)} slice(bf16[256,2048]{1,0:T(8,128)(2,1)} %tokens_hbm.1), slice={[248:256], [0:2048]} | slice | bytes 65536 | tf_op jit(solution)/shard_map/slice | solution.py:409
  0.8 0.0 copy-start.1
  0.8 0.0 copy-start.2
  0.8 3.0 %collective-permute-start = (bf16[8,2048]{1,0:T(8,128)(2,1)S(1)}, bf16[8,2048]{1,0:T(8,128)(2,1)S(1)}, u32[]{:S(2)}, u32[]{:S(2)}) collective-permute-start(bf16[8,2048]{1,0:T(8,128)(2,1)S(1)} %slice.9), channel_id=1, source_target_pairs={{0,4},{4,8},{8,12},{12,16},{16,20},{20,24},{24,28},{28,32},{32,36}... | collective-permute-start | bytes 98312 | tf_op jit(solution)/shard_map/ppermute | solution.py:405
  3.8 4.6 %project.1 = (bf16[3,256,512]{2,1,0:T(8,128)(2,1)S(1)}, bf16[3,2048,512]{2,1,0:T(8,128)(2,1)S(1)}, f32[256,4]{1,0:T(8,128)S(1)}, bf16[2,128,2048]{2,1,0:T(8,128)(2,1)S(1)}) custom-call(bf16[256,2048]{1,0:T(8,128)(2,1)} %tokens_hbm.1, bf16[3,2048,512]{2,1,0:T(8,128)(2,1)} %w_hbm.1, bf16[4,2048]{1,0:T(4,128)(2,1)} %beta_w_hbm.1, bf16[512,2048]{1,0:T(8,128)(2,1)} %w_out_hbm.1), custom_call_target="tpu_custom_call" | custom-call | flops 60000002048 | bytes 1048576 | tf_op jit(solution)/shard_map/project/pallas_call | solution.py:83
  8.4 2.8 %collective-permute-start.14 = (bf16[2,128,2048]{2,1,0:T(8,128)(2,1)S(1)}, bf16[2,128,2048]{2,1,0:T(8,128)(2,1)S(1)}, u32[]{:S(2)}, u32[]{:S(2)}) collective-permute-start(bf16[2,128,2048]{2,1,0:T(8,128)(2,1)S(1)} %get-tuple-element.56.w_own), channel_id=1, source_target_pairs={{0,3},{1,0},{2,1},{3,2},{4,7},{5,4},{6,5},{7,6},{8,11},{9,8},{10,9... | collective-permute-start | bytes 3145736 | tf_op jit(solution)/shard_map/ppermute | solution.py:405
  11.2 0.0 collective-permute-start.13
  11.2 0.0 collective-permute-done.edge_ref
  11.2 0.0 copy-done.1
  11.2 0.0 copy-done.2
  11.3 4.5 %local_maps.1 = (bf16[4,256,128]{2,1,0:T(8,128)(2,1)S(1)}, bf16[4,128,256]{2,1,0:T(8,128)(2,1)S(1)}, bf16[4,256,256]{2,1,0:T(8,128)(2,1)S(1)}, bf16[2,128,256]{2,1,0:T(8,128)(2,1)S(1)}, bf16[2,128,256]{2,1,0:T(8,128)(2,1)S(1)}) custom-call(bf16[3,256,512]{2,1,0:T(8,128)(2,1)S(1)} %get-tuple-element.33.proj_ref, ...), custom_call_target="tpu_custom_call" | custom-call | flops 60000002048 | bytes 1048576 | tf_op jit(solution)/shard_map/local_maps/pallas_call | solution.py:210
  15.8 0.2 collective-permute-start.1
  16.0 1.2 %collective-permute-done.1.other_ref.other_maps = bf16[2,128,256]{2,1,0:T(8,128)(2,1)S(1)} collective-permute-done((bf16[2,128,256]{2,1,0:T(8,128)(2,1)S(1)}, bf16[2,128,256]{2,1,0:T(8,128)(2,1)S(1)}, u32[]{:S(2)}, u32[]{:S(2)}) %collective-permute-start.1) | collective-permute-done | bytes 131104 | tf_op jit(solution)/shard_map/ppermute | solution.py:400
  17.2 0.2 chip_map.1
  17.5 5.6 %collective-permute-start.4 = (bf16[128,256]{1,0:T(8,128)(2,1)S(1)}, bf16[128,256]{1,0:T(8,128)(2,1)S(1)}, u32[]{:S(2)}, u32[]{:S(2)}) collective-permute-start(bf16[128,256]{1,0:T(8,128)(2,1)S(1)} %get-tuple-element.39), channel_id=1, source_target_pairs={{0,24},{4,28},{8,16},{12,20},{16,8},{20,12},{24,0},{28,4},{32,56},... | collective-permute-start | bytes 196616 | tf_op jit(solution)/shard_map/ppermute | solution.py:400
  23.1 0.0 collective-permute-start.2
  23.1 0.4 collective-permute-start.3
  23.5 1.9 %collective-permute-done.4.diagonal_ref = bf16[128,256]{1,0:T(8,128)(2,1)S(1)} collective-permute-done((bf16[128,256]{1,0:T(8,128)(2,1)S(1)}, bf16[128,256]{1,0:T(8,128)(2,1)S(1)}, u32[]{:S(2)}, u32[]{:S(2)}) %collective-permute-start.4) | collective-permute-done | bytes 65568 | tf_op jit(solution)/shard_map/ppermute | solution.py:400
  25.4 1.2 %collective-permute-done.2.pair_ref.other_ref = bf16[128,256]{1,0:T(8,128)(2,1)S(1)} collective-permute-done((bf16[128,256]{1,0:T(8,128)(2,1)S(1)}, bf16[128,256]{1,0:T(8,128)(2,1)S(1)}, u32[]{:S(2)}, u32[]{:S(2)}) %collective-permute-start.2) | collective-permute-done | bytes 65568 | tf_op jit(solution)/shard_map/ppermute | solution.py:400
  26.7 0.8 %collective-permute-done.3.across_ref = bf16[128,256]{1,0:T(8,128)(2,1)S(1)} collective-permute-done((bf16[128,256]{1,0:T(8,128)(2,1)S(1)}, bf16[128,256]{1,0:T(8,128)(2,1)S(1)}, u32[]{:S(2)}, u32[]{:S(2)}) %collective-permute-start.3) | collective-permute-done | bytes 65568 | tf_op jit(solution)/shard_map/ppermute | solution.py:400
  27.4 0.4 four_map.1
  27.8 2.2 %collective-permute-start.5 = (bf16[128,256]{1,0:T(8,128)(2,1)S(1)}, bf16[128,256]{1,0:T(8,128)(2,1)S(1)}, u32[]{:S(2)}, u32[]{:S(2)}) collective-permute-start(bf16[128,256]{1,0:T(8,128)(2,1)S(1)} %get-tuple-element.40.own_ref), channel_id=1, source_target_pairs={{0,48},{4,52},{8,56},{12,60},{16,32},{20,36},{24,40},{28,44},{32,1... | collective-permute-start | bytes 196616 | tf_op jit(solution)/shard_map/ppermute | solution.py:400
  30.0 3.1 %collective-permute-done.5.other_ref = bf16[128,256]{1,0:T(8,128)(2,1)S(1)} collective-permute-done((bf16[128,256]{1,0:T(8,128)(2,1)S(1)}, bf16[128,256]{1,0:T(8,128)(2,1)S(1)}, u32[]{:S(2)}, u32[]{:S(2)}) %collective-permute-start.5) | collective-permute-done | bytes 65568 | tf_op jit(solution)/shard_map/ppermute | solution.py:400
  33.1 0.2 far_map.1
  33.3 1.5 %collective-permute-start.6 = (bf16[128,256]{1,0:T(8,128)(2,1)S(1)}, bf16[128,256]{1,0:T(8,128)(2,1)S(1)}, u32[]{:S(2)}, u32[]{:S(2)}) collective-permute-start(bf16[128,256]{1,0:T(8,128)(2,1)S(1)} %get-tuple-element.42.own_ref), channel_id=1, source_target_pairs={{0,64},{4,68},{8,72},{12,76},{16,80},{20,84},{24,88},{28,92},{32,9... | collective-permute-start | bytes 196616 | tf_op jit(solution)/shard_map/ppermute | solution.py:400
  34.8 0.5 inner_outputs.1
  35.3 3.6 %collective-permute-start.9 = (bf16[2,2,256,128]{3,2,1,0:T(8,128)(2,1)S(1)}, bf16[2,2,256,128]{3,2,1,0:T(8,128)(2,1)S(1)}, u32[]{:S(2)}, u32[]{:S(2)}) collective-permute-start(bf16[2,2,256,128]{3,2,1,0:T(8,128)(2,1)S(1)} %get-tuple-element.51), channel_id=1, source_target_pairs={{0,4},{4,0},{8,12},{12,8},{16,20},{20,16},{24,28},{28,24},{32,36},... | collective-permute-start | bytes 786440 | tf_op jit(solution)/shard_map/ppermute | solution.py:400
  38.9 0.0 collective-permute-done.6.other_ref.row_ref
  38.9 0.2 rows_state.1
  39.1 1.9 %collective-permute-start.7 = (bf16[128,128]{1,0:T(8,128)(2,1)S(1)}, bf16[128,128]{1,0:T(8,128)(2,1)S(1)}, u32[]{:S(2)}, u32[]{:S(2)}) collective-permute-start(bf16[128,128]{1,0:T(8,128)(2,1)S(1)} %rows_state.1), channel_id=1, source_target_pairs={{0,192},{4,196},{8,200},{12,204},{16,208},{20,212},{24,216},{28,22... | collective-permute-start | bytes 98312 | tf_op jit(solution)/shard_map/ppermute | solution.py:400
  41.0 0.0 collective-permute-done.14.w_three
  41.0 0.0 collective-permute-done.13.w_one
  41.1 2.7 %collective-permute-start.16 = (bf16[128,2048]{1,0:T(8,128)(2,1)S(1)}, bf16[128,2048]{1,0:T(8,128)(2,1)S(1)}, u32[]{:S(2)}, u32[]{:S(2)}) collective-permute-start(bf16[128,2048]{1,0:T(8,128)(2,1)S(1)} %slice_bitcast_fusion), channel_id=1, source_target_pairs={{0,3},{1,0},{2,1},{3,2},{4,7},{5,4},{6,5},{7,6},{8,11},{9,8},{10,9... | collective-permute-start | bytes 1572872 | tf_op jit(solution)/shard_map/ppermute | solution.py:405
  43.8 0.0 collective-permute-start.15
  43.8 0.0 collective-permute-done.7.rows_ref
  43.8 0.0 copy-start
  43.8 0.4 pair_start.1
  44.2 1.7 %collective-permute-start.8 = (bf16[128,128]{1,0:T(8,128)(2,1)S(1)}, bf16[128,128]{1,0:T(8,128)(2,1)S(1)}, u32[]{:S(2)}, u32[]{:S(2)}) collective-permute-start(bf16[128,128]{1,0:T(8,128)(2,1)S(1)} %get-tuple-element.45), channel_id=1, source_target_pairs={{0,8},{4,12},{8,0},{12,4},{16,24},{20,28},{24,16},{28,20},{32,40},... | collective-permute-start | bytes 98312 | tf_op jit(solution)/shard_map/ppermute | solution.py:400
  46.0 0.0 collective-permute-done.9.both_in
  46.0 1.6 %collective-permute-done.8.other_state = bf16[128,128]{1,0:T(8,128)(2,1)S(1)} collective-permute-done((bf16[128,128]{1,0:T(8,128)(2,1)S(1)}, bf16[128,128]{1,0:T(8,128)(2,1)S(1)}, u32[]{:S(2)}, u32[]{:S(2)}) %collective-permute-start.8) | collective-permute-done | bytes 32800 | tf_op jit(solution)/shard_map/ppermute | solution.py:400
  47.6 0.0 copy-done
  47.6 0.6 finish.1
  48.2 0.1 collective-permute-start.10
  48.3 3.8 %collective-permute-start.11 = (bf16[2,64,256]{2,1,0:T(8,128)(2,1)S(1)}, bf16[2,64,256]{2,1,0:T(8,128)(2,1)S(1)}, u32[]{:S(2)}, u32[]{:S(2)}) collective-permute-start(bf16[2,64,256]{2,1,0:T(8,128)(2,1)S(1)} %get-tuple-element.54), channel_id=1, source_target_pairs={{0,2},{1,3},{2,0},{3,1},{4,6},{5,7},{6,4},{7,5},{8,10},{9,11},{10,... | collective-permute-start | bytes 196616 | tf_op jit(solution)/shard_map/ppermute | solution.py:405
  52.2 0.0 collective-permute-start.12
  52.2 5.0 %collective-permute-done.10.one = bf16[2,64,256]{2,1,0:T(8,128)(2,1)S(1)} collective-permute-done((bf16[2,64,256]{2,1,0:T(8,128)(2,1)S(1)}, bf16[2,64,256]{2,1,0:T(8,128)(2,1)S(1)}, u32[]{:S(2)}, u32[]{:S(2)}) %collective-permute-start.10) | collective-permute-done | bytes 65568 | tf_op jit(solution)/shard_map/ppermute | solution.py:405
  57.2 0.0 collective-permute-done.11.two
  57.2 0.0 collective-permute-done.12.three
  57.2 0.0 collective-permute-done.16.w_two1
  57.2 0.0 collective-permute-done.15.w_two0
  57.2 0.7 %merge.1 = (f32[64,2048]{1,0:T(8,128)S(1)}, bf16[64,2048]{1,0:T(8,128)(2,1)S(1)}) custom-call(bf16[2,64,256]{2,1,0:T(8,128)(2,1)S(1)} %get-tuple-element.52.mine_ref, bf16[2,64,256]{2,1,0:T(8,128)(2,1)S(1)} %collective-permute-done.10.one, bf16[2,64,256]{2,1,0:T(8,128)(2,1)S(1)} %collective-permute-done.11.two, ...), custom_call_target="tpu_custom_call" | custom-call | tf_op jit(solution)/shard_map/merge/pallas_call | solution.py:394
  57.9 5.1 %collective-permute-start.17 = (bf16[64,2048]{1,0:T(8,128)(2,1)S(1)}, bf16[64,2048]{1,0:T(8,128)(2,1)S(1)}, u32[]{:S(2)}, u32[]{:S(2)}) collective-permute-start(bf16[64,2048]{1,0:T(8,128)(2,1)S(1)} %get-tuple-element.60), channel_id=1, source_target_pairs={{0,4},{4,0},{8,12},{12,8},{16,20},{20,16},{24,28},{28,24},{32,36},... | collective-permute-start | bytes 786440 | tf_op jit(solution)/shard_map/ppermute | solution.py:400
  63.0 1.2 %collective-permute-done.17 = bf16[64,2048]{1,0:T(8,128)(2,1)S(1)} collective-permute-done((bf16[64,2048]{1,0:T(8,128)(2,1)S(1)}, bf16[64,2048]{1,0:T(8,128)(2,1)S(1)}, u32[]{:S(2)}, u32[]{:S(2)}) %collective-permute-start.17) | collective-permute-done | bytes 262176 | tf_op jit(solution)/shard_map/ppermute | solution.py:400
  64.2 0.8 %add_convert_fusion = bf16[64,2048]{1,0:T(8,128)(2,1)} fusion(f32[64,2048]{1,0:T(8,128)S(1)} %get-tuple-element.59, bf16[64,2048]{1,0:T(8,128)(2,1)S(1)} %collective-permute-done.17), kind=kLoop, calls=%fused_computation | loop fusion | flops 393216 | bytes 1048576 | tf_op jit(solution)/shard_map/convert_element_type | solution.py:438
  (2 shorter events, 0.1 us)
Async XLA Ops:
  0.8 10.5 %copy-start.1 = (f32[3,4,512]{2,1,0:T(4,128)S(1)}, f32[3,4,512]{2,1,0:T(4,128)}, u32[]{:S(2)}) copy-start(f32[3,4,512]{2,1,0:T(4,128)} %conv_ref.1) | copy-start | bytes 73732
  0.8 10.5 %copy-start.2 = (f32[4]{0:T(128)S(1)}, f32[4]{0:T(128)}, u32[]{:S(2)}) copy-start(f32[4]{0:T(128)} %param.11) | copy-start | bytes 52
  0.8 10.5 %collective-permute-start = (bf16[8,2048]{1,0:T(8,128)(2,1)S(1)}, bf16[8,2048]{1,0:T(8,128)(2,1)S(1)}, u32[]{:S(2)}, u32[]{:S(2)}) collective-permute-start(bf16[8,2048]{1,0:T(8,128)(2,1)S(1)} %slice.9), channel_id=1, source_target_pairs={{0,4},{4,8},{8,12},{12,16},{16,20},{20,24},{24,28},{28,32},{32,36}... | collective-permute-start | bytes 98312 | tf_op jit(solution)/shard_map/ppermute | solution.py:405
  8.4 32.5 %collective-permute-start.14 = (bf16[2,128,2048]{2,1,0:T(8,128)(2,1)S(1)}, bf16[2,128,2048]{2,1,0:T(8,128)(2,1)S(1)}, u32[]{:S(2)}, u32[]{:S(2)}) collective-permute-start(bf16[2,128,2048]{2,1,0:T(8,128)(2,1)S(1)} %get-tuple-element.56.w_own), channel_id=1, source_target_pairs={{0,3},{1,0},{2,1},{3,2},{4,7},{5,4},{6,5},{7,6},{8,11},{9,8},{10,9... | collective-permute-start | bytes 3145736 | tf_op jit(solution)/shard_map/ppermute | solution.py:405
  11.2 29.7 %collective-permute-start.13 = (bf16[2,128,2048]{2,1,0:T(8,128)(2,1)S(1)}, bf16[2,128,2048]{2,1,0:T(8,128)(2,1)S(1)}, u32[]{:S(2)}, u32[]{:S(2)}) collective-permute-start(bf16[2,128,2048]{2,1,0:T(8,128)(2,1)S(1)} %get-tuple-element.56.w_own), channel_id=1, source_target_pairs={{0,1},{1,2},{2,3},{3,0},{4,5},{5,6},{6,7},{7,4},{8,9},{9,10},{10,1... | collective-permute-start | bytes 3145736 | tf_op jit(solution)/shard_map/ppermute | solution.py:405
  15.8 1.4 %collective-permute-start.1 = (bf16[2,128,256]{2,1,0:T(8,128)(2,1)S(1)}, bf16[2,128,256]{2,1,0:T(8,128)(2,1)S(1)}, u32[]{:S(2)}, u32[]{:S(2)}) collective-permute-start(bf16[2,128,256]{2,1,0:T(8,128)(2,1)S(1)} %get-tuple-element.37), channel_id=1, source_target_pairs={{0,4},{4,0},{8,12},{12,8},{16,20},{20,16},{24,28},{28,24},{32,36},... | collective-permute-start | bytes 393224 | tf_op jit(solution)/shard_map/ppermute | solution.py:400
  17.5 8.0 %collective-permute-start.4 = (bf16[128,256]{1,0:T(8,128)(2,1)S(1)}, bf16[128,256]{1,0:T(8,128)(2,1)S(1)}, u32[]{:S(2)}, u32[]{:S(2)}) collective-permute-start(bf16[128,256]{1,0:T(8,128)(2,1)S(1)} %get-tuple-element.39), channel_id=1, source_target_pairs={{0,24},{4,28},{8,16},{12,20},{16,8},{20,12},{24,0},{28,4},{32,56},... | collective-permute-start | bytes 196616 | tf_op jit(solution)/shard_map/ppermute | solution.py:400
  23.1 3.5 %collective-permute-start.2 = (bf16[128,256]{1,0:T(8,128)(2,1)S(1)}, bf16[128,256]{1,0:T(8,128)(2,1)S(1)}, u32[]{:S(2)}, u32[]{:S(2)}) collective-permute-start(bf16[128,256]{1,0:T(8,128)(2,1)S(1)} %get-tuple-element.39), channel_id=1, source_target_pairs={{0,8},{4,12},{8,0},{12,4},{16,24},{20,28},{24,16},{28,20},{32,40},... | collective-permute-start | bytes 196616 | tf_op jit(solution)/shard_map/ppermute | solution.py:400
  23.1 4.3 %collective-permute-start.3 = (bf16[128,256]{1,0:T(8,128)(2,1)S(1)}, bf16[128,256]{1,0:T(8,128)(2,1)S(1)}, u32[]{:S(2)}, u32[]{:S(2)}) collective-permute-start(bf16[128,256]{1,0:T(8,128)(2,1)S(1)} %get-tuple-element.38.own_ref), channel_id=1, source_target_pairs={{0,16},{4,20},{8,24},{12,28},{16,0},{20,4},{24,8},{28,12},{32,48},... | collective-permute-start | bytes 196616 | tf_op jit(solution)/shard_map/ppermute | solution.py:400
  27.8 5.4 %collective-permute-start.5 = (bf16[128,256]{1,0:T(8,128)(2,1)S(1)}, bf16[128,256]{1,0:T(8,128)(2,1)S(1)}, u32[]{:S(2)}, u32[]{:S(2)}) collective-permute-start(bf16[128,256]{1,0:T(8,128)(2,1)S(1)} %get-tuple-element.40.own_ref), channel_id=1, source_target_pairs={{0,48},{4,52},{8,56},{12,60},{16,32},{20,36},{24,40},{28,44},{32,1... | collective-permute-start | bytes 196616 | tf_op jit(solution)/shard_map/ppermute | solution.py:400
  33.3 5.6 %collective-permute-start.6 = (bf16[128,256]{1,0:T(8,128)(2,1)S(1)}, bf16[128,256]{1,0:T(8,128)(2,1)S(1)}, u32[]{:S(2)}, u32[]{:S(2)}) collective-permute-start(bf16[128,256]{1,0:T(8,128)(2,1)S(1)} %get-tuple-element.42.own_ref), channel_id=1, source_target_pairs={{0,64},{4,68},{8,72},{12,76},{16,80},{20,84},{24,88},{28,92},{32,9... | collective-permute-start | bytes 196616 | tf_op jit(solution)/shard_map/ppermute | solution.py:400
  35.3 10.6 %collective-permute-start.9 = (bf16[2,2,256,128]{3,2,1,0:T(8,128)(2,1)S(1)}, bf16[2,2,256,128]{3,2,1,0:T(8,128)(2,1)S(1)}, u32[]{:S(2)}, u32[]{:S(2)}) collective-permute-start(bf16[2,2,256,128]{3,2,1,0:T(8,128)(2,1)S(1)} %get-tuple-element.51), channel_id=1, source_target_pairs={{0,4},{4,0},{8,12},{12,8},{16,20},{20,16},{24,28},{28,24},{32,36},... | collective-permute-start | bytes 786440 | tf_op jit(solution)/shard_map/ppermute | solution.py:400
  39.1 4.7 %collective-permute-start.7 = (bf16[128,128]{1,0:T(8,128)(2,1)S(1)}, bf16[128,128]{1,0:T(8,128)(2,1)S(1)}, u32[]{:S(2)}, u32[]{:S(2)}) collective-permute-start(bf16[128,128]{1,0:T(8,128)(2,1)S(1)} %rows_state.1), channel_id=1, source_target_pairs={{0,192},{4,196},{8,200},{12,204},{16,208},{20,212},{24,216},{28,22... | collective-permute-start | bytes 98312 | tf_op jit(solution)/shard_map/ppermute | solution.py:400
  41.1 16.1 %collective-permute-start.16 = (bf16[128,2048]{1,0:T(8,128)(2,1)S(1)}, bf16[128,2048]{1,0:T(8,128)(2,1)S(1)}, u32[]{:S(2)}, u32[]{:S(2)}) collective-permute-start(bf16[128,2048]{1,0:T(8,128)(2,1)S(1)} %slice_bitcast_fusion), channel_id=1, source_target_pairs={{0,3},{1,0},{2,1},{3,2},{4,7},{5,4},{6,5},{7,6},{8,11},{9,8},{10,9... | collective-permute-start | bytes 1572872 | tf_op jit(solution)/shard_map/ppermute | solution.py:405
  43.8 13.4 %collective-permute-start.15 = (bf16[128,2048]{1,0:T(8,128)(2,1)S(1)}, bf16[128,2048]{1,0:T(8,128)(2,1)S(1)}, u32[]{:S(2)}, u32[]{:S(2)}) collective-permute-start(bf16[128,2048]{1,0:T(8,128)(2,1)S(1)} %slice_bitcast_fusion.1), channel_id=1, source_target_pairs={{0,1},{1,2},{2,3},{3,0},{4,5},{5,6},{6,7},{7,4},{8,9},{9,10},{10,1... | collective-permute-start | bytes 1572872 | tf_op jit(solution)/shard_map/ppermute | solution.py:405
  43.8 3.8 %copy-start = (f32[512]{0:T(512)S(1)}, f32[512]{0:T(512)}, u32[]{:S(2)}) copy-start(f32[512]{0:T(512)} %param.12) | copy-start | bytes 6148
  44.2 3.3 %collective-permute-start.8 = (bf16[128,128]{1,0:T(8,128)(2,1)S(1)}, bf16[128,128]{1,0:T(8,128)(2,1)S(1)}, u32[]{:S(2)}, u32[]{:S(2)}) collective-permute-start(bf16[128,128]{1,0:T(8,128)(2,1)S(1)} %get-tuple-element.45), channel_id=1, source_target_pairs={{0,8},{4,12},{8,0},{12,4},{16,24},{20,28},{24,16},{28,20},{32,40},... | collective-permute-start | bytes 98312 | tf_op jit(solution)/shard_map/ppermute | solution.py:400
  48.2 8.9 %collective-permute-start.10 = (bf16[2,64,256]{2,1,0:T(8,128)(2,1)S(1)}, bf16[2,64,256]{2,1,0:T(8,128)(2,1)S(1)}, u32[]{:S(2)}, u32[]{:S(2)}) collective-permute-start(bf16[2,64,256]{2,1,0:T(8,128)(2,1)S(1)} %get-tuple-element.53), channel_id=1, source_target_pairs={{0,1},{1,2},{2,3},{3,0},{4,5},{5,6},{6,7},{7,4},{8,9},{9,10},{10,1... | collective-permute-start | bytes 196616 | tf_op jit(solution)/shard_map/ppermute | solution.py:405
  48.3 8.8 %collective-permute-start.11 = (bf16[2,64,256]{2,1,0:T(8,128)(2,1)S(1)}, bf16[2,64,256]{2,1,0:T(8,128)(2,1)S(1)}, u32[]{:S(2)}, u32[]{:S(2)}) collective-permute-start(bf16[2,64,256]{2,1,0:T(8,128)(2,1)S(1)} %get-tuple-element.54), channel_id=1, source_target_pairs={{0,2},{1,3},{2,0},{3,1},{4,6},{5,7},{6,4},{7,5},{8,10},{9,11},{10,... | collective-permute-start | bytes 196616 | tf_op jit(solution)/shard_map/ppermute | solution.py:405
  52.2 5.0 %collective-permute-start.12 = (bf16[2,64,256]{2,1,0:T(8,128)(2,1)S(1)}, bf16[2,64,256]{2,1,0:T(8,128)(2,1)S(1)}, u32[]{:S(2)}, u32[]{:S(2)}) collective-permute-start(bf16[2,64,256]{2,1,0:T(8,128)(2,1)S(1)} %get-tuple-element.55), channel_id=1, source_target_pairs={{0,3},{1,0},{2,1},{3,2},{4,7},{5,4},{6,5},{7,6},{8,11},{9,8},{10,9... | collective-permute-start | bytes 196616 | tf_op jit(solution)/shard_map/ppermute | solution.py:405
  57.9 6.3 %collective-permute-start.17 = (bf16[64,2048]{1,0:T(8,128)(2,1)S(1)}, bf16[64,2048]{1,0:T(8,128)(2,1)S(1)}, u32[]{:S(2)}, u32[]{:S(2)}) collective-permute-start(bf16[64,2048]{1,0:T(8,128)(2,1)S(1)} %get-tuple-element.60), channel_id=1, source_target_pairs={{0,4},{4,0},{8,12},{12,8},{16,20},{20,16},{24,28},{28,24},{32,36},... | collective-permute-start | bytes 786440 | tf_op jit(solution)/shard_map/ppermute | solution.py:400

commit v9 on v8

--- a/solution.py
+++ b/solution.py
@@ -1,3 +1,5 @@
+import functools
+
 import jax
 import jax.numpy as jnp
 from jax import lax
@@ -115,13 +117,14 @@
 
 def inverse_pairs(systems):
     row, wide = grid_index(BLOCK, 2 * BLOCK)
-    column = wide % BLOCK
+    column = wide & (BLOCK - 1)
     left = wide < BLOCK
     eye = jnp.where(row == column, 1.0, 0.0).astype(f32)
 
+    apart = row ^ column
+
     def below(size):
-        same = (row // (2 * size)) == (column // (2 * size))
-        return same & ((row % (2 * size)) >= size) & ((column % (2 * size)) < size)
+        return (apart >= size) & (apart < 2 * size)
 
     found = [eye - jnp.where(below(1), system, 0.0) for system in systems]
     size = 2
@@ -147,9 +150,21 @@
     return [x - eye for x in fixed]
 
 
+def conv_silu(padded, taps, lanes, length):
+    total = jnp.zeros((length, DK), f32)
+    for j in range(4):
+        start = EDGE - 3 + j
+        total = total + taps[j : j + 1, lanes] * padded[start : start + length, lanes]
+    return total / (1.0 + jnp.exp(-total))
+
+
+def unit_rows(x):
+    return x * lax.rsqrt(jnp.sum(x * x, axis=-1, keepdims=True) + EPS)
+
+
 def local_kernel(
     proj_ref, w_ref, edge_ref, conv_ref, logits_ref, bias_ref,
-    queries_ref, keys_t_ref, uw_ref, keep_ref, send_ref, padded, maps
+    edge_out_ref, keys_t_ref, uw_ref, keep_ref, send_ref, padded, maps
 ):
     length = proj_ref.shape[1]
     heads = logits_ref.shape[1]
@@ -158,24 +173,21 @@
     first = lax.axis_index("ctx") == 0
     for s in range(3):
         edge = dot(edge_ref[...], w_ref[s]).astype(bf16).astype(f32)
-        padded[s, :EDGE] = jnp.where(first, jnp.zeros_like(edge), edge)
-        padded[s, EDGE:] = proj_ref[s].astype(f32)
+        edge = jnp.where(first, jnp.zeros_like(edge), edge)
+        if s == 0:
+            edge_out_ref[...] = edge
+        else:
+            padded[s - 1, :EDGE] = edge
+            padded[s - 1, EDGE:] = proj_ref[s].astype(f32)
     row, column = grid_index(length, length)
     strict = row > column
     systems, corners, right, keys_t = [], [], [], []
     for h in range(heads):
         lanes = slice(h * DK, (h + 1) * DK)
-        mixed = []
-        for s in range(3):
-            total = jnp.zeros((length, DK), f32)
-            for j in range(4):
-                start = EDGE - 3 + j
-                total = total + conv_ref[s, j : j + 1, lanes] * padded[s, start : start + length, lanes]
-            mixed.append(total / (1.0 + jnp.exp(-total)))
-        query, key, value = mixed
-        query = query * lax.rsqrt(jnp.sum(query * query, axis=-1, keepdims=True) + EPS)
-        key = key * lax.rsqrt(jnp.sum(key * key, axis=-1, keepdims=True) + EPS)
-        queries_ref[h] = query.astype(bf16)
+        key, value = (
+            conv_silu(padded.at[s - 1], conv_ref.at[s], lanes, length) for s in (1, 2)
+        )
+        key = unit_rows(key)
         small = key.astype(bf16)
         small_t = key.T.astype(bf16)
         keys_t_ref[h] = small_t
@@ -212,13 +224,13 @@
         in_specs=whole(6),
         out_specs=whole(5),
         out_shape=[
-            shape((heads, length, DK), bf16),
+            shape((EDGE, columns), f32),
             shape((heads, DK, length), bf16),
             shape((heads, length, 2 * DK), bf16),
             two, two,
         ],
         scratch_shapes=[
-            pltpu.VMEM((3, EDGE + length, columns), f32),
+            pltpu.VMEM((2, EDGE + length, columns), f32),
             pltpu.VMEM((heads, DK, 2 * DK), bf16),
         ],
         compiler_params=params(),
@@ -227,8 +239,15 @@
     )(projected, weights, edge, conv_weight, logits, beta_bias[None, :])
 
 
-def inner_kernel(queries_ref, keys_t_ref, uw_ref, base_ref, gate_ref, both_out):
-    length = queries_ref.shape[1]
+def inner_kernel(
+    proj_ref, edge_ref, conv_ref, keys_t_ref, uw_ref, base_ref, gate_ref, both_out, padded, queries
+):
+    length = proj_ref.shape[1]
+    padded[:EDGE] = edge_ref[...]
+    padded[EDGE:] = proj_ref[0].astype(f32)
+    for h in range(4):
+        lanes = slice(h * DK, (h + 1) * DK)
+        queries[h] = unit_rows(conv_silu(padded, conv_ref.at[0], lanes, length)).astype(bf16)
     row, column = grid_index(length, length)
     core = bit(1)
     for j in range(2):
@@ -236,28 +255,33 @@
             (2 * j + core, base_ref.at[j], gate_ref.at[j]),
             (2 * j + 1 - core, both_out.at[0, j], both_out.at[1, j]),
         ):
-            query = queries_ref[h]
+            query = queries[h]
             scores = jnp.where(row >= column, dot(query, keys_t_ref[h]), 0.0).astype(bf16)
             both = dot(scores, uw_ref[h])
             base[...] = both[:, :DK].astype(base.dtype)
             gate[...] = (query.astype(f32) - both[:, DK:]).astype(bf16)
 
 
-def inner_outputs(queries, keys_t, uw):
-    heads, length, _ = queries.shape
+def inner_outputs(projected, edge, conv_weight, keys_t, uw):
+    length, columns = projected.shape[1:]
+    heads = keys_t.shape[0]
     outs = [shape((2, length, DK), f32), shape((2, length, DK), bf16)]
     outs.append(shape((2, 2, length, DK), bf16))
     return pl.pallas_call(
         inner_kernel,
-        in_specs=whole(3),
+        in_specs=whole(5),
         out_specs=whole(3),
         out_shape=outs,
+        scratch_shapes=[
+            pltpu.VMEM((EDGE + length, columns), f32),
+            pltpu.VMEM((heads, length, DK), bf16),
+        ],
         compiler_params=params(),
         cost_estimate=pl.CostEstimate(
             flops=2 * heads * length * length * 3 * DK, bytes_accessed=2 << 20, transcendentals=0
         ),
         name="inner_outputs",
-    )(queries, keys_t, uw)
+    )(projected, edge, conv_weight, keys_t, uw)
 
 
 def then(earlier, later):
@@ -343,7 +367,7 @@
 
 def finish_kernel(
     own_state, other_state, own_maps, other_maps, base_ref, gate_ref, both_in, gain_ref,
-    mine_ref, one, two, three, normed
+    mine_ref, one, three, two, normed
 ):
     late, upper = bit(1) == 1, bit(2) == 1
     core = bit(1)
@@ -361,7 +385,7 @@
             scale = lax.rsqrt(jnp.mean(heads_out * heads_out, axis=-1, keepdims=True) + EPS)
             normed[slot, :, j * DK : (j + 1) * DK] = (heads_out * scale * gain).astype(bf16)
     rows = mine_ref.shape[1]
-    for s, ref in enumerate((mine_ref, one, two, three)):
+    for s, ref in ((0, mine_ref), (1, one), (3, three), (2, two)):
         start = pl.multiple_of((here + s) % 4 * rows, rows)
         for slot in range(2):
             ref[slot] = normed[slot, pl.ds(start, rows), :]
@@ -376,24 +400,23 @@
 
 
 def merge_kernel(
-    mine_ref, one, two, three, w_own, w_one, w_two0, w_two1, w_three, keep_ref, send_ref
+    mine_ref, one, two, three, w_own, w_one, w_two0, w_two1, w_three, *rest, slot
 ):
-    _, rows, width = mine_ref.shape
+    rows, width = mine_ref.shape[1:]
     total = None
     for ref, weight in ((mine_ref, w_own), (one, w_one), (three, w_three)):
-        term = dot(ref[...].reshape(2 * rows, width), weight[...].reshape(width, -1))
+        term = dot(ref[slot], weight[...].reshape(width, -1))
         total = term if total is None else total + term
     both = jnp.concatenate([w_two0[...], w_two1[...]], axis=0)
-    total = total + dot(two[...].reshape(2 * rows, width), both)
-    keep_ref[...] = total[:rows]
-    send_ref[...] = total[rows:].astype(bf16)
-
-
-def merge(parts, weights):
+    total = total + dot(two[slot], both)
+    out_ref = rest[-1]
+    out_ref[...] = total.astype(out_ref.dtype)
+
+
+def merge(parts, weights, slot, kind, name, cost=None):
     rows, width = parts[0].shape[1], weights[0].shape[-1]
-    return small_call(
-        merge_kernel, [shape((rows, width), f32), shape((rows, width), bf16)], "merge"
-    )(*parts, *weights)
+    kernel = functools.partial(merge_kernel, slot=slot)
+    return small_call(kernel, [shape((rows, width), kind)], name, (), cost)(*parts, *weights)[0]
 
 
 def swapped(x, by):
@@ -409,11 +432,11 @@
     edge = turned(tokens_in[-EDGE:], "ctx", 1)
     projected, weights, logits, w_own = project(tokens_in, w_qkv, beta_weight, w_out)
     w_one, w_three = turned(w_own, "head", 1), turned(w_own, "head", 3)
-    queries, keys_t, uw, maps, send = local_maps(
+    edge, keys_t, uw, maps, send = local_maps(
         projected, weights, edge, conv_weight, logits, beta_bias
     )
     sibling = swapped(send, 1)
-    base, gate, both = inner_outputs(queries, keys_t, uw)
+    base, gate, both = inner_outputs(projected, edge, conv_weight, keys_t, uw)
     inner_in = swapped(both, 1)
     chip, send = small_call(
         chip_kernel, [MAP, MAP], "chip_map", [pltpu.VMEM((2, DK, 2 * DK), bf16)]
@@ -430,12 +453,13 @@
         rows, other_row, before, chip, pair
     )
     back = swapped(send, 2)
-    mine, one, two, three = finish(
+    mine, one, three, two = finish(
         (state, back), (maps, sibling), (base, gate), inner_in, norm_gain
     )
     one, three, two = turned(one, "head", 1), turned(three, "head", 3), turned(two, "head", 2)
-    keep, send = merge([mine, one, two, three], [w_own, w_one, *w_two, w_three])
-    return (keep + swapped(send, 1).astype(f32)).astype(bf16)
+    parts, weights = [mine, one, two, three], [w_own, w_one, *w_two, w_three]
+    arrived = swapped(merge(parts, weights, 1, bf16, "merge_other"), 1)
+    return (merge(parts, weights, 0, f32, "merge_own") + arrived.astype(f32)).astype(bf16)
 
 
 def solution(mesh):

time: 65.1 us -> 65.2 us (level)
  Pallas kernels: 12.4 us -> 13.4 us
    pallas_call x2 -> x3, Pallas kernels: 1.26 us -> 2.78 us  [the longest x2 1.68 us: merge(): small_call(kernel, [shape((rows, width), kind)], name, (), cost)]
    ppermute x10, waiting for transfers between devices: 11.1 us -> 10.2 us  [swapped(): lax.ppermute(x, 'ctx', [(i, i ^ by) for i in range(lax.axis_size('ctx'))])]
  transfers between devices with their start and end apart: 18 -> 18, of which waited for: 8 -> 8; matrix products, arithmetic and copies ran while one was open for 0% -> 0% of each run, Pallas kernels for 18% -> 19%
where the time goes in v9:
time: 65.2 us; the launch traced here: 65.1 us
  starting transfers between devices  34.1 us (52%)
  waiting for transfers between devices  15.8 us (24%)
  Pallas kernels  13.4 us (21%)
  local copies, waits for them, and re-layouts  0.84 us (1%)
  other arithmetic  0.75 us (1%)
    ppermute x10, starting transfers between devices, swapped(): lax.ppermute(x, 'ctx', [(i, i ^ by) for i in range(lax.axis_size('ctx'))])  21.6 us
    ppermute x8, starting transfers between devices, turned(): return lax.ppermute(x, axis, [(i, (i + by) % count) for i in range(count)])  12.5 us
    ppermute x10, waiting for transfers between devices, swapped(): lax.ppermute(x, 'ctx', [(i, i ^ by) for i in range(lax.axis_size('ctx'))])  10.2 us
    ppermute x8, waiting for transfers between devices, turned(): return lax.ppermute(x, axis, [(i, (i + by) % count) for i in range(count)])  5.6 us
    pallas_call x1, Pallas kernels, project(): pl.pallas_call(project_kernel, in_specs=[pl.BlockSpec(memory_space=pltpu....  4.62 us
    pallas_call x1, Pallas kernels, local_maps(): pl.pallas_call(local_kernel, in_specs=whole(6), out_specs=whole(5), out_s...  4.02 us
    pallas_call x2, Pallas kernels, merge(): small_call(kernel, [shape((rows, width), kind)], name, (), cost)  1.68 us
  transfers between devices with their start and end apart: 18, of which 8 were waited for; matrix products, arithmetic and copies ran while one was open for 0% of the time, Pallas kernels for 19%

profile of v9, /device:TPU:1, one launch (start us, length us, event | category | flops | bytes accessed | tf_op | source)
XLA Modules:
  0.0 65.1 jit_solution(1265069009743552271)
XLA Ops:
  0.0 0.8 %slice.9 = bf16[8,2048]{1,0:T(8,128)(2,1)S(1)} slice(bf16[256,2048]{1,0:T(8,128)(2,1)} %tokens_hbm.1), slice={[248:256], [0:2048]} | slice | bytes 65536 | tf_op jit(solution)/shard_map/slice | solution.py:432
  0.8 0.0 copy-start
  0.8 0.0 copy-start.2
  0.8 3.0 %collective-permute-start = (bf16[8,2048]{1,0:T(8,128)(2,1)S(1)}, bf16[8,2048]{1,0:T(8,128)(2,1)S(1)}, u32[]{:S(2)}, u32[]{:S(2)}) collective-permute-start(bf16[8,2048]{1,0:T(8,128)(2,1)S(1)} %slice.9), channel_id=1, source_target_pairs={{0,4},{4,8},{8,12},{12,16},{16,20},{20,24},{24,28},{28,32},{32,36}... | collective-permute-start | bytes 98312 | tf_op jit(solution)/shard_map/ppermute | solution.py:428
  3.8 4.6 %project.1 = (bf16[3,256,512]{2,1,0:T(8,128)(2,1)S(1)}, bf16[3,2048,512]{2,1,0:T(8,128)(2,1)S(1)}, f32[256,4]{1,0:T(8,128)S(1)}, bf16[2,128,2048]{2,1,0:T(8,128)(2,1)S(1)}) custom-call(bf16[256,2048]{1,0:T(8,128)(2,1)} %tokens_hbm.1, bf16[3,2048,512]{2,1,0:T(8,128)(2,1)} %w_hbm.1, bf16[4,2048]{1,0:T(4,128)(2,1)} %beta_w_hbm.1, bf16[512,2048]{1,0:T(8,128)(2,1)} %w_out_hbm.1), custom_call_target="tpu_custom_call" | custom-call | flops 60000002048 | bytes 1048576 | tf_op jit(solution)/shard_map/project/pallas_call | solution.py:85
  8.4 2.8 %collective-permute-start.14 = (bf16[2,128,2048]{2,1,0:T(8,128)(2,1)S(1)}, bf16[2,128,2048]{2,1,0:T(8,128)(2,1)S(1)}, u32[]{:S(2)}, u32[]{:S(2)}) collective-permute-start(bf16[2,128,2048]{2,1,0:T(8,128)(2,1)S(1)} %get-tuple-element.54.w_own), channel_id=1, source_target_pairs={{0,3},{1,0},{2,1},{3,2},{4,7},{5,4},{6,5},{7,6},{8,11},{9,8},{10,9... | collective-permute-start | bytes 3145736 | tf_op jit(solution)/shard_map/ppermute | solution.py:428
  11.2 0.0 collective-permute-start.13
  11.2 0.0 collective-permute-done.edge_ref
  11.2 0.0 copy-done
  11.2 0.0 copy-done.2
  11.3 4.0 %local_maps.1 = (f32[8,512]{1,0:T(8,128)S(1)}, bf16[4,128,256]{2,1,0:T(8,128)(2,1)S(1)}, bf16[4,256,256]{2,1,0:T(8,128)(2,1)S(1)}, bf16[2,128,256]{2,1,0:T(8,128)(2,1)S(1)}, bf16[2,128,256]{2,1,0:T(8,128)(2,1)S(1)}) custom-call(bf16[3,256,512]{2,1,0:T(8,128)(2,1)S(1)} %get-tuple-element.31.proj_ref, bf16[3,2048,512]{2,1,0:T(8,128)(2,1)S(1)} %get-tuple-element.32.w_ref, ...), custom_call_target="tpu_custom_call" | custom-call | flops 60000002048 | bytes 1048576 | tf_op jit(solution)/shard_map/local_maps/pallas_call | solution.py:222
  15.3 0.2 collective-permute-start.1
  15.5 1.3 %collective-permute-done.1.other_ref.other_maps = bf16[2,128,256]{2,1,0:T(8,128)(2,1)S(1)} collective-permute-done((bf16[2,128,256]{2,1,0:T(8,128)(2,1)S(1)}, bf16[2,128,256]{2,1,0:T(8,128)(2,1)S(1)}, u32[]{:S(2)}, u32[]{:S(2)}) %collective-permute-start.1) | collective-permute-done | bytes 131104 | tf_op jit(solution)/shard_map/ppermute | solution.py:423
  16.7 0.2 chip_map.1
  17.0 5.6 %collective-permute-start.4 = (bf16[128,256]{1,0:T(8,128)(2,1)S(1)}, bf16[128,256]{1,0:T(8,128)(2,1)S(1)}, u32[]{:S(2)}, u32[]{:S(2)}) collective-permute-start(bf16[128,256]{1,0:T(8,128)(2,1)S(1)} %get-tuple-element.37), channel_id=1, source_target_pairs={{0,24},{4,28},{8,16},{12,20},{16,8},{20,12},{24,0},{28,4},{32,56},... | collective-permute-start | bytes 196616 | tf_op jit(solution)/shard_map/ppermute | solution.py:423
  22.6 0.0 collective-permute-start.2
  22.6 0.4 collective-permute-start.3
  23.0 1.9 %collective-permute-done.4.diagonal_ref = bf16[128,256]{1,0:T(8,128)(2,1)S(1)} collective-permute-done((bf16[128,256]{1,0:T(8,128)(2,1)S(1)}, bf16[128,256]{1,0:T(8,128)(2,1)S(1)}, u32[]{:S(2)}, u32[]{:S(2)}) %collective-permute-start.4) | collective-permute-done | bytes 65568 | tf_op jit(solution)/shard_map/ppermute | solution.py:423
  24.9 1.2 %collective-permute-done.2.pair_ref.other_ref = bf16[128,256]{1,0:T(8,128)(2,1)S(1)} collective-permute-done((bf16[128,256]{1,0:T(8,128)(2,1)S(1)}, bf16[128,256]{1,0:T(8,128)(2,1)S(1)}, u32[]{:S(2)}, u32[]{:S(2)}) %collective-permute-start.2) | collective-permute-done | bytes 65568 | tf_op jit(solution)/shard_map/ppermute | solution.py:423
  26.1 0.8 %collective-permute-done.3.across_ref = bf16[128,256]{1,0:T(8,128)(2,1)S(1)} collective-permute-done((bf16[128,256]{1,0:T(8,128)(2,1)S(1)}, bf16[128,256]{1,0:T(8,128)(2,1)S(1)}, u32[]{:S(2)}, u32[]{:S(2)}) %collective-permute-start.3) | collective-permute-done | bytes 65568 | tf_op jit(solution)/shard_map/ppermute | solution.py:423
  26.9 0.4 four_map.1
  27.3 2.2 %collective-permute-start.5 = (bf16[128,256]{1,0:T(8,128)(2,1)S(1)}, bf16[128,256]{1,0:T(8,128)(2,1)S(1)}, u32[]{:S(2)}, u32[]{:S(2)}) collective-permute-start(bf16[128,256]{1,0:T(8,128)(2,1)S(1)} %get-tuple-element.38.own_ref), channel_id=1, source_target_pairs={{0,48},{4,52},{8,56},{12,60},{16,32},{20,36},{24,40},{28,44},{32,1... | collective-permute-start | bytes 196616 | tf_op jit(solution)/shard_map/ppermute | solution.py:423
  29.5 3.1 %collective-permute-done.5.other_ref = bf16[128,256]{1,0:T(8,128)(2,1)S(1)} collective-permute-done((bf16[128,256]{1,0:T(8,128)(2,1)S(1)}, bf16[128,256]{1,0:T(8,128)(2,1)S(1)}, u32[]{:S(2)}, u32[]{:S(2)}) %collective-permute-start.5) | collective-permute-done | bytes 65568 | tf_op jit(solution)/shard_map/ppermute | solution.py:423
  32.6 0.2 far_map.1
  32.8 1.5 %collective-permute-start.6 = (bf16[128,256]{1,0:T(8,128)(2,1)S(1)}, bf16[128,256]{1,0:T(8,128)(2,1)S(1)}, u32[]{:S(2)}, u32[]{:S(2)}) collective-permute-start(bf16[128,256]{1,0:T(8,128)(2,1)S(1)} %get-tuple-element.40.own_ref), channel_id=1, source_target_pairs={{0,64},{4,68},{8,72},{12,76},{16,80},{20,84},{24,88},{28,92},{32,9... | collective-permute-start | bytes 196616 | tf_op jit(solution)/shard_map/ppermute | solution.py:423
  34.3 1.1 %inner_outputs.1 = (f32[2,256,128]{2,1,0:T(8,128)S(1)}, bf16[2,256,128]{2,1,0:T(8,128)(2,1)S(1)}, bf16[2,2,256,128]{3,2,1,0:T(8,128)(2,1)S(1)}) custom-call(bf16[3,256,512]{2,1,0:T(8,128)(2,1)S(1)} %get-tuple-element.31.proj_ref, f32[8,512]{1,0:T(8,128)S(1)} %get-tuple-element.44.edge_ref, f32[3,4,512]{2,1,0:T(4,128)S(1)} %copy-done, ...), custom_call_target="tpu_custom_call" | custom-call | flops 201326592 | bytes 2097152 | tf_op jit(solution)/shard_map/inner_outputs/pallas_call | solution.py:270
  35.4 3.6 %collective-permute-start.9 = (bf16[2,2,256,128]{3,2,1,0:T(8,128)(2,1)S(1)}, bf16[2,2,256,128]{3,2,1,0:T(8,128)(2,1)S(1)}, u32[]{:S(2)}, u32[]{:S(2)}) collective-permute-start(bf16[2,2,256,128]{3,2,1,0:T(8,128)(2,1)S(1)} %get-tuple-element.49), channel_id=1, source_target_pairs={{0,4},{4,0},{8,12},{12,8},{16,20},{20,16},{24,28},{28,24},{32,36},... | collective-permute-start | bytes 786440 | tf_op jit(solution)/shard_map/ppermute | solution.py:423
  39.0 0.0 collective-permute-done.6.other_ref.row_ref
  39.0 0.2 rows_state.1
  39.1 1.9 %collective-permute-start.7 = (bf16[128,128]{1,0:T(8,128)(2,1)S(1)}, bf16[128,128]{1,0:T(8,128)(2,1)S(1)}, u32[]{:S(2)}, u32[]{:S(2)}) collective-permute-start(bf16[128,128]{1,0:T(8,128)(2,1)S(1)} %rows_state.1), channel_id=1, source_target_pairs={{0,192},{4,196},{8,200},{12,204},{16,208},{20,212},{24,216},{28,22... | collective-permute-start | bytes 98312 | tf_op jit(solution)/shard_map/ppermute | solution.py:423
  41.0 0.0 collective-permute-done.14.w_three
  41.0 0.0 collective-permute-done.13.w_one
  41.1 2.7 %collective-permute-start.16 = (bf16[128,2048]{1,0:T(8,128)(2,1)S(1)}, bf16[128,2048]{1,0:T(8,128)(2,1)S(1)}, u32[]{:S(2)}, u32[]{:S(2)}) collective-permute-start(bf16[128,2048]{1,0:T(8,128)(2,1)S(1)} %slice_bitcast_fusion), channel_id=1, source_target_pairs={{0,3},{1,0},{2,1},{3,2},{4,7},{5,4},{6,5},{7,6},{8,11},{9,8},{10,9... | collective-permute-start | bytes 1572872 | tf_op jit(solution)/shard_map/ppermute | solution.py:428
  43.8 0.0 collective-permute-start.15
  43.8 0.0 collective-permute-done.7.rows_ref
  43.8 0.0 copy-start.1
  43.8 0.4 pair_start.1
  44.3 1.7 %collective-permute-start.8 = (bf16[128,128]{1,0:T(8,128)(2,1)S(1)}, bf16[128,128]{1,0:T(8,128)(2,1)S(1)}, u32[]{:S(2)}, u32[]{:S(2)}) collective-permute-start(bf16[128,128]{1,0:T(8,128)(2,1)S(1)} %get-tuple-element.43), channel_id=1, source_target_pairs={{0,8},{4,12},{8,0},{12,4},{16,24},{20,28},{24,16},{28,20},{32,40},... | collective-permute-start | bytes 98312 | tf_op jit(solution)/shard_map/ppermute | solution.py:423
  46.0 0.0 collective-permute-done.9.both_in
  46.0 1.6 %collective-permute-done.8.other_state = bf16[128,128]{1,0:T(8,128)(2,1)S(1)} collective-permute-done((bf16[128,128]{1,0:T(8,128)(2,1)S(1)}, bf16[128,128]{1,0:T(8,128)(2,1)S(1)}, u32[]{:S(2)}, u32[]{:S(2)}) %collective-permute-start.8) | collective-permute-done | bytes 32800 | tf_op jit(solution)/shard_map/ppermute | solution.py:423
  47.6 0.0 copy-done.1
  47.6 0.6 finish.1
  48.3 0.1 collective-permute-start.10
  48.4 3.8 %collective-permute-start.11 = (bf16[2,64,256]{2,1,0:T(8,128)(2,1)S(1)}, bf16[2,64,256]{2,1,0:T(8,128)(2,1)S(1)}, u32[]{:S(2)}, u32[]{:S(2)}) collective-permute-start(bf16[2,64,256]{2,1,0:T(8,128)(2,1)S(1)} %get-tuple-element.52), channel_id=1, source_target_pairs={{0,2},{1,3},{2,0},{3,1},{4,6},{5,7},{6,4},{7,5},{8,10},{9,11},{10,... | collective-permute-start | bytes 196616 | tf_op jit(solution)/shard_map/ppermute | solution.py:428
  52.2 0.0 collective-permute-start.12
  52.2 5.6 %collective-permute-done.10.one = bf16[2,64,256]{2,1,0:T(8,128)(2,1)S(1)} collective-permute-done((bf16[2,64,256]{2,1,0:T(8,128)(2,1)S(1)}, bf16[2,64,256]{2,1,0:T(8,128)(2,1)S(1)}, u32[]{:S(2)}, u32[]{:S(2)}) %collective-permute-start.10) | collective-permute-done | bytes 65568 | tf_op jit(solution)/shard_map/ppermute | solution.py:428
  57.8 0.0 collective-permute-done.11.two
  57.8 0.0 collective-permute-done.12.three
  57.8 0.0 collective-permute-done.16.w_two1
  57.8 0.0 collective-permute-done.15.w_two0
  57.8 0.8 %merge_other.1 = bf16[64,2048]{1,0:T(8,128)(2,1)S(1)} custom-call(bf16[2,64,256]{2,1,0:T(8,128)(2,1)S(1)} %get-tuple-element.50.mine_ref, bf16[2,64,256]{2,1,0:T(8,128)(2,1)S(1)} %collective-permute-done.10.one, bf16[2,64,256]{2,1,0:T(8,128)(2,1)S(1)} %collective-permute-done.11.two, bf16[2,64,256]{2,1,0:T(8,128)(2,1)S(1)} %collective-permute-done.12.three, ...), custom_call_target="tpu_custom_call" | custom-call | tf_op jit(solution)/shard_map/merge_other/pallas_call | solution.py:419
  58.7 4.5 %collective-permute-start.17 = (bf16[64,2048]{1,0:T(8,128)(2,1)S(1)}, bf16[64,2048]{1,0:T(8,128)(2,1)S(1)}, u32[]{:S(2)}, u32[]{:S(2)}) collective-permute-start(bf16[64,2048]{1,0:T(8,128)(2,1)S(1)} %merge_other.1), channel_id=1, source_target_pairs={{0,4},{4,0},{8,12},{12,8},{16,20},{20,16},{24,28},{28,24},{32,36},... | collective-permute-start | bytes 786440 | tf_op jit(solution)/shard_map/ppermute | solution.py:423
  63.2 0.8 %merge_own.1 = f32[64,2048]{1,0:T(8,128)S(1)} custom-call(bf16[2,64,256]{2,1,0:T(8,128)(2,1)S(1)} %get-tuple-element.50.mine_ref, bf16[2,64,256]{2,1,0:T(8,128)(2,1)S(1)} %collective-permute-done.10.one, bf16[2,64,256]{2,1,0:T(8,128)(2,1)S(1)} %collective-permute-done.11.two, bf16[2,64,256]{2,1,0:T(8,128)(2,1)S(1)} %collective-permute-done.12.three, ...), custom_call_target="tpu_custom_call" | custom-call | tf_op jit(solution)/shard_map/merge_own/pallas_call | solution.py:419
  64.0 0.3 collective-permute-done.17
  64.3 0.8 %add_convert_fusion = bf16[64,2048]{1,0:T(8,128)(2,1)} fusion(f32[64,2048]{1,0:T(8,128)S(1)} %merge_own.1, bf16[64,2048]{1,0:T(8,128)(2,1)S(1)} %collective-permute-done.17), kind=kLoop, calls=%fused_computation | loop fusion | flops 393216 | bytes 1048576 | tf_op jit(solution)/shard_map/convert_element_type | solution.py:462
  (2 shorter events, 0.1 us)
Async XLA Ops:
  0.8 10.5 %copy-start = (f32[3,4,512]{2,1,0:T(4,128)S(1)}, f32[3,4,512]{2,1,0:T(4,128)}, u32[]{:S(2)}) copy-start(f32[3,4,512]{2,1,0:T(4,128)} %conv_ref.3) | copy-start | bytes 73732
  0.8 10.5 %copy-start.2 = (f32[4]{0:T(128)S(1)}, f32[4]{0:T(128)}, u32[]{:S(2)}) copy-start(f32[4]{0:T(128)} %param.11) | copy-start | bytes 52
  0.8 10.5 %collective-permute-start = (bf16[8,2048]{1,0:T(8,128)(2,1)S(1)}, bf16[8,2048]{1,0:T(8,128)(2,1)S(1)}, u32[]{:S(2)}, u32[]{:S(2)}) collective-permute-start(bf16[8,2048]{1,0:T(8,128)(2,1)S(1)} %slice.9), channel_id=1, source_target_pairs={{0,4},{4,8},{8,12},{12,16},{16,20},{20,24},{24,28},{28,32},{32,36}... | collective-permute-start | bytes 98312 | tf_op jit(solution)/shard_map/ppermute | solution.py:428
  8.4 32.6 %collective-permute-start.14 = (bf16[2,128,2048]{2,1,0:T(8,128)(2,1)S(1)}, bf16[2,128,2048]{2,1,0:T(8,128)(2,1)S(1)}, u32[]{:S(2)}, u32[]{:S(2)}) collective-permute-start(bf16[2,128,2048]{2,1,0:T(8,128)(2,1)S(1)} %get-tuple-element.54.w_own), channel_id=1, source_target_pairs={{0,3},{1,0},{2,1},{3,2},{4,7},{5,4},{6,5},{7,6},{8,11},{9,8},{10,9... | collective-permute-start | bytes 3145736 | tf_op jit(solution)/shard_map/ppermute | solution.py:428
  11.2 29.8 %collective-permute-start.13 = (bf16[2,128,2048]{2,1,0:T(8,128)(2,1)S(1)}, bf16[2,128,2048]{2,1,0:T(8,128)(2,1)S(1)}, u32[]{:S(2)}, u32[]{:S(2)}) collective-permute-start(bf16[2,128,2048]{2,1,0:T(8,128)(2,1)S(1)} %get-tuple-element.54.w_own), channel_id=1, source_target_pairs={{0,1},{1,2},{2,3},{3,0},{4,5},{5,6},{6,7},{7,4},{8,9},{9,10},{10,1... | collective-permute-start | bytes 3145736 | tf_op jit(solution)/shard_map/ppermute | solution.py:428
  15.3 1.4 %collective-permute-start.1 = (bf16[2,128,256]{2,1,0:T(8,128)(2,1)S(1)}, bf16[2,128,256]{2,1,0:T(8,128)(2,1)S(1)}, u32[]{:S(2)}, u32[]{:S(2)}) collective-permute-start(bf16[2,128,256]{2,1,0:T(8,128)(2,1)S(1)} %get-tuple-element.35), channel_id=1, source_target_pairs={{0,4},{4,0},{8,12},{12,8},{16,20},{20,16},{24,28},{28,24},{32,36},... | collective-permute-start | bytes 393224 | tf_op jit(solution)/shard_map/ppermute | solution.py:423
  17.0 8.0 %collective-permute-start.4 = (bf16[128,256]{1,0:T(8,128)(2,1)S(1)}, bf16[128,256]{1,0:T(8,128)(2,1)S(1)}, u32[]{:S(2)}, u32[]{:S(2)}) collective-permute-start(bf16[128,256]{1,0:T(8,128)(2,1)S(1)} %get-tuple-element.37), channel_id=1, source_target_pairs={{0,24},{4,28},{8,16},{12,20},{16,8},{20,12},{24,0},{28,4},{32,56},... | collective-permute-start | bytes 196616 | tf_op jit(solution)/shard_map/ppermute | solution.py:423
  22.6 3.5 %collective-permute-start.2 = (bf16[128,256]{1,0:T(8,128)(2,1)S(1)}, bf16[128,256]{1,0:T(8,128)(2,1)S(1)}, u32[]{:S(2)}, u32[]{:S(2)}) collective-permute-start(bf16[128,256]{1,0:T(8,128)(2,1)S(1)} %get-tuple-element.37), channel_id=1, source_target_pairs={{0,8},{4,12},{8,0},{12,4},{16,24},{20,28},{24,16},{28,20},{32,40},... | collective-permute-start | bytes 196616 | tf_op jit(solution)/shard_map/ppermute | solution.py:423
  22.6 4.3 %collective-permute-start.3 = (bf16[128,256]{1,0:T(8,128)(2,1)S(1)}, bf16[128,256]{1,0:T(8,128)(2,1)S(1)}, u32[]{:S(2)}, u32[]{:S(2)}) collective-permute-start(bf16[128,256]{1,0:T(8,128)(2,1)S(1)} %get-tuple-element.36.own_ref), channel_id=1, source_target_pairs={{0,16},{4,20},{8,24},{12,28},{16,0},{20,4},{24,8},{28,12},{32,48},... | collective-permute-start | bytes 196616 | tf_op jit(solution)/shard_map/ppermute | solution.py:423
  27.3 5.4 %collective-permute-start.5 = (bf16[128,256]{1,0:T(8,128)(2,1)S(1)}, bf16[128,256]{1,0:T(8,128)(2,1)S(1)}, u32[]{:S(2)}, u32[]{:S(2)}) collective-permute-start(bf16[128,256]{1,0:T(8,128)(2,1)S(1)} %get-tuple-element.38.own_ref), channel_id=1, source_target_pairs={{0,48},{4,52},{8,56},{12,60},{16,32},{20,36},{24,40},{28,44},{32,1... | collective-permute-start | bytes 196616 | tf_op jit(solution)/shard_map/ppermute | solution.py:423
  32.8 6.2 %collective-permute-start.6 = (bf16[128,256]{1,0:T(8,128)(2,1)S(1)}, bf16[128,256]{1,0:T(8,128)(2,1)S(1)}, u32[]{:S(2)}, u32[]{:S(2)}) collective-permute-start(bf16[128,256]{1,0:T(8,128)(2,1)S(1)} %get-tuple-element.40.own_ref), channel_id=1, source_target_pairs={{0,64},{4,68},{8,72},{12,76},{16,80},{20,84},{24,88},{28,92},{32,9... | collective-permute-start | bytes 196616 | tf_op jit(solution)/shard_map/ppermute | solution.py:423
  35.4 10.6 %collective-permute-start.9 = (bf16[2,2,256,128]{3,2,1,0:T(8,128)(2,1)S(1)}, bf16[2,2,256,128]{3,2,1,0:T(8,128)(2,1)S(1)}, u32[]{:S(2)}, u32[]{:S(2)}) collective-permute-start(bf16[2,2,256,128]{3,2,1,0:T(8,128)(2,1)S(1)} %get-tuple-element.49), channel_id=1, source_target_pairs={{0,4},{4,0},{8,12},{12,8},{16,20},{20,16},{24,28},{28,24},{32,36},... | collective-permute-start | bytes 786440 | tf_op jit(solution)/shard_map/ppermute | solution.py:423
  39.1 4.7 %collective-permute-start.7 = (bf16[128,128]{1,0:T(8,128)(2,1)S(1)}, bf16[128,128]{1,0:T(8,128)(2,1)S(1)}, u32[]{:S(2)}, u32[]{:S(2)}) collective-permute-start(bf16[128,128]{1,0:T(8,128)(2,1)S(1)} %rows_state.1), channel_id=1, source_target_pairs={{0,192},{4,196},{8,200},{12,204},{16,208},{20,212},{24,216},{28,22... | collective-permute-start | bytes 98312 | tf_op jit(solution)/shard_map/ppermute | solution.py:423
  41.1 16.7 %collective-permute-start.16 = (bf16[128,2048]{1,0:T(8,128)(2,1)S(1)}, bf16[128,2048]{1,0:T(8,128)(2,1)S(1)}, u32[]{:S(2)}, u32[]{:S(2)}) collective-permute-start(bf16[128,2048]{1,0:T(8,128)(2,1)S(1)} %slice_bitcast_fusion), channel_id=1, source_target_pairs={{0,3},{1,0},{2,1},{3,2},{4,7},{5,4},{6,5},{7,6},{8,11},{9,8},{10,9... | collective-permute-start | bytes 1572872 | tf_op jit(solution)/shard_map/ppermute | solution.py:428
  43.8 14.0 %collective-permute-start.15 = (bf16[128,2048]{1,0:T(8,128)(2,1)S(1)}, bf16[128,2048]{1,0:T(8,128)(2,1)S(1)}, u32[]{:S(2)}, u32[]{:S(2)}) collective-permute-start(bf16[128,2048]{1,0:T(8,128)(2,1)S(1)} %slice_bitcast_fusion.1), channel_id=1, source_target_pairs={{0,1},{1,2},{2,3},{3,0},{4,5},{5,6},{6,7},{7,4},{8,9},{9,10},{10,1... | collective-permute-start | bytes 1572872 | tf_op jit(solution)/shard_map/ppermute | solution.py:428
  43.8 3.8 %copy-start.1 = (f32[512]{0:T(512)S(1)}, f32[512]{0:T(512)}, u32[]{:S(2)}) copy-start(f32[512]{0:T(512)} %param.12) | copy-start | bytes 6148
  44.3 3.3 %collective-permute-start.8 = (bf16[128,128]{1,0:T(8,128)(2,1)S(1)}, bf16[128,128]{1,0:T(8,128)(2,1)S(1)}, u32[]{:S(2)}, u32[]{:S(2)}) collective-permute-start(bf16[128,128]{1,0:T(8,128)(2,1)S(1)} %get-tuple-element.43), channel_id=1, source_target_pairs={{0,8},{4,12},{8,0},{12,4},{16,24},{20,28},{24,16},{28,20},{32,40},... | collective-permute-start | bytes 98312 | tf_op jit(solution)/shard_map/ppermute | solution.py:423
  48.3 9.5 %collective-permute-start.10 = (bf16[2,64,256]{2,1,0:T(8,128)(2,1)S(1)}, bf16[2,64,256]{2,1,0:T(8,128)(2,1)S(1)}, u32[]{:S(2)}, u32[]{:S(2)}) collective-permute-start(bf16[2,64,256]{2,1,0:T(8,128)(2,1)S(1)} %get-tuple-element.51), channel_id=1, source_target_pairs={{0,1},{1,2},{2,3},{3,0},{4,5},{5,6},{6,7},{7,4},{8,9},{9,10},{10,1... | collective-permute-start | bytes 196616 | tf_op jit(solution)/shard_map/ppermute | solution.py:428
  48.4 9.4 %collective-permute-start.11 = (bf16[2,64,256]{2,1,0:T(8,128)(2,1)S(1)}, bf16[2,64,256]{2,1,0:T(8,128)(2,1)S(1)}, u32[]{:S(2)}, u32[]{:S(2)}) collective-permute-start(bf16[2,64,256]{2,1,0:T(8,128)(2,1)S(1)} %get-tuple-element.52), channel_id=1, source_target_pairs={{0,2},{1,3},{2,0},{3,1},{4,6},{5,7},{6,4},{7,5},{8,10},{9,11},{10,... | collective-permute-start | bytes 196616 | tf_op jit(solution)/shard_map/ppermute | solution.py:428
  52.2 5.6 %collective-permute-start.12 = (bf16[2,64,256]{2,1,0:T(8,128)(2,1)S(1)}, bf16[2,64,256]{2,1,0:T(8,128)(2,1)S(1)}, u32[]{:S(2)}, u32[]{:S(2)}) collective-permute-start(bf16[2,64,256]{2,1,0:T(8,128)(2,1)S(1)} %get-tuple-element.53), channel_id=1, source_target_pairs={{0,3},{1,0},{2,1},{3,2},{4,7},{5,4},{6,5},{7,6},{8,11},{9,8},{10,9... | collective-permute-start | bytes 196616 | tf_op jit(solution)/shard_map/ppermute | solution.py:428
  58.7 5.7 %collective-permute-start.17 = (bf16[64,2048]{1,0:T(8,128)(2,1)S(1)}, bf16[64,2048]{1,0:T(8,128)(2,1)S(1)}, u32[]{:S(2)}, u32[]{:S(2)}) collective-permute-start(bf16[64,2048]{1,0:T(8,128)(2,1)S(1)} %merge_other.1), channel_id=1, source_target_pairs={{0,4},{4,0},{8,12},{12,8},{16,20},{20,16},{24,28},{28,24},{32,36},... | collective-permute-start | bytes 786440 | tf_op jit(solution)/shard_map/ppermute | solution.py:423

commit v10 on v9

--- a/solution.py
+++ b/solution.py
@@ -1,5 +1,3 @@
-import functools
-
 import jax
 import jax.numpy as jnp
 from jax import lax
@@ -38,6 +36,7 @@
     return jax.ShapeDtypeStruct(dims, kind)
 
 
+SHORT = pl.CostEstimate(flops=4_000_000_000, bytes_accessed=1 << 20, transcendentals=0)
 LONG = pl.CostEstimate(flops=60_000_000_000, bytes_accessed=1 << 20, transcendentals=0)
 
 
@@ -400,23 +399,24 @@
 
 
 def merge_kernel(
-    mine_ref, one, two, three, w_own, w_one, w_two0, w_two1, w_three, *rest, slot
+    mine_ref, one, two, three, w_own, w_one, w_two0, w_two1, w_three, keep_ref, send_ref
 ):
-    rows, width = mine_ref.shape[1:]
+    _, rows, width = mine_ref.shape
     total = None
     for ref, weight in ((mine_ref, w_own), (one, w_one), (three, w_three)):
-        term = dot(ref[slot], weight[...].reshape(width, -1))
+        term = dot(ref[...].reshape(2 * rows, width), weight[...].reshape(width, -1))
         total = term if total is None else total + term
     both = jnp.concatenate([w_two0[...], w_two1[...]], axis=0)
-    total = total + dot(two[slot], both)
-    out_ref = rest[-1]
-    out_ref[...] = total.astype(out_ref.dtype)
-
-
-def merge(parts, weights, slot, kind, name, cost=None):
+    total = total + dot(two[...].reshape(2 * rows, width), both)
+    keep_ref[...] = total[:rows]
+    send_ref[...] = total[rows:].astype(bf16)
+
+
+def merge(parts, weights):
     rows, width = parts[0].shape[1], weights[0].shape[-1]
-    kernel = functools.partial(merge_kernel, slot=slot)
-    return small_call(kernel, [shape((rows, width), kind)], name, (), cost)(*parts, *weights)[0]
+    return small_call(
+        merge_kernel, [shape((rows, width), f32), shape((rows, width), bf16)], "merge"
+    )(*parts, *weights)
 
 
 def swapped(x, by):
@@ -436,20 +436,21 @@
         projected, weights, edge, conv_weight, logits, beta_bias
     )
     sibling = swapped(send, 1)
-    base, gate, both = inner_outputs(projected, edge, conv_weight, keys_t, uw)
-    inner_in = swapped(both, 1)
     chip, send = small_call(
         chip_kernel, [MAP, MAP], "chip_map", [pltpu.VMEM((2, DK, 2 * DK), bf16)]
     )(maps, sibling)
     pair, across, diagonal = swapped(send, 2), swapped(chip, 4), swapped(send, 6)
     four, near = small_call(four_kernel, [MAP, MAP], "four_map")(chip, pair, across, diagonal)
     row, before = small_call(far_kernel, [MAP, MAP], "far_map")(four, swapped(four, 12), near)
+    _, w_one, w_three = lax.optimization_barrier((row, w_one, w_three))
+    w_two = turned(w_one[0], "head", 1), turned(w_three[1], "head", 3)
     other_row = swapped(row, 16)
-    (two_rows,) = small_call(rows_kernel, [STATE], "rows_state")(row, other_row)
-    _, w_one, w_three = lax.optimization_barrier((two_rows, w_one, w_three))
-    w_two = turned(w_one[0], "head", 1), turned(w_three[1], "head", 3)
+    (two_rows,) = small_call(rows_kernel, [STATE], "rows_state", (), LONG)(row, other_row)
+    _, edge = lax.optimization_barrier((two_rows, edge))
+    base, gate, both = inner_outputs(projected, edge, conv_weight, keys_t, uw)
+    inner_in = swapped(both, 1)
     rows = swapped(two_rows, 48)
-    state, send = small_call(pair_start_kernel, [STATE, STATE], "pair_start", (), LONG)(
+    state, send = small_call(pair_start_kernel, [STATE, STATE], "pair_start", (), SHORT)(
         rows, other_row, before, chip, pair
     )
     back = swapped(send, 2)
@@ -457,9 +458,8 @@
         (state, back), (maps, sibling), (base, gate), inner_in, norm_gain
     )
     one, three, two = turned(one, "head", 1), turned(three, "head", 3), turned(two, "head", 2)
-    parts, weights = [mine, one, two, three], [w_own, w_one, *w_two, w_three]
-    arrived = swapped(merge(parts, weights, 1, bf16, "merge_other"), 1)
-    return (merge(parts, weights, 0, f32, "merge_own") + arrived.astype(f32)).astype(bf16)
+    keep, send = merge([mine, one, two, three], [w_own, w_one, *w_two, w_three])
+    return (keep + swapped(send, 1).astype(f32)).astype(bf16)
 
 
 def solution(mesh):

time: 65.2 us -> 63.1 us (0.968)
  starting transfers between devices: 34.1 us -> 31.9 us
  waiting for transfers between devices: 15.8 us -> 16.9 us
  Pallas kernels: 13.4 us -> 12.5 us
    ppermute x8, starting transfers between devices: 12.5 us -> 11.3 us  [turned(): return lax.ppermute(x, axis, [(i, (i + by) % count) for i in range(count)])]
    ppermute x10, starting transfers between devices: 21.6 us -> 20.6 us  [swapped(): lax.ppermute(x, 'ctx', [(i, i ^ by) for i in range(lax.axis_size('ctx'))])]
    pallas_call x4 -> x3, Pallas kernels: 2.27 us -> 1.33 us  [the longest x1 0.75 us: merge(): small_call(merge_kernel, [shape((rows, width), f32), shape((rows, width),...]
    ppermute x10, waiting for transfers between devices: 10.2 us -> 11.1 us  [swapped(): lax.ppermute(x, 'ctx', [(i, i ^ by) for i in range(lax.axis_size('ctx'))])]
  transfers between devices with their start and end apart: 18 -> 18, of which waited for: 8 -> 11; matrix products, arithmetic and copies ran while one was open for 0% -> 0% of each run, Pallas kernels for 19% -> 19%
where the time goes in v10:
time: 63.1 us; the launch traced here: 63 us
  starting transfers between devices  31.9 us (51%)
  waiting for transfers between devices  16.9 us (27%)
  Pallas kernels  12.5 us (20%)
  local copies, waits for them, and re-layouts  0.84 us (1%)
  other arithmetic  0.76 us (1%)
    ppermute x10, starting transfers between devices, swapped(): lax.ppermute(x, 'ctx', [(i, i ^ by) for i in range(lax.axis_size('ctx'))])  20.6 us
    ppermute x8, starting transfers between devices, turned(): return lax.ppermute(x, axis, [(i, (i + by) % count) for i in range(count)])  11.3 us
    ppermute x10, waiting for transfers between devices, swapped(): lax.ppermute(x, 'ctx', [(i, i ^ by) for i in range(lax.axis_size('ctx'))])  11.1 us
    ppermute x8, waiting for transfers between devices, turned(): return lax.ppermute(x, axis, [(i, (i + by) % count) for i in range(count)])  5.85 us
    pallas_call x1, Pallas kernels, project(): pl.pallas_call(project_kernel, in_specs=[pl.BlockSpec(memory_space=pltpu....  4.62 us
    pallas_call x1, Pallas kernels, local_maps(): pl.pallas_call(local_kernel, in_specs=whole(6), out_specs=whole(5), out_s...  4.02 us
  transfers between devices with their start and end apart: 18, of which 11 were waited for; matrix products, arithmetic and copies ran while one was open for 0% of the time, Pallas kernels for 19%

profile of v10, /device:TPU:1, one launch (start us, length us, event | category | flops | bytes accessed | tf_op | source)
XLA Modules:
  0.0 63.0 jit_solution(3625399614030408133)
XLA Ops:
  0.0 0.8 %slice.9 = bf16[8,2048]{1,0:T(8,128)(2,1)S(1)} slice(bf16[256,2048]{1,0:T(8,128)(2,1)} %tokens_hbm.1), slice={[248:256], [0:2048]} | slice | bytes 65536 | tf_op jit(solution)/shard_map/slice | solution.py:432
  0.8 0.0 copy-start
  0.8 0.0 copy-start.2
  0.8 3.0 %collective-permute-start = (bf16[8,2048]{1,0:T(8,128)(2,1)S(1)}, bf16[8,2048]{1,0:T(8,128)(2,1)S(1)}, u32[]{:S(2)}, u32[]{:S(2)}) collective-permute-start(bf16[8,2048]{1,0:T(8,128)(2,1)S(1)} %slice.9), channel_id=1, source_target_pairs={{0,4},{4,8},{8,12},{12,16},{16,20},{20,24},{24,28},{28,32},{32,36}... | collective-permute-start | bytes 98312 | tf_op jit(solution)/shard_map/ppermute | solution.py:428
  3.8 4.6 %project.1 = (bf16[3,256,512]{2,1,0:T(8,128)(2,1)S(1)}, bf16[3,2048,512]{2,1,0:T(8,128)(2,1)S(1)}, f32[256,4]{1,0:T(8,128)S(1)}, bf16[2,128,2048]{2,1,0:T(8,128)(2,1)S(1)}) custom-call(bf16[256,2048]{1,0:T(8,128)(2,1)} %tokens_hbm.1, bf16[3,2048,512]{2,1,0:T(8,128)(2,1)} %w_hbm.1, bf16[4,2048]{1,0:T(4,128)(2,1)} %beta_w_hbm.1, bf16[512,2048]{1,0:T(8,128)(2,1)} %w_out_hbm.1), custom_call_target="tpu_custom_call" | custom-call | flops 60000002048 | bytes 1048576 | tf_op jit(solution)/shard_map/project/pallas_call | solution.py:84
  8.4 2.8 %collective-permute-start.14 = (bf16[2,128,2048]{2,1,0:T(8,128)(2,1)S(1)}, bf16[2,128,2048]{2,1,0:T(8,128)(2,1)S(1)}, u32[]{:S(2)}, u32[]{:S(2)}) collective-permute-start(bf16[2,128,2048]{2,1,0:T(8,128)(2,1)S(1)} %get-tuple-element.58.w_own), channel_id=1, source_target_pairs={{0,3},{1,0},{2,1},{3,2},{4,7},{5,4},{6,5},{7,6},{8,11},{9,8},{10,9... | collective-permute-start | bytes 3145736 | tf_op jit(solution)/shard_map/ppermute | solution.py:428
  11.2 0.0 collective-permute-start.13
  11.2 0.0 collective-permute-done.edge_ref
  11.2 0.0 copy-done
  11.2 0.0 copy-done.2
  11.3 4.0 %local_maps.1 = (f32[8,512]{1,0:T(8,128)S(1)}, bf16[4,128,256]{2,1,0:T(8,128)(2,1)S(1)}, bf16[4,256,256]{2,1,0:T(8,128)(2,1)S(1)}, bf16[2,128,256]{2,1,0:T(8,128)(2,1)S(1)}, bf16[2,128,256]{2,1,0:T(8,128)(2,1)S(1)}) custom-call(bf16[3,256,512]{2,1,0:T(8,128)(2,1)S(1)} %get-tuple-element.34.proj_ref, bf16[3,2048,512]{2,1,0:T(8,128)(2,1)S(1)} %get-tuple-element.35.w_ref, ...), custom_call_target="tpu_custom_call" | custom-call | flops 60000002048 | bytes 1048576 | tf_op jit(solution)/shard_map/local_maps/pallas_call | solution.py:221
  15.3 0.2 collective-permute-start.1
  15.5 1.3 %collective-permute-done.1.other_ref.other_maps = bf16[2,128,256]{2,1,0:T(8,128)(2,1)S(1)} collective-permute-done((bf16[2,128,256]{2,1,0:T(8,128)(2,1)S(1)}, bf16[2,128,256]{2,1,0:T(8,128)(2,1)S(1)}, u32[]{:S(2)}, u32[]{:S(2)}) %collective-permute-start.1) | collective-permute-done | bytes 131104 | tf_op jit(solution)/shard_map/ppermute | solution.py:423
  16.7 0.2 chip_map.1
  17.0 5.6 %collective-permute-start.4 = (bf16[128,256]{1,0:T(8,128)(2,1)S(1)}, bf16[128,256]{1,0:T(8,128)(2,1)S(1)}, u32[]{:S(2)}, u32[]{:S(2)}) collective-permute-start(bf16[128,256]{1,0:T(8,128)(2,1)S(1)} %get-tuple-element.40), channel_id=1, source_target_pairs={{0,24},{4,28},{8,16},{12,20},{16,8},{20,12},{24,0},{28,4},{32,56},... | collective-permute-start | bytes 196616 | tf_op jit(solution)/shard_map/ppermute | solution.py:423
  22.6 0.0 collective-permute-start.2
  22.6 0.4 collective-permute-start.3
  23.0 1.9 %collective-permute-done.4.diagonal_ref = bf16[128,256]{1,0:T(8,128)(2,1)S(1)} collective-permute-done((bf16[128,256]{1,0:T(8,128)(2,1)S(1)}, bf16[128,256]{1,0:T(8,128)(2,1)S(1)}, u32[]{:S(2)}, u32[]{:S(2)}) %collective-permute-start.4) | collective-permute-done | bytes 65568 | tf_op jit(solution)/shard_map/ppermute | solution.py:423
  24.9 1.2 %collective-permute-done.2.pair_ref.other_ref = bf16[128,256]{1,0:T(8,128)(2,1)S(1)} collective-permute-done((bf16[128,256]{1,0:T(8,128)(2,1)S(1)}, bf16[128,256]{1,0:T(8,128)(2,1)S(1)}, u32[]{:S(2)}, u32[]{:S(2)}) %collective-permute-start.2) | collective-permute-done | bytes 65568 | tf_op jit(solution)/shard_map/ppermute | solution.py:423
  26.1 0.8 %collective-permute-done.3.across_ref = bf16[128,256]{1,0:T(8,128)(2,1)S(1)} collective-permute-done((bf16[128,256]{1,0:T(8,128)(2,1)S(1)}, bf16[128,256]{1,0:T(8,128)(2,1)S(1)}, u32[]{:S(2)}, u32[]{:S(2)}) %collective-permute-start.3) | collective-permute-done | bytes 65568 | tf_op jit(solution)/shard_map/ppermute | solution.py:423
  26.9 0.4 four_map.1
  27.3 2.2 %collective-permute-start.5 = (bf16[128,256]{1,0:T(8,128)(2,1)S(1)}, bf16[128,256]{1,0:T(8,128)(2,1)S(1)}, u32[]{:S(2)}, u32[]{:S(2)}) collective-permute-start(bf16[128,256]{1,0:T(8,128)(2,1)S(1)} %get-tuple-element.41.own_ref), channel_id=1, source_target_pairs={{0,48},{4,52},{8,56},{12,60},{16,32},{20,36},{24,40},{28,44},{32,1... | collective-permute-start | bytes 196616 | tf_op jit(solution)/shard_map/ppermute | solution.py:423
  29.5 3.1 %collective-permute-done.5.other_ref = bf16[128,256]{1,0:T(8,128)(2,1)S(1)} collective-permute-done((bf16[128,256]{1,0:T(8,128)(2,1)S(1)}, bf16[128,256]{1,0:T(8,128)(2,1)S(1)}, u32[]{:S(2)}, u32[]{:S(2)}) %collective-permute-start.5) | collective-permute-done | bytes 65568 | tf_op jit(solution)/shard_map/ppermute | solution.py:423
  32.6 0.2 far_map.1
  32.8 1.3 %collective-permute-start.6 = (bf16[128,256]{1,0:T(8,128)(2,1)S(1)}, bf16[128,256]{1,0:T(8,128)(2,1)S(1)}, u32[]{:S(2)}, u32[]{:S(2)}) collective-permute-start(bf16[128,256]{1,0:T(8,128)(2,1)S(1)} %get-tuple-element.43.own_ref), channel_id=1, source_target_pairs={{0,64},{4,68},{8,72},{12,76},{16,80},{20,84},{24,88},{28,92},{32,9... | collective-permute-start | bytes 196616 | tf_op jit(solution)/shard_map/ppermute | solution.py:423
  34.1 0.0 collective-permute-done.14.w_three
  34.1 2.4 %collective-permute-done.13.w_one = bf16[2,128,2048]{2,1,0:T(8,128)(2,1)S(1)} collective-permute-done((bf16[2,128,2048]{2,1,0:T(8,128)(2,1)S(1)}, bf16[2,128,2048]{2,1,0:T(8,128)(2,1)S(1)}, u32[]{:S(2)}, u32[]{:S(2)}) %collective-permute-start.13) | collective-permute-done | bytes 1048608 | tf_op jit(solution)/shard_map/ppermute | solution.py:428
  36.6 0.3 collective-permute-start.16
  37.0 1.2 %collective-permute-start.15 = (bf16[128,2048]{1,0:T(8,128)(2,1)S(1)}, bf16[128,2048]{1,0:T(8,128)(2,1)S(1)}, u32[]{:S(2)}, u32[]{:S(2)}) collective-permute-start(bf16[128,2048]{1,0:T(8,128)(2,1)S(1)} %slice_bitcast_fusion.1), channel_id=1, source_target_pairs={{0,1},{1,2},{2,3},{3,0},{4,5},{5,6},{6,7},{7,4},{8,9},{9,10},{10,1... | collective-permute-start | bytes 1572872 | tf_op jit(solution)/shard_map/ppermute | solution.py:428
  38.2 0.0 collective-permute-done.6.other_ref.row_ref
  38.2 0.2 rows_state.1
  38.3 2.5 %collective-permute-start.7 = (bf16[128,128]{1,0:T(8,128)(2,1)S(1)}, bf16[128,128]{1,0:T(8,128)(2,1)S(1)}, u32[]{:S(2)}, u32[]{:S(2)}) collective-permute-start(bf16[128,128]{1,0:T(8,128)(2,1)S(1)} %rows_state.1), channel_id=1, source_target_pairs={{0,192},{4,196},{8,200},{12,204},{16,208},{20,212},{24,216},{28,22... | collective-permute-start | bytes 98312 | tf_op jit(solution)/shard_map/ppermute | solution.py:423
  40.9 1.1 %inner_outputs.1 = (f32[2,256,128]{2,1,0:T(8,128)S(1)}, bf16[2,256,128]{2,1,0:T(8,128)(2,1)S(1)}, bf16[2,2,256,128]{3,2,1,0:T(8,128)(2,1)S(1)}) custom-call(bf16[3,256,512]{2,1,0:T(8,128)(2,1)S(1)} %get-tuple-element.34.proj_ref, f32[8,512]{1,0:T(8,128)S(1)} %get-tuple-element.48.edge_ref, f32[3,4,512]{2,1,0:T(4,128)S(1)} %copy-done, ...), custom_call_target="tpu_custom_call" | custom-call | flops 201326592 | bytes 2097152 | tf_op jit(solution)/shard_map/inner_outputs/pallas_call | solution.py:269
  42.0 2.5 %collective-permute-start.9 = (bf16[2,2,256,128]{3,2,1,0:T(8,128)(2,1)S(1)}, bf16[2,2,256,128]{3,2,1,0:T(8,128)(2,1)S(1)}, u32[]{:S(2)}, u32[]{:S(2)}) collective-permute-start(bf16[2,2,256,128]{3,2,1,0:T(8,128)(2,1)S(1)} %get-tuple-element.53), channel_id=1, source_target_pairs={{0,4},{4,0},{8,12},{12,8},{16,20},{20,16},{24,28},{28,24},{32,36},... | collective-permute-start | bytes 786440 | tf_op jit(solution)/shard_map/ppermute | solution.py:423
  44.5 0.0 collective-permute-done.7.rows_ref
  44.5 0.0 copy-start.1
  44.5 0.4 pair_start.1
  45.0 1.7 %collective-permute-start.8 = (bf16[128,128]{1,0:T(8,128)(2,1)S(1)}, bf16[128,128]{1,0:T(8,128)(2,1)S(1)}, u32[]{:S(2)}, u32[]{:S(2)}) collective-permute-start(bf16[128,128]{1,0:T(8,128)(2,1)S(1)} %get-tuple-element.46), channel_id=1, source_target_pairs={{0,8},{4,12},{8,0},{12,4},{16,24},{20,28},{24,16},{28,20},{32,40},... | collective-permute-start | bytes 98312 | tf_op jit(solution)/shard_map/ppermute | solution.py:423
  46.7 1.6 %collective-permute-done.8.other_state = bf16[128,128]{1,0:T(8,128)(2,1)S(1)} collective-permute-done((bf16[128,128]{1,0:T(8,128)(2,1)S(1)}, bf16[128,128]{1,0:T(8,128)(2,1)S(1)}, u32[]{:S(2)}, u32[]{:S(2)}) %collective-permute-start.8) | collective-permute-done | bytes 32800 | tf_op jit(solution)/shard_map/ppermute | solution.py:423
  48.3 0.0 collective-permute-done.9.both_in
  48.3 0.0 copy-done.1
  48.3 0.7 %finish.1 = (bf16[2,64,256]{2,1,0:T(8,128)(2,1)S(1)}, bf16[2,64,256]{2,1,0:T(8,128)(2,1)S(1)}, bf16[2,64,256]{2,1,0:T(8,128)(2,1)S(1)}, bf16[2,64,256]{2,1,0:T(8,128)(2,1)S(1)}) custom-call(bf16[128,128]{1,0:T(8,128)(2,1)S(1)} %get-tuple-element.45.own_state, bf16[128,128]{1,0:T(8,128)(2,1)S(1)} %collective-permute-done.8.other_state, ...), custom_call_target="tpu_custom_call" | custom-call | tf_op jit(solution)/shard_map/finish/pallas_call | solution.py:396
  49.0 0.1 collective-permute-start.10
  49.1 3.8 %collective-permute-start.11 = (bf16[2,64,256]{2,1,0:T(8,128)(2,1)S(1)}, bf16[2,64,256]{2,1,0:T(8,128)(2,1)S(1)}, u32[]{:S(2)}, u32[]{:S(2)}) collective-permute-start(bf16[2,64,256]{2,1,0:T(8,128)(2,1)S(1)} %get-tuple-element.56), channel_id=1, source_target_pairs={{0,2},{1,3},{2,0},{3,1},{4,6},{5,7},{6,4},{7,5},{8,10},{9,11},{10,... | collective-permute-start | bytes 196616 | tf_op jit(solution)/shard_map/ppermute | solution.py:428
  52.9 0.0 collective-permute-start.12
  52.9 0.5 collective-permute-done.10.one
  53.4 1.9 %collective-permute-done.11.two = bf16[2,64,256]{2,1,0:T(8,128)(2,1)S(1)} collective-permute-done((bf16[2,64,256]{2,1,0:T(8,128)(2,1)S(1)}, bf16[2,64,256]{2,1,0:T(8,128)(2,1)S(1)}, u32[]{:S(2)}, u32[]{:S(2)}) %collective-permute-start.11) | collective-permute-done | bytes 65568 | tf_op jit(solution)/shard_map/ppermute | solution.py:428
  55.2 1.1 %collective-permute-done.12.three = bf16[2,64,256]{2,1,0:T(8,128)(2,1)S(1)} collective-permute-done((bf16[2,64,256]{2,1,0:T(8,128)(2,1)S(1)}, bf16[2,64,256]{2,1,0:T(8,128)(2,1)S(1)}, u32[]{:S(2)}, u32[]{:S(2)}) %collective-permute-start.12) | collective-permute-done | bytes 65568 | tf_op jit(solution)/shard_map/ppermute | solution.py:428
  56.3 0.0 collective-permute-done.16.w_two1
  56.3 0.0 collective-permute-done.15.w_two0
  56.3 0.7 %merge.1 = (f32[64,2048]{1,0:T(8,128)S(1)}, bf16[64,2048]{1,0:T(8,128)(2,1)S(1)}) custom-call(bf16[2,64,256]{2,1,0:T(8,128)(2,1)S(1)} %get-tuple-element.54.mine_ref, bf16[2,64,256]{2,1,0:T(8,128)(2,1)S(1)} %collective-permute-done.10.one, bf16[2,64,256]{2,1,0:T(8,128)(2,1)S(1)} %collective-permute-done.11.two, ...), custom_call_target="tpu_custom_call" | custom-call | tf_op jit(solution)/shard_map/merge/pallas_call | solution.py:417
  57.1 4.0 %collective-permute-start.17 = (bf16[64,2048]{1,0:T(8,128)(2,1)S(1)}, bf16[64,2048]{1,0:T(8,128)(2,1)S(1)}, u32[]{:S(2)}, u32[]{:S(2)}) collective-permute-start(bf16[64,2048]{1,0:T(8,128)(2,1)S(1)} %get-tuple-element.62), channel_id=1, source_target_pairs={{0,4},{4,0},{8,12},{12,8},{16,20},{20,16},{24,28},{28,24},{32,36},... | collective-permute-start | bytes 786440 | tf_op jit(solution)/shard_map/ppermute | solution.py:423
  61.1 1.2 %collective-permute-done.17 = bf16[64,2048]{1,0:T(8,128)(2,1)S(1)} collective-permute-done((bf16[64,2048]{1,0:T(8,128)(2,1)S(1)}, bf16[64,2048]{1,0:T(8,128)(2,1)S(1)}, u32[]{:S(2)}, u32[]{:S(2)}) %collective-permute-start.17) | collective-permute-done | bytes 262176 | tf_op jit(solution)/shard_map/ppermute | solution.py:423
  62.2 0.8 %add_convert_fusion = bf16[64,2048]{1,0:T(8,128)(2,1)} fusion(f32[64,2048]{1,0:T(8,128)S(1)} %get-tuple-element.61, bf16[64,2048]{1,0:T(8,128)(2,1)S(1)} %collective-permute-done.17), kind=kLoop, calls=%fused_computation | loop fusion | flops 393216 | bytes 1048576 | tf_op jit(solution)/shard_map/convert_element_type | solution.py:462
  (2 shorter events, 0.1 us)
Async XLA Ops:
  0.8 10.5 %copy-start = (f32[3,4,512]{2,1,0:T(4,128)S(1)}, f32[3,4,512]{2,1,0:T(4,128)}, u32[]{:S(2)}) copy-start(f32[3,4,512]{2,1,0:T(4,128)} %conv_ref.3) | copy-start | bytes 73732
  0.8 10.5 %copy-start.2 = (f32[4]{0:T(128)S(1)}, f32[4]{0:T(128)}, u32[]{:S(2)}) copy-start(f32[4]{0:T(128)} %param.11) | copy-start | bytes 52
  0.8 10.5 %collective-permute-start = (bf16[8,2048]{1,0:T(8,128)(2,1)S(1)}, bf16[8,2048]{1,0:T(8,128)(2,1)S(1)}, u32[]{:S(2)}, u32[]{:S(2)}) collective-permute-start(bf16[8,2048]{1,0:T(8,128)(2,1)S(1)} %slice.9), channel_id=1, source_target_pairs={{0,4},{4,8},{8,12},{12,16},{16,20},{20,24},{24,28},{28,32},{32,36}... | collective-permute-start | bytes 98312 | tf_op jit(solution)/shard_map/ppermute | solution.py:428
  8.4 25.7 %collective-permute-start.14 = (bf16[2,128,2048]{2,1,0:T(8,128)(2,1)S(1)}, bf16[2,128,2048]{2,1,0:T(8,128)(2,1)S(1)}, u32[]{:S(2)}, u32[]{:S(2)}) collective-permute-start(bf16[2,128,2048]{2,1,0:T(8,128)(2,1)S(1)} %get-tuple-element.58.w_own), channel_id=1, source_target_pairs={{0,3},{1,0},{2,1},{3,2},{4,7},{5,4},{6,5},{7,6},{8,11},{9,8},{10,9... | collective-permute-start | bytes 3145736 | tf_op jit(solution)/shard_map/ppermute | solution.py:428
  11.2 25.3 %collective-permute-start.13 = (bf16[2,128,2048]{2,1,0:T(8,128)(2,1)S(1)}, bf16[2,128,2048]{2,1,0:T(8,128)(2,1)S(1)}, u32[]{:S(2)}, u32[]{:S(2)}) collective-permute-start(bf16[2,128,2048]{2,1,0:T(8,128)(2,1)S(1)} %get-tuple-element.58.w_own), channel_id=1, source_target_pairs={{0,1},{1,2},{2,3},{3,0},{4,5},{5,6},{6,7},{7,4},{8,9},{9,10},{10,1... | collective-permute-start | bytes 3145736 | tf_op jit(solution)/shard_map/ppermute | solution.py:428
  15.3 1.4 %collective-permute-start.1 = (bf16[2,128,256]{2,1,0:T(8,128)(2,1)S(1)}, bf16[2,128,256]{2,1,0:T(8,128)(2,1)S(1)}, u32[]{:S(2)}, u32[]{:S(2)}) collective-permute-start(bf16[2,128,256]{2,1,0:T(8,128)(2,1)S(1)} %get-tuple-element.38), channel_id=1, source_target_pairs={{0,4},{4,0},{8,12},{12,8},{16,20},{20,16},{24,28},{28,24},{32,36},... | collective-permute-start | bytes 393224 | tf_op jit(solution)/shard_map/ppermute | solution.py:423
  17.0 8.0 %collective-permute-start.4 = (bf16[128,256]{1,0:T(8,128)(2,1)S(1)}, bf16[128,256]{1,0:T(8,128)(2,1)S(1)}, u32[]{:S(2)}, u32[]{:S(2)}) collective-permute-start(bf16[128,256]{1,0:T(8,128)(2,1)S(1)} %get-tuple-element.40), channel_id=1, source_target_pairs={{0,24},{4,28},{8,16},{12,20},{16,8},{20,12},{24,0},{28,4},{32,56},... | collective-permute-start | bytes 196616 | tf_op jit(solution)/shard_map/ppermute | solution.py:423
  22.6 3.5 %collective-permute-start.2 = (bf16[128,256]{1,0:T(8,128)(2,1)S(1)}, bf16[128,256]{1,0:T(8,128)(2,1)S(1)}, u32[]{:S(2)}, u32[]{:S(2)}) collective-permute-start(bf16[128,256]{1,0:T(8,128)(2,1)S(1)} %get-tuple-element.40), channel_id=1, source_target_pairs={{0,8},{4,12},{8,0},{12,4},{16,24},{20,28},{24,16},{28,20},{32,40},... | collective-permute-start | bytes 196616 | tf_op jit(solution)/shard_map/ppermute | solution.py:423
  22.6 4.3 %collective-permute-start.3 = (bf16[128,256]{1,0:T(8,128)(2,1)S(1)}, bf16[128,256]{1,0:T(8,128)(2,1)S(1)}, u32[]{:S(2)}, u32[]{:S(2)}) collective-permute-start(bf16[128,256]{1,0:T(8,128)(2,1)S(1)} %get-tuple-element.39.own_ref), channel_id=1, source_target_pairs={{0,16},{4,20},{8,24},{12,28},{16,0},{20,4},{24,8},{28,12},{32,48},... | collective-permute-start | bytes 196616 | tf_op jit(solution)/shard_map/ppermute | solution.py:423
  27.3 5.4 %collective-permute-start.5 = (bf16[128,256]{1,0:T(8,128)(2,1)S(1)}, bf16[128,256]{1,0:T(8,128)(2,1)S(1)}, u32[]{:S(2)}, u32[]{:S(2)}) collective-permute-start(bf16[128,256]{1,0:T(8,128)(2,1)S(1)} %get-tuple-element.41.own_ref), channel_id=1, source_target_pairs={{0,48},{4,52},{8,56},{12,60},{16,32},{20,36},{24,40},{28,44},{32,1... | collective-permute-start | bytes 196616 | tf_op jit(solution)/shard_map/ppermute | solution.py:423
  32.8 5.4 %collective-permute-start.6 = (bf16[128,256]{1,0:T(8,128)(2,1)S(1)}, bf16[128,256]{1,0:T(8,128)(2,1)S(1)}, u32[]{:S(2)}, u32[]{:S(2)}) collective-permute-start(bf16[128,256]{1,0:T(8,128)(2,1)S(1)} %get-tuple-element.43.own_ref), channel_id=1, source_target_pairs={{0,64},{4,68},{8,72},{12,76},{16,80},{20,84},{24,88},{28,92},{32,9... | collective-permute-start | bytes 196616 | tf_op jit(solution)/shard_map/ppermute | solution.py:423
  36.6 19.7 %collective-permute-start.16 = (bf16[128,2048]{1,0:T(8,128)(2,1)S(1)}, bf16[128,2048]{1,0:T(8,128)(2,1)S(1)}, u32[]{:S(2)}, u32[]{:S(2)}) collective-permute-start(bf16[128,2048]{1,0:T(8,128)(2,1)S(1)} %slice_bitcast_fusion), channel_id=1, source_target_pairs={{0,3},{1,0},{2,1},{3,2},{4,7},{5,4},{6,5},{7,6},{8,11},{9,8},{10,9... | collective-permute-start | bytes 1572872 | tf_op jit(solution)/shard_map/ppermute | solution.py:428
  37.0 19.3 %collective-permute-start.15 = (bf16[128,2048]{1,0:T(8,128)(2,1)S(1)}, bf16[128,2048]{1,0:T(8,128)(2,1)S(1)}, u32[]{:S(2)}, u32[]{:S(2)}) collective-permute-start(bf16[128,2048]{1,0:T(8,128)(2,1)S(1)} %slice_bitcast_fusion.1), channel_id=1, source_target_pairs={{0,1},{1,2},{2,3},{3,0},{4,5},{5,6},{6,7},{7,4},{8,9},{9,10},{10,1... | collective-permute-start | bytes 1572872 | tf_op jit(solution)/shard_map/ppermute | solution.py:428
  38.3 6.2 %collective-permute-start.7 = (bf16[128,128]{1,0:T(8,128)(2,1)S(1)}, bf16[128,128]{1,0:T(8,128)(2,1)S(1)}, u32[]{:S(2)}, u32[]{:S(2)}) collective-permute-start(bf16[128,128]{1,0:T(8,128)(2,1)S(1)} %rows_state.1), channel_id=1, source_target_pairs={{0,192},{4,196},{8,200},{12,204},{16,208},{20,212},{24,216},{28,22... | collective-permute-start | bytes 98312 | tf_op jit(solution)/shard_map/ppermute | solution.py:423
  42.0 6.3 %collective-permute-start.9 = (bf16[2,2,256,128]{3,2,1,0:T(8,128)(2,1)S(1)}, bf16[2,2,256,128]{3,2,1,0:T(8,128)(2,1)S(1)}, u32[]{:S(2)}, u32[]{:S(2)}) collective-permute-start(bf16[2,2,256,128]{3,2,1,0:T(8,128)(2,1)S(1)} %get-tuple-element.53), channel_id=1, source_target_pairs={{0,4},{4,0},{8,12},{12,8},{16,20},{20,16},{24,28},{28,24},{32,36},... | collective-permute-start | bytes 786440 | tf_op jit(solution)/shard_map/ppermute | solution.py:423
  44.5 3.8 %copy-start.1 = (f32[512]{0:T(512)S(1)}, f32[512]{0:T(512)}, u32[]{:S(2)}) copy-start(f32[512]{0:T(512)} %param.12) | copy-start | bytes 6148
  45.0 3.3 %collective-permute-start.8 = (bf16[128,128]{1,0:T(8,128)(2,1)S(1)}, bf16[128,128]{1,0:T(8,128)(2,1)S(1)}, u32[]{:S(2)}, u32[]{:S(2)}) collective-permute-start(bf16[128,128]{1,0:T(8,128)(2,1)S(1)} %get-tuple-element.46), channel_id=1, source_target_pairs={{0,8},{4,12},{8,0},{12,4},{16,24},{20,28},{24,16},{28,20},{32,40},... | collective-permute-start | bytes 98312 | tf_op jit(solution)/shard_map/ppermute | solution.py:423
  49.0 4.4 %collective-permute-start.10 = (bf16[2,64,256]{2,1,0:T(8,128)(2,1)S(1)}, bf16[2,64,256]{2,1,0:T(8,128)(2,1)S(1)}, u32[]{:S(2)}, u32[]{:S(2)}) collective-permute-start(bf16[2,64,256]{2,1,0:T(8,128)(2,1)S(1)} %get-tuple-element.55), channel_id=1, source_target_pairs={{0,1},{1,2},{2,3},{3,0},{4,5},{5,6},{6,7},{7,4},{8,9},{9,10},{10,1... | collective-permute-start | bytes 196616 | tf_op jit(solution)/shard_map/ppermute | solution.py:428
  49.1 6.2 %collective-permute-start.11 = (bf16[2,64,256]{2,1,0:T(8,128)(2,1)S(1)}, bf16[2,64,256]{2,1,0:T(8,128)(2,1)S(1)}, u32[]{:S(2)}, u32[]{:S(2)}) collective-permute-start(bf16[2,64,256]{2,1,0:T(8,128)(2,1)S(1)} %get-tuple-element.56), channel_id=1, source_target_pairs={{0,2},{1,3},{2,0},{3,1},{4,6},{5,7},{6,4},{7,5},{8,10},{9,11},{10,... | collective-permute-start | bytes 196616 | tf_op jit(solution)/shard_map/ppermute | solution.py:428
  52.9 3.4 %collective-permute-start.12 = (bf16[2,64,256]{2,1,0:T(8,128)(2,1)S(1)}, bf16[2,64,256]{2,1,0:T(8,128)(2,1)S(1)}, u32[]{:S(2)}, u32[]{:S(2)}) collective-permute-start(bf16[2,64,256]{2,1,0:T(8,128)(2,1)S(1)} %get-tuple-element.57), channel_id=1, source_target_pairs={{0,3},{1,0},{2,1},{3,2},{4,7},{5,4},{6,5},{7,6},{8,11},{9,8},{10,9... | collective-permute-start | bytes 196616 | tf_op jit(solution)/shard_map/ppermute | solution.py:428
  57.1 5.2 %collective-permute-start.17 = (bf16[64,2048]{1,0:T(8,128)(2,1)S(1)}, bf16[64,2048]{1,0:T(8,128)(2,1)S(1)}, u32[]{:S(2)}, u32[]{:S(2)}) collective-permute-start(bf16[64,2048]{1,0:T(8,128)(2,1)S(1)} %get-tuple-element.62), channel_id=1, source_target_pairs={{0,4},{4,0},{8,12},{12,8},{16,20},{20,16},{24,28},{28,24},{32,36},... | collective-permute-start | bytes 786440 | tf_op jit(solution)/shard_map/ppermute | solution.py:423

commit v11 on v10

--- a/solution.py
+++ b/solution.py
@@ -324,7 +324,7 @@
     send_ref[...] = kept[1 - bit(2)]
 
 
-def four_kernel(own_ref, pair_ref, across_ref, diagonal_ref, total_ref, before_ref):
+def four_kernel(own_ref, diagonal_ref, across_ref, pair_ref, total_ref, before_ref):
     upper, late = bit(2) == 1, bit(4) == 1
     own, pair, across, diagonal = (
         ref[...].astype(f32) for ref in (own_ref, pair_ref, across_ref, diagonal_ref)
@@ -399,7 +399,7 @@
 
 
 def merge_kernel(
-    mine_ref, one, two, three, w_own, w_one, w_two0, w_two1, w_three, keep_ref, send_ref
+    mine_ref, one, three, two, w_own, w_one, w_three, w_two0, w_two1, keep_ref, send_ref
 ):
     _, rows, width = mine_ref.shape
     total = None
@@ -440,7 +440,9 @@
         chip_kernel, [MAP, MAP], "chip_map", [pltpu.VMEM((2, DK, 2 * DK), bf16)]
     )(maps, sibling)
     pair, across, diagonal = swapped(send, 2), swapped(chip, 4), swapped(send, 6)
-    four, near = small_call(four_kernel, [MAP, MAP], "four_map")(chip, pair, across, diagonal)
+    four, near = small_call(four_kernel, [MAP, MAP], "four_map")(
+        chip, diagonal, across, pair
+    )
     row, before = small_call(far_kernel, [MAP, MAP], "far_map")(four, swapped(four, 12), near)
     _, w_one, w_three = lax.optimization_barrier((row, w_one, w_three))
     w_two = turned(w_one[0], "head", 1), turned(w_three[1], "head", 3)
@@ -458,7 +460,7 @@
         (state, back), (maps, sibling), (base, gate), inner_in, norm_gain
     )
     one, three, two = turned(one, "head", 1), turned(three, "head", 3), turned(two, "head", 2)
-    keep, send = merge([mine, one, two, three], [w_own, w_one, *w_two, w_three])
+    keep, send = merge([mine, one, three, two], [w_own, w_one, w_three, *w_two])
     return (keep + swapped(send, 1).astype(f32)).astype(bf16)
 
 

time: 63.1 us -> 64.4 us (1.021)
  waiting for transfers between devices: 16.9 us -> 20.9 us
  starting transfers between devices: 31.9 us -> 29.1 us
    ppermute x10, waiting for transfers between devices: 11.1 us -> 17.3 us  [swapped(): lax.ppermute(x, 'ctx', [(i, i ^ by) for i in range(lax.axis_size('ctx'))])]
    ppermute x10, starting transfers between devices: 20.6 us -> 16.6 us  [swapped(): lax.ppermute(x, 'ctx', [(i, i ^ by) for i in range(lax.axis_size('ctx'))])]
    ppermute x8, waiting for transfers between devices: 5.85 us -> 3.65 us  [turned(): return lax.ppermute(x, axis, [(i, (i + by) % count) for i in range(count)])]
    ppermute x8, starting transfers between devices: 11.3 us -> 12.5 us  [turned(): return lax.ppermute(x, axis, [(i, (i + by) % count) for i in range(count)])]
  transfers between devices with their start and end apart: 18 -> 18, of which waited for: 11 -> 8; matrix products, arithmetic and copies ran while one was open for 0% -> 0% of each run, Pallas kernels for 19% -> 18%
where the time goes in v11:
time: 64.4 us; the launch traced here: 64.2 us
  starting transfers between devices  29.1 us (45%)
  waiting for transfers between devices  20.9 us (32%)
  Pallas kernels  12.5 us (19%)
  local copies, waits for them, and re-layouts  0.85 us (1%)
  other arithmetic  0.75 us (1%)
    ppermute x10, waiting for transfers between devices, swapped(): lax.ppermute(x, 'ctx', [(i, i ^ by) for i in range(lax.axis_size('ctx'))])  17.3 us
    ppermute x10, starting transfers between devices, swapped(): lax.ppermute(x, 'ctx', [(i, i ^ by) for i in range(lax.axis_size('ctx'))])  16.6 us
    ppermute x8, starting transfers between devices, turned(): return lax.ppermute(x, axis, [(i, (i + by) % count) for i in range(count)])  12.5 us
    pallas_call x1, Pallas kernels, project(): pl.pallas_call(project_kernel, in_specs=[pl.BlockSpec(memory_space=pltpu....  4.62 us
    pallas_call x1, Pallas kernels, local_maps(): pl.pallas_call(local_kernel, in_specs=whole(6), out_specs=whole(5), out_s...  4.02 us
    ppermute x8, waiting for transfers between devices, turned(): return lax.ppermute(x, axis, [(i, (i + by) % count) for i in range(count)])  3.65 us
  transfers between devices with their start and end apart: 18, of which 8 were waited for; matrix products, arithmetic and copies ran while one was open for 0% of the time, Pallas kernels for 18%

profile of v11, /device:TPU:1, one launch (start us, length us, event | category | flops | bytes accessed | tf_op | source)
XLA Modules:
  0.0 64.2 jit_solution(11124423103430463206)
XLA Ops:
  0.0 0.8 %slice.9 = bf16[8,2048]{1,0:T(8,128)(2,1)S(1)} slice(bf16[256,2048]{1,0:T(8,128)(2,1)} %tokens_hbm.1), slice={[248:256], [0:2048]} | slice | bytes 65536 | tf_op jit(solution)/shard_map/slice | solution.py:432
  0.8 0.0 copy-start
  0.8 0.0 copy-start.2
  0.8 3.0 %collective-permute-start = (bf16[8,2048]{1,0:T(8,128)(2,1)S(1)}, bf16[8,2048]{1,0:T(8,128)(2,1)S(1)}, u32[]{:S(2)}, u32[]{:S(2)}) collective-permute-start(bf16[8,2048]{1,0:T(8,128)(2,1)S(1)} %slice.9), channel_id=1, source_target_pairs={{0,4},{4,8},{8,12},{12,16},{16,20},{20,24},{24,28},{28,32},{32,36}... | collective-permute-start | bytes 98312 | tf_op jit(solution)/shard_map/ppermute | solution.py:428
  3.8 4.6 %project.1 = (bf16[3,256,512]{2,1,0:T(8,128)(2,1)S(1)}, bf16[3,2048,512]{2,1,0:T(8,128)(2,1)S(1)}, f32[256,4]{1,0:T(8,128)S(1)}, bf16[2,128,2048]{2,1,0:T(8,128)(2,1)S(1)}) custom-call(bf16[256,2048]{1,0:T(8,128)(2,1)} %tokens_hbm.1, bf16[3,2048,512]{2,1,0:T(8,128)(2,1)} %w_hbm.1, bf16[4,2048]{1,0:T(4,128)(2,1)} %beta_w_hbm.1, bf16[512,2048]{1,0:T(8,128)(2,1)} %w_out_hbm.1), custom_call_target="tpu_custom_call" | custom-call | flops 60000002048 | bytes 1048576 | tf_op jit(solution)/shard_map/project/pallas_call | solution.py:84
  8.4 2.8 %collective-permute-start.14 = (bf16[2,128,2048]{2,1,0:T(8,128)(2,1)S(1)}, bf16[2,128,2048]{2,1,0:T(8,128)(2,1)S(1)}, u32[]{:S(2)}, u32[]{:S(2)}) collective-permute-start(bf16[2,128,2048]{2,1,0:T(8,128)(2,1)S(1)} %get-tuple-element.58.w_own), channel_id=1, source_target_pairs={{0,3},{1,0},{2,1},{3,2},{4,7},{5,4},{6,5},{7,6},{8,11},{9,8},{10,9... | collective-permute-start | bytes 3145736 | tf_op jit(solution)/shard_map/ppermute | solution.py:428
  11.2 0.0 collective-permute-start.13
  11.2 0.0 collective-permute-done.edge_ref
  11.2 0.0 copy-done
  11.2 0.0 copy-done.2
  11.3 4.0 %local_maps.1 = (f32[8,512]{1,0:T(8,128)S(1)}, bf16[4,128,256]{2,1,0:T(8,128)(2,1)S(1)}, bf16[4,256,256]{2,1,0:T(8,128)(2,1)S(1)}, bf16[2,128,256]{2,1,0:T(8,128)(2,1)S(1)}, bf16[2,128,256]{2,1,0:T(8,128)(2,1)S(1)}) custom-call(bf16[3,256,512]{2,1,0:T(8,128)(2,1)S(1)} %get-tuple-element.34.proj_ref, bf16[3,2048,512]{2,1,0:T(8,128)(2,1)S(1)} %get-tuple-element.35.w_ref, ...), custom_call_target="tpu_custom_call" | custom-call | flops 60000002048 | bytes 1048576 | tf_op jit(solution)/shard_map/local_maps/pallas_call | solution.py:221
  15.3 0.2 collective-permute-start.1
  15.5 1.3 %collective-permute-done.1.other_ref.other_maps = bf16[2,128,256]{2,1,0:T(8,128)(2,1)S(1)} collective-permute-done((bf16[2,128,256]{2,1,0:T(8,128)(2,1)S(1)}, bf16[2,128,256]{2,1,0:T(8,128)(2,1)S(1)}, u32[]{:S(2)}, u32[]{:S(2)}) %collective-permute-start.1) | collective-permute-done | bytes 131104 | tf_op jit(solution)/shard_map/ppermute | solution.py:423
  16.7 0.2 chip_map.1
  17.0 1.7 %collective-permute-start.4 = (bf16[128,256]{1,0:T(8,128)(2,1)S(1)}, bf16[128,256]{1,0:T(8,128)(2,1)S(1)}, u32[]{:S(2)}, u32[]{:S(2)}) collective-permute-start(bf16[128,256]{1,0:T(8,128)(2,1)S(1)} %get-tuple-element.40), channel_id=1, source_target_pairs={{0,8},{4,12},{8,0},{12,4},{16,24},{20,28},{24,16},{28,20},{32,40},... | collective-permute-start | bytes 196616 | tf_op jit(solution)/shard_map/ppermute | solution.py:423
  18.7 4.0 %collective-permute-start.2 = (bf16[128,256]{1,0:T(8,128)(2,1)S(1)}, bf16[128,256]{1,0:T(8,128)(2,1)S(1)}, u32[]{:S(2)}, u32[]{:S(2)}) collective-permute-start(bf16[128,256]{1,0:T(8,128)(2,1)S(1)} %get-tuple-element.40), channel_id=1, source_target_pairs={{0,24},{4,28},{8,16},{12,20},{16,8},{20,12},{24,0},{28,4},{32,56},... | collective-permute-start | bytes 196616 | tf_op jit(solution)/shard_map/ppermute | solution.py:423
  22.7 0.2 collective-permute-start.3
  22.9 0.0 collective-permute-done.4.pair_ref.other_ref
  22.9 3.4 %collective-permute-done.2.diagonal_ref = bf16[128,256]{1,0:T(8,128)(2,1)S(1)} collective-permute-done((bf16[128,256]{1,0:T(8,128)(2,1)S(1)}, bf16[128,256]{1,0:T(8,128)(2,1)S(1)}, u32[]{:S(2)}, u32[]{:S(2)}) %collective-permute-start.2) | collective-permute-done | bytes 65568 | tf_op jit(solution)/shard_map/ppermute | solution.py:423
  26.3 3.3 %collective-permute-done.3.across_ref = bf16[128,256]{1,0:T(8,128)(2,1)S(1)} collective-permute-done((bf16[128,256]{1,0:T(8,128)(2,1)S(1)}, bf16[128,256]{1,0:T(8,128)(2,1)S(1)}, u32[]{:S(2)}, u32[]{:S(2)}) %collective-permute-start.3) | collective-permute-done | bytes 65568 | tf_op jit(solution)/shard_map/ppermute | solution.py:423
  29.6 0.3 four_map.1
  30.0 0.3 collective-permute-start.5
  30.3 5.1 %collective-permute-done.5.other_ref = bf16[128,256]{1,0:T(8,128)(2,1)S(1)} collective-permute-done((bf16[128,256]{1,0:T(8,128)(2,1)S(1)}, bf16[128,256]{1,0:T(8,128)(2,1)S(1)}, u32[]{:S(2)}, u32[]{:S(2)}) %collective-permute-start.5) | collective-permute-done | bytes 65568 | tf_op jit(solution)/shard_map/ppermute | solution.py:423
  35.3 0.2 far_map.1
  35.5 1.3 %collective-permute-start.6 = (bf16[128,256]{1,0:T(8,128)(2,1)S(1)}, bf16[128,256]{1,0:T(8,128)(2,1)S(1)}, u32[]{:S(2)}, u32[]{:S(2)}) collective-permute-start(bf16[128,256]{1,0:T(8,128)(2,1)S(1)} %get-tuple-element.43.own_ref), channel_id=1, source_target_pairs={{0,64},{4,68},{8,72},{12,76},{16,80},{20,84},{24,88},{28,92},{32,9... | collective-permute-start | bytes 196616 | tf_op jit(solution)/shard_map/ppermute | solution.py:423
  36.8 0.0 collective-permute-done.14.w_three
  36.8 0.0 collective-permute-done.13.w_one
  36.9 2.7 %collective-permute-start.16 = (bf16[128,2048]{1,0:T(8,128)(2,1)S(1)}, bf16[128,2048]{1,0:T(8,128)(2,1)S(1)}, u32[]{:S(2)}, u32[]{:S(2)}) collective-permute-start(bf16[128,2048]{1,0:T(8,128)(2,1)S(1)} %slice_bitcast_fusion), channel_id=1, source_target_pairs={{0,3},{1,0},{2,1},{3,2},{4,7},{5,4},{6,5},{7,6},{8,11},{9,8},{10,9... | collective-permute-start | bytes 1572872 | tf_op jit(solution)/shard_map/ppermute | solution.py:428
  39.7 0.0 collective-permute-start.15
  39.7 0.0 collective-permute-done.6.other_ref.row_ref
  39.7 0.2 rows_state.1
  39.8 1.9 %collective-permute-start.7 = (bf16[128,128]{1,0:T(8,128)(2,1)S(1)}, bf16[128,128]{1,0:T(8,128)(2,1)S(1)}, u32[]{:S(2)}, u32[]{:S(2)}) collective-permute-start(bf16[128,128]{1,0:T(8,128)(2,1)S(1)} %rows_state.1), channel_id=1, source_target_pairs={{0,192},{4,196},{8,200},{12,204},{16,208},{20,212},{24,216},{28,22... | collective-permute-start | bytes 98312 | tf_op jit(solution)/shard_map/ppermute | solution.py:423
  41.7 1.1 %inner_outputs.1 = (f32[2,256,128]{2,1,0:T(8,128)S(1)}, bf16[2,256,128]{2,1,0:T(8,128)(2,1)S(1)}, bf16[2,2,256,128]{3,2,1,0:T(8,128)(2,1)S(1)}) custom-call(bf16[3,256,512]{2,1,0:T(8,128)(2,1)S(1)} %get-tuple-element.34.proj_ref, f32[8,512]{1,0:T(8,128)S(1)} %get-tuple-element.48.edge_ref, f32[3,4,512]{2,1,0:T(4,128)S(1)} %copy-done, ...), custom_call_target="tpu_custom_call" | custom-call | flops 201326592 | bytes 2097152 | tf_op jit(solution)/shard_map/inner_outputs/pallas_call | solution.py:269
  42.8 2.9 %collective-permute-start.9 = (bf16[2,2,256,128]{3,2,1,0:T(8,128)(2,1)S(1)}, bf16[2,2,256,128]{3,2,1,0:T(8,128)(2,1)S(1)}, u32[]{:S(2)}, u32[]{:S(2)}) collective-permute-start(bf16[2,2,256,128]{3,2,1,0:T(8,128)(2,1)S(1)} %get-tuple-element.53), channel_id=1, source_target_pairs={{0,4},{4,0},{8,12},{12,8},{16,20},{20,16},{24,28},{28,24},{32,36},... | collective-permute-start | bytes 786440 | tf_op jit(solution)/shard_map/ppermute | solution.py:423
  45.7 0.0 collective-permute-done.7.rows_ref
  45.7 0.0 copy-start.1
  45.7 0.4 pair_start.1
  46.1 0.1 collective-permute-start.8
  46.2 3.0 %collective-permute-done.8.other_state = bf16[128,128]{1,0:T(8,128)(2,1)S(1)} collective-permute-done((bf16[128,128]{1,0:T(8,128)(2,1)S(1)}, bf16[128,128]{1,0:T(8,128)(2,1)S(1)}, u32[]{:S(2)}, u32[]{:S(2)}) %collective-permute-start.8) | collective-permute-done | bytes 32800 | tf_op jit(solution)/shard_map/ppermute | solution.py:423
  49.2 0.0 collective-permute-done.9.both_in
  49.2 0.0 copy-done.1
  49.3 0.7 %finish.1 = (bf16[2,64,256]{2,1,0:T(8,128)(2,1)S(1)}, bf16[2,64,256]{2,1,0:T(8,128)(2,1)S(1)}, bf16[2,64,256]{2,1,0:T(8,128)(2,1)S(1)}, bf16[2,64,256]{2,1,0:T(8,128)(2,1)S(1)}) custom-call(bf16[128,128]{1,0:T(8,128)(2,1)S(1)} %get-tuple-element.45.own_state, bf16[128,128]{1,0:T(8,128)(2,1)S(1)} %collective-permute-done.8.other_state, ...), custom_call_target="tpu_custom_call" | custom-call | tf_op jit(solution)/shard_map/finish/pallas_call | solution.py:396
  49.9 0.1 collective-permute-start.10
  50.0 2.7 %collective-permute-start.11 = (bf16[2,64,256]{2,1,0:T(8,128)(2,1)S(1)}, bf16[2,64,256]{2,1,0:T(8,128)(2,1)S(1)}, u32[]{:S(2)}, u32[]{:S(2)}) collective-permute-start(bf16[2,64,256]{2,1,0:T(8,128)(2,1)S(1)} %get-tuple-element.56), channel_id=1, source_target_pairs={{0,3},{1,0},{2,1},{3,2},{4,7},{5,4},{6,5},{7,6},{8,11},{9,8},{10,9... | collective-permute-start | bytes 196616 | tf_op jit(solution)/shard_map/ppermute | solution.py:428
  52.7 1.1 %collective-permute-start.12 = (bf16[2,64,256]{2,1,0:T(8,128)(2,1)S(1)}, bf16[2,64,256]{2,1,0:T(8,128)(2,1)S(1)}, u32[]{:S(2)}, u32[]{:S(2)}) collective-permute-start(bf16[2,64,256]{2,1,0:T(8,128)(2,1)S(1)} %get-tuple-element.57), channel_id=1, source_target_pairs={{0,2},{1,3},{2,0},{3,1},{4,6},{5,7},{6,4},{7,5},{8,10},{9,11},{10,... | collective-permute-start | bytes 196616 | tf_op jit(solution)/shard_map/ppermute | solution.py:428
  53.8 1.5 %collective-permute-done.10.one = bf16[2,64,256]{2,1,0:T(8,128)(2,1)S(1)} collective-permute-done((bf16[2,64,256]{2,1,0:T(8,128)(2,1)S(1)}, bf16[2,64,256]{2,1,0:T(8,128)(2,1)S(1)}, u32[]{:S(2)}, u32[]{:S(2)}) %collective-permute-start.10) | collective-permute-done | bytes 65568 | tf_op jit(solution)/shard_map/ppermute | solution.py:428
  55.4 0.0 collective-permute-done.11.three
  55.4 2.1 %collective-permute-done.12.two = bf16[2,64,256]{2,1,0:T(8,128)(2,1)S(1)} collective-permute-done((bf16[2,64,256]{2,1,0:T(8,128)(2,1)S(1)}, bf16[2,64,256]{2,1,0:T(8,128)(2,1)S(1)}, u32[]{:S(2)}, u32[]{:S(2)}) %collective-permute-start.12) | collective-permute-done | bytes 65568 | tf_op jit(solution)/shard_map/ppermute | solution.py:428
  57.5 0.0 collective-permute-done.16.w_two1
  57.5 0.0 collective-permute-done.15.w_two0
  57.5 0.7 %merge.1 = (f32[64,2048]{1,0:T(8,128)S(1)}, bf16[64,2048]{1,0:T(8,128)(2,1)S(1)}) custom-call(bf16[2,64,256]{2,1,0:T(8,128)(2,1)S(1)} %get-tuple-element.54.mine_ref, bf16[2,64,256]{2,1,0:T(8,128)(2,1)S(1)} %collective-permute-done.10.one, bf16[2,64,256]{2,1,0:T(8,128)(2,1)S(1)} %collective-permute-done.11.three, ...), custom_call_target="tpu_custom_call" | custom-call | tf_op jit(solution)/shard_map/merge/pallas_call | solution.py:417
  58.2 4.1 %collective-permute-start.17 = (bf16[64,2048]{1,0:T(8,128)(2,1)S(1)}, bf16[64,2048]{1,0:T(8,128)(2,1)S(1)}, u32[]{:S(2)}, u32[]{:S(2)}) collective-permute-start(bf16[64,2048]{1,0:T(8,128)(2,1)S(1)} %get-tuple-element.62), channel_id=1, source_target_pairs={{0,4},{4,0},{8,12},{12,8},{16,20},{20,16},{24,28},{28,24},{32,36},... | collective-permute-start | bytes 786440 | tf_op jit(solution)/shard_map/ppermute | solution.py:423
  62.3 1.2 %collective-permute-done.17 = bf16[64,2048]{1,0:T(8,128)(2,1)S(1)} collective-permute-done((bf16[64,2048]{1,0:T(8,128)(2,1)S(1)}, bf16[64,2048]{1,0:T(8,128)(2,1)S(1)}, u32[]{:S(2)}, u32[]{:S(2)}) %collective-permute-start.17) | collective-permute-done | bytes 262176 | tf_op jit(solution)/shard_map/ppermute | solution.py:423
  63.5 0.8 %add_convert_fusion = bf16[64,2048]{1,0:T(8,128)(2,1)} fusion(f32[64,2048]{1,0:T(8,128)S(1)} %get-tuple-element.61, bf16[64,2048]{1,0:T(8,128)(2,1)S(1)} %collective-permute-done.17), kind=kLoop, calls=%fused_computation | loop fusion | flops 393216 | bytes 1048576 | tf_op jit(solution)/shard_map/convert_element_type | solution.py:464
  (2 shorter events, 0.1 us)
Async XLA Ops:
  0.8 10.5 %copy-start = (f32[3,4,512]{2,1,0:T(4,128)S(1)}, f32[3,4,512]{2,1,0:T(4,128)}, u32[]{:S(2)}) copy-start(f32[3,4,512]{2,1,0:T(4,128)} %conv_ref.3) | copy-start | bytes 73732
  0.8 10.5 %copy-start.2 = (f32[4]{0:T(128)S(1)}, f32[4]{0:T(128)}, u32[]{:S(2)}) copy-start(f32[4]{0:T(128)} %param.11) | copy-start | bytes 52
  0.8 10.5 %collective-permute-start = (bf16[8,2048]{1,0:T(8,128)(2,1)S(1)}, bf16[8,2048]{1,0:T(8,128)(2,1)S(1)}, u32[]{:S(2)}, u32[]{:S(2)}) collective-permute-start(bf16[8,2048]{1,0:T(8,128)(2,1)S(1)} %slice.9), channel_id=1, source_target_pairs={{0,4},{4,8},{8,12},{12,16},{16,20},{20,24},{24,28},{28,32},{32,36}... | collective-permute-start | bytes 98312 | tf_op jit(solution)/shard_map/ppermute | solution.py:428
  8.4 28.4 %collective-permute-start.14 = (bf16[2,128,2048]{2,1,0:T(8,128)(2,1)S(1)}, bf16[2,128,2048]{2,1,0:T(8,128)(2,1)S(1)}, u32[]{:S(2)}, u32[]{:S(2)}) collective-permute-start(bf16[2,128,2048]{2,1,0:T(8,128)(2,1)S(1)} %get-tuple-element.58.w_own), channel_id=1, source_target_pairs={{0,3},{1,0},{2,1},{3,2},{4,7},{5,4},{6,5},{7,6},{8,11},{9,8},{10,9... | collective-permute-start | bytes 3145736 | tf_op jit(solution)/shard_map/ppermute | solution.py:428
  11.2 25.6 %collective-permute-start.13 = (bf16[2,128,2048]{2,1,0:T(8,128)(2,1)S(1)}, bf16[2,128,2048]{2,1,0:T(8,128)(2,1)S(1)}, u32[]{:S(2)}, u32[]{:S(2)}) collective-permute-start(bf16[2,128,2048]{2,1,0:T(8,128)(2,1)S(1)} %get-tuple-element.58.w_own), channel_id=1, source_target_pairs={{0,1},{1,2},{2,3},{3,0},{4,5},{5,6},{6,7},{7,4},{8,9},{9,10},{10,1... | collective-permute-start | bytes 3145736 | tf_op jit(solution)/shard_map/ppermute | solution.py:428
  15.3 1.4 %collective-permute-start.1 = (bf16[2,128,256]{2,1,0:T(8,128)(2,1)S(1)}, bf16[2,128,256]{2,1,0:T(8,128)(2,1)S(1)}, u32[]{:S(2)}, u32[]{:S(2)}) collective-permute-start(bf16[2,128,256]{2,1,0:T(8,128)(2,1)S(1)} %get-tuple-element.38), channel_id=1, source_target_pairs={{0,4},{4,0},{8,12},{12,8},{16,20},{20,16},{24,28},{28,24},{32,36},... | collective-permute-start | bytes 393224 | tf_op jit(solution)/shard_map/ppermute | solution.py:423
  17.0 5.9 %collective-permute-start.4 = (bf16[128,256]{1,0:T(8,128)(2,1)S(1)}, bf16[128,256]{1,0:T(8,128)(2,1)S(1)}, u32[]{:S(2)}, u32[]{:S(2)}) collective-permute-start(bf16[128,256]{1,0:T(8,128)(2,1)S(1)} %get-tuple-element.40), channel_id=1, source_target_pairs={{0,8},{4,12},{8,0},{12,4},{16,24},{20,28},{24,16},{28,20},{32,40},... | collective-permute-start | bytes 196616 | tf_op jit(solution)/shard_map/ppermute | solution.py:423
  18.7 7.6 %collective-permute-start.2 = (bf16[128,256]{1,0:T(8,128)(2,1)S(1)}, bf16[128,256]{1,0:T(8,128)(2,1)S(1)}, u32[]{:S(2)}, u32[]{:S(2)}) collective-permute-start(bf16[128,256]{1,0:T(8,128)(2,1)S(1)} %get-tuple-element.40), channel_id=1, source_target_pairs={{0,24},{4,28},{8,16},{12,20},{16,8},{20,12},{24,0},{28,4},{32,56},... | collective-permute-start | bytes 196616 | tf_op jit(solution)/shard_map/ppermute | solution.py:423
  22.7 6.9 %collective-permute-start.3 = (bf16[128,256]{1,0:T(8,128)(2,1)S(1)}, bf16[128,256]{1,0:T(8,128)(2,1)S(1)}, u32[]{:S(2)}, u32[]{:S(2)}) collective-permute-start(bf16[128,256]{1,0:T(8,128)(2,1)S(1)} %get-tuple-element.39.own_ref), channel_id=1, source_target_pairs={{0,16},{4,20},{8,24},{12,28},{16,0},{20,4},{24,8},{28,12},{32,48},... | collective-permute-start | bytes 196616 | tf_op jit(solution)/shard_map/ppermute | solution.py:423
  30.0 5.4 %collective-permute-start.5 = (bf16[128,256]{1,0:T(8,128)(2,1)S(1)}, bf16[128,256]{1,0:T(8,128)(2,1)S(1)}, u32[]{:S(2)}, u32[]{:S(2)}) collective-permute-start(bf16[128,256]{1,0:T(8,128)(2,1)S(1)} %get-tuple-element.41.own_ref), channel_id=1, source_target_pairs={{0,48},{4,52},{8,56},{12,60},{16,32},{20,36},{24,40},{28,44},{32,1... | collective-permute-start | bytes 196616 | tf_op jit(solution)/shard_map/ppermute | solution.py:423
  35.5 4.2 %collective-permute-start.6 = (bf16[128,256]{1,0:T(8,128)(2,1)S(1)}, bf16[128,256]{1,0:T(8,128)(2,1)S(1)}, u32[]{:S(2)}, u32[]{:S(2)}) collective-permute-start(bf16[128,256]{1,0:T(8,128)(2,1)S(1)} %get-tuple-element.43.own_ref), channel_id=1, source_target_pairs={{0,64},{4,68},{8,72},{12,76},{16,80},{20,84},{24,88},{28,92},{32,9... | collective-permute-start | bytes 196616 | tf_op jit(solution)/shard_map/ppermute | solution.py:423
  36.9 20.5 %collective-permute-start.16 = (bf16[128,2048]{1,0:T(8,128)(2,1)S(1)}, bf16[128,2048]{1,0:T(8,128)(2,1)S(1)}, u32[]{:S(2)}, u32[]{:S(2)}) collective-permute-start(bf16[128,2048]{1,0:T(8,128)(2,1)S(1)} %slice_bitcast_fusion), channel_id=1, source_target_pairs={{0,3},{1,0},{2,1},{3,2},{4,7},{5,4},{6,5},{7,6},{8,11},{9,8},{10,9... | collective-permute-start | bytes 1572872 | tf_op jit(solution)/shard_map/ppermute | solution.py:428
  39.7 17.8 %collective-permute-start.15 = (bf16[128,2048]{1,0:T(8,128)(2,1)S(1)}, bf16[128,2048]{1,0:T(8,128)(2,1)S(1)}, u32[]{:S(2)}, u32[]{:S(2)}) collective-permute-start(bf16[128,2048]{1,0:T(8,128)(2,1)S(1)} %slice_bitcast_fusion.1), channel_id=1, source_target_pairs={{0,1},{1,2},{2,3},{3,0},{4,5},{5,6},{6,7},{7,4},{8,9},{9,10},{10,1... | collective-permute-start | bytes 1572872 | tf_op jit(solution)/shard_map/ppermute | solution.py:428
  39.8 5.8 %collective-permute-start.7 = (bf16[128,128]{1,0:T(8,128)(2,1)S(1)}, bf16[128,128]{1,0:T(8,128)(2,1)S(1)}, u32[]{:S(2)}, u32[]{:S(2)}) collective-permute-start(bf16[128,128]{1,0:T(8,128)(2,1)S(1)} %rows_state.1), channel_id=1, source_target_pairs={{0,192},{4,196},{8,200},{12,204},{16,208},{20,212},{24,216},{28,22... | collective-permute-start | bytes 98312 | tf_op jit(solution)/shard_map/ppermute | solution.py:423
  42.8 6.4 %collective-permute-start.9 = (bf16[2,2,256,128]{3,2,1,0:T(8,128)(2,1)S(1)}, bf16[2,2,256,128]{3,2,1,0:T(8,128)(2,1)S(1)}, u32[]{:S(2)}, u32[]{:S(2)}) collective-permute-start(bf16[2,2,256,128]{3,2,1,0:T(8,128)(2,1)S(1)} %get-tuple-element.53), channel_id=1, source_target_pairs={{0,4},{4,0},{8,12},{12,8},{16,20},{20,16},{24,28},{28,24},{32,36},... | collective-permute-start | bytes 786440 | tf_op jit(solution)/shard_map/ppermute | solution.py:423
  45.7 3.6 %copy-start.1 = (f32[512]{0:T(512)S(1)}, f32[512]{0:T(512)}, u32[]{:S(2)}) copy-start(f32[512]{0:T(512)} %param.12) | copy-start | bytes 6148
  46.1 3.1 %collective-permute-start.8 = (bf16[128,128]{1,0:T(8,128)(2,1)S(1)}, bf16[128,128]{1,0:T(8,128)(2,1)S(1)}, u32[]{:S(2)}, u32[]{:S(2)}) collective-permute-start(bf16[128,128]{1,0:T(8,128)(2,1)S(1)} %get-tuple-element.46), channel_id=1, source_target_pairs={{0,8},{4,12},{8,0},{12,4},{16,24},{20,28},{24,16},{28,20},{32,40},... | collective-permute-start | bytes 98312 | tf_op jit(solution)/shard_map/ppermute | solution.py:423
  49.9 5.5 %collective-permute-start.10 = (bf16[2,64,256]{2,1,0:T(8,128)(2,1)S(1)}, bf16[2,64,256]{2,1,0:T(8,128)(2,1)S(1)}, u32[]{:S(2)}, u32[]{:S(2)}) collective-permute-start(bf16[2,64,256]{2,1,0:T(8,128)(2,1)S(1)} %get-tuple-element.55), channel_id=1, source_target_pairs={{0,1},{1,2},{2,3},{3,0},{4,5},{5,6},{6,7},{7,4},{8,9},{9,10},{10,1... | collective-permute-start | bytes 196616 | tf_op jit(solution)/shard_map/ppermute | solution.py:428
  50.0 5.4 %collective-permute-start.11 = (bf16[2,64,256]{2,1,0:T(8,128)(2,1)S(1)}, bf16[2,64,256]{2,1,0:T(8,128)(2,1)S(1)}, u32[]{:S(2)}, u32[]{:S(2)}) collective-permute-start(bf16[2,64,256]{2,1,0:T(8,128)(2,1)S(1)} %get-tuple-element.56), channel_id=1, source_target_pairs={{0,3},{1,0},{2,1},{3,2},{4,7},{5,4},{6,5},{7,6},{8,11},{9,8},{10,9... | collective-permute-start | bytes 196616 | tf_op jit(solution)/shard_map/ppermute | solution.py:428
  52.7 4.7 %collective-permute-start.12 = (bf16[2,64,256]{2,1,0:T(8,128)(2,1)S(1)}, bf16[2,64,256]{2,1,0:T(8,128)(2,1)S(1)}, u32[]{:S(2)}, u32[]{:S(2)}) collective-permute-start(bf16[2,64,256]{2,1,0:T(8,128)(2,1)S(1)} %get-tuple-element.57), channel_id=1, source_target_pairs={{0,2},{1,3},{2,0},{3,1},{4,6},{5,7},{6,4},{7,5},{8,10},{9,11},{10,... | collective-permute-start | bytes 196616 | tf_op jit(solution)/shard_map/ppermute | solution.py:428
  58.2 5.2 %collective-permute-start.17 = (bf16[64,2048]{1,0:T(8,128)(2,1)S(1)}, bf16[64,2048]{1,0:T(8,128)(2,1)S(1)}, u32[]{:S(2)}, u32[]{:S(2)}) collective-permute-start(bf16[64,2048]{1,0:T(8,128)(2,1)S(1)} %get-tuple-element.62), channel_id=1, source_target_pairs={{0,4},{4,0},{8,12},{12,8},{16,20},{20,16},{24,28},{28,24},{32,36},... | collective-permute-start | bytes 786440 | tf_op jit(solution)/shard_map/ppermute | solution.py:423

commit v12 on v11

--- a/solution.py
+++ b/solution.py
@@ -36,7 +36,6 @@
     return jax.ShapeDtypeStruct(dims, kind)
 
 
-SHORT = pl.CostEstimate(flops=4_000_000_000, bytes_accessed=1 << 20, transcendentals=0)
 LONG = pl.CostEstimate(flops=60_000_000_000, bytes_accessed=1 << 20, transcendentals=0)
 
 
@@ -436,6 +435,8 @@
         projected, weights, edge, conv_weight, logits, beta_bias
     )
     sibling = swapped(send, 1)
+    base, gate, both = inner_outputs(projected, edge, conv_weight, keys_t, uw)
+    inner_in = swapped(both, 1)
     chip, send = small_call(
         chip_kernel, [MAP, MAP], "chip_map", [pltpu.VMEM((2, DK, 2 * DK), bf16)]
     )(maps, sibling)
@@ -444,15 +445,12 @@
         chip, diagonal, across, pair
     )
     row, before = small_call(far_kernel, [MAP, MAP], "far_map")(four, swapped(four, 12), near)
-    _, w_one, w_three = lax.optimization_barrier((row, w_one, w_three))
+    other_row = swapped(row, 16)
+    (two_rows,) = small_call(rows_kernel, [STATE], "rows_state")(row, other_row)
+    _, w_one, w_three = lax.optimization_barrier((two_rows, w_one, w_three))
     w_two = turned(w_one[0], "head", 1), turned(w_three[1], "head", 3)
-    other_row = swapped(row, 16)
-    (two_rows,) = small_call(rows_kernel, [STATE], "rows_state", (), LONG)(row, other_row)
-    _, edge = lax.optimization_barrier((two_rows, edge))
-    base, gate, both = inner_outputs(projected, edge, conv_weight, keys_t, uw)
-    inner_in = swapped(both, 1)
     rows = swapped(two_rows, 48)
-    state, send = small_call(pair_start_kernel, [STATE, STATE], "pair_start", (), SHORT)(
+    state, send = small_call(pair_start_kernel, [STATE, STATE], "pair_start", (), LONG)(
         rows, other_row, before, chip, pair
     )
     back = swapped(send, 2)

time: 64.4 us -> 66.3 us (1.030)
  waiting for transfers between devices: 20.9 us -> 23 us
    ppermute x8, waiting for transfers between devices: 3.65 us -> 5.78 us  [turned(): return lax.ppermute(x, axis, [(i, (i + by) % count) for i in range(count)])]
  transfers between devices with their start and end apart: 18 -> 18, of which waited for: 8 -> 7; matrix products, arithmetic and copies ran while one was open for 0% -> 0% of each run, Pallas kernels for 18% -> 18%
where the time goes in v12:
time: 66.3 us; the launch traced here: 66.1 us
  starting transfers between devices  28.8 us (43%)
  waiting for transfers between devices  23 us (35%)
  Pallas kernels  12.5 us (19%)
  local copies, waits for them, and re-layouts  0.85 us (1%)
  other arithmetic  0.75 us (1%)
    ppermute x10, waiting for transfers between devices, swapped(): lax.ppermute(x, 'ctx', [(i, i ^ by) for i in range(lax.axis_size('ctx'))])  17.3 us
    ppermute x10, starting transfers between devices, swapped(): lax.ppermute(x, 'ctx', [(i, i ^ by) for i in range(lax.axis_size('ctx'))])  16.3 us
    ppermute x8, starting transfers between devices, turned(): return lax.ppermute(x, axis, [(i, (i + by) % count) for i in range(count)])  12.5 us
    ppermute x8, waiting for transfers between devices, turned(): return lax.ppermute(x, axis, [(i, (i + by) % count) for i in range(count)])  5.78 us
    pallas_call x1, Pallas kernels, project(): pl.pallas_call(project_kernel, in_specs=[pl.BlockSpec(memory_space=pltpu....  4.62 us
    pallas_call x1, Pallas kernels, local_maps(): pl.pallas_call(local_kernel, in_specs=whole(6), out_specs=whole(5), out_s...  4.02 us
  transfers between devices with their start and end apart: 18, of which 7 were waited for; matrix products, arithmetic and copies ran while one was open for 0% of the time, Pallas kernels for 18%

profile of v12, /device:TPU:1, one launch (start us, length us, event | category | flops | bytes accessed | tf_op | source)
XLA Modules:
  0.0 66.1 jit_solution(9781023621820312495)
XLA Ops:
  0.0 0.8 %slice.9 = bf16[8,2048]{1,0:T(8,128)(2,1)S(1)} slice(bf16[256,2048]{1,0:T(8,128)(2,1)} %tokens_hbm.1), slice={[248:256], [0:2048]} | slice | bytes 65536 | tf_op jit(solution)/shard_map/slice | solution.py:431
  0.8 0.0 copy-start
  0.8 0.0 copy-start.2
  0.8 3.0 %collective-permute-start = (bf16[8,2048]{1,0:T(8,128)(2,1)S(1)}, bf16[8,2048]{1,0:T(8,128)(2,1)S(1)}, u32[]{:S(2)}, u32[]{:S(2)}) collective-permute-start(bf16[8,2048]{1,0:T(8,128)(2,1)S(1)} %slice.9), channel_id=1, source_target_pairs={{0,4},{4,8},{8,12},{12,16},{16,20},{20,24},{24,28},{28,32},{32,36}... | collective-permute-start | bytes 98312 | tf_op jit(solution)/shard_map/ppermute | solution.py:427
  3.8 4.6 %project.1 = (bf16[3,256,512]{2,1,0:T(8,128)(2,1)S(1)}, bf16[3,2048,512]{2,1,0:T(8,128)(2,1)S(1)}, f32[256,4]{1,0:T(8,128)S(1)}, bf16[2,128,2048]{2,1,0:T(8,128)(2,1)S(1)}) custom-call(bf16[256,2048]{1,0:T(8,128)(2,1)} %tokens_hbm.1, bf16[3,2048,512]{2,1,0:T(8,128)(2,1)} %w_hbm.1, bf16[4,2048]{1,0:T(4,128)(2,1)} %beta_w_hbm.1, bf16[512,2048]{1,0:T(8,128)(2,1)} %w_out_hbm.1), custom_call_target="tpu_custom_call" | custom-call | flops 60000002048 | bytes 1048576 | tf_op jit(solution)/shard_map/project/pallas_call | solution.py:83
  8.4 2.8 %collective-permute-start.14 = (bf16[2,128,2048]{2,1,0:T(8,128)(2,1)S(1)}, bf16[2,128,2048]{2,1,0:T(8,128)(2,1)S(1)}, u32[]{:S(2)}, u32[]{:S(2)}) collective-permute-start(bf16[2,128,2048]{2,1,0:T(8,128)(2,1)S(1)} %get-tuple-element.56.w_own), channel_id=1, source_target_pairs={{0,3},{1,0},{2,1},{3,2},{4,7},{5,4},{6,5},{7,6},{8,11},{9,8},{10,9... | collective-permute-start | bytes 3145736 | tf_op jit(solution)/shard_map/ppermute | solution.py:427
  11.2 0.0 collective-permute-start.13
  11.2 0.0 collective-permute-done.edge_ref
  11.2 0.0 copy-done
  11.2 0.0 copy-done.2
  11.3 4.0 %local_maps.1 = (f32[8,512]{1,0:T(8,128)S(1)}, bf16[4,128,256]{2,1,0:T(8,128)(2,1)S(1)}, bf16[4,256,256]{2,1,0:T(8,128)(2,1)S(1)}, bf16[2,128,256]{2,1,0:T(8,128)(2,1)S(1)}, bf16[2,128,256]{2,1,0:T(8,128)(2,1)S(1)}) custom-call(bf16[3,256,512]{2,1,0:T(8,128)(2,1)S(1)} %get-tuple-element.33.proj_ref, bf16[3,2048,512]{2,1,0:T(8,128)(2,1)S(1)} %get-tuple-element.34.w_ref, ...), custom_call_target="tpu_custom_call" | custom-call | flops 60000002048 | bytes 1048576 | tf_op jit(solution)/shard_map/local_maps/pallas_call | solution.py:220
  15.3 0.2 collective-permute-start.1
  15.5 1.3 %collective-permute-done.1.other_ref.other_maps = bf16[2,128,256]{2,1,0:T(8,128)(2,1)S(1)} collective-permute-done((bf16[2,128,256]{2,1,0:T(8,128)(2,1)S(1)}, bf16[2,128,256]{2,1,0:T(8,128)(2,1)S(1)}, u32[]{:S(2)}, u32[]{:S(2)}) %collective-permute-start.1) | collective-permute-done | bytes 131104 | tf_op jit(solution)/shard_map/ppermute | solution.py:422
  16.7 0.2 chip_map.1
  17.0 1.7 %collective-permute-start.4 = (bf16[128,256]{1,0:T(8,128)(2,1)S(1)}, bf16[128,256]{1,0:T(8,128)(2,1)S(1)}, u32[]{:S(2)}, u32[]{:S(2)}) collective-permute-start(bf16[128,256]{1,0:T(8,128)(2,1)S(1)} %get-tuple-element.39), channel_id=1, source_target_pairs={{0,8},{4,12},{8,0},{12,4},{16,24},{20,28},{24,16},{28,20},{32,40},... | collective-permute-start | bytes 196616 | tf_op jit(solution)/shard_map/ppermute | solution.py:422
  18.7 4.0 %collective-permute-start.2 = (bf16[128,256]{1,0:T(8,128)(2,1)S(1)}, bf16[128,256]{1,0:T(8,128)(2,1)S(1)}, u32[]{:S(2)}, u32[]{:S(2)}) collective-permute-start(bf16[128,256]{1,0:T(8,128)(2,1)S(1)} %get-tuple-element.39), channel_id=1, source_target_pairs={{0,24},{4,28},{8,16},{12,20},{16,8},{20,12},{24,0},{28,4},{32,56},... | collective-permute-start | bytes 196616 | tf_op jit(solution)/shard_map/ppermute | solution.py:422
  22.7 0.2 collective-permute-start.3
  22.9 0.0 collective-permute-done.4.pair_ref.other_ref
  22.9 3.4 %collective-permute-done.2.diagonal_ref = bf16[128,256]{1,0:T(8,128)(2,1)S(1)} collective-permute-done((bf16[128,256]{1,0:T(8,128)(2,1)S(1)}, bf16[128,256]{1,0:T(8,128)(2,1)S(1)}, u32[]{:S(2)}, u32[]{:S(2)}) %collective-permute-start.2) | collective-permute-done | bytes 65568 | tf_op jit(solution)/shard_map/ppermute | solution.py:422
  26.3 3.3 %collective-permute-done.3.across_ref = bf16[128,256]{1,0:T(8,128)(2,1)S(1)} collective-permute-done((bf16[128,256]{1,0:T(8,128)(2,1)S(1)}, bf16[128,256]{1,0:T(8,128)(2,1)S(1)}, u32[]{:S(2)}, u32[]{:S(2)}) %collective-permute-start.3) | collective-permute-done | bytes 65568 | tf_op jit(solution)/shard_map/ppermute | solution.py:422
  29.6 0.3 four_map.1
  30.0 0.3 collective-permute-start.5
  30.3 5.1 %collective-permute-done.5.other_ref = bf16[128,256]{1,0:T(8,128)(2,1)S(1)} collective-permute-done((bf16[128,256]{1,0:T(8,128)(2,1)S(1)}, bf16[128,256]{1,0:T(8,128)(2,1)S(1)}, u32[]{:S(2)}, u32[]{:S(2)}) %collective-permute-start.5) | collective-permute-done | bytes 65568 | tf_op jit(solution)/shard_map/ppermute | solution.py:422
  35.3 0.2 far_map.1
  35.5 1.5 %collective-permute-start.6 = (bf16[128,256]{1,0:T(8,128)(2,1)S(1)}, bf16[128,256]{1,0:T(8,128)(2,1)S(1)}, u32[]{:S(2)}, u32[]{:S(2)}) collective-permute-start(bf16[128,256]{1,0:T(8,128)(2,1)S(1)} %get-tuple-element.42.own_ref), channel_id=1, source_target_pairs={{0,64},{4,68},{8,72},{12,76},{16,80},{20,84},{24,88},{28,92},{32,9... | collective-permute-start | bytes 196616 | tf_op jit(solution)/shard_map/ppermute | solution.py:422
  37.0 1.1 %inner_outputs.1 = (f32[2,256,128]{2,1,0:T(8,128)S(1)}, bf16[2,256,128]{2,1,0:T(8,128)(2,1)S(1)}, bf16[2,2,256,128]{3,2,1,0:T(8,128)(2,1)S(1)}) custom-call(bf16[3,256,512]{2,1,0:T(8,128)(2,1)S(1)} %get-tuple-element.33.proj_ref, f32[8,512]{1,0:T(8,128)S(1)} %get-tuple-element.46.edge_ref, f32[3,4,512]{2,1,0:T(4,128)S(1)} %copy-done, ...), custom_call_target="tpu_custom_call" | custom-call | flops 201326592 | bytes 2097152 | tf_op jit(solution)/shard_map/inner_outputs/pallas_call | solution.py:268
  38.1 2.0 %collective-permute-start.9 = (bf16[2,2,256,128]{3,2,1,0:T(8,128)(2,1)S(1)}, bf16[2,2,256,128]{3,2,1,0:T(8,128)(2,1)S(1)}, u32[]{:S(2)}, u32[]{:S(2)}) collective-permute-start(bf16[2,2,256,128]{3,2,1,0:T(8,128)(2,1)S(1)} %get-tuple-element.51), channel_id=1, source_target_pairs={{0,4},{4,0},{8,12},{12,8},{16,20},{20,16},{24,28},{28,24},{32,36},... | collective-permute-start | bytes 786440 | tf_op jit(solution)/shard_map/ppermute | solution.py:422
  40.1 0.0 collective-permute-done.6.other_ref.row_ref
  40.1 0.2 rows_state.1
  40.3 1.9 %collective-permute-start.7 = (bf16[128,128]{1,0:T(8,128)(2,1)S(1)}, bf16[128,128]{1,0:T(8,128)(2,1)S(1)}, u32[]{:S(2)}, u32[]{:S(2)}) collective-permute-start(bf16[128,128]{1,0:T(8,128)(2,1)S(1)} %rows_state.1), channel_id=1, source_target_pairs={{0,192},{4,196},{8,200},{12,204},{16,208},{20,212},{24,216},{28,22... | collective-permute-start | bytes 98312 | tf_op jit(solution)/shard_map/ppermute | solution.py:422
  42.1 0.0 collective-permute-done.14.w_three
  42.1 0.0 collective-permute-done.13.w_one
  42.2 2.7 %collective-permute-start.16 = (bf16[128,2048]{1,0:T(8,128)(2,1)S(1)}, bf16[128,2048]{1,0:T(8,128)(2,1)S(1)}, u32[]{:S(2)}, u32[]{:S(2)}) collective-permute-start(bf16[128,2048]{1,0:T(8,128)(2,1)S(1)} %slice_bitcast_fusion), channel_id=1, source_target_pairs={{0,3},{1,0},{2,1},{3,2},{4,7},{5,4},{6,5},{7,6},{8,11},{9,8},{10,9... | collective-permute-start | bytes 1572872 | tf_op jit(solution)/shard_map/ppermute | solution.py:427
  45.0 0.0 collective-permute-start.15
  45.0 0.0 collective-permute-done.7.rows_ref
  45.0 0.0 copy-start.1
  45.0 0.4 pair_start.1
  45.4 0.1 collective-permute-start.8
  45.5 0.0 collective-permute-done.9.both_in
  45.5 3.0 %collective-permute-done.8.other_state = bf16[128,128]{1,0:T(8,128)(2,1)S(1)} collective-permute-done((bf16[128,128]{1,0:T(8,128)(2,1)S(1)}, bf16[128,128]{1,0:T(8,128)(2,1)S(1)}, u32[]{:S(2)}, u32[]{:S(2)}) %collective-permute-start.8) | collective-permute-done | bytes 32800 | tf_op jit(solution)/shard_map/ppermute | solution.py:422
  48.6 0.0 copy-done.1
  48.6 0.6 finish.1
  49.2 0.1 collective-permute-start.10
  49.3 2.7 %collective-permute-start.11 = (bf16[2,64,256]{2,1,0:T(8,128)(2,1)S(1)}, bf16[2,64,256]{2,1,0:T(8,128)(2,1)S(1)}, u32[]{:S(2)}, u32[]{:S(2)}) collective-permute-start(bf16[2,64,256]{2,1,0:T(8,128)(2,1)S(1)} %get-tuple-element.54), channel_id=1, source_target_pairs={{0,3},{1,0},{2,1},{3,2},{4,7},{5,4},{6,5},{7,6},{8,11},{9,8},{10,9... | collective-permute-start | bytes 196616 | tf_op jit(solution)/shard_map/ppermute | solution.py:427
  52.1 1.1 %collective-permute-start.12 = (bf16[2,64,256]{2,1,0:T(8,128)(2,1)S(1)}, bf16[2,64,256]{2,1,0:T(8,128)(2,1)S(1)}, u32[]{:S(2)}, u32[]{:S(2)}) collective-permute-start(bf16[2,64,256]{2,1,0:T(8,128)(2,1)S(1)} %get-tuple-element.55), channel_id=1, source_target_pairs={{0,2},{1,3},{2,0},{3,1},{4,6},{5,7},{6,4},{7,5},{8,10},{9,11},{10,... | collective-permute-start | bytes 196616 | tf_op jit(solution)/shard_map/ppermute | solution.py:427
  53.2 5.8 %collective-permute-done.10.one = bf16[2,64,256]{2,1,0:T(8,128)(2,1)S(1)} collective-permute-done((bf16[2,64,256]{2,1,0:T(8,128)(2,1)S(1)}, bf16[2,64,256]{2,1,0:T(8,128)(2,1)S(1)}, u32[]{:S(2)}, u32[]{:S(2)}) %collective-permute-start.10) | collective-permute-done | bytes 65568 | tf_op jit(solution)/shard_map/ppermute | solution.py:427
  58.9 0.0 collective-permute-done.11.three
  58.9 0.0 collective-permute-done.12.two
  58.9 0.0 collective-permute-done.16.w_two1
  58.9 0.0 collective-permute-done.15.w_two0
  58.9 0.7 %merge.1 = (f32[64,2048]{1,0:T(8,128)S(1)}, bf16[64,2048]{1,0:T(8,128)(2,1)S(1)}) custom-call(bf16[2,64,256]{2,1,0:T(8,128)(2,1)S(1)} %get-tuple-element.52.mine_ref, bf16[2,64,256]{2,1,0:T(8,128)(2,1)S(1)} %collective-permute-done.10.one, bf16[2,64,256]{2,1,0:T(8,128)(2,1)S(1)} %collective-permute-done.11.three, ...), custom_call_target="tpu_custom_call" | custom-call | tf_op jit(solution)/shard_map/merge/pallas_call | solution.py:416
  59.7 4.5 %collective-permute-start.17 = (bf16[64,2048]{1,0:T(8,128)(2,1)S(1)}, bf16[64,2048]{1,0:T(8,128)(2,1)S(1)}, u32[]{:S(2)}, u32[]{:S(2)}) collective-permute-start(bf16[64,2048]{1,0:T(8,128)(2,1)S(1)} %get-tuple-element.60), channel_id=1, source_target_pairs={{0,4},{4,0},{8,12},{12,8},{16,20},{20,16},{24,28},{28,24},{32,36},... | collective-permute-start | bytes 786440 | tf_op jit(solution)/shard_map/ppermute | solution.py:422
  64.2 1.2 %collective-permute-done.17 = bf16[64,2048]{1,0:T(8,128)(2,1)S(1)} collective-permute-done((bf16[64,2048]{1,0:T(8,128)(2,1)S(1)}, bf16[64,2048]{1,0:T(8,128)(2,1)S(1)}, u32[]{:S(2)}, u32[]{:S(2)}) %collective-permute-start.17) | collective-permute-done | bytes 262176 | tf_op jit(solution)/shard_map/ppermute | solution.py:422
  65.4 0.8 %add_convert_fusion = bf16[64,2048]{1,0:T(8,128)(2,1)} fusion(f32[64,2048]{1,0:T(8,128)S(1)} %get-tuple-element.59, bf16[64,2048]{1,0:T(8,128)(2,1)S(1)} %collective-permute-done.17), kind=kLoop, calls=%fused_computation | loop fusion | flops 393216 | bytes 1048576 | tf_op jit(solution)/shard_map/convert_element_type | solution.py:462
  (2 shorter events, 0.1 us)
Async XLA Ops:
  0.8 10.5 %copy-start = (f32[3,4,512]{2,1,0:T(4,128)S(1)}, f32[3,4,512]{2,1,0:T(4,128)}, u32[]{:S(2)}) copy-start(f32[3,4,512]{2,1,0:T(4,128)} %conv_ref.3) | copy-start | bytes 73732
  0.8 10.5 %copy-start.2 = (f32[4]{0:T(128)S(1)}, f32[4]{0:T(128)}, u32[]{:S(2)}) copy-start(f32[4]{0:T(128)} %param.11) | copy-start | bytes 52
  0.8 10.5 %collective-permute-start = (bf16[8,2048]{1,0:T(8,128)(2,1)S(1)}, bf16[8,2048]{1,0:T(8,128)(2,1)S(1)}, u32[]{:S(2)}, u32[]{:S(2)}) collective-permute-start(bf16[8,2048]{1,0:T(8,128)(2,1)S(1)} %slice.9), channel_id=1, source_target_pairs={{0,4},{4,8},{8,12},{12,16},{16,20},{20,24},{24,28},{28,32},{32,36}... | collective-permute-start | bytes 98312 | tf_op jit(solution)/shard_map/ppermute | solution.py:427
  8.4 33.7 %collective-permute-start.14 = (bf16[2,128,2048]{2,1,0:T(8,128)(2,1)S(1)}, bf16[2,128,2048]{2,1,0:T(8,128)(2,1)S(1)}, u32[]{:S(2)}, u32[]{:S(2)}) collective-permute-start(bf16[2,128,2048]{2,1,0:T(8,128)(2,1)S(1)} %get-tuple-element.56.w_own), channel_id=1, source_target_pairs={{0,3},{1,0},{2,1},{3,2},{4,7},{5,4},{6,5},{7,6},{8,11},{9,8},{10,9... | collective-permute-start | bytes 3145736 | tf_op jit(solution)/shard_map/ppermute | solution.py:427
  11.2 30.9 %collective-permute-start.13 = (bf16[2,128,2048]{2,1,0:T(8,128)(2,1)S(1)}, bf16[2,128,2048]{2,1,0:T(8,128)(2,1)S(1)}, u32[]{:S(2)}, u32[]{:S(2)}) collective-permute-start(bf16[2,128,2048]{2,1,0:T(8,128)(2,1)S(1)} %get-tuple-element.56.w_own), channel_id=1, source_target_pairs={{0,1},{1,2},{2,3},{3,0},{4,5},{5,6},{6,7},{7,4},{8,9},{9,10},{10,1... | collective-permute-start | bytes 3145736 | tf_op jit(solution)/shard_map/ppermute | solution.py:427
  15.3 1.4 %collective-permute-start.1 = (bf16[2,128,256]{2,1,0:T(8,128)(2,1)S(1)}, bf16[2,128,256]{2,1,0:T(8,128)(2,1)S(1)}, u32[]{:S(2)}, u32[]{:S(2)}) collective-permute-start(bf16[2,128,256]{2,1,0:T(8,128)(2,1)S(1)} %get-tuple-element.37), channel_id=1, source_target_pairs={{0,4},{4,0},{8,12},{12,8},{16,20},{20,16},{24,28},{28,24},{32,36},... | collective-permute-start | bytes 393224 | tf_op jit(solution)/shard_map/ppermute | solution.py:422
  17.0 5.9 %collective-permute-start.4 = (bf16[128,256]{1,0:T(8,128)(2,1)S(1)}, bf16[128,256]{1,0:T(8,128)(2,1)S(1)}, u32[]{:S(2)}, u32[]{:S(2)}) collective-permute-start(bf16[128,256]{1,0:T(8,128)(2,1)S(1)} %get-tuple-element.39), channel_id=1, source_target_pairs={{0,8},{4,12},{8,0},{12,4},{16,24},{20,28},{24,16},{28,20},{32,40},... | collective-permute-start | bytes 196616 | tf_op jit(solution)/shard_map/ppermute | solution.py:422
  18.7 7.6 %collective-permute-start.2 = (bf16[128,256]{1,0:T(8,128)(2,1)S(1)}, bf16[128,256]{1,0:T(8,128)(2,1)S(1)}, u32[]{:S(2)}, u32[]{:S(2)}) collective-permute-start(bf16[128,256]{1,0:T(8,128)(2,1)S(1)} %get-tuple-element.39), channel_id=1, source_target_pairs={{0,24},{4,28},{8,16},{12,20},{16,8},{20,12},{24,0},{28,4},{32,56},... | collective-permute-start | bytes 196616 | tf_op jit(solution)/shard_map/ppermute | solution.py:422
  22.7 6.9 %collective-permute-start.3 = (bf16[128,256]{1,0:T(8,128)(2,1)S(1)}, bf16[128,256]{1,0:T(8,128)(2,1)S(1)}, u32[]{:S(2)}, u32[]{:S(2)}) collective-permute-start(bf16[128,256]{1,0:T(8,128)(2,1)S(1)} %get-tuple-element.38.own_ref), channel_id=1, source_target_pairs={{0,16},{4,20},{8,24},{12,28},{16,0},{20,4},{24,8},{28,12},{32,48},... | collective-permute-start | bytes 196616 | tf_op jit(solution)/shard_map/ppermute | solution.py:422
  30.0 5.4 %collective-permute-start.5 = (bf16[128,256]{1,0:T(8,128)(2,1)S(1)}, bf16[128,256]{1,0:T(8,128)(2,1)S(1)}, u32[]{:S(2)}, u32[]{:S(2)}) collective-permute-start(bf16[128,256]{1,0:T(8,128)(2,1)S(1)} %get-tuple-element.40.own_ref), channel_id=1, source_target_pairs={{0,48},{4,52},{8,56},{12,60},{16,32},{20,36},{24,40},{28,44},{32,1... | collective-permute-start | bytes 196616 | tf_op jit(solution)/shard_map/ppermute | solution.py:422
  35.5 4.6 %collective-permute-start.6 = (bf16[128,256]{1,0:T(8,128)(2,1)S(1)}, bf16[128,256]{1,0:T(8,128)(2,1)S(1)}, u32[]{:S(2)}, u32[]{:S(2)}) collective-permute-start(bf16[128,256]{1,0:T(8,128)(2,1)S(1)} %get-tuple-element.42.own_ref), channel_id=1, source_target_pairs={{0,64},{4,68},{8,72},{12,76},{16,80},{20,84},{24,88},{28,92},{32,9... | collective-permute-start | bytes 196616 | tf_op jit(solution)/shard_map/ppermute | solution.py:422
  38.1 7.4 %collective-permute-start.9 = (bf16[2,2,256,128]{3,2,1,0:T(8,128)(2,1)S(1)}, bf16[2,2,256,128]{3,2,1,0:T(8,128)(2,1)S(1)}, u32[]{:S(2)}, u32[]{:S(2)}) collective-permute-start(bf16[2,2,256,128]{3,2,1,0:T(8,128)(2,1)S(1)} %get-tuple-element.51), channel_id=1, source_target_pairs={{0,4},{4,0},{8,12},{12,8},{16,20},{20,16},{24,28},{28,24},{32,36},... | collective-permute-start | bytes 786440 | tf_op jit(solution)/shard_map/ppermute | solution.py:422
  40.3 4.7 %collective-permute-start.7 = (bf16[128,128]{1,0:T(8,128)(2,1)S(1)}, bf16[128,128]{1,0:T(8,128)(2,1)S(1)}, u32[]{:S(2)}, u32[]{:S(2)}) collective-permute-start(bf16[128,128]{1,0:T(8,128)(2,1)S(1)} %rows_state.1), channel_id=1, source_target_pairs={{0,192},{4,196},{8,200},{12,204},{16,208},{20,212},{24,216},{28,22... | collective-permute-start | bytes 98312 | tf_op jit(solution)/shard_map/ppermute | solution.py:422
  42.2 16.7 %collective-permute-start.16 = (bf16[128,2048]{1,0:T(8,128)(2,1)S(1)}, bf16[128,2048]{1,0:T(8,128)(2,1)S(1)}, u32[]{:S(2)}, u32[]{:S(2)}) collective-permute-start(bf16[128,2048]{1,0:T(8,128)(2,1)S(1)} %slice_bitcast_fusion), channel_id=1, source_target_pairs={{0,3},{1,0},{2,1},{3,2},{4,7},{5,4},{6,5},{7,6},{8,11},{9,8},{10,9... | collective-permute-start | bytes 1572872 | tf_op jit(solution)/shard_map/ppermute | solution.py:427
  45.0 14.0 %collective-permute-start.15 = (bf16[128,2048]{1,0:T(8,128)(2,1)S(1)}, bf16[128,2048]{1,0:T(8,128)(2,1)S(1)}, u32[]{:S(2)}, u32[]{:S(2)}) collective-permute-start(bf16[128,2048]{1,0:T(8,128)(2,1)S(1)} %slice_bitcast_fusion.1), channel_id=1, source_target_pairs={{0,1},{1,2},{2,3},{3,0},{4,5},{5,6},{6,7},{7,4},{8,9},{9,10},{10,1... | collective-permute-start | bytes 1572872 | tf_op jit(solution)/shard_map/ppermute | solution.py:427
  45.0 3.6 %copy-start.1 = (f32[512]{0:T(512)S(1)}, f32[512]{0:T(512)}, u32[]{:S(2)}) copy-start(f32[512]{0:T(512)} %param.12) | copy-start | bytes 6148
  45.4 3.1 %collective-permute-start.8 = (bf16[128,128]{1,0:T(8,128)(2,1)S(1)}, bf16[128,128]{1,0:T(8,128)(2,1)S(1)}, u32[]{:S(2)}, u32[]{:S(2)}) collective-permute-start(bf16[128,128]{1,0:T(8,128)(2,1)S(1)} %get-tuple-element.45), channel_id=1, source_target_pairs={{0,8},{4,12},{8,0},{12,4},{16,24},{20,28},{24,16},{28,20},{32,40},... | collective-permute-start | bytes 98312 | tf_op jit(solution)/shard_map/ppermute | solution.py:422
  49.2 9.7 %collective-permute-start.10 = (bf16[2,64,256]{2,1,0:T(8,128)(2,1)S(1)}, bf16[2,64,256]{2,1,0:T(8,128)(2,1)S(1)}, u32[]{:S(2)}, u32[]{:S(2)}) collective-permute-start(bf16[2,64,256]{2,1,0:T(8,128)(2,1)S(1)} %get-tuple-element.53), channel_id=1, source_target_pairs={{0,1},{1,2},{2,3},{3,0},{4,5},{5,6},{6,7},{7,4},{8,9},{9,10},{10,1... | collective-permute-start | bytes 196616 | tf_op jit(solution)/shard_map/ppermute | solution.py:427
  49.3 9.6 %collective-permute-start.11 = (bf16[2,64,256]{2,1,0:T(8,128)(2,1)S(1)}, bf16[2,64,256]{2,1,0:T(8,128)(2,1)S(1)}, u32[]{:S(2)}, u32[]{:S(2)}) collective-permute-start(bf16[2,64,256]{2,1,0:T(8,128)(2,1)S(1)} %get-tuple-element.54), channel_id=1, source_target_pairs={{0,3},{1,0},{2,1},{3,2},{4,7},{5,4},{6,5},{7,6},{8,11},{9,8},{10,9... | collective-permute-start | bytes 196616 | tf_op jit(solution)/shard_map/ppermute | solution.py:427
  52.1 6.9 %collective-permute-start.12 = (bf16[2,64,256]{2,1,0:T(8,128)(2,1)S(1)}, bf16[2,64,256]{2,1,0:T(8,128)(2,1)S(1)}, u32[]{:S(2)}, u32[]{:S(2)}) collective-permute-start(bf16[2,64,256]{2,1,0:T(8,128)(2,1)S(1)} %get-tuple-element.55), channel_id=1, source_target_pairs={{0,2},{1,3},{2,0},{3,1},{4,6},{5,7},{6,4},{7,5},{8,10},{9,11},{10,... | collective-permute-start | bytes 196616 | tf_op jit(solution)/shard_map/ppermute | solution.py:427
  59.7 5.7 %collective-permute-start.17 = (bf16[64,2048]{1,0:T(8,128)(2,1)S(1)}, bf16[64,2048]{1,0:T(8,128)(2,1)S(1)}, u32[]{:S(2)}, u32[]{:S(2)}) collective-permute-start(bf16[64,2048]{1,0:T(8,128)(2,1)S(1)} %get-tuple-element.60), channel_id=1, source_target_pairs={{0,4},{4,0},{8,12},{12,8},{16,20},{20,16},{24,28},{28,24},{32,36},... | collective-permute-start | bytes 786440 | tf_op jit(solution)/shard_map/ppermute | solution.py:422
